TPU v7x, 32 devices: a whole 2x2x4 slice. The times are simulated.
32 devices in a mesh: ctx: 16 (over z, x, core), fsdp: 2 (over y).
Axes of the slice: x: 2, y: 2, z: 4, core: 2. Of those that a mesh axis runs over, the one named last changes fastest.
Arguments:
- block_input: bfloat16 [2, 2048, 2048], P('fsdp', 'ctx'), may hold values from -36 to 36
- query_weight: bfloat16 [2048, 2048], P(('ctx', 'fsdp')), may hold values from -0.125 to 0.125
- key_weight: bfloat16 [2048, 1024], P(('ctx', 'fsdp')), may hold values from -0.125 to 0.125
- value_weight: bfloat16 [2048, 1024], P(('ctx', 'fsdp')), may hold values from -0.125 to 0.125
- output_weight: bfloat16 [2048, 2048], P(('ctx', 'fsdp')), may hold values from -0.375 to 0.375
- gate_weight: bfloat16 [2048, 6144], P(('ctx', 'fsdp')), may hold values from -0.125 to 0.125
- up_weight: bfloat16 [2048, 6144], P(('ctx', 'fsdp')), may hold values from -0.125 to 0.125
- down_weight: bfloat16 [2048, 6144], P(('ctx', 'fsdp')), may hold values from -0.078125 to 0.078125
- attn_gain: float32 [2048], replicated, may hold values from 0.5 to 1.5
- mlp_gain: float32 [2048], replicated, may hold values from 0.5 to 1.5
- query_gain: float32 [128], replicated, may hold values from 0.7 to 2.2
- key_gain: float32 [128], replicated, may hold values from 0.7 to 2.2
- block_order: int32 [32], replicated, may hold values from 0 to 31, each once
- cotangent: bfloat16 [2, 2048, 2048], P('fsdp', 'ctx'), may hold values from -18 to 18
Outputs:
- block_output: bfloat16 [2, 2048, 2048], P('fsdp', 'ctx')
- input_grad: float32 [2, 2048, 2048], P('fsdp', 'ctx')
- query_weight_grad: float32 [2048, 2048], P(('ctx', 'fsdp'))
- key_weight_grad: float32 [2048, 1024], P(('ctx', 'fsdp'))
- value_weight_grad: float32 [2048, 1024], P(('ctx', 'fsdp'))
- output_weight_grad: float32 [2048, 2048], P(('ctx', 'fsdp'))
- gate_weight_grad: float32 [2048, 6144], P(('ctx', 'fsdp'))
- up_weight_grad: float32 [2048, 6144], P(('ctx', 'fsdp'))
- down_weight_grad: float32 [2048, 6144], P(('ctx', 'fsdp'))
- attn_gain_grad: float32 [2048], replicated
- mlp_gain_grad: float32 [2048], replicated
- query_gain_grad: float32 [128], replicated
- key_gain_grad: float32 [128], replicated
Inputs may be any that keep to these rules, and one draw needn't show every extreme that they name: `block_order`: each value appears exactly once.
All inputs are finite; a program needn't handle non-finite values.
Results may differ from a plain program's by a relative error of at most 0.025.
Values may be sent and summed in bfloat16 or wider, within the bound.
No kernel may reach another device: no remote copies, remote signals or barrier semaphores. Data moves between devices by JAX's collectives and lax.ppermute only.
A program may use at most 512 MiB of HBM per device.

v0:
```python
import math

import jax
import jax.numpy as jnp
from jax import lax
from jax.sharding import PartitionSpec as P

eps_model = 1e-06
rope_base = 1000000.0


def inv_root(field):
    return lax.rsqrt(jnp.mean(field * field, axis=-1, keepdims=True) + eps_model)


def norm_back(field, factor, gain, grad_in):
    weighted = gain * grad_in
    inner_mean = jnp.mean(weighted * field, axis=-1, keepdims=True)
    return factor * weighted - field * (factor * factor * factor) * inner_mean


def rope_tables(positions, head_size):
    half_size = head_size // 2
    exponent = jnp.arange(half_size, dtype=jnp.float32) * jnp.float32(2.0 / head_size)
    inverse = jnp.exp(-exponent * jnp.float32(math.log(rope_base)))
    angles = positions.astype(jnp.float32)[:, None] * inverse[None, :]
    return (jnp.cos(angles)[:, None, :], jnp.sin(angles)[:, None, :])


def rotate(field, cosine, sine):
    first_half, second_half = jnp.split(field, 2, axis=-1)
    return jnp.concatenate(
        [first_half * cosine - second_half * sine, second_half * cosine + first_half * sine],
        axis=-1,
    )


def rotate_back(grad_in, cosine, sine):
    first_half, second_half = jnp.split(grad_in, 2, axis=-1)
    return jnp.concatenate(
        [first_half * cosine + second_half * sine, second_half * cosine - first_half * sine],
        axis=-1,
    )


def slot_positions(block_order, first_index, count, half_rows):
    row_index = first_index + jnp.arange(count, dtype=jnp.int32)
    slot_index = row_index // half_rows
    table = jnp.arange(block_order.shape[0], dtype=jnp.int32)
    picked = jnp.sum(
        jnp.where(slot_index[:, None] == table[None, :], block_order[None, :], 0), axis=1
    )
    return picked * half_rows + row_index % half_rows


def outer_rows(left, right):
    return lax.dot_general(
        left, right, (((0,), (0,)), ((), ())), preferred_element_type=jnp.float32
    )


def keep_state(state):
    return state


def stacked_terms(top_left, top_right, low_left, low_right):
    rows = top_left.shape[0]
    left = jnp.concatenate([top_left, low_left], axis=0)
    upper = jnp.concatenate(
        [top_right, jnp.zeros((rows, low_right.shape[1]), top_right.dtype)], axis=1
    )
    lower = jnp.concatenate(
        [jnp.zeros((rows, top_right.shape[1]), low_right.dtype), low_right], axis=1
    )
    return (left, jnp.concatenate([upper, lower], axis=0))


def shards(
    block_input,
    query_weight,
    key_weight,
    value_weight,
    output_weight,
    gate_weight,
    up_weight,
    down_weight,
    attn_gain,
    mlp_gain,
    query_gain,
    key_gain,
    block_order,
    cotangent,
):
    f32 = jnp.float32
    bf16 = jnp.bfloat16
    ctx_size = lax.axis_size("ctx")
    ctx_rank = lax.axis_index("ctx")
    tokens = block_input.shape[1]
    half_rows = tokens // 2
    head_size = query_gain.shape[0]
    heads = query_weight.shape[1] // head_size
    kv_heads = key_weight.shape[1] // head_size
    group = heads // kv_heads
    kv_width = kv_heads * head_size
    hidden_units = gate_weight.shape[1]
    score_scale = 1.0 / math.sqrt(head_size)
    step_cap = max(tokens, 1024)
    forward_weights = (
        lax.all_gather(query_weight, ("ctx", "fsdp"), axis=0, tiled=True),
        lax.all_gather(key_weight, ("ctx", "fsdp"), axis=0, tiled=True),
        lax.all_gather(value_weight, ("ctx", "fsdp"), axis=0, tiled=True),
        lax.all_gather(output_weight, ("ctx", "fsdp"), axis=0, tiled=True),
        lax.all_gather(gate_weight, ("ctx", "fsdp"), axis=0, tiled=True),
        lax.all_gather(up_weight, ("ctx", "fsdp"), axis=0, tiled=True),
        lax.all_gather(down_weight, ("ctx", "fsdp"), axis=0, tiled=True),
    )
    full_query, full_key, full_value, full_output, full_gate, full_up, full_down = forward_weights
    query_pos = slot_positions(block_order, ctx_rank * tokens, tokens, half_rows)
    cosine, sine = rope_tables(query_pos, head_size)
    inputs32 = block_input[0].astype(f32)
    scale_attn = inv_root(inputs32)
    normed_attn = (inputs32 * scale_attn * attn_gain).astype(bf16)
    query_raw = jnp.dot(normed_attn, full_query, preferred_element_type=f32).reshape(
        tokens, heads, head_size
    )
    key_raw = jnp.dot(normed_attn, full_key, preferred_element_type=f32).reshape(
        tokens, kv_heads, head_size
    )
    value_bf = jnp.dot(normed_attn, full_value, preferred_element_type=f32).astype(bf16)
    scale_query = inv_root(query_raw)
    scale_key = inv_root(key_raw)
    query_flat = (
        rotate(query_raw * scale_query * query_gain, cosine, sine)
        .astype(bf16)
        .reshape(tokens, kv_heads, group, head_size)
    )
    query_rot = jnp.transpose(query_flat, (1, 2, 0, 3))
    key_rot = rotate(key_raw * scale_key * key_gain, cosine, sine).astype(bf16)
    keyvals = jnp.concatenate([key_rot.reshape(tokens, kv_width), value_bf], axis=1)

    def attend_block(state, key_block, key_pos):
        weighted_sum, exp_total = state
        block_rows = key_block.shape[0]
        key_heads = key_block[:, :kv_width].reshape(block_rows, kv_heads, head_size)
        value_heads = key_block[:, kv_width:].reshape(block_rows, kv_heads, head_size)
        scores = (
            jnp.einsum("gjqd,kgd->gjqk", query_rot, key_heads, preferred_element_type=f32)
            * score_scale
        )
        allowed = key_pos[None, :] <= query_pos[:, None]
        exp_scores = jnp.where(allowed, jnp.exp(scores), 0.0)
        exp_total = exp_total + jnp.sum(exp_scores, axis=-1)
        weighted_sum = weighted_sum + jnp.einsum(
            "gjqk,kgd->gjqd", exp_scores.astype(bf16), value_heads, preferred_element_type=f32
        )
        return (weighted_sum, exp_total)

    start_sum = jnp.zeros((kv_heads, group, tokens, head_size), f32)
    start_total = jnp.zeros((kv_heads, group, tokens), f32)
    shard_rows = lax.all_gather(keyvals, "ctx", axis=0, tiled=True)
    row_count = shard_rows.shape[0]
    step_rows = math.gcd(row_count, step_cap)

    def turn_step(turn_index, state):
        first_row = turn_index * step_rows
        key_block = lax.dynamic_slice_in_dim(shard_rows, first_row, step_rows, 0)
        key_pos = slot_positions(block_order, first_row, step_rows, half_rows)
        return lax.cond(
            jnp.min(key_pos) <= jnp.max(query_pos),
            lambda inner: attend_block(inner, key_block, key_pos),
            keep_state,
            state,
        )

    weighted_sum, exp_total = lax.fori_loop(
        0, row_count // step_rows, turn_step, (start_sum, start_total)
    )
    attn_heads = weighted_sum / exp_total[..., None]
    attn_four = attn_heads.astype(bf16)
    attn_bf = jnp.transpose(attn_four, (2, 0, 1, 3)).reshape(tokens, heads * head_size)
    log_total = jnp.log(exp_total)
    hidden_one = inputs32 + jnp.einsum(
        "th,dh->td", attn_bf, full_output, preferred_element_type=f32
    )
    scale_mlp = inv_root(hidden_one)
    normed_mlp = (hidden_one * scale_mlp * mlp_gain).astype(bf16)
    gate_pre = jnp.dot(normed_mlp, full_gate, preferred_element_type=f32)
    up_pre = jnp.dot(normed_mlp, full_up, preferred_element_type=f32)
    activated = (jax.nn.silu(gate_pre) * up_pre).astype(bf16)
    block_out = (
        hidden_one + jnp.einsum("tf,df->td", activated, full_down, preferred_element_type=f32)
    ).astype(bf16)
    back_gate, back_up, back_down = (
        lax.all_gather(gate_weight, ("ctx", "fsdp"), axis=0, tiled=True),
        lax.all_gather(up_weight, ("ctx", "fsdp"), axis=0, tiled=True),
        lax.all_gather(down_weight, ("ctx", "fsdp"), axis=0, tiled=True),
    )
    grad_bf = cotangent[0]
    act_grad = jnp.dot(grad_bf, back_down, preferred_element_type=f32)
    sigma = jax.nn.sigmoid(gate_pre)
    gate_grad_in = (act_grad * up_pre * sigma * (1.0 + gate_pre * (1.0 - sigma))).astype(bf16)
    up_grad_in = (act_grad * gate_pre * sigma).astype(bf16)
    normed_mlp_grad = jnp.einsum(
        "tf,df->td", gate_grad_in, back_gate, preferred_element_type=f32
    ) + jnp.einsum("tf,df->td", up_grad_in, back_up, preferred_element_type=f32)
    mlp_gain_part = jnp.sum(normed_mlp_grad * hidden_one * scale_mlp, axis=0)
    hidden_grad = grad_bf.astype(f32) + norm_back(hidden_one, scale_mlp, mlp_gain, normed_mlp_grad)
    hidden_grad_bf = hidden_grad.astype(bf16)
    mlp_left, mlp_right = stacked_terms(
        normed_mlp, jnp.concatenate([gate_grad_in, up_grad_in], axis=1), grad_bf, activated
    )
    mlp_summed = lax.psum_scatter(
        outer_rows(mlp_left, mlp_right), ("ctx", "fsdp"), scatter_dimension=0, tiled=True
    )
    back_query, back_key, back_value, back_output = (
        lax.all_gather(query_weight, ("ctx", "fsdp"), axis=0, tiled=True),
        lax.all_gather(key_weight, ("ctx", "fsdp"), axis=0, tiled=True),
        lax.all_gather(value_weight, ("ctx", "fsdp"), axis=0, tiled=True),
        lax.all_gather(output_weight, ("ctx", "fsdp"), axis=0, tiled=True),
    )
    attn_grad = jnp.dot(hidden_grad_bf, back_output, preferred_element_type=f32).astype(bf16)
    grad_heads = jnp.transpose(attn_grad.reshape(tokens, kv_heads, group, head_size), (1, 2, 0, 3))
    delta_heads = jnp.sum(grad_heads.astype(f32) * attn_four.astype(f32), axis=-1)

    def block_grads(key_block, key_pos, query_grad):
        block_rows = key_block.shape[0]

        def work_block(grad_in):
            key_heads = key_block[:, :kv_width].reshape(block_rows, kv_heads, head_size)
            value_heads = key_block[:, kv_width:].reshape(block_rows, kv_heads, head_size)
            scores = (
                jnp.einsum("gjqd,kgd->gjqk", query_rot, key_heads, preferred_element_type=f32)
                * score_scale
            )
            allowed = key_pos[None, :] <= query_pos[:, None]
            probs = jnp.where(allowed, jnp.exp(scores - log_total[..., None]), 0.0)
            value_part = jnp.einsum(
                "gjqk,gjqd->kgd", probs.astype(bf16), grad_heads, preferred_element_type=f32
            )
            d_probs = jnp.einsum(
                "gjqd,kgd->gjqk", grad_heads, value_heads, preferred_element_type=f32
            )
            d_scores = (probs * (d_probs - delta_heads[..., None])).astype(bf16)
            grad_next = (
                grad_in
                + jnp.einsum("gjqk,kgd->gjqd", d_scores, key_heads, preferred_element_type=f32)
                * score_scale
            )
            key_part = (
                jnp.einsum("gjqk,gjqd->kgd", d_scores, query_rot, preferred_element_type=f32)
                * score_scale
            )
            return (
                grad_next,
                jnp.concatenate(
                    [
                        key_part.reshape(block_rows, kv_width),
                        value_part.reshape(block_rows, kv_width),
                    ],
                    axis=1,
                ),
            )

        def skip_block(grad_in):
            return (grad_in, jnp.zeros((block_rows, 2 * kv_width), f32))

        return lax.cond(jnp.min(key_pos) <= jnp.max(query_pos), work_block, skip_block, query_grad)

    zero_query = jnp.zeros((kv_heads, group, tokens, head_size), f32)
    start_buffer = jnp.zeros((tokens * ctx_size, 2 * kv_width), f32)
    fold_shard_rows = lax.all_gather(keyvals, "ctx", axis=0, tiled=True)
    row_count = fold_shard_rows.shape[0]
    fold_step_rows = math.gcd(row_count, step_cap)

    def turn_step(turn_index, state):
        query_grad, key_buffer = state
        first_row = turn_index * fold_step_rows
        key_block = lax.dynamic_slice_in_dim(fold_shard_rows, first_row, fold_step_rows, 0)
        key_pos = slot_positions(block_order, first_row, fold_step_rows, half_rows)
        query_grad, block_grad = block_grads(key_block, key_pos, query_grad)
        key_buffer = lax.dynamic_update_slice_in_dim(key_buffer, block_grad, first_row, 0)
        return (query_grad, key_buffer)

    query_grad, key_buffer = lax.fori_loop(
        0, row_count // fold_step_rows, turn_step, (zero_query, start_buffer)
    )
    key_grads = lax.psum_scatter(key_buffer, "ctx", scatter_dimension=0, tiled=True)
    query_flat_grad = jnp.transpose(query_grad, (2, 0, 1, 3)).reshape(tokens, heads, head_size)
    query_normed_grad = rotate_back(query_flat_grad, cosine, sine)
    key_normed_grad = rotate_back(
        key_grads[:, :kv_width].reshape(tokens, kv_heads, head_size), cosine, sine
    )
    query_gain_part = jnp.sum(query_normed_grad * query_raw * scale_query, axis=(0, 1))
    key_gain_part = jnp.sum(key_normed_grad * key_raw * scale_key, axis=(0, 1))
    query_pre_grad = (
        norm_back(query_raw, scale_query, query_gain, query_normed_grad)
        .reshape(tokens, heads * head_size)
        .astype(bf16)
    )
    key_pre_grad = (
        norm_back(key_raw, scale_key, key_gain, key_normed_grad)
        .reshape(tokens, kv_width)
        .astype(bf16)
    )
    value_pre_grad = key_grads[:, kv_width:].astype(bf16)
    normed_attn_grad = (
        jnp.einsum("th,dh->td", query_pre_grad, back_query, preferred_element_type=f32)
        + jnp.einsum("th,dh->td", key_pre_grad, back_key, preferred_element_type=f32)
        + jnp.einsum("th,dh->td", value_pre_grad, back_value, preferred_element_type=f32)
    )
    attn_gain_part = jnp.sum(normed_attn_grad * inputs32 * scale_attn, axis=0)
    input_grad = hidden_grad + norm_back(inputs32, scale_attn, attn_gain, normed_attn_grad)
    first_grads = jnp.concatenate([query_pre_grad, key_pre_grad, value_pre_grad], axis=1)
    attn_left, attn_right = stacked_terms(normed_attn, first_grads, hidden_grad_bf, attn_bf)
    attn_summed = lax.psum_scatter(
        outer_rows(attn_left, attn_right), ("ctx", "fsdp"), scatter_dimension=0, tiled=True
    )
    gain_sums = lax.psum(
        (attn_gain_part, mlp_gain_part, query_gain_part, key_gain_part), ("ctx", "fsdp")
    )
    query_cols = heads * head_size
    query_part = attn_summed[:, :query_cols]
    key_part = attn_summed[:, query_cols : query_cols + kv_width]
    value_part = attn_summed[:, query_cols + kv_width : query_cols + 2 * kv_width]
    output_part = attn_summed[:, query_cols + 2 * kv_width :]
    gate_part = mlp_summed[:, :hidden_units]
    up_part = mlp_summed[:, hidden_units : 2 * hidden_units]
    down_part = mlp_summed[:, 2 * hidden_units :]
    return (
        block_out[None],
        input_grad[None],
        query_part,
        key_part,
        value_part,
        output_part,
        gate_part,
        up_part,
        down_part,
        gain_sums[0],
        gain_sums[1],
        gain_sums[2],
        gain_sums[3],
    )


def solution(mesh):
    in_specs = (
        P("fsdp", "ctx", None),
        P(("ctx", "fsdp"), None),
        P(("ctx", "fsdp"), None),
        P(("ctx", "fsdp"), None),
        P(("ctx", "fsdp"), None),
        P(("ctx", "fsdp"), None),
        P(("ctx", "fsdp"), None),
        P(("ctx", "fsdp"), None),
        P(),
        P(),
        P(),
        P(),
        P(),
        P("fsdp", "ctx", None),
    )
    out_specs = (
        P("fsdp", "ctx", None),
        P("fsdp", "ctx", None),
        P(("ctx", "fsdp"), None),
        P(("ctx", "fsdp"), None),
        P(("ctx", "fsdp"), None),
        P(("ctx", "fsdp"), None),
        P(("ctx", "fsdp"), None),
        P(("ctx", "fsdp"), None),
        P(("ctx", "fsdp"), None),
        P(),
        P(),
        P(),
        P(),
    )
    return jax.shard_map(shards, mesh=mesh, in_specs=in_specs, out_specs=out_specs, check_vma=False)
```

profile of v0, /device:TPU:9, one launch (start us, length us, event | category | flops | bytes accessed | tf_op | source)
XLA Modules:
  0.0 2864.6 jit_solution(12603607756975838349)
XLA Ops:
  13.5 61.1 %all-gather.9.cloned.1.call-done = bf16[2048,1024]{1,0:T(8,128)(2,1)} async-done(((bf16[64,1024]{1,0:T(8,128)(2,1)}), bf16[2048,1024]{1,0:T(8,128)(2,1)}) %all-gather.9.cloned.1.call-update) | async-done | bytes 4194320 | tf_op jit(solution)/shard_map/all_gather | solution.py:110
  74.5 6.5 copy.71
  81.1 3.5 multiply_reduce_fusion.9
  85.8 52.3 %all-gather.11.cloned.1.call-done = bf16[2048,1024]{1,0:T(8,128)(2,1)} async-done(((bf16[64,1024]{1,0:T(8,128)(2,1)}), bf16[2048,1024]{1,0:T(8,128)(2,1)}) %all-gather.11.cloned.1.call-update) | async-done | bytes 4194320 | tf_op jit(solution)/shard_map/all_gather | solution.py:111
  138.1 2.9 convolution_convert_fusion.1
  145.4 71.9 %all-gather.15.cloned.1.call-done = bf16[2048,2048]{1,0:T(8,128)(2,1)} async-done(((bf16[64,2048]{1,0:T(8,128)(2,1)}), bf16[2048,2048]{1,0:T(8,128)(2,1)}) %all-gather.15.cloned.1.call-update) | async-done | bytes 8388624 | tf_op jit(solution)/shard_map/all_gather | solution.py:109
  217.3 12.3 copy.73
  229.6 5.9 multiply_reduce_fusion.6
  237.1 55.7 %all-gather.13.cloned.1.call-done = bf16[2048,2048]{1,0:T(8,128)(2,1)} async-done(((bf16[128,2048]{1,0:T(8,128)(2,1)}), bf16[2048,2048]{1,0:T(8,128)(2,1)}) %all-gather.13.cloned.1.call-update) | async-done | bytes 8388624 | tf_op jit(solution)/shard_map/all_gather | solution.py:160
  292.8 12.3 copy.74
  305.2 19.6 while.37
  307.2 7.6 conditional.4
  307.5 2.7 constant_dynamic-slice_fusion
  310.2 2.1 fusion
  312.2 2.6 fusion.7
  316.9 7.6 conditional.4
  317.2 2.7 constant_dynamic-slice_fusion
  319.8 2.1 fusion
  321.9 2.6 fusion.7
  325.3 46.7 %all-gather.17.cloned.1.call-done = bf16[2048,2048]{1,0:T(8,128)(2,1)} async-done(((bf16[64,2048]{1,0:T(8,128)(2,1)}), bf16[2048,2048]{1,0:T(8,128)(2,1)}) %all-gather.17.cloned.1.call-update) | async-done | bytes 8388624 | tf_op jit(solution)/shard_map/all_gather | solution.py:112
  372.1 6.4 multiply_reduce_fusion.5
  378.6 147.6 %all-gather.21.cloned.1.call-done = bf16[2048,6144]{1,0:T(8,128)(2,1)} async-done(((bf16[64,6144]{1,0:T(8,128)(2,1)}), bf16[2048,6144]{1,0:T(8,128)(2,1)}) %all-gather.21.cloned.1.call-update) | async-done | bytes 25165840 | tf_op jit(solution)/shard_map/all_gather | solution.py:114
  526.2 13.2 fusion.114
  539.4 142.5 %all-gather.19.cloned.1.call-done = bf16[2048,6144]{1,0:T(8,128)(2,1)} async-done(((bf16[64,6144]{1,0:T(8,128)(2,1)}), bf16[2048,6144]{1,0:T(8,128)(2,1)}) %all-gather.19.cloned.1.call-update) | async-done | bytes 25165840 | tf_op jit(solution)/shard_map/all_gather | solution.py:113
  681.9 13.2 fusion.113
  695.2 142.5 %all-gather.23.cloned.1.call-done = bf16[2048,6144]{1,0:T(8,128)(2,1)} async-done(((bf16[64,6144]{1,0:T(8,128)(2,1)}), bf16[2048,6144]{1,0:T(8,128)(2,1)}) %all-gather.23.cloned.1.call-update) | async-done | bytes 25165840 | tf_op jit(solution)/shard_map/all_gather | solution.py:115
  837.7 14.9 multiply_convert_fusion
  852.6 14.6 fusion.115
  867.3 14.6 multiply_reduce_fusion.1
  881.9 1.3 fusion.104
  884.1 4.8 convolution_convert_fusion
  889.4 7.9 broadcast_in_dim.158
  897.3 53.7 %while.38 = (s32[]{:T(128)}, f32[8,2,128,128]{3,2,1,0:T(8,128)S(1)}, f32[2048,2048]{0,1:T(8,128)}, s32[32]{0:T(128)S(1)}, s32[]{:T(128)}, /*index=5*/s32[128]{0:...) while((s32[]{:T(128)}, ...), condition=%wide.region_20.21_spmd, body=%wide.region_15.20_spmd.sunk | while | flops 2709256192 | bytes 99009984 | solution.py:284
  899.5 16.4 conditional.5
  899.7 2.7 fusion.107
  903.7 3.0 fusion.18
  906.7 1.8 fusion.20
  908.5 1.8 fusion.26
  910.3 1.5 bitcast_multiply_fusion.1
  911.8 4.1 pad_maximum_fusion
  915.9 8.3 constant_dynamic-update-slice_fusion.2
  926.2 16.4 conditional.5
  926.5 2.7 fusion.107
  930.5 3.0 fusion.18
  933.5 1.8 fusion.20
  935.3 1.8 fusion.26
  937.1 1.5 bitcast_multiply_fusion.1
  938.6 4.1 pad_maximum_fusion
  942.7 8.3 constant_dynamic-update-slice_fusion.2
  952.4 1.4 multiply_add_fusion
  954.7 173.1 %reduce-scatter.4.cloned.1.call-done = f32[128,2048]{0,1:T(8,128)} async-done(((f32[2048,2048]{0,1:T(8,128)}), f32[128,2048]{0,1:T(8,128)}) %reduce-scatter.4.cloned.1.call-update) | async-done | bytes 1048592 | tf_op jit(solution)/shard_map/reduce_scatter | solution.py:287
  1130.5 20.5 fusion.49
  1153.4 80.0 %fusion.37 = f32[2048,18432]{1,0:T(8,128)} fusion(bf16[128,6144]{1,0:T(8,128)(2,1)S(1)} %copy-done.9, bf16[128,6144]{1,0:T(8,128)(2,1)} %broadcast_in_dim.161, bf16[128,6144]{1,0:T(8,128)(2,1)} %get-tuple-element.687, bf16[128,6144]{1,0:T(8,128)(2,1)S(1)} %copy-done.8, bf16[128,2048]{1,0:T(8,128)(2,1)} %bitcast.183, bf16[128,2048]{1,0:T(8,128)(2,1)} %copy-done.10), kind=kOutput, calls=%fused_computation.63 | convolution fusion | flops 19376635904 | bytes 158334976 | tf_op jit(solution)/shard_map/dot_general | solution.py:57
  1234.5 7.4 fusion.116
  1241.9 14.1 fusion.61
  1256.0 4.5 convolution_add_fusion.1
  1260.5 1.7 fusion.77
  1262.3 44.6 %all-reduce.2 = (f32[2048]{0:T(1024)}, f32[2048]{0:T(1024)}, f32[128]{0:T(128)}, f32[128]{0:T(128)}) all-reduce(f32[2048]{0:T(1024)S(1)} %get-tuple-element.627, f32[2048]{0:T(1024)S(1)} %copy-done.38, f32[128]{0:T(128)S(1)} %get-tuple-element.623, f32[128]{0:T(128)S(1)} %get-tuple-element.629), channel_id=1, replica_groups=mesh['ctx'=16,'fsdp'=2] {'ctx','fsdp'}, use_global_device_ids=true, to_apply=%region_28.29 | all-reduce | flops 4352 | bytes 34816 | tf_op jit(solution)/shard_map/psum | solution.py:318
  1306.9 1.4 fusion.74
  1308.3 274.2 %reduce-scatter.6.cloned.1.call-done = f32[64,6144]{1,0:T(8,128)} async-done(((f32[2048,6144]{1,0:T(8,128)}), f32[64,6144]{1,0:T(8,128)}) %reduce-scatter.6.cloned.1.call-update) | async-done | bytes 1572880 | tf_op jit(solution)/shard_map/reduce_scatter | solution.py:315
  1582.5 1.9 fusion.110
  1584.4 2.3 fusion.109
  1586.7 1266.5 %reduce-scatter.8.cloned.1.call-done = f32[64,18432]{1,0:T(8,128)} async-done(((f32[2048,18432]{1,0:T(8,128)}), f32[64,18432]{1,0:T(8,128)}) %reduce-scatter.8.cloned.1.call-update) | async-done | bytes 4718608 | tf_op jit(solution)/shard_map/reduce_scatter | solution.py:212
  2853.2 4.6 fusion.108
  (180 shorter events, 29.9 us)
Async XLA Ops:
  7.2 67.4 %all-gather.9.cloned.1.call-start = ((), (), s32[]{:S(2)}) async-start(), calls=%async_computation.3 | async-start | bytes 4325376 | tf_op jit(solution)/shard_map/all_gather | solution.py:110
  7.9 130.2 %all-gather.11.cloned.1.call-start = ((), (), s32[]{:S(2)}) async-start(), calls=%async_computation.4 | async-start | bytes 4325376 | tf_op jit(solution)/shard_map/all_gather | solution.py:111
  8.7 208.6 %all-gather.15.cloned.1.call-start = ((), (), s32[]{:S(2)}) async-start(), calls=%async_computation.6 | async-start | bytes 8650752 | tf_op jit(solution)/shard_map/all_gather | solution.py:109
  9.4 283.4 %all-gather.13.cloned.1.call-start = ((), (), s32[]{:S(2)}) async-start(), calls=%async_computation.5 | async-start | bytes 8912896 | tf_op jit(solution)/shard_map/all_gather | solution.py:160
  12.0 217.6 %copy-start.40 = (f32[128]{0:T(128)}, f32[128]{0:T(128)S(1)}, u32[]{:S(2)}) copy-start(f32[128]{0:T(128)S(1)} %get-tuple-element.712) | copy-start | bytes 1540
  12.2 224.2 %copy-start.25 = (f32[128,64]{0,1:T(8,128)}, f32[128,64]{0,1:T(8,128)S(1)}, u32[]{:S(2)}) copy-start(f32[128,64]{0,1:T(8,128)S(1)} %get-tuple-element.709) | copy-start | bytes 98308
  12.2 224.2 %copy-start.27 = (f32[128,64]{0,1:T(8,128)}, f32[128,64]{0,1:T(8,128)S(1)}, u32[]{:S(2)}) copy-start(f32[128,64]{0,1:T(8,128)S(1)} %get-tuple-element.710) | copy-start | bytes 98308
  13.4 124.6 %copy-start.17 = (bf16[128,2048]{1,0:T(8,128)(2,1)}, bf16[128,2048]{1,0:T(8,128)(2,1)S(1)}, u32[]{:S(2)}) copy-start(bf16[128,2048]{1,0:T(8,128)(2,1)S(1)} %fusion.70) | copy-start | bytes 1572868
  74.5 6.6 copy-start.2
  74.5 6.6 copy-start.29
  81.1 4.3 copy-start.42
  84.6 0.8 copy-start.13
  85.3 56.5 %copy-start.34 = (f32[128,8]{0,1:T(8,128)}, f32[128,8]{0,1:T(8,128)S(1)}, u32[]{:S(2)}) copy-start(f32[128,8]{0,1:T(8,128)S(1)} %get-tuple-element.708) | copy-start | bytes 12292
  141.8 230.2 %all-gather.17.cloned.1.call-start = ((), (), s32[]{:S(2)}) async-start(), calls=%async_computation.7 | async-start | bytes 8650752 | tf_op jit(solution)/shard_map/all_gather | solution.py:112
  142.4 383.8 %all-gather.21.cloned.1.call-start = ((), (), s32[]{:S(2)}) async-start(), calls=%async_computation.9 | async-start | bytes 25952256 | tf_op jit(solution)/shard_map/all_gather | solution.py:114
  143.0 538.9 %all-gather.19.cloned.1.call-start = ((), (), s32[]{:S(2)}) async-start(), calls=%async_computation.8 | async-start | bytes 25952256 | tf_op jit(solution)/shard_map/all_gather | solution.py:113
  143.8 693.9 %all-gather.23.cloned.1.call-start = ((), (), s32[]{:S(2)}) async-start(), calls=%async_computation.10 | async-start | bytes 25952256 | tf_op jit(solution)/shard_map/all_gather | solution.py:115
  144.5 983.3 %reduce-scatter.4.cloned.1.call-start = ((), (), s32[]{:S(2)}) async-start(), calls=%async_computation.11 | async-start | bytes 17825792 | tf_op jit(solution)/shard_map/reduce_scatter | solution.py:287
  229.6 6.6 copy-start.44
  235.5 1.1 copy-start.4
  236.2 0.6 copy-start.31
  237.1 68.1 %copy-start.36 = (s32[32]{0:T(128)S(1)}, s32[32]{0:T(128)}, u32[]{:S(2)}) copy-start(s32[32]{0:T(128)} %param.34) | copy-start | bytes 388
  325.1 46.9 %copy-start.11 = (f32[8,2,128,128]{2,3,1,0:T(8,128)}, f32[8,2,128,128]{2,3,1,0:T(8,128)S(1)}, u32[]{:S(2)}) copy-start(f32[8,2,128,128]{2,3,1,0:T(8,128)S(1)} %copy.76) | copy-start | bytes 3145732
  325.3 53.1 %copy-start.21 = (bf16[8,2,128,128]{2,3,1,0:T(8,128)(2,1)}, bf16[8,2,128,128]{2,3,1,0:T(8,128)(2,1)S(1)}, u32[]{:S(2)}) copy-start(bf16[8,2,128,128]{2,3,1,0:T(8,128)(2,1)S(1)} %divide_convert_fusion) | copy-start | bytes 1572868
  372.1 6.4 copy-start.33
  378.4 503.5 %copy-start = (f32[128,2048]{1,0:T(8,128)}, f32[128,2048]{1,0:T(8,128)S(1)}, u32[]{:S(2)}) copy-start(f32[128,2048]{1,0:T(8,128)S(1)} %get-tuple-element.720) | copy-start | bytes 3145732
  378.6 303.3 %copy-start.10 = (bf16[128,2048]{1,0:T(8,128)(2,1)}, bf16[128,2048]{1,0:T(8,128)(2,1)S(1)}, u32[]{:S(2)}) copy-start(bf16[128,2048]{1,0:T(8,128)(2,1)S(1)} %multiply_convert_fusion.3) | copy-start | bytes 1572868
  852.6 14.6 copy-start.7
  867.3 14.7 copy-start.23
  883.3 0.8 copy-start.15
  884.1 5.0 copy-start.12
  950.9 1.4 copy-start.26
  950.9 1.4 copy-start.28
  951.0 2.8 copy-start.5
  951.0 2.8 copy-start.32
  951.0 2.8 copy-start.45
  951.0 3.3 copy-start.37
  951.0 631.5 %reduce-scatter.6.cloned.1.call-start = ((), (), s32[]{:S(2)}) async-start(), calls=%async_computation.12 | async-start | bytes 51904512 | tf_op jit(solution)/shard_map/reduce_scatter | solution.py:315
  952.4 176.6 %copy-start.14 = (f32[128,8,128]{0,2,1:T(8,128)S(1)}, f32[128,8,128]{0,2,1:T(8,128)}, u32[]{:S(2)}) copy-start(f32[128,8,128]{0,2,1:T(8,128)} %copy-done.13) | copy-start | bytes 1572868
  952.4 176.6 %copy-start.35 = (f32[128,8]{0,1:T(8,128)S(1)}, f32[128,8]{0,1:T(8,128)}, u32[]{:S(2)}) copy-start(f32[128,8]{0,1:T(8,128)} %copy-done.34) | copy-start | bytes 12292
  952.4 176.6 %copy-start.43 = (f32[128]{0:T(128)S(1)}, f32[128]{0:T(128)}, u32[]{:S(2)}) copy-start(f32[128]{0:T(128)} %param.33) | copy-start | bytes 1540
  953.8 175.3 %copy-start.39 = (f32[128,8]{0,1:T(8,128)S(1)}, f32[128,8]{0,1:T(8,128)}, u32[]{:S(2)}) copy-start(f32[128,8]{0,1:T(8,128)} %get-tuple-element.707) | copy-start | bytes 12292
  954.3 176.2 %copy-start.16 = (bf16[128,2048]{1,0:T(8,128)(2,1)S(1)}, bf16[128,2048]{1,0:T(8,128)(2,1)}, u32[]{:S(2)}) copy-start(bf16[128,2048]{1,0:T(8,128)(2,1)} %copy-done.15) | copy-start | bytes 1572868
  954.3 176.2 %copy-start.18 = (bf16[128,2048]{1,0:T(8,128)(2,1)S(1)}, bf16[128,2048]{1,0:T(8,128)(2,1)}, u32[]{:S(2)}) copy-start(bf16[128,2048]{1,0:T(8,128)(2,1)} %copy-done.17) | copy-start | bytes 1572868
  954.6 196.3 %copy-start.19 = (bf16[128,16,128]{0,2,1:T(8,128)(2,1)}, bf16[128,16,128]{0,2,1:T(8,128)(2,1)S(1)}, u32[]{:S(2)}) copy-start(bf16[128,16,128]{0,2,1:T(8,128)(2,1)S(1)} %subtract_convert_fusion) | copy-start | bytes 1572868
  1150.9 2.0 copy-start.8
  1150.9 2.4 copy-start.9
  1151.0 1702.2 %reduce-scatter.8.cloned.1.call-start = ((), (), s32[]{:S(2)}) async-start(), calls=%async_computation.13 | async-start | bytes 155713536 | tf_op jit(solution)/shard_map/reduce_scatter | solution.py:212
  1233.4 1.0 copy-start.20
  1234.5 7.4 copy-start.1
  1256.0 4.5 copy-start.3
  1256.0 4.5 copy-start.6
  1256.0 4.5 copy-start.24
  1256.0 4.5 copy-start.30
  1256.0 4.5 copy-start.41
  1260.5 1.8 copy-start.38
  1260.5 46.3 %copy-start.22 = (f32[128,2048]{1,0:T(8,128)S(1)}, f32[128,2048]{1,0:T(8,128)}, u32[]{:S(2)}) copy-start(f32[128,2048]{1,0:T(8,128)} %get-tuple-element.678) | copy-start | bytes 3145732
  1260.5 46.3 %copy-start.46 = (f32[128]{0:T(128)S(1)}, f32[128]{0:T(128)}, u32[]{:S(2)}) copy-start(f32[128]{0:T(128)} %get-tuple-element.711) | copy-start | bytes 1540
Sparse Core Ops, SparseCore 0:
  10.9 63.5 all-gather.8
  77.4 60.6 all-gather.10
  141.2 76.0 all-gather.14
  219.9 72.8 all-gather.12
  295.7 76.2 all-gather.16
  374.8 151.3 all-gather.20
  529.1 152.8 all-gather.18
  684.8 152.8 all-gather.22
  951.1 176.6 reduce-scatter.3
  1151.1 431.3 reduce-scatter.5
  1589.0 1264.1 reduce-scatter.7
where the time goes:
time: 2870 us; the launch traced here: 2860 us
  waiting for transfers between devices  2440 us (85%)
  matrix products  250 us (9%)
  local copies, waits for them, and re-layouts  84.5 us (3%)
  blocking collectives  44.6 us (2%)
    reduce_scatter x1, waiting for transfers between devices, shards(): lax.psum_scatter(outer_rows(mlp_left, mlp_right), ('ctx', 'fsdp'), scatte...  1270 us
    reduce_scatter x1, waiting for transfers between devices, shards(): lax.psum_scatter(outer_rows(attn_left, attn_right), ('ctx', 'fsdp'), scat...  274 us
    reduce_scatter x1, waiting for transfers between devices, shards(): lax.psum_scatter(key_buffer, 'ctx', scatter_dimension=0, tiled=True)  173 us
    all_gather x1, waiting for transfers between devices, shards(): lax.all_gather(up_weight, ('ctx', 'fsdp'), axis=0, tiled=True)  148 us
    all_gather x1, waiting for transfers between devices, shards(): lax.all_gather(down_weight, ('ctx', 'fsdp'), axis=0, tiled=True)  143 us
    all_gather x1, waiting for transfers between devices, shards(): lax.all_gather(gate_weight, ('ctx', 'fsdp'), axis=0, tiled=True)  143 us
    dot_general x2, matrix products, outer_rows(): lax.dot_general(left, right, (((0,), (0,)), ((), ())), preferred_element_...  100 us
    all_gather x1, waiting for transfers between devices, shards(): lax.all_gather(query_weight, ('ctx', 'fsdp'), axis=0, tiled=True)  71.9 us
  transfers between devices with their start and end apart: 11, of which 11 were waited for; matrix products, arithmetic and copies ran while one was open for 8% of the time, Pallas kernels for 0%

commit v1 on v0

v1 whole, which is shorter than its diff:
```python
import functools
import math

import jax
import jax.numpy as jnp
from jax import lax
from jax.experimental import pallas as pl
from jax.experimental.pallas import tpu as pltpu
from jax.sharding import PartitionSpec as P

eps_model = 1e-06
rope_base = 1000000.0
f32 = jnp.float32
bf16 = jnp.bfloat16


def inv_root(field):
    return lax.rsqrt(jnp.mean(field * field, axis=-1, keepdims=True) + eps_model)


def norm_back(field, factor, gain, grad_in):
    weighted = gain * grad_in
    inner_mean = jnp.mean(weighted * field, axis=-1, keepdims=True)
    return factor * weighted - field * (factor * factor * factor) * inner_mean


def rope_tables(positions, head_size):
    half_size = head_size // 2
    exponent = jnp.arange(half_size, dtype=f32) * f32(2.0 / head_size)
    inverse = jnp.exp(-exponent * f32(math.log(rope_base)))
    angles = positions.astype(f32)[:, None] * inverse[None, :]
    return jnp.cos(angles), jnp.sin(angles)


def rotate(field, cosine, sine):
    first_half, second_half = jnp.split(field, 2, axis=-1)
    return jnp.concatenate(
        [first_half * cosine - second_half * sine, second_half * cosine + first_half * sine],
        axis=-1,
    )


def rotate_back(grad_in, cosine, sine):
    first_half, second_half = jnp.split(grad_in, 2, axis=-1)
    return jnp.concatenate(
        [first_half * cosine + second_half * sine, second_half * cosine - first_half * sine],
        axis=-1,
    )


def dot_nn(left, right):
    return lax.dot_general(left, right, (((1,), (0,)), ((), ())), preferred_element_type=f32)


def dot_nt(left, right):
    return lax.dot_general(left, right, (((1,), (1,)), ((), ())), preferred_element_type=f32)


def dot_tn(left, right):
    return lax.dot_general(left, right, (((0,), (0,)), ((), ())), preferred_element_type=f32)


def sort_rows(source, target, table, blocks, rows):
    def move(index, carry):
        start = pl.multiple_of(table[index] * rows, rows)
        place = pl.multiple_of(index * rows, rows)
        target[pl.ds(place, rows), :] = source[pl.ds(start, rows), :]
        return carry

    lax.fori_loop(0, blocks, move, 0)


def unsort_rows(source, target, table, blocks, rows):
    def move(index, carry):
        start = pl.multiple_of(table[index] * rows, rows)
        place = pl.multiple_of(index * rows, rows)
        target[pl.ds(start, rows), :] = source[pl.ds(place, rows), :]
        return carry

    lax.fori_loop(0, blocks, move, 0)


def allowed_tile(key_first, query_tile, pos_table, tile_k, tile_q, rows, sorted_all):
    key_pos = key_first + lax.broadcasted_iota(jnp.int32, (tile_k, tile_q), 0)
    lane = lax.broadcasted_iota(jnp.int32, (1, tile_q), 1)
    if sorted_all:
        query_pos = query_tile * tile_q + lane
    else:
        per_tile = tile_q // rows
        query_pos = jnp.zeros((1, tile_q), jnp.int32)
        for piece in range(per_tile):
            first = pos_table[query_tile * per_tile + piece] * rows
            inside = (lane >= piece * rows) & (lane < (piece + 1) * rows)
            query_pos = jnp.where(inside, first + lane - piece * rows, query_pos)
    return key_pos <= query_pos


def tile_loop(query_tile, key_tiles, sorted_all, work):
    if sorted_all:
        for key_tile in range(query_tile):
            work(key_tile, False)
        work(query_tile, True)
    else:

        @pl.loop(0, key_tiles)
        def _(key_tile):
            work(key_tile, True)


def query_loop(query_tiles, sorted_all, work):
    if sorted_all:
        for query_tile in range(query_tiles):
            work(query_tile)
    else:

        @pl.loop(0, query_tiles)
        def _(query_tile):
            work(query_tile)


def attend_kernel(
    geometry, key_table, query_table, pos_table, q_ref, k_ref, v_ref, out_ref, lse_ref,
    q_sorted, k_sorted, v_sorted, v_turned, acc, total, out_sorted,
):
    rows, tile, sorted_all, scale = geometry
    keys, queries = k_ref.shape[0], q_ref.shape[0]
    key_tiles, query_tiles = keys // tile, queries // tile
    sort_rows(k_ref, k_sorted, key_table, keys // rows, rows)
    sort_rows(v_ref, v_sorted, key_table, keys // rows, rows)
    sort_rows(q_ref, q_sorted, query_table, queries // rows, rows)
    for key_tile in range(key_tiles):
        piece = v_sorted[key_tile * tile : (key_tile + 1) * tile, :]
        v_turned[:, key_tile * tile : (key_tile + 1) * tile] = piece.astype(f32).T.astype(bf16)

    def query_work(query_tile):
        q_start = pl.multiple_of(query_tile * tile, tile)
        q_tile = q_sorted[pl.ds(q_start, tile), :]
        acc[...] = jnp.zeros_like(acc)
        total[...] = jnp.zeros_like(total)

        def work(key_tile, masked):
            k_start = pl.multiple_of(key_tile * tile, tile)
            scores = dot_nt(k_sorted[pl.ds(k_start, tile), :], q_tile)
            probs = jnp.exp(scores * scale)
            if masked:
                keep = allowed_tile(k_start, query_tile, pos_table, tile, tile, rows, sorted_all)
                probs = jnp.where(keep, probs, 0.0)
            total[...] += jnp.sum(probs, axis=0, keepdims=True)
            acc[...] += dot_nn(v_turned[:, pl.ds(k_start, tile)], probs.astype(bf16))

        tile_loop(query_tile, key_tiles, sorted_all, work)
        lse_ref[:, pl.ds(q_start, tile)] = jnp.log(total[...])
        out_sorted[pl.ds(q_start, tile), :] = (acc[...] / total[...]).T.astype(bf16)

    query_loop(query_tiles, sorted_all, query_work)
    unsort_rows(out_sorted, out_ref, query_table, queries // rows, rows)


def attend(tables, query_rot, key_rot, value, rows, sorted_all, scale):
    queries, head = query_rot.shape
    keys = key_rot.shape[0]
    tile = math.gcd(math.gcd(queries, keys), 512)
    whole = lambda shape: pl.BlockSpec(shape, lambda i, *_: (0, 0))
    return pl.pallas_call(
        functools.partial(attend_kernel, (rows, tile, sorted_all, scale)),
        out_shape=(
            jax.ShapeDtypeStruct((queries, head), bf16),
            jax.ShapeDtypeStruct((1, queries), f32),
        ),
        grid_spec=pltpu.PrefetchScalarGridSpec(
            num_scalar_prefetch=3,
            grid=(1,),
            in_specs=[whole((queries, head)), whole((keys, head)), whole((keys, head))],
            out_specs=(whole((queries, head)), whole((1, queries))),
            scratch_shapes=[
                pltpu.VMEM((queries, head), bf16),
                pltpu.VMEM((keys, head), bf16),
                pltpu.VMEM((keys, head), bf16),
                pltpu.VMEM((head, keys), bf16),
                pltpu.VMEM((head, tile), f32),
                pltpu.VMEM((1, tile), f32),
                pltpu.VMEM((queries, head), bf16),
            ],
        ),
        compiler_params=pltpu.CompilerParams(vmem_limit_bytes=48 * 2**20),
        cost_estimate=pl.CostEstimate(
            flops=2 * queries * keys * head, bytes_accessed=8 * keys * head, transcendentals=queries * keys // 2
        ),
        name="attend",
    )(*tables, query_rot, key_rot, value)


def attend_back_kernel(
    geometry, key_table, query_table, pos_table, q_ref, k_ref, v_ref, o_ref, do_ref, lse_ref,
    dq_ref, dk_ref, dv_ref,
    q_sorted, k_sorted, v_sorted, do_sorted, o_sorted, k_turned, delta, dq_turned, dq_sorted, dk_sorted, dv_sorted,
):
    rows, tile, sorted_all, scale = geometry
    keys, queries = k_ref.shape[0], q_ref.shape[0]
    key_tiles, query_tiles = keys // tile, queries // tile
    sort_rows(k_ref, k_sorted, key_table, keys // rows, rows)
    sort_rows(v_ref, v_sorted, key_table, keys // rows, rows)
    sort_rows(q_ref, q_sorted, query_table, queries // rows, rows)
    sort_rows(do_ref, do_sorted, query_table, queries // rows, rows)
    sort_rows(o_ref, o_sorted, query_table, queries // rows, rows)
    for key_tile in range(key_tiles):
        piece = k_sorted[key_tile * tile : (key_tile + 1) * tile, :]
        k_turned[:, key_tile * tile : (key_tile + 1) * tile] = piece.astype(f32).T.astype(bf16)
    dk_sorted[...] = jnp.zeros_like(dk_sorted)
    dv_sorted[...] = jnp.zeros_like(dv_sorted)

    def query_work(query_tile):
        q_start = pl.multiple_of(query_tile * tile, tile)
        q_tile = q_sorted[pl.ds(q_start, tile), :]
        do_tile = do_sorted[pl.ds(q_start, tile), :]
        product = do_tile.astype(f32) * o_sorted[pl.ds(q_start, tile), :].astype(f32)
        delta[...] = jnp.sum(product.T, axis=0, keepdims=True)
        dq_turned[...] = jnp.zeros_like(dq_turned)

        def work(key_tile, masked):
            k_start = pl.multiple_of(key_tile * tile, tile)
            here = pl.ds(k_start, tile)
            scores = dot_nt(k_sorted[here, :], q_tile)
            probs = jnp.exp(scores * scale - lse_ref[:, pl.ds(q_start, tile)])
            if masked:
                keep = allowed_tile(k_start, query_tile, pos_table, tile, tile, rows, sorted_all)
                probs = jnp.where(keep, probs, 0.0)
            dv_sorted[here, :] += dot_nn(probs.astype(bf16), do_tile)
            d_probs = dot_nt(v_sorted[here, :], do_tile)
            d_scores = (probs * (d_probs - delta[...])).astype(bf16)
            dk_sorted[here, :] += dot_nn(d_scores, q_tile)
            dq_turned[...] += dot_nn(k_turned[:, here], d_scores)

        tile_loop(query_tile, key_tiles, sorted_all, work)
        dq_sorted[pl.ds(q_start, tile), :] = dq_turned[...].T * scale

    query_loop(query_tiles, sorted_all, query_work)
    dk_sorted[...] = dk_sorted[...] * scale
    unsort_rows(dq_sorted, dq_ref, query_table, queries // rows, rows)
    unsort_rows(dk_sorted, dk_ref, key_table, keys // rows, rows)
    unsort_rows(dv_sorted, dv_ref, key_table, keys // rows, rows)


def attend_back(tables, query_rot, key_rot, value, out, d_out, lse, rows, sorted_all, scale):
    queries, head = query_rot.shape
    keys = key_rot.shape[0]
    tile = math.gcd(math.gcd(queries, keys), 512)
    whole = lambda shape: pl.BlockSpec(shape, lambda i, *_: (0, 0))
    q_spec, k_spec = whole((queries, head)), whole((keys, head))
    return pl.pallas_call(
        functools.partial(attend_back_kernel, (rows, tile, sorted_all, scale)),
        out_shape=(
            jax.ShapeDtypeStruct((queries, head), f32),
            jax.ShapeDtypeStruct((keys, head), f32),
            jax.ShapeDtypeStruct((keys, head), f32),
        ),
        grid_spec=pltpu.PrefetchScalarGridSpec(
            num_scalar_prefetch=3,
            grid=(1,),
            in_specs=[q_spec, k_spec, k_spec, q_spec, q_spec, whole((1, queries))],
            out_specs=(q_spec, k_spec, k_spec),
            scratch_shapes=[
                pltpu.VMEM((queries, head), bf16),
                pltpu.VMEM((keys, head), bf16),
                pltpu.VMEM((keys, head), bf16),
                pltpu.VMEM((queries, head), bf16),
                pltpu.VMEM((queries, head), bf16),
                pltpu.VMEM((head, keys), bf16),
                pltpu.VMEM((1, tile), f32),
                pltpu.VMEM((head, tile), f32),
                pltpu.VMEM((queries, head), f32),
                pltpu.VMEM((keys, head), f32),
                pltpu.VMEM((keys, head), f32),
            ],
        ),
        compiler_params=pltpu.CompilerParams(vmem_limit_bytes=56 * 2**20),
        cost_estimate=pl.CostEstimate(
            flops=5 * queries * keys * head, bytes_accessed=20 * keys * head, transcendentals=queries * keys // 2
        ),
        name="attend_back",
    )(*tables, query_rot, key_rot, value, out, d_out, lse)


class Ring:
    def __init__(self, size):
        self.chips = size // 2
        self.reach = self.chips // 2
        order = list(range(0, self.chips, 2)) + list(range(self.chips - 1, 0, -2))
        self.order = order
        self.swap_pairs = [(i, i ^ 1) for i in range(size)]
        self.pass_pairs = []
        for place, chip in enumerate(order):
            after = order[(place + 1) % self.chips]
            self.pass_pairs.append((2 * chip, 2 * after))
            self.pass_pairs.append((2 * after + 1, 2 * chip + 1))

    def swap(self, field):
        return lax.ppermute(field, "ctx", self.swap_pairs)

    def hop(self, field):
        return lax.ppermute(field, "ctx", self.pass_pairs)

    def members(self, rank):
        chip, core = rank // 2, rank % 2
        order = jnp.array(self.order, jnp.int32)
        place = jnp.sum(jnp.where(order == chip, jnp.arange(self.chips, dtype=jnp.int32), 0))
        at = lambda shift: jnp.sum(
            jnp.where(
                jnp.arange(self.chips, dtype=jnp.int32) == (place + shift + self.chips) % self.chips,
                order,
                0,
            )
        )
        sign = 2 * core - 1
        chunks = [[rank, rank ^ 1]]
        for step in range(1, self.reach):
            near, far = at(sign * step), at(-sign * step)
            chunks.append([2 * near + core, 2 * near + 1 - core])
            chunks.append([2 * far + 1 - core, 2 * far + core])
        last = at(self.reach)
        chunks.append([2 * last + core])
        chunks.append([2 * last + 1 - core])
        return chunks

    def gather(self, block):
        rows = block.shape[0]
        held = jnp.concatenate([block, self.swap(block)], axis=0)
        chunks = [held]
        for step in range(1, self.reach + 1):
            if step == self.reach:
                held = held[:rows]
            held = self.hop(held)
            chunks += [held, self.swap(held)]
        return chunks

    def scatter_sum(self, term):
        held = None
        for step in range(self.reach, 0, -1):
            index = 2 * step - 1
            mine, other = term(index), term(index + 1)
            given = self.swap(mine)
            total = other.astype(f32) + given.astype(f32)
            if held is not None:
                rows = held.shape[0]
                if rows == total.shape[0]:
                    total = total + held.astype(f32)
                else:
                    total = jnp.concatenate([total[:rows] + held.astype(f32), total[rows:]], axis=0)
            held = self.hop(total.astype(bf16))
        own = term(0).astype(f32)
        rows = own.shape[0] // 2
        arrived = held.astype(f32)
        given = self.swap((arrived[:rows] + own[rows:]).astype(bf16))
        return arrived[rows:] + own[:rows] + given.astype(f32)


def to_columns(rows_block, fsdp_rank):
    received = lax.all_to_all(rows_block, "ctx", split_axis=0, concat_axis=0, tiled=False)
    partner = lax.ppermute(received, "fsdp", [(0, 1), (1, 0)])
    first = jnp.where(fsdp_rank == 0, received, partner)
    second = jnp.where(fsdp_rank == 0, partner, received)
    both = jnp.stack([first, second], axis=1)
    return both.reshape(-1, rows_block.shape[-1])


def to_rows(columns_grad, extra, fsdp_rank, ctx_size):
    width = columns_grad.shape[1]
    split = columns_grad.reshape(ctx_size, 2, -1, width)
    keep = lax.dynamic_index_in_dim(split, fsdp_rank, 1, keepdims=False)
    give = lax.dynamic_index_in_dim(split, 1 - fsdp_rank, 1, keepdims=False)
    rows = keep.shape[1]
    count = extra.shape[0]
    lines = -(-count // width)
    lines = -(-lines // 16) * 16
    extra_block = jnp.pad(extra, (0, lines * width - count)).reshape(lines, width)
    give_all = jnp.concatenate([give.reshape(-1, width).astype(bf16), extra_block.astype(bf16)], axis=0)
    given = lax.ppermute(give_all, "fsdp", [(0, 1), (1, 0)]).astype(f32)
    grads = keep + given[: ctx_size * rows].reshape(ctx_size, rows, width)
    extras = extra_block + given[ctx_size * rows :]
    sent = jnp.concatenate(
        [
            grads.astype(bf16),
            jnp.broadcast_to(extras.astype(bf16)[None], (ctx_size, lines, width)),
        ],
        axis=1,
    )
    received = lax.all_to_all(sent, "ctx", split_axis=0, concat_axis=0, tiled=False).astype(f32)
    extra_sum = jnp.sum(received[:, rows:], axis=0).reshape(-1)[:count]
    return received[:, :rows], extra_sum


def side_by_side(pieces):
    count, rows, width = pieces.shape
    return jnp.transpose(pieces, (1, 0, 2)).reshape(rows, count * width)


def shards(
    block_input,
    query_weight,
    key_weight,
    value_weight,
    output_weight,
    gate_weight,
    up_weight,
    down_weight,
    attn_gain,
    mlp_gain,
    query_gain,
    key_gain,
    block_order,
    cotangent,
):
    ctx_size = lax.axis_size("ctx")
    ctx_rank = lax.axis_index("ctx")
    fsdp_rank = lax.axis_index("fsdp")
    tokens = block_input.shape[1]
    model = block_input.shape[2]
    head_size = query_gain.shape[0]
    heads = query_weight.shape[1] // head_size
    kv_heads = key_weight.shape[1] // head_size
    slots = block_order.shape[0]
    length = tokens * ctx_size
    half_rows = length // slots
    per_block = tokens // half_rows
    weight_rows = query_weight.shape[0]
    hidden_slice = gate_weight.shape[1] // ctx_size
    splits = ctx_size // heads
    group = ctx_size // kv_heads
    split_rank = ctx_rank % splits
    sorted_all = splits == 1
    score_scale = 1.0 / math.sqrt(head_size)
    ring = Ring(ctx_size)
    head_groups = [[h * splits + s for h in range(heads)] for s in range(splits)]

    inputs_all = lax.all_gather(block_input[0], "ctx", axis=0, tiled=True)
    full_output = lax.all_gather(output_weight, ("ctx", "fsdp"), axis=0, tiled=True)
    cot_slots = lax.all_gather(cotangent[0], "ctx", axis=0, tiled=True)

    def by_head(weight, repeats):
        split = weight.reshape(weight_rows, -1, head_size)
        return jnp.repeat(jnp.transpose(split, (1, 0, 2)), repeats, axis=0)

    head_block = jnp.concatenate(
        [by_head(query_weight, splits), by_head(key_weight, group), by_head(value_weight, group)],
        axis=2,
    )
    head_weight = to_columns(head_block, fsdp_rank)

    def by_slice(weight):
        return jnp.transpose(weight.reshape(weight_rows, ctx_size, hidden_slice), (1, 0, 2))

    mlp_block = jnp.concatenate(
        [by_slice(gate_weight), by_slice(up_weight), by_slice(down_weight)], axis=2
    )
    mlp_weight = to_columns(mlp_block, fsdp_rank)
    gate_up = mlp_weight[:, : 2 * hidden_slice]
    down_part = mlp_weight[:, 2 * hidden_slice :]

    slot_index = jnp.arange(slots, dtype=jnp.int32)
    slot_of = jnp.sum(
        jnp.where(block_order[None, :] == slot_index[:, None], slot_index[None, :], 0), axis=1
    )
    positions = (
        block_order[:, None] * half_rows + jnp.arange(half_rows, dtype=jnp.int32)[None, :]
    ).reshape(-1)
    cosine, sine = rope_tables(positions, head_size)
    if sorted_all:
        tables = (slot_of, slot_of, slot_index)
    else:
        compact = jnp.arange(heads * per_block, dtype=jnp.int32)
        owner = (compact // per_block) * splits + split_rank
        own_pos = jnp.take(block_order, owner * per_block + compact % per_block)
        sequence = jnp.argsort(own_pos)
        tables = (slot_of, compact[sequence], own_pos[sequence])

    def own_queries(field):
        if splits == 1:
            return field
        parts = field.reshape((heads, splits, tokens) + field.shape[1:])
        picked = lax.dynamic_index_in_dim(parts, split_rank, 1, keepdims=False)
        return picked.reshape((heads * tokens,) + field.shape[1:])

    def all_queries(field):
        if splits == 1:
            return field
        parts = jnp.zeros((heads, splits, tokens) + field.shape[1:], field.dtype)
        value = field.reshape((heads, 1, tokens) + field.shape[1:])
        placed = lax.dynamic_update_slice_in_dim(parts, value, split_rank, 1)
        return placed.reshape((length,) + field.shape[1:])

    wide = inputs_all.astype(f32)
    normed_attn = (wide * inv_root(wide) * attn_gain).astype(bf16)
    projected = dot_nn(normed_attn, head_weight)
    query_raw = projected[:, :head_size]
    key_raw = projected[:, head_size : 2 * head_size]
    value_bf = projected[:, 2 * head_size :].astype(bf16)
    scale_query = inv_root(query_raw)
    scale_key = inv_root(key_raw)
    query_rot = rotate(query_raw * scale_query * query_gain, cosine, sine).astype(bf16)
    key_rot = rotate(key_raw * scale_key * key_gain, cosine, sine).astype(bf16)
    query_own = own_queries(query_rot)
    attn_own, lse = attend(tables, query_own, key_rot, value_bf, half_rows, sorted_all, score_scale)

    def exchange(pieces):
        return lax.all_to_all(
            pieces, "ctx", split_axis=0, concat_axis=0, axis_index_groups=head_groups, tiled=False
        )

    attn_bf = side_by_side(exchange(attn_own.reshape(heads, tokens, head_size)))
    inputs32 = block_input[0].astype(f32)
    scale_attn = inv_root(inputs32)
    hidden_one = inputs32 + dot_nt(attn_bf, full_output)
    scale_mlp = inv_root(hidden_one)
    normed_mlp = (hidden_one * scale_mlp * mlp_gain).astype(bf16)

    members = ring.members(ctx_rank)

    def pick(field, index):
        blocks = [
            lax.dynamic_slice_in_dim(field, member * tokens, tokens, 0) for member in members[index]
        ]
        return blocks[0] if len(blocks) == 1 else jnp.concatenate(blocks, axis=0)

    act_grad_slots = dot_nn(cot_slots, down_part)
    normed_chunks = ring.gather(normed_mlp)
    activated_chunks, back_chunks = [], []
    for index, chunk in enumerate(normed_chunks):
        pre = dot_nn(chunk, gate_up)
        gate_pre, up_pre = pre[:, :hidden_slice], pre[:, hidden_slice:]
        sigma = jax.nn.sigmoid(gate_pre)
        act_grad = pick(act_grad_slots, index)
        activated_chunks.append((gate_pre * sigma * up_pre).astype(bf16))
        back_chunks.append(
            jnp.concatenate(
                [
                    (act_grad * up_pre * sigma * (1.0 + gate_pre * (1.0 - sigma))).astype(bf16),
                    (act_grad * gate_pre * sigma).astype(bf16),
                ],
                axis=1,
            )
        )

    normed_mlp_grad = ring.scatter_sum(lambda i: dot_nt(back_chunks[i], gate_up).astype(bf16))
    mlp_out = ring.scatter_sum(lambda i: dot_nt(activated_chunks[i], down_part).astype(bf16))
    block_out = (hidden_one + mlp_out).astype(bf16)

    cot_ring = jnp.concatenate([pick(cot_slots, i) for i in range(len(members))], axis=0)
    gate_up_grad = dot_tn(
        jnp.concatenate(normed_chunks, axis=0), jnp.concatenate(back_chunks, axis=0)
    )
    down_grad = dot_tn(cot_ring, jnp.concatenate(activated_chunks, axis=0))
    mlp_gain_part = jnp.sum(gate_up_grad * gate_up.astype(f32), axis=1) / mlp_gain
    mlp_rows, mlp_gain_sum = to_rows(
        jnp.concatenate([gate_up_grad, down_grad], axis=1), mlp_gain_part, fsdp_rank, ctx_size
    )

    grad32 = cotangent[0].astype(f32)
    hidden_grad = grad32 + norm_back(hidden_one, scale_mlp, mlp_gain, normed_mlp_grad)
    hidden_grad_bf = hidden_grad.astype(bf16)
    hidden_grad_all = lax.all_gather(hidden_grad_bf, "ctx", axis=0, tiled=True)
    attn_grad = dot_nn(hidden_grad_bf, full_output).astype(bf16)
    attn_grad_own = exchange(
        jnp.transpose(attn_grad.reshape(tokens, heads, head_size), (1, 0, 2))
    ).reshape(-1, head_size)
    query_grad, key_grad, value_grad = attend_back(
        tables, query_own, key_rot, value_bf, attn_own, attn_grad_own, lse, half_rows, sorted_all, score_scale
    )
    query_normed_grad = rotate_back(all_queries(query_grad), cosine, sine)
    key_normed_grad = rotate_back(key_grad, cosine, sine)
    query_gain_part = jnp.sum(query_normed_grad * query_raw * scale_query, axis=0)
    key_gain_part = jnp.sum(key_normed_grad * key_raw * scale_key, axis=0)
    first_grads = jnp.concatenate(
        [
            norm_back(query_raw, scale_query, query_gain, query_normed_grad).astype(bf16),
            norm_back(key_raw, scale_key, key_gain, key_normed_grad).astype(bf16),
            value_grad.astype(bf16),
        ],
        axis=1,
    )
    normed_attn_grad = ring.scatter_sum(
        lambda i: dot_nt(pick(first_grads, i), head_weight).astype(bf16)
    )
    input_grad = hidden_grad + norm_back(inputs32, scale_attn, attn_gain, normed_attn_grad)
    head_grad = dot_tn(normed_attn, first_grads)
    output_grad = dot_tn(own_queries(hidden_grad_all), attn_own)
    attn_gain_part = jnp.sum(head_grad * head_weight.astype(f32), axis=1) / attn_gain
    attn_rows, attn_extra = to_rows(
        jnp.concatenate([head_grad, output_grad], axis=1),
        jnp.concatenate([attn_gain_part, query_gain_part, key_gain_part]),
        fsdp_rank,
        ctx_size,
    )

    def home(first, count):
        part = attn_rows[:, :, first * head_size : (first + 1) * head_size]
        if count != ctx_size:
            part = jnp.sum(part.reshape(count, ctx_size // count, weight_rows, head_size), axis=1)
        return side_by_side(part)

    def mlp_home(first):
        return side_by_side(mlp_rows[:, :, first * hidden_slice : (first + 1) * hidden_slice])

    return (
        block_out[None],
        input_grad[None],
        home(0, heads),
        home(1, kv_heads),
        home(2, kv_heads),
        home(3, heads),
        mlp_home(0),
        mlp_home(1),
        mlp_home(2),
        attn_extra[:model],
        mlp_gain_sum,
        attn_extra[model : model + head_size],
        attn_extra[model + head_size :],
    )


def solution(mesh):
    in_specs = (
        P("fsdp", "ctx", None),
        P(("ctx", "fsdp"), None),
        P(("ctx", "fsdp"), None),
        P(("ctx", "fsdp"), None),
        P(("ctx", "fsdp"), None),
        P(("ctx", "fsdp"), None),
        P(("ctx", "fsdp"), None),
        P(("ctx", "fsdp"), None),
        P(),
        P(),
        P(),
        P(),
        P(),
        P("fsdp", "ctx", None),
    )
    out_specs = (
        P("fsdp", "ctx", None),
        P("fsdp", "ctx", None),
        P(("ctx", "fsdp"), None),
        P(("ctx", "fsdp"), None),
        P(("ctx", "fsdp"), None),
        P(("ctx", "fsdp"), None),
        P(("ctx", "fsdp"), None),
        P(("ctx", "fsdp"), None),
        P(("ctx", "fsdp"), None),
        P(),
        P(),
        P(),
        P(),
    )
    return jax.shard_map(shards, mesh=mesh, in_specs=in_specs, out_specs=out_specs, check_vma=False)
```

time: 2870 us -> 812 us (0.28)
  waiting for transfers between devices: 2440 us -> 431 us
  matrix products: 250 us -> 92.7 us
  starting transfers between devices: 0.6 us -> 71.1 us
  other arithmetic: 25.1 us -> 82.4 us
  blocking collectives: 44.6 us -> 0 us
    reduce_scatter x3 -> x0, waiting for transfers between devices: 1710 us -> none  [the longest x1 1270 us: shards(): lax.psum_scatter(outer_rows(mlp_left, mlp_right), ('ctx', 'fsdp'), scatte...]
    all_gather x7 -> x3, waiting for transfers between devices: 674 us -> 0.02 us  [the longest x1 0.02 us: shards(): cot_slots = lax.all_gather(cotangent[0], 'ctx', axis=0, tiled=True)]
    ppermute x0 -> x40, waiting for transfers between devices: none -> 272 us  [the longest x16 160 us: hop(): return lax.ppermute(field, 'ctx', self.pass_pairs)]
    dot_general x30 -> x44, matrix products: 250 us -> 92.7 us  [the longest x28 36.1 us: dot_nt(): lax.dot_general(left, right, (((1,), (1,)), ((), ())), preferred_element_...]
    all_to_all x0 -> x6, waiting for transfers between devices: none -> 125 us  [the longest x2 102 us: to_columns(): lax.all_to_all(rows_block, 'ctx', split_axis=0, concat_axis=0, tiled=False)]
    psum x1 -> x0, blocking collectives: 44.6 us -> none  [shards(): lax.psum((attn_gain_part, mlp_gain_part, query_gain_part, key_gain_part),...]
    all_to_all x0 -> x6, starting transfers between devices: none -> 42.1 us  [the longest x2 16.3 us: to_columns(): lax.all_to_all(rows_block, 'ctx', split_axis=0, concat_axis=0, tiled=False)]
    unnamed x94 -> x166, local copies, waits for them, and re-layouts: 3.41 us -> 45.4 us
  transfers between devices with their start and end apart: 11 -> 50, of which waited for: 11 -> 22; matrix products, arithmetic and copies ran while one was open for 8% -> 30% of each run, Pallas kernels for 0% -> 2%
where the time goes in v1:
time: 812 us; the launch traced here: 807 us
  waiting for transfers between devices  431 us (53%)
  matrix products  92.7 us (11%)
  local copies, waits for them, and re-layouts  87.6 us (11%)
  other arithmetic  82.4 us (10%)
  starting transfers between devices  71.1 us (9%)
  between operations  25.1 us (3%)
  Pallas kernels  17.3 us (2%)
    ppermute x16, waiting for transfers between devices, hop(): return lax.ppermute(field, 'ctx', self.pass_pairs)  160 us
    all_to_all x2, waiting for transfers between devices, to_columns(): lax.all_to_all(rows_block, 'ctx', split_axis=0, concat_axis=0, tiled=False)  102 us
    ppermute x2, waiting for transfers between devices, to_rows(): given = lax.ppermute(give_all, 'fsdp', [(0, 1), (1, 0)]).astype(f32)  69.1 us
    unnamed x166, local copies, waits for them, and re-layouts  45.4 us
    ppermute x2, waiting for transfers between devices, to_columns(): partner = lax.ppermute(received, 'fsdp', [(0, 1), (1, 0)])  41.2 us
    dot_general x28, matrix products, dot_nt(): lax.dot_general(left, right, (((1,), (1,)), ((), ())), preferred_element_...  36.1 us
    all_gather x1, waiting for transfers between devices, shards(): lax.all_gather(output_weight, ('ctx', 'fsdp'), axis=0, tiled=True)  32.2 us
    dot_general x4, matrix products, dot_tn(): lax.dot_general(left, right, (((0,), (0,)), ((), ())), preferred_element_...  31.7 us
  transfers between devices with their start and end apart: 50, of which 22 were waited for; matrix products, arithmetic and copies ran while one was open for 30% of the time, Pallas kernels for 2%

profile of v1, /device:TPU:9, one launch (start us, length us, event | category | flops | bytes accessed | tf_op | source)
XLA Modules:
  0.0 807.0 jit_solution(8841989657906754282)
XLA Ops:
  10.4 1.9 copy.199
  12.3 6.7 all-to-all-start.2
  21.4 87.0 %all-to-all-done.2 = bf16[16,64,1152]{2,1,0:T(8,128)(2,1)} async-done(((bf16[16,64,1152]{2,1,0:T(8,128)(2,1)}), bf16[16,64,1152]{2,1,0:T(8,128)(2,1)}, u32[]{:S(2)}, u32[]{:S(2)}) %all-to-all-start.2) | async-done | bytes 2359328 | tf_op jit(solution)/shard_map/all_to_all | solution.py:358
  108.5 9.6 %all-to-all-start = ((bf16[16,64,384]{2,1,0:T(8,128)(2,1)}), bf16[16,64,384]{2,1,0:T(8,128)(2,1)S(1)}, u32[]{:S(2)}, u32[]{:S(2)}) async-start(bf16[16,64,384]{2,1,0:T(8,128)(2,1)} %copy.193), calls=%async_computation | async-start | bytes 1572864 | tf_op jit(solution)/shard_map/all_to_all | solution.py:358
  124.5 15.1 %all-to-all-done = bf16[16,64,384]{2,1,0:T(8,128)(2,1)S(1)} async-done(((bf16[16,64,384]{2,1,0:T(8,128)(2,1)}), bf16[16,64,384]{2,1,0:T(8,128)(2,1)S(1)}, u32[]{:S(2)}, u32[]{:S(2)}) %all-to-all-start) | async-done | bytes 786464 | tf_op jit(solution)/shard_map/all_to_all | solution.py:358
  146.5 41.2 %collective-permute-done = bf16[16,64,384]{2,1,0:T(8,128)(2,1)S(1)} collective-permute-done((bf16[16,64,384]{2,1,0:T(8,128)(2,1)S(1)}, bf16[16,64,384]{2,1,0:T(8,128)(2,1)S(1)}, u32[]{:S(2)}, u32[]{:S(2)}) %collective-permute-start) | collective-permute-done | bytes 786464 | tf_op jit(solution)/shard_map/ppermute | solution.py:359
  188.3 3.4 select_bitcast_fusion.1
  192.6 2.2 copy-done.9
  196.7 4.8 copy.231
  201.5 5.4 fusion
  207.4 4.6 fusion.20
  213.8 5.0 fusion.48
  219.5 5.0 attend.1
  226.1 6.8 all-to-all-start.1
  233.0 2.0 bitcast_dynamic-update-slice_fusion.15
  235.1 2.6 bitcast_dynamic-update-slice_fusion.14
  254.0 7.7 fusion.3
  261.7 32.2 %all-gather.7.cloned.1.call-done = bf16[2048,2048]{1,0:T(8,128)(2,1)} async-done(((bf16[64,2048]{1,0:T(8,128)(2,1)}), bf16[2048,2048]{1,0:T(8,128)(2,1)}) %all-gather.7.cloned.1.call-update) | async-done | bytes 8388624 | tf_op jit(solution)/shard_map/all_gather | solution.py:436
  293.9 6.6 multiply_reduce_fusion.7
  301.9 2.1 bitcast_dynamic-update-slice_fusion.1
  310.6 9.7 %collective-permute-done.2 = bf16[256,2048]{1,0:T(8,128)(2,1)S(1)} collective-permute-done((bf16[256,2048]{1,0:T(8,128)(2,1)S(1)}, bf16[256,2048]{1,0:T(8,128)(2,1)S(1)}, u32[]{:S(2)}, u32[]{:S(2)}) %collective-permute-start.2) | collective-permute-done | bytes 1048608 | tf_op jit(solution)/shard_map/ppermute | solution.py:301
  326.8 8.7 %collective-permute-done.6 = bf16[256,2048]{1,0:T(8,128)(2,1)S(1)} collective-permute-done((bf16[256,2048]{1,0:T(8,128)(2,1)S(1)}, bf16[256,2048]{1,0:T(8,128)(2,1)S(1)}, u32[]{:S(2)}, u32[]{:S(2)}) %collective-permute-start.6) | collective-permute-done | bytes 1048608 | tf_op jit(solution)/shard_map/ppermute | solution.py:301
  337.8 2.0 collective-permute-start.21
  347.6 8.6 %collective-permute-done.9 = bf16[256,2048]{1,0:T(8,128)(2,1)S(1)} collective-permute-done((bf16[256,2048]{1,0:T(8,128)(2,1)S(1)}, bf16[256,2048]{1,0:T(8,128)(2,1)S(1)}, u32[]{:S(2)}, u32[]{:S(2)}) %collective-permute-start.9) | collective-permute-done | bytes 1048608 | tf_op jit(solution)/shard_map/ppermute | solution.py:301
  360.5 2.2 collective-permute-start.10
  365.1 2.0 convolution_convert_fusion.15
  378.3 6.2 collective-permute-done.24
  385.6 4.6 collective-permute-done.15
  393.9 7.5 collective-permute-done.25
  402.7 9.9 %collective-permute-done.16 = bf16[256,2048]{1,0:T(8,128)(2,1)S(1)} collective-permute-done((bf16[256,2048]{1,0:T(8,128)(2,1)S(1)}, bf16[256,2048]{1,0:T(8,128)(2,1)S(1)}, u32[]{:S(2)}, u32[]{:S(2)}) %collective-permute-start.16) | collective-permute-done | bytes 1048608 | tf_op jit(solution)/shard_map/ppermute | solution.py:301
  415.1 8.8 %collective-permute-done.26 = bf16[256,2048]{1,0:T(8,128)(2,1)S(1)} collective-permute-done((bf16[256,2048]{1,0:T(8,128)(2,1)S(1)}, bf16[256,2048]{1,0:T(8,128)(2,1)S(1)}, u32[]{:S(2)}, u32[]{:S(2)}) %collective-permute-start.26) | collective-permute-done | bytes 1048608 | tf_op jit(solution)/shard_map/ppermute | solution.py:301
  425.2 9.9 %collective-permute-done.17 = bf16[256,2048]{1,0:T(8,128)(2,1)S(1)} collective-permute-done((bf16[256,2048]{1,0:T(8,128)(2,1)S(1)}, bf16[256,2048]{1,0:T(8,128)(2,1)S(1)}, u32[]{:S(2)}, u32[]{:S(2)}) %collective-permute-start.17) | collective-permute-done | bytes 1048608 | tf_op jit(solution)/shard_map/ppermute | solution.py:301
  438.1 8.2 %collective-permute-done.27 = bf16[256,2048]{1,0:T(8,128)(2,1)S(1)} collective-permute-done((bf16[256,2048]{1,0:T(8,128)(2,1)S(1)}, bf16[256,2048]{1,0:T(8,128)(2,1)S(1)}, u32[]{:S(2)}, u32[]{:S(2)}) %collective-permute-start.27) | collective-permute-done | bytes 1048608 | tf_op jit(solution)/shard_map/ppermute | solution.py:301
  448.1 9.4 %collective-permute-done.18 = bf16[256,2048]{1,0:T(8,128)(2,1)S(1)} collective-permute-done((bf16[256,2048]{1,0:T(8,128)(2,1)S(1)}, bf16[256,2048]{1,0:T(8,128)(2,1)S(1)}, u32[]{:S(2)}, u32[]{:S(2)}) %collective-permute-start.18) | collective-permute-done | bytes 1048608 | tf_op jit(solution)/shard_map/ppermute | solution.py:301
  463.5 12.0 %multiply_reduce_fusion = (f32[2048]{0:T(1024)S(1)}, f32[2048,768]{0,1:T(8,128)}) fusion(bf16[2048,768]{0,1:T(8,128)(2,1)S(1)} %copy-done.22, bf16[2048,2048]{1,0:T(8,128)(2,1)} %constant_dynamic-update-slice_fusion, bf16[2048,768]{1,0:T(8,128)(2,1)} %copy-done.51), kind=kOutput, calls=%fused_computation.8 | convolution fusion | flops 6447167488 | bytes 20979712 | tf_op jit(solution)/shard_map/dot_general | solution.py:60
  475.5 9.1 %fusion.193 = f32[2048,384]{0,1:T(8,128)} fusion(bf16[2048,2048]{1,0:T(8,128)(2,1)} %bitcast_dynamic-update-slice_fusion, bf16[2048,384]{1,0:T(8,128)(2,1)} %copy-done.52), kind=kOutput, calls=%fused_computation.448 | convolution fusion | flops 3221225472 | bytes 13107200 | tf_op jit(solution)/shard_map/dot_general | solution.py:60
  484.7 6.5 pad_maximum_fusion
  491.2 9.6 %copy.225 = f32[2048,1152]{1,0:T(8,128)} copy(f32[2048,1152]{0,1:T(8,128)} %pad_maximum_fusion) | data formatting | bytes 18874368 | tf_op jit(solution)/shard_map/concatenate | solution.py:554
  500.8 2.7 dynamic-slice_convert_fusion
  507.9 50.7 %collective-permute-done.39 = bf16[1040,1152]{1,0:T(8,128)(2,1)} collective-permute-done((bf16[1040,1152]{1,0:T(8,128)(2,1)}, bf16[1040,1152]{1,0:T(8,128)(2,1)}, u32[]{:S(2)}, u32[]{:S(2)}) %collective-permute-start.39) | collective-permute-done | bytes 2396192 | tf_op jit(solution)/shard_map/ppermute | solution.py:377
  558.6 4.2 convert_element_type.558
  562.9 4.6 fusion.42
  568.4 6.5 all-to-all-start.3
  576.4 2.0 slice.305
  578.4 4.5 fusion.5
  582.9 6.1 all-to-all-done.3
  589.8 12.3 %attend_back.1 = (f32[2048,128]{1,0:T(8,128)}, f32[2048,128]{1,0:T(8,128)}, f32[2048,128]{1,0:T(8,128)}) custom-call(s32[32]{0:T(128)} %copy-done.5, s32[32]{0:T(128)} %copy-done.5, s32[32]{0:T(128)} %iota.54.pos_table, bf16[2048,128]{1,0:T(8,128)(2,1)} %copy-done, bf16[2048,128]{1,0:T(8,128)(2,1)} %copy-done.1, bf16[2048,128]{1,0:T(8,128)(2,1)} %copy-done.4, ...), custom_call_target="tpu_custom_call" | custom-call | flops 2684354560 | bytes 5242880 | tf_op jit(solution)/shard_map/attend_back/pallas_call | solution.py:250
  603.4 7.7 fusion.53
  613.0 2.6 subtract_convert_fusion.1
  622.4 5.0 all-to-all-start.5
  634.8 2.1 convert_add_fusion
  637.0 61.5 %collective-permute-done.33 = bf16[128,2048]{1,0:T(8,128)(2,1)S(1)} collective-permute-done((bf16[128,2048]{1,0:T(8,128)(2,1)S(1)}, bf16[128,2048]{1,0:T(8,128)(2,1)S(1)}, u32[]{:S(2)}, u32[]{:S(2)}) %collective-permute-start.33) | collective-permute-done | bytes 524320 | tf_op jit(solution)/shard_map/ppermute | solution.py:301
  699.9 5.8 multiply_reduce_fusion.1
  706.5 7.3 collective-permute-done.34
  713.7 3.1 add_convert_fusion.1
  716.8 4.8 fusion.192
  721.7 2.3 pad_maximum_fusion.2
  724.0 5.4 copy.219
  732.6 2.7 add_convert_fusion
  735.6 18.4 %collective-permute-done.38 = bf16[1040,512]{1,0:T(8,128)(2,1)S(1)} collective-permute-done((bf16[1040,512]{1,0:T(8,128)(2,1)S(1)}, bf16[1040,512]{1,0:T(8,128)(2,1)S(1)}, u32[]{:S(2)}, u32[]{:S(2)}) %collective-permute-start.38) | collective-permute-done | bytes 1064992 | tf_op jit(solution)/shard_map/ppermute | solution.py:377
  756.2 7.5 all-to-all-start.4
  764.5 3.0 convert_element_type.561
  774.1 1.9 fusion.55
  777.6 16.5 %all-to-all-done.4 = bf16[16,80,512]{2,1,0:T(8,128)(2,1)} async-done(((bf16[16,80,512]{2,1,0:T(8,128)(2,1)}), bf16[16,80,512]{2,1,0:T(8,128)(2,1)}, u32[]{:S(2)}, u32[]{:S(2)}) %all-to-all-start.4) | async-done | bytes 1310752 | tf_op jit(solution)/shard_map/all_to_all | solution.py:387
  (400 shorter events, 143.9 us)
Async XLA Ops:
  7.2 194.3 %all-gather.11.cloned.1.call-start = ((), (), s32[]{:S(2)}) async-start(), calls=%async_computation.8 | async-start | bytes 8912896 | tf_op jit(solution)/shard_map/all_gather | solution.py:435
  7.9 225.1 %all-gather.13.cloned.1.call-start = ((), (), s32[]{:S(2)}) async-start(), calls=%async_computation.9 | async-start | bytes 8912896 | tf_op jit(solution)/shard_map/all_gather | solution.py:437
  12.3 96.1 %all-to-all-start.2 = ((bf16[16,64,1152]{2,1,0:T(8,128)(2,1)}), bf16[16,64,1152]{2,1,0:T(8,128)(2,1)}, u32[]{:S(2)}, u32[]{:S(2)}) async-start(bf16[16,64,1152]{2,1,0:T(8,128)(2,1)} %copy.199), calls=%async_computation.2 | async-start | bytes 4718592 | tf_op jit(solution)/shard_map/all_to_all | solution.py:358
  19.0 274.9 %all-gather.7.cloned.1.call-start = ((), (), s32[]{:S(2)}) async-start(), calls=%async_computation.6 | async-start | bytes 8650752 | tf_op jit(solution)/shard_map/all_gather | solution.py:436
  19.8 99.4 %copy-start.57 = (s32[8]{0:T(128)S(1)}, s32[8]{0:T(128)}, u32[]{:S(2)}) copy-start(s32[8]{0:T(128)} %constant.122.clone) | copy-start | bytes 100
  19.9 126.4 %copy-start.58 = (s32[32]{0:T(128)S(1)}, s32[32]{0:T(128)}, u32[]{:S(2)}) copy-start(s32[32]{0:T(128)} %param.27) | copy-start | bytes 388
  108.5 31.2 %all-to-all-start = ((bf16[16,64,384]{2,1,0:T(8,128)(2,1)}), bf16[16,64,384]{2,1,0:T(8,128)(2,1)S(1)}, u32[]{:S(2)}, u32[]{:S(2)}) async-start(bf16[16,64,384]{2,1,0:T(8,128)(2,1)} %copy.193), calls=%async_computation | async-start | bytes 1572864 | tf_op jit(solution)/shard_map/all_to_all | solution.py:358
  118.0 70.2 %collective-permute-start.4 = (bf16[16,64,1152]{2,1,0:T(8,128)(2,1)}, bf16[16,64,1152]{2,1,0:T(8,128)(2,1)}, u32[]{:S(2)}, u32[]{:S(2)}) collective-permute-start(bf16[16,64,1152]{2,1,0:T(8,128)(2,1)} %all-to-all-done.2), channel_id=1, source_target_pairs={{0,1},{1,0},{2,3},{3,2},{4,5},{5,4},{6,7},{7,6},{8,9},{9,8},{10,11... | collective-permute-start | bytes 7077896 | tf_op jit(solution)/shard_map/ppermute | solution.py:359
  139.6 48.1 %collective-permute-start = (bf16[16,64,384]{2,1,0:T(8,128)(2,1)S(1)}, bf16[16,64,384]{2,1,0:T(8,128)(2,1)S(1)}, u32[]{:S(2)}, u32[]{:S(2)}) collective-permute-start(bf16[16,64,384]{2,1,0:T(8,128)(2,1)S(1)} %all-to-all-done), channel_id=1, source_target_pairs={{0,1},{1,0},{2,3},{3,2},{4,5},{5,4},{6,7},{7,6},{8,9},{9,8},{10,11... | collective-permute-start | bytes 2359304 | tf_op jit(solution)/shard_map/ppermute | solution.py:359
  146.5 73.0 %copy-start.5 = (s32[32]{0:T(128)}, s32[32]{0:T(128)S(1)}, u32[]{:S(2)}) copy-start(s32[32]{0:T(128)S(1)} %select_reduce_fusion.key_table.query_table) | copy-start | bytes 388
  226.1 67.8 %all-to-all-start.1 = ((bf16[16,128,128]{1,2,0:T(8,128)(2,1)}), bf16[16,128,128]{1,2,0:T(8,128)(2,1)S(1)}, u32[]{:S(2)}, u32[]{:S(2)}) async-start(bf16[16,128,128]{1,2,0:T(8,128)(2,1)} %copy.198), calls=%async_computation.1 | async-start | bytes 1048576 | tf_op jit(solution)/shard_map/all_to_all | solution.py:505
  232.9 483.9 %all-gather.9.cloned.1.call-start = ((), (), s32[]{:S(2)}) async-start(), calls=%async_computation.7 | async-start | bytes 8912896 | tf_op jit(solution)/shard_map/all_gather | solution.py:560
  254.0 39.9 %copy-start.18 = (bf16[1,128,2048]{2,1,0:T(8,128)(2,1)S(1)}, bf16[1,128,2048]{2,1,0:T(8,128)(2,1)}, u32[]{:S(2)}) copy-start(bf16[1,128,2048]{2,1,0:T(8,128)(2,1)} %param.15) | copy-start | bytes 1572868
  301.5 4.4 collective-permute-start.1
  306.0 14.4 %collective-permute-start.2 = (bf16[256,2048]{1,0:T(8,128)(2,1)S(1)}, bf16[256,2048]{1,0:T(8,128)(2,1)S(1)}, u32[]{:S(2)}, u32[]{:S(2)}) collective-permute-start(bf16[256,2048]{1,0:T(8,128)(2,1)S(1)} %pad_maximum_fusion.10), channel_id=1, source_target_pairs={{0,8},{10,2},{8,16},{18,10},{16,24},{26,18},{24,28},{30,26},{28,20... | collective-permute-start | bytes 3145736 | tf_op jit(solution)/shard_map/ppermute | solution.py:301
  321.6 14.0 %collective-permute-start.6 = (bf16[256,2048]{1,0:T(8,128)(2,1)S(1)}, bf16[256,2048]{1,0:T(8,128)(2,1)S(1)}, u32[]{:S(2)}, u32[]{:S(2)}) collective-permute-start(bf16[256,2048]{1,0:T(8,128)(2,1)S(1)} %collective-permute-done.2), channel_id=1, source_target_pairs={{0,8},{10,2},{8,16},{18,10},{16,24},{26,18},{24,28},{30,26},{28,20... | collective-permute-start | bytes 3145736 | tf_op jit(solution)/shard_map/ppermute | solution.py:301
  322.9 92.2 %collective-permute-start.20 = (bf16[256,2048]{1,0:T(8,128)(2,1)S(1)}, bf16[256,2048]{1,0:T(8,128)(2,1)S(1)}, u32[]{:S(2)}, u32[]{:S(2)}) collective-permute-start(bf16[256,2048]{1,0:T(8,128)(2,1)S(1)} %convolution_convert_fusion.19), channel_id=1, source_target_pairs={{0,2},{2,0},{4,6},{6,4},{8,10},{10,8},{12,14},{14,12},{16,18},{18,... | collective-permute-start | bytes 3145736 | tf_op jit(solution)/shard_map/ppermute | solution.py:298
  324.8 15.0 %collective-permute-start.3 = (bf16[256,2048]{1,0:T(8,128)(2,1)S(1)}, bf16[256,2048]{1,0:T(8,128)(2,1)S(1)}, u32[]{:S(2)}, u32[]{:S(2)}) collective-permute-start(bf16[256,2048]{1,0:T(8,128)(2,1)S(1)} %collective-permute-done.2), channel_id=1, source_target_pairs={{0,2},{2,0},{4,6},{6,4},{8,10},{10,8},{12,14},{14,12},{16,18},{18,... | collective-permute-start | bytes 3145736 | tf_op jit(solution)/shard_map/ppermute | solution.py:298
  337.8 54.9 %collective-permute-start.21 = (bf16[256,2048]{1,0:T(8,128)(2,1)S(1)}, bf16[256,2048]{1,0:T(8,128)(2,1)S(1)}, u32[]{:S(2)}, u32[]{:S(2)}) collective-permute-start(bf16[256,2048]{1,0:T(8,128)(2,1)S(1)} %convolution_convert_fusion.17), channel_id=1, source_target_pairs={{0,2},{2,0},{4,6},{6,4},{8,10},{10,8},{12,14},{14,12},{16,18},{18,... | collective-permute-start | bytes 3145736 | tf_op jit(solution)/shard_map/ppermute | solution.py:298
  341.9 60.9 %collective-permute-start.8 = (bf16[256,2048]{1,0:T(8,128)(2,1)S(1)}, bf16[256,2048]{1,0:T(8,128)(2,1)S(1)}, u32[]{:S(2)}, u32[]{:S(2)}) collective-permute-start(bf16[256,2048]{1,0:T(8,128)(2,1)S(1)} %convolution_convert_fusion.10), channel_id=1, source_target_pairs={{0,2},{2,0},{4,6},{6,4},{8,10},{10,8},{12,14},{14,12},{16,18},{18,... | collective-permute-start | bytes 3145736 | tf_op jit(solution)/shard_map/ppermute | solution.py:298
  342.2 14.0 %collective-permute-start.9 = (bf16[256,2048]{1,0:T(8,128)(2,1)S(1)}, bf16[256,2048]{1,0:T(8,128)(2,1)S(1)}, u32[]{:S(2)}, u32[]{:S(2)}) collective-permute-start(bf16[256,2048]{1,0:T(8,128)(2,1)S(1)} %collective-permute-done.6), channel_id=1, source_target_pairs={{0,8},{10,2},{8,16},{18,10},{16,24},{26,18},{24,28},{30,26},{28,20... | collective-permute-start | bytes 3145736 | tf_op jit(solution)/shard_map/ppermute | solution.py:301
  342.5 14.2 %collective-permute-start.7 = (bf16[256,2048]{1,0:T(8,128)(2,1)S(1)}, bf16[256,2048]{1,0:T(8,128)(2,1)S(1)}, u32[]{:S(2)}, u32[]{:S(2)}) collective-permute-start(bf16[256,2048]{1,0:T(8,128)(2,1)S(1)} %collective-permute-done.6), channel_id=1, source_target_pairs={{0,2},{2,0},{4,6},{6,4},{8,10},{10,8},{12,14},{14,12},{16,18},{18,... | collective-permute-start | bytes 3145736 | tf_op jit(solution)/shard_map/ppermute | solution.py:298
  356.2 10.9 %collective-permute-start.12 = (bf16[128,2048]{1,0:T(8,128)(2,1)S(1)}, bf16[128,2048]{1,0:T(8,128)(2,1)S(1)}, u32[]{:S(2)}, u32[]{:S(2)}) collective-permute-start(bf16[128,2048]{1,0:T(8,128)(2,1)S(1)} %slice.275), channel_id=1, source_target_pairs={{0,8},{10,2},{8,16},{18,10},{16,24},{26,18},{24,28},{30,26},{28,20... | collective-permute-start | bytes 1572872 | tf_op jit(solution)/shard_map/ppermute | solution.py:301
  360.5 7.2 collective-permute-start.10
  367.1 2.2 collective-permute-start.13
  367.7 4.0 collective-permute-start.22
  369.3 4.0 collective-permute-start.11
  371.7 3.3 collective-permute-start.23
  374.9 2.2 collective-permute-start.14
  376.1 8.4 %collective-permute-start.24 = (bf16[128,2048]{1,0:T(8,128)(2,1)S(1)}, bf16[128,2048]{1,0:T(8,128)(2,1)S(1)}, u32[]{:S(2)}, u32[]{:S(2)}) collective-permute-start(bf16[128,2048]{1,0:T(8,128)(2,1)S(1)} %add_convert_fusion.7), channel_id=1, source_target_pairs={{0,8},{10,2},{8,16},{18,10},{16,24},{26,18},{24,28},{30,26},{28,20... | collective-permute-start | bytes 1572872 | tf_op jit(solution)/shard_map/ppermute | solution.py:301
  377.7 12.4 %collective-permute-start.15 = (bf16[128,2048]{1,0:T(8,128)(2,1)S(1)}, bf16[128,2048]{1,0:T(8,128)(2,1)S(1)}, u32[]{:S(2)}, u32[]{:S(2)}) collective-permute-start(bf16[128,2048]{1,0:T(8,128)(2,1)S(1)} %add_convert_fusion.8), channel_id=1, source_target_pairs={{0,8},{10,2},{8,16},{18,10},{16,24},{26,18},{24,28},{30,26},{28,20... | collective-permute-start | bytes 1572872 | tf_op jit(solution)/shard_map/ppermute | solution.py:301
  384.7 16.6 %collective-permute-start.25 = (bf16[256,2048]{1,0:T(8,128)(2,1)S(1)}, bf16[256,2048]{1,0:T(8,128)(2,1)S(1)}, u32[]{:S(2)}, u32[]{:S(2)}) collective-permute-start(bf16[256,2048]{1,0:T(8,128)(2,1)S(1)} %pad_maximum_fusion.12), channel_id=1, source_target_pairs={{0,8},{10,2},{8,16},{18,10},{16,24},{26,18},{24,28},{30,26},{28,20... | collective-permute-start | bytes 3145736 | tf_op jit(solution)/shard_map/ppermute | solution.py:301
  390.4 22.2 %collective-permute-start.16 = (bf16[256,2048]{1,0:T(8,128)(2,1)S(1)}, bf16[256,2048]{1,0:T(8,128)(2,1)S(1)}, u32[]{:S(2)}, u32[]{:S(2)}) collective-permute-start(bf16[256,2048]{1,0:T(8,128)(2,1)S(1)} %pad_maximum_fusion.11), channel_id=1, source_target_pairs={{0,8},{10,2},{8,16},{18,10},{16,24},{26,18},{24,28},{30,26},{28,20... | collective-permute-start | bytes 3145736 | tf_op jit(solution)/shard_map/ppermute | solution.py:301
  392.7 32.5 %collective-permute-start.5 = (bf16[256,2048]{1,0:T(8,128)(2,1)S(1)}, bf16[256,2048]{1,0:T(8,128)(2,1)S(1)}, u32[]{:S(2)}, u32[]{:S(2)}) collective-permute-start(bf16[256,2048]{1,0:T(8,128)(2,1)S(1)} %convolution_convert_fusion.12), channel_id=1, source_target_pairs={{0,2},{2,0},{4,6},{6,4},{8,10},{10,8},{12,14},{14,12},{16,18},{18,... | collective-permute-start | bytes 3145736 | tf_op jit(solution)/shard_map/ppermute | solution.py:298
  401.9 21.9 %collective-permute-start.26 = (bf16[256,2048]{1,0:T(8,128)(2,1)S(1)}, bf16[256,2048]{1,0:T(8,128)(2,1)S(1)}, u32[]{:S(2)}, u32[]{:S(2)}) collective-permute-start(bf16[256,2048]{1,0:T(8,128)(2,1)S(1)} %add_convert_fusion.3), channel_id=1, source_target_pairs={{0,8},{10,2},{8,16},{18,10},{16,24},{26,18},{24,28},{30,26},{28,20... | collective-permute-start | bytes 3145736 | tf_op jit(solution)/shard_map/ppermute | solution.py:301
  413.1 22.0 %collective-permute-start.17 = (bf16[256,2048]{1,0:T(8,128)(2,1)S(1)}, bf16[256,2048]{1,0:T(8,128)(2,1)S(1)}, u32[]{:S(2)}, u32[]{:S(2)}) collective-permute-start(bf16[256,2048]{1,0:T(8,128)(2,1)S(1)} %add_convert_fusion.5), channel_id=1, source_target_pairs={{0,8},{10,2},{8,16},{18,10},{16,24},{26,18},{24,28},{30,26},{28,20... | collective-permute-start | bytes 3145736 | tf_op jit(solution)/shard_map/ppermute | solution.py:301
  424.4 21.9 %collective-permute-start.27 = (bf16[256,2048]{1,0:T(8,128)(2,1)S(1)}, bf16[256,2048]{1,0:T(8,128)(2,1)S(1)}, u32[]{:S(2)}, u32[]{:S(2)}) collective-permute-start(bf16[256,2048]{1,0:T(8,128)(2,1)S(1)} %add_convert_fusion.2), channel_id=1, source_target_pairs={{0,8},{10,2},{8,16},{18,10},{16,24},{26,18},{24,28},{30,26},{28,20... | collective-permute-start | bytes 3145736 | tf_op jit(solution)/shard_map/ppermute | solution.py:301
  435.6 21.9 %collective-permute-start.18 = (bf16[256,2048]{1,0:T(8,128)(2,1)S(1)}, bf16[256,2048]{1,0:T(8,128)(2,1)S(1)}, u32[]{:S(2)}, u32[]{:S(2)}) collective-permute-start(bf16[256,2048]{1,0:T(8,128)(2,1)S(1)} %add_convert_fusion.4), channel_id=1, source_target_pairs={{0,8},{10,2},{8,16},{18,10},{16,24},{26,18},{24,28},{30,26},{28,20... | collective-permute-start | bytes 3145736 | tf_op jit(solution)/shard_map/ppermute | solution.py:301
  446.7 12.7 %collective-permute-start.28 = (bf16[128,2048]{1,0:T(8,128)(2,1)S(1)}, bf16[128,2048]{1,0:T(8,128)(2,1)S(1)}, u32[]{:S(2)}, u32[]{:S(2)}) collective-permute-start(bf16[128,2048]{1,0:T(8,128)(2,1)S(1)} %fusion.65), channel_id=1, source_target_pairs={{0,2},{2,0},{4,6},{6,4},{8,10},{10,8},{12,14},{14,12},{16,18},{18,... | collective-permute-start | bytes 1572872 | tf_op jit(solution)/shard_map/ppermute | solution.py:298
  457.9 2.9 collective-permute-start.19
  505.1 53.5 %collective-permute-start.39 = (bf16[1040,1152]{1,0:T(8,128)(2,1)}, bf16[1040,1152]{1,0:T(8,128)(2,1)}, u32[]{:S(2)}, u32[]{:S(2)}) collective-permute-start(bf16[1040,1152]{1,0:T(8,128)(2,1)} %pad_maximum_fusion.4), channel_id=1, source_target_pairs={{0,1},{1,0},{2,3},{3,2},{4,5},{5,4},{6,7},{7,6},{8,9},{9,8},{10,11... | collective-permute-start | bytes 7188488 | tf_op jit(solution)/shard_map/ppermute | solution.py:377
  507.9 55.0 %copy-start.20 = (bf16[128,2048]{1,0:T(8,128)(2,1)S(1)}, bf16[128,2048]{1,0:T(8,128)(2,1)}, u32[]{:S(2)}) copy-start(bf16[128,2048]{1,0:T(8,128)(2,1)} %get-tuple-element.62) | copy-start | bytes 1572868
  568.4 20.5 %all-to-all-start.3 = ((bf16[16,128,128]{2,1,0:T(8,128)(2,1)}), bf16[16,128,128]{2,1,0:T(8,128)(2,1)S(1)}, u32[]{:S(2)}, u32[]{:S(2)}) async-start(bf16[16,128,128]{2,1,0:T(8,128)(2,1)} %bitcast.255), calls=%async_computation.3 | async-start | bytes 1048576 | tf_op jit(solution)/shard_map/all_to_all | solution.py:505
  618.6 16.1 %collective-permute-start.31 = (bf16[256,2048]{1,0:T(8,128)(2,1)}, bf16[256,2048]{1,0:T(8,128)(2,1)}, u32[]{:S(2)}, u32[]{:S(2)}) collective-permute-start(bf16[256,2048]{1,0:T(8,128)(2,1)} %convolution_convert_fusion.1), channel_id=1, source_target_pairs={{0,2},{2,0},{4,6},{6,4},{8,10},{10,8},{12,14},{14,12},{16,18},{18,... | collective-permute-start | bytes 3145736 | tf_op jit(solution)/shard_map/ppermute | solution.py:298
  620.0 9.5 %collective-permute-start.32 = (bf16[128,2048]{1,0:T(8,128)(2,1)}, bf16[128,2048]{1,0:T(8,128)(2,1)}, u32[]{:S(2)}, u32[]{:S(2)}) collective-permute-start(bf16[128,2048]{1,0:T(8,128)(2,1)} %convolution_convert_fusion.22), channel_id=1, source_target_pairs={{0,2},{2,0},{4,6},{6,4},{8,10},{10,8},{12,14},{14,12},{16,18},{18,... | collective-permute-start | bytes 1572872 | tf_op jit(solution)/shard_map/ppermute | solution.py:298
  622.4 133.8 %all-to-all-start.5 = ((bf16[16,80,1152]{2,1,0:T(8,128)(2,1)}), bf16[16,80,1152]{2,1,0:T(8,128)(2,1)}, u32[]{:S(2)}, u32[]{:S(2)}) async-start(bf16[16,80,1152]{2,1,0:T(8,128)(2,1)} %pad_maximum_fusion.3), calls=%async_computation.5 | async-start | bytes 5898240 | tf_op jit(solution)/shard_map/all_to_all | solution.py:387
  629.1 77.4 %collective-permute-start.30 = (bf16[256,2048]{1,0:T(8,128)(2,1)}, bf16[256,2048]{1,0:T(8,128)(2,1)}, u32[]{:S(2)}, u32[]{:S(2)}) collective-permute-start(bf16[256,2048]{1,0:T(8,128)(2,1)} %convolution_convert_fusion.3), channel_id=1, source_target_pairs={{0,2},{2,0},{4,6},{6,4},{8,10},{10,8},{12,14},{14,12},{16,18},{18,... | collective-permute-start | bytes 3145736 | tf_op jit(solution)/shard_map/ppermute | solution.py:298
  629.5 70.3 %slice-start.2 = ((s8[8388608]{0:T(1024)(128)(4,1)}), s8[4194304]{0:T(1024)(128)(4,1)S(1)}, s32[]{:S(2)}) async-start(s8[8388608]{0:T(1024)(128)(4,1)} %bitcast.305), calls=%async_computation.12 | async-start | bytes 8388608
  631.3 67.3 %collective-permute-start.33 = (bf16[128,2048]{1,0:T(8,128)(2,1)S(1)}, bf16[128,2048]{1,0:T(8,128)(2,1)S(1)}, u32[]{:S(2)}, u32[]{:S(2)}) collective-permute-start(bf16[128,2048]{1,0:T(8,128)(2,1)S(1)} %add_convert_fusion.6), channel_id=1, source_target_pairs={{0,8},{10,2},{8,16},{18,10},{16,24},{26,18},{24,28},{30,26},{28,20... | collective-permute-start | bytes 1572872 | tf_op jit(solution)/shard_map/ppermute | solution.py:301
  633.1 99.4 %collective-permute-start.29 = (bf16[256,2048]{1,0:T(8,128)(2,1)}, bf16[256,2048]{1,0:T(8,128)(2,1)S(1)}, u32[]{:S(2)}, u32[]{:S(2)}) collective-permute-start(bf16[256,2048]{1,0:T(8,128)(2,1)} %convolution_convert_fusion.5), channel_id=1, source_target_pairs={{0,2},{2,0},{4,6},{6,4},{8,10},{10,8},{12,14},{14,12},{16,18},{18,... | collective-permute-start | bytes 3145736 | tf_op jit(solution)/shard_map/ppermute | solution.py:298
  634.8 65.0 %slice-start.3 = ((s8[8388608]{0:T(1024)(128)(4,1)}), s8[4194304]{0:T(1024)(128)(4,1)S(1)}, s32[]{:S(2)}) async-start(s8[8388608]{0:T(1024)(128)(4,1)} %bitcast.305), calls=%async_computation.13 | async-start | bytes 8388608
  636.9 62.9 %copy-start.27 = (bf16[2048,128]{1,0:T(8,128)(2,1)S(1)}, bf16[2048,128]{1,0:T(8,128)(2,1)}, u32[]{:S(2)}) copy-start(bf16[2048,128]{1,0:T(8,128)(2,1)} %copy-done.26) | copy-start | bytes 1572868
  636.9 62.9 %copy-start.29 = (bf16[2048,128]{1,0:T(8,128)(2,1)S(1)}, bf16[2048,128]{1,0:T(8,128)(2,1)}, u32[]{:S(2)}) copy-start(bf16[2048,128]{1,0:T(8,128)(2,1)} %copy-done.28) | copy-start | bytes 1572868
  636.9 62.9 %copy-start.31 = (bf16[2048,128]{1,0:T(8,128)(2,1)S(1)}, bf16[2048,128]{1,0:T(8,128)(2,1)}, u32[]{:S(2)}) copy-start(bf16[2048,128]{1,0:T(8,128)(2,1)} %copy-done.30) | copy-start | bytes 1572868
  636.9 62.9 %copy-start.32 = (bf16[2048,384]{0,1:T(8,128)(2,1)S(1)}, bf16[2048,384]{0,1:T(8,128)(2,1)}, u32[]{:S(2)}) copy-start(bf16[2048,384]{0,1:T(8,128)(2,1)} %copy.220) | copy-start | bytes 4718596
  637.0 62.9 %copy-start.50 = (f32[2048]{0:T(1024)S(1)}, f32[2048]{0:T(1024)}, u32[]{:S(2)}) copy-start(f32[2048]{0:T(1024)} %param.23) | copy-start | bytes 24580
  637.0 62.9 %copy-start.54 = (f32[2048]{0:T(1024)S(1)}, f32[2048]{0:T(1024)}, u32[]{:S(2)}) copy-start(f32[2048]{0:T(1024)} %copy-done.53) | copy-start | bytes 24580
  699.8 14.0 %collective-permute-start.34 = (bf16[256,2048]{1,0:T(8,128)(2,1)}, bf16[256,2048]{1,0:T(8,128)(2,1)}, u32[]{:S(2)}, u32[]{:S(2)}) collective-permute-start(bf16[256,2048]{1,0:T(8,128)(2,1)} %pad_maximum_fusion.15), channel_id=1, source_target_pairs={{0,8},{10,2},{8,16},{18,10},{16,24},{26,18},{24,28},{30,26},{28,20... | collective-permute-start | bytes 3145736 | tf_op jit(solution)/shard_map/ppermute | solution.py:301
  716.8 15.8 %collective-permute-start.35 = (bf16[256,2048]{1,0:T(8,128)(2,1)}, bf16[256,2048]{1,0:T(8,128)(2,1)}, u32[]{:S(2)}, u32[]{:S(2)}) collective-permute-start(bf16[256,2048]{1,0:T(8,128)(2,1)} %add_convert_fusion.1), channel_id=1, source_target_pairs={{0,8},{10,2},{8,16},{18,10},{16,24},{26,18},{24,28},{30,26},{28,20... | collective-permute-start | bytes 3145736 | tf_op jit(solution)/shard_map/ppermute | solution.py:301
  731.2 22.7 %collective-permute-start.38 = (bf16[1040,512]{1,0:T(8,128)(2,1)S(1)}, bf16[1040,512]{1,0:T(8,128)(2,1)S(1)}, u32[]{:S(2)}, u32[]{:S(2)}) collective-permute-start(bf16[1040,512]{1,0:T(8,128)(2,1)S(1)} %pad_maximum_fusion.9), channel_id=1, source_target_pairs={{0,1},{1,0},{2,3},{3,2},{4,5},{5,4},{6,7},{7,6},{8,9},{9,8},{10,11... | collective-permute-start | bytes 3194888 | tf_op jit(solution)/shard_map/ppermute | solution.py:377
  735.3 19.3 %copy-start.14 = (f32[2048,512]{1,0:T(8,128)S(1)}, f32[2048,512]{1,0:T(8,128)}, u32[]{:S(2)}) copy-start(f32[2048,512]{1,0:T(8,128)} %copy.219) | copy-start | bytes 12582916
  735.3 32.2 %collective-permute-start.36 = (bf16[256,2048]{1,0:T(8,128)(2,1)}, bf16[256,2048]{1,0:T(8,128)(2,1)S(1)}, u32[]{:S(2)}, u32[]{:S(2)}) collective-permute-start(bf16[256,2048]{1,0:T(8,128)(2,1)} %add_convert_fusion), channel_id=1, source_target_pairs={{0,8},{10,2},{8,16},{18,10},{16,24},{26,18},{24,28},{30,26},{28,20... | collective-permute-start | bytes 3145736 | tf_op jit(solution)/shard_map/ppermute | solution.py:301
  756.2 37.8 %all-to-all-start.4 = ((bf16[16,80,512]{2,1,0:T(8,128)(2,1)}), bf16[16,80,512]{2,1,0:T(8,128)(2,1)}, u32[]{:S(2)}, u32[]{:S(2)}) async-start(bf16[16,80,512]{2,1,0:T(8,128)(2,1)} %pad_maximum_fusion.8), calls=%async_computation.4 | async-start | bytes 2621440 | tf_op jit(solution)/shard_map/all_to_all | solution.py:387
  768.6 5.5 collective-permute-start.37
  (51 other events, 301.6 us)
Sparse Core Ops, SparseCore 0:
  10.2 117.4 all-gather.10
  129.9 82.3 all-gather.12
  215.4 78.4 all-gather.6
  462.9 73.4 all-gather.8

commit v2 on v1

v2 whole, which is shorter than its diff:
```python
import functools
import math

import jax
import jax.numpy as jnp
import numpy as np
from jax import lax
from jax.experimental import pallas as pl
from jax.experimental.pallas import tpu as pltpu
from jax.sharding import PartitionSpec as P

eps_model = 1e-06
rope_base = 1000000.0
f32 = jnp.float32
bf16 = jnp.bfloat16


def inv_root(field):
    return lax.rsqrt(jnp.mean(field * field, axis=-1, keepdims=True) + eps_model)


def norm_back(field, factor, gain, grad_in):
    weighted = gain * grad_in
    inner_mean = jnp.mean(weighted * field, axis=-1, keepdims=True)
    return factor * weighted - field * (factor * factor * factor) * inner_mean


def rope_tables(positions, head_size):
    half_size = head_size // 2
    exponent = jnp.arange(half_size, dtype=f32) * f32(2.0 / head_size)
    inverse = jnp.exp(-exponent * f32(math.log(rope_base)))
    angles = positions.astype(f32)[:, None] * inverse[None, :]
    cosine, sine = jnp.cos(angles), jnp.sin(angles)
    return jnp.concatenate([cosine, cosine], axis=1), jnp.concatenate([-sine, sine], axis=1)


def dot_nn(left, right):
    return lax.dot_general(left, right, (((1,), (0,)), ((), ())), preferred_element_type=f32)


def dot_nt(left, right):
    return lax.dot_general(left, right, (((1,), (1,)), ((), ())), preferred_element_type=f32)


def dot_tn(left, right):
    return lax.dot_general(left, right, (((0,), (0,)), ((), ())), preferred_element_type=f32)


def allowed_tile(key_first, query_tile, pos_table, tile_k, tile_q, rows, sorted_all):
    key_pos = key_first + lax.broadcasted_iota(jnp.int32, (tile_k, tile_q), 0)
    lane = lax.broadcasted_iota(jnp.int32, (1, tile_q), 1)
    if sorted_all:
        query_pos = query_tile * tile_q + lane
    else:
        per_tile = tile_q // rows
        query_pos = jnp.zeros((1, tile_q), jnp.int32)
        for piece in range(per_tile):
            first = pos_table[query_tile * per_tile + piece] * rows
            inside = (lane >= piece * rows) & (lane < (piece + 1) * rows)
            query_pos = jnp.where(inside, first + lane - piece * rows, query_pos)
    return key_pos <= query_pos


def tile_loop(query_tile, key_tiles, sorted_all, work):
    if sorted_all:
        for key_tile in range(query_tile):
            work(key_tile, False)
        work(query_tile, True)
    else:

        @pl.loop(0, key_tiles)
        def _(key_tile):
            work(key_tile, True)


def query_loop(query_tiles, sorted_all, work):
    if sorted_all:
        for query_tile in range(query_tiles):
            work(query_tile)
    else:

        @pl.loop(0, query_tiles)
        def _(query_tile):
            work(query_tile)


def block_loop(blocks, work):
    def step(index, carry):
        work(index)
        return carry

    lax.fori_loop(0, blocks, step, 0, unroll=4)


def rows_at(index, rows):
    return pl.ds(pl.multiple_of(index * rows, rows), rows)


def each_key(key_pos, blocks, rows, work):
    for part in range(2):
        block_loop(
            blocks // 2,
            lambda index: work(
                part, rows_at(index, rows), rows_at(key_pos[part * (blocks // 2) + index], rows)
            ),
        )


def each_query(key_pos, query_table, pos_table, blocks, count, rows, sorted_all, work):
    if sorted_all:
        each_key(key_pos, blocks, rows, lambda part, here, place: work(part, here, place, place))
        return

    @pl.loop(0, count)
    def _(index):
        local = query_table[index]
        place, at_pos = rows_at(index, rows), rows_at(pos_table[index], rows)
        for part in range(2):
            inner = local - part * (blocks // 2)

            @pl.when((inner >= 0) & (inner < blocks // 2))
            def _():
                work(part, rows_at(inner, rows), place, at_pos)


def turn(field):
    return pltpu.roll(field, field.shape[-1] // 2, 1)


def attend_kernel(
    geometry, key_pos, query_table, pos_table, raw_a, raw_b, cos_ref, sin_ref, q_gain, k_gain,
    out_a, out_b, lse_ref, q_sorted, k_sorted, v_sorted, v_turned, acc, total, out_sorted,
):
    rows, tile, sorted_all, scale = geometry
    head = q_gain.shape[1]
    keys, queries = k_sorted.shape[0], q_sorted.shape[0]
    key_tiles, query_tiles = keys // tile, queries // tile
    raw, out = (raw_a, raw_b), (out_a, out_b)
    walk = (key_pos, query_table, pos_table, keys // rows, queries // rows, rows, sorted_all)

    def rope(field, gain, place):
        normed = field * inv_root(field) * gain[...]
        return (normed * cos_ref[place, :] + turn(normed) * sin_ref[place, :]).astype(bf16)

    def take_keys(part, here, place):
        k_sorted[place, :] = rope(raw[part][here, head : 2 * head], k_gain, place)
        v_sorted[place, :] = raw[part][here, 2 * head : 3 * head].astype(bf16)

    def take_queries(part, here, place, at_pos):
        q_sorted[place, :] = rope(raw[part][here, :head], q_gain, at_pos)

    each_key(key_pos, keys // rows, rows, take_keys)
    each_query(*walk, take_queries)
    for key_tile in range(key_tiles):
        piece = v_sorted[key_tile * tile : (key_tile + 1) * tile, :]
        v_turned[:, key_tile * tile : (key_tile + 1) * tile] = piece.astype(f32).T.astype(bf16)
    if not sorted_all:
        out_a[...] = jnp.zeros_like(out_a)
        out_b[...] = jnp.zeros_like(out_b)

    def query_work(query_tile):
        q_start = pl.multiple_of(query_tile * tile, tile)
        q_tile = q_sorted[pl.ds(q_start, tile), :]
        acc[...] = jnp.zeros_like(acc)
        total[...] = jnp.zeros_like(total)

        def work(key_tile, masked):
            k_start = pl.multiple_of(key_tile * tile, tile)
            scores = dot_nt(k_sorted[pl.ds(k_start, tile), :], q_tile)
            probs = jnp.exp(scores * scale)
            if masked:
                keep = allowed_tile(k_start, query_tile, pos_table, tile, tile, rows, sorted_all)
                probs = jnp.where(keep, probs, 0.0)
            total[...] += jnp.sum(probs, axis=0, keepdims=True)
            acc[...] += dot_nn(v_turned[:, pl.ds(k_start, tile)], probs.astype(bf16))

        tile_loop(query_tile, key_tiles, sorted_all, work)
        lse_ref[:, pl.ds(q_start, tile)] = jnp.log(total[...])
        out_sorted[pl.ds(q_start, tile), :] = (acc[...] / total[...]).T.astype(bf16)

    query_loop(query_tiles, sorted_all, query_work)

    def put(part, here, place, at_pos):
        out[part][here, :] = out_sorted[place, :]

    each_query(*walk, put)


def whole_spec(shape):
    return pl.BlockSpec(shape, lambda i, *_: (0, 0), pipeline_mode=pl.Buffered(1))


def attend(tables, raw, cosine, sine, query_gain, key_gain, rows, sorted_all, scale):
    head = query_gain.shape[1]
    keys = cosine.shape[0]
    queries = tables[1].shape[0] * rows
    tile = math.gcd(math.gcd(queries, keys), 512)
    narrow, row, part = whole_spec((keys, head)), whole_spec((1, head)), whole_spec((keys // 2, head))
    return pl.pallas_call(
        functools.partial(attend_kernel, (rows, tile, sorted_all, scale)),
        out_shape=(
            jax.ShapeDtypeStruct((keys // 2, head), bf16),
            jax.ShapeDtypeStruct((keys // 2, head), bf16),
            jax.ShapeDtypeStruct((1, queries), f32),
            jax.ShapeDtypeStruct((queries, head), bf16),
            jax.ShapeDtypeStruct((keys, head), bf16),
            jax.ShapeDtypeStruct((keys, head), bf16),
        ),
        grid_spec=pltpu.PrefetchScalarGridSpec(
            num_scalar_prefetch=3,
            grid=(1,),
            in_specs=[whole_spec(raw[0].shape), whole_spec(raw[1].shape), narrow, narrow, row, row],
            out_specs=(part, part, whole_spec((1, queries)), whole_spec((queries, head)), narrow, narrow),
            scratch_shapes=[
                pltpu.VMEM((head, keys), bf16),
                pltpu.VMEM((head, tile), f32),
                pltpu.VMEM((1, tile), f32),
                pltpu.VMEM((queries, head), bf16),
            ],
        ),
        compiler_params=pltpu.CompilerParams(vmem_limit_bytes=48 * 2**20),
        cost_estimate=pl.CostEstimate(
            flops=4 * queries * keys * head, bytes_accessed=28 * keys * head, transcendentals=queries * keys
        ),
        name="attend",
    )(*tables, *raw, cosine, sine, query_gain, key_gain)


def attend_back_kernel(
    geometry, key_pos, query_table, pos_table, raw_a, raw_b, cos_ref, sin_ref, q_gain, k_gain,
    q_sorted, k_sorted, v_sorted, o_a, o_b, do_a, do_b, lse_ref,
    grads_a, grads_b, q_part, k_part,
    do_sorted, o_sorted, k_turned, delta, dq_turned, dq_sorted, dk_sorted, dv_sorted,
):
    rows, tile, sorted_all, scale = geometry
    head = q_gain.shape[1]
    keys, queries = k_sorted.shape[0], q_sorted.shape[0]
    key_tiles, query_tiles = keys // tile, queries // tile
    raw, o_ref, do_ref, grads = (raw_a, raw_b), (o_a, o_b), (do_a, do_b), (grads_a, grads_b)
    walk = (key_pos, query_table, pos_table, keys // rows, queries // rows, rows, sorted_all)

    def take(part, here, place, at_pos):
        do_sorted[place, :] = do_ref[part][here, :]
        o_sorted[place, :] = o_ref[part][here, :]

    each_query(*walk, take)
    for key_tile in range(key_tiles):
        piece = k_sorted[key_tile * tile : (key_tile + 1) * tile, :]
        k_turned[:, key_tile * tile : (key_tile + 1) * tile] = piece.astype(f32).T.astype(bf16)
    dk_sorted[...] = jnp.zeros_like(dk_sorted)
    dv_sorted[...] = jnp.zeros_like(dv_sorted)
    if not sorted_all:
        for part in range(2):
            grads[part][:, :head] = jnp.zeros((keys // 2, head), bf16)

    def query_work(query_tile):
        q_start = pl.multiple_of(query_tile * tile, tile)
        q_tile = q_sorted[pl.ds(q_start, tile), :]
        do_tile = do_sorted[pl.ds(q_start, tile), :]
        product = do_tile.astype(f32) * o_sorted[pl.ds(q_start, tile), :].astype(f32)
        delta[...] = jnp.sum(product.T, axis=0, keepdims=True)
        dq_turned[...] = jnp.zeros_like(dq_turned)

        def work(key_tile, masked):
            k_start = pl.multiple_of(key_tile * tile, tile)
            here = pl.ds(k_start, tile)
            scores = dot_nt(k_sorted[here, :], q_tile)
            probs = jnp.exp(scores * scale - lse_ref[:, pl.ds(q_start, tile)])
            if masked:
                keep = allowed_tile(k_start, query_tile, pos_table, tile, tile, rows, sorted_all)
                probs = jnp.where(keep, probs, 0.0)
            dv_sorted[here, :] += dot_nn(probs.astype(bf16), do_tile)
            d_probs = dot_nt(v_sorted[here, :], do_tile)
            d_scores = (probs * (d_probs - delta[...])).astype(bf16)
            dk_sorted[here, :] += dot_nn(d_scores, q_tile)
            dq_turned[...] += dot_nn(k_turned[:, here], d_scores)

        tile_loop(query_tile, key_tiles, sorted_all, work)
        dq_sorted[pl.ds(q_start, tile), :] = dq_turned[...].T

    query_loop(query_tiles, sorted_all, query_work)
    q_part[...] = jnp.zeros_like(q_part)
    k_part[...] = jnp.zeros_like(k_part)

    def through_norm(field, grad, gain, at_pos, gain_part):
        scaled = grad * scale
        normed_grad = scaled * cos_ref[at_pos, :] - turn(scaled) * sin_ref[at_pos, :]
        factor = inv_root(field)
        gain_part[...] += jnp.sum(normed_grad * field * factor, axis=0, keepdims=True)
        return norm_back(field, factor, gain[...], normed_grad).astype(bf16)

    def put_queries(part, here, place, at_pos):
        grads[part][here, :head] = through_norm(
            raw[part][here, :head], dq_sorted[place, :], q_gain, at_pos, q_part
        )

    def put_keys(part, here, place):
        grads[part][here, head : 2 * head] = through_norm(
            raw[part][here, head : 2 * head], dk_sorted[place, :], k_gain, place, k_part
        )
        grads[part][here, 2 * head :] = dv_sorted[place, :].astype(bf16)

    each_query(*walk, put_queries)
    each_key(key_pos, keys // rows, rows, put_keys)


def attend_back(tables, raw, cosine, sine, query_gain, key_gain, saved, out, d_out, lse, rows, sorted_all, scale):
    head = query_gain.shape[1]
    keys = cosine.shape[0]
    queries = tables[1].shape[0] * rows
    tile = math.gcd(math.gcd(queries, keys), 512)
    narrow, row, part = whole_spec((keys, head)), whole_spec((1, head)), whole_spec((keys // 2, head))
    q_spec, wide = whole_spec((queries, head)), whole_spec((keys // 2, 3 * head))
    return pl.pallas_call(
        functools.partial(attend_back_kernel, (rows, tile, sorted_all, scale)),
        out_shape=(
            jax.ShapeDtypeStruct((keys // 2, 3 * head), bf16),
            jax.ShapeDtypeStruct((keys // 2, 3 * head), bf16),
            jax.ShapeDtypeStruct((1, head), f32),
            jax.ShapeDtypeStruct((1, head), f32),
        ),
        grid_spec=pltpu.PrefetchScalarGridSpec(
            num_scalar_prefetch=3,
            grid=(1,),
            in_specs=[
                whole_spec(raw[0].shape), whole_spec(raw[1].shape), narrow, narrow, row, row,
                q_spec, narrow, narrow, part, part, part, part, whole_spec((1, queries)),
            ],
            out_specs=(wide, wide, row, row),
            scratch_shapes=[
                pltpu.VMEM((queries, head), bf16),
                pltpu.VMEM((queries, head), bf16),
                pltpu.VMEM((head, keys), bf16),
                pltpu.VMEM((1, tile), f32),
                pltpu.VMEM((head, tile), f32),
                pltpu.VMEM((queries, head), f32),
                pltpu.VMEM((keys, head), f32),
                pltpu.VMEM((keys, head), f32),
            ],
        ),
        compiler_params=pltpu.CompilerParams(vmem_limit_bytes=60 * 2**20),
        cost_estimate=pl.CostEstimate(
            flops=10 * queries * keys * head, bytes_accessed=40 * keys * head, transcendentals=queries * keys
        ),
        name="attend_back",
    )(*tables, *raw, cosine, sine, query_gain, key_gain, *saved, *out, *d_out, lse)


class Ring:
    def __init__(self, size):
        self.chips = size // 2
        self.reach = self.chips // 2
        self.order = list(range(0, self.chips, 2)) + list(range(self.chips - 1, 0, -2))
        self.swap_pairs = [(i, i ^ 1) for i in range(size)]
        self.out_pairs = []
        for place, chip in enumerate(self.order):
            after_it = self.order[(place + 1) % self.chips]
            self.out_pairs.append((2 * chip, 2 * after_it))
            self.out_pairs.append((2 * after_it + 1, 2 * chip + 1))
        self.home_pairs = [(target, source) for source, target in self.out_pairs]

    def swap(self, field):
        return lax.ppermute(field, "ctx", self.swap_pairs)

    def out(self, field):
        return lax.ppermute(field, "ctx", self.out_pairs)

    def home(self, field):
        return lax.ppermute(field, "ctx", self.home_pairs)

    def members(self, rank):
        chip, core = rank // 2, rank % 2
        place = self.order.index(chip)
        blocks = [rank]
        for step in range(1, self.reach + 1):
            near = self.order[(place + (2 * core - 1) * step) % self.chips]
            blocks.append(2 * near + core)
            if step < self.reach:
                blocks.append(2 * near + 1 - core)
        return blocks

    def gather(self, block):
        first, second = block, self.swap(block)
        blocks = [block]
        for step in range(1, self.reach + 1):
            first = self.out(first)
            blocks.append(first)
            if step < self.reach:
                second = self.out(second)
                blocks.append(second)
        return blocks

    def scatter_sum(self, term, needs=None):
        needs = needs or {}
        first = self.home(term(2 * self.reach - 1))
        second = None
        marks = {self.reach: first}
        for step in range(self.reach - 1, 0, -1):
            if step in needs:
                first = after(first, needs[step])
            first = self.home((term(2 * step - 1).astype(f32) + first.astype(f32)).astype(bf16))
            other = term(2 * step)
            if second is not None:
                other = (other.astype(f32) + second.astype(f32)).astype(bf16)
            second = self.home(other)
            marks[step] = first
        total = first.astype(f32) + term(0).astype(f32) + self.swap(second).astype(f32)
        return total, marks


def after(value, *events):
    return lax.optimization_barrier((value, events))[0]


def spread(rows_block):
    return lax.all_to_all(rows_block, "ctx", split_axis=0, concat_axis=0, tiled=False)


def swap_rows(field):
    return lax.ppermute(field, "fsdp", [(0, 1), (1, 0)])


def to_columns(received, partner, fsdp_rank):
    first = jnp.where(fsdp_rank == 0, received, partner)
    second = jnp.where(fsdp_rank == 0, partner, received)
    both = jnp.stack([first, second], axis=1)
    return both.reshape(-1, received.shape[-1])


def to_rows(grads, extra, fsdp_rank, ctx_size, events=()):
    width = grads.shape[1]
    split = grads.reshape(ctx_size, 2, -1, width)
    rows = split.shape[2]
    keep = jnp.where(fsdp_rank == 0, split[:, 0], split[:, 1])
    give = jnp.where(fsdp_rank == 0, split[:, 1], split[:, 0])
    if extra is None:
        given = after(swap_rows(give), *events)
        return (keep.astype(f32) + given.astype(f32)).astype(bf16)
    count = extra.shape[0]
    lines = -(-count // width)
    lines = -(-lines // 16) * 16
    extra_block = jnp.pad(extra, (0, lines * width - count)).reshape(lines, width).astype(bf16)
    given = swap_rows(jnp.concatenate([give.reshape(-1, width), extra_block], axis=0))
    given = after(given, *events)
    body = given[: ctx_size * rows].reshape(ctx_size, rows, width)
    total = (keep.astype(f32) + body.astype(f32)).astype(bf16)
    extras = (extra_block.astype(f32) + given[ctx_size * rows :].astype(f32)).astype(bf16)
    return jnp.concatenate(
        [total, jnp.broadcast_to(extras[None], (ctx_size, lines, width))], axis=1
    )


def come_home(sent, rows, count):
    received = spread(sent)
    extra_sum = jnp.sum(received[:, rows:].astype(f32), axis=0).reshape(-1)[:count]
    return received[:, :rows], extra_sum


def side_by_side(pieces):
    count, rows, width = pieces.shape
    return jnp.transpose(pieces, (1, 0, 2)).reshape(rows, count * width)


def shards(
    block_input,
    query_weight,
    key_weight,
    value_weight,
    output_weight,
    gate_weight,
    up_weight,
    down_weight,
    attn_gain,
    mlp_gain,
    query_gain,
    key_gain,
    block_order,
    cotangent,
):
    ctx_size = lax.axis_size("ctx")
    ctx_rank = lax.axis_index("ctx")
    fsdp_rank = lax.axis_index("fsdp")
    core = ctx_rank % 2
    tokens = block_input.shape[1]
    model = block_input.shape[2]
    head_size = query_gain.shape[0]
    kv_heads = key_weight.shape[1] // head_size
    slots = block_order.shape[0]
    length = tokens * ctx_size
    half_rows = length // slots
    per_block = tokens // half_rows
    weight_rows = query_weight.shape[0]
    hidden_slice = gate_weight.shape[1] // ctx_size
    splits = ctx_size // 2 // kv_heads
    split_rank = (ctx_rank // 2) % splits
    sorted_all = splits == 1
    score_scale = 1.0 / math.sqrt(head_size)
    ring = Ring(ctx_size)

    def block_rows(field, index):
        return field[index * tokens : (index + 1) * tokens]

    def by_head(weight):
        split = jnp.transpose(weight.reshape(weight_rows, kv_heads, -1, head_size), (1, 2, 0, 3))
        return jnp.broadcast_to(split[:, None], (kv_heads, splits) + split.shape[1:]).reshape(
            -1, weight_rows, head_size
        )

    key_value = jnp.stack(
        [key_weight.reshape(weight_rows, kv_heads, head_size),
         value_weight.reshape(weight_rows, kv_heads, head_size)],
        axis=2,
    ).reshape(weight_rows, -1)
    head_block = jnp.concatenate(
        [by_head(query_weight), by_head(output_weight), by_head(key_value)], axis=2
    )
    head_received = spread(head_block)
    head_mine = to_columns(head_received, swap_rows(head_received), fsdp_rank)
    head_other = ring.swap(head_mine)

    def column(field, index):
        return field[:, index * head_size : (index + 1) * head_size]

    def key_first(mine, other):
        return jnp.where(core == 0, mine, other), jnp.where(core == 0, other, mine)

    key_columns, value_columns = key_first(column(head_mine, 2), column(head_other, 2))
    head_weight = jnp.concatenate(
        [column(head_mine, 0), key_columns, value_columns, column(head_other, 0)], axis=1
    )
    output_part = jnp.concatenate([column(head_mine, 1), column(head_other, 1)], axis=1)

    member_table = np.array(
        [ring.members(rank) + ring.members(rank ^ 1) for rank in range(ctx_size)], np.int32
    )
    ranks = jnp.arange(ctx_size, dtype=jnp.int32)
    listed = jnp.sum(jnp.where(ranks[:, None] == ctx_rank, member_table, 0), axis=0)
    slot_index = jnp.arange(slots, dtype=jnp.int32)
    local_slot = (
        listed[:, None] * per_block + jnp.arange(per_block, dtype=jnp.int32)[None, :]
    ).reshape(-1)
    local_pos = jnp.sum(
        jnp.where(local_slot[:, None] == slot_index[None, :], block_order[None, :], 0), axis=1
    )
    cosine, sine = rope_tables(jnp.arange(length, dtype=jnp.int32), head_size)
    if sorted_all:
        tables = (local_pos, slot_index, slot_index)
    else:
        local_of_pos = jnp.sum(
            jnp.where(local_pos[None, :] == slot_index[:, None], slot_index[None, :], 0), axis=1
        )
        compact = jnp.arange(slots // splits, dtype=jnp.int32)
        owner = (compact // per_block) * splits + split_rank
        own_pos = jnp.sort(jnp.take(block_order, owner * per_block + compact % per_block))
        tables = (local_pos, jnp.take(local_of_pos, own_pos), own_pos)
    query_row, key_row = query_gain[None, :], key_gain[None, :]

    input_blocks = ring.gather(block_input[0])
    input_blocks[3], tables, cosine, sine = lax.optimization_barrier(
        (input_blocks[3], tables, cosine, sine)
    )
    input_blocks[4] = after(input_blocks[4], head_received)

    def by_slice(weight):
        return jnp.transpose(weight.reshape(weight_rows, ctx_size, hidden_slice), (1, 0, 2))

    gate_up_block = jnp.concatenate([by_slice(gate_weight), by_slice(up_weight)], axis=2)
    down_block = by_slice(down_weight)
    input_blocks[5], gate_up_block, down_block = lax.optimization_barrier(
        (input_blocks[5], gate_up_block, down_block)
    )
    normed_list = []
    for block in input_blocks:
        wide = block.astype(f32)
        normed_list.append((wide * inv_root(wide) * attn_gain).astype(bf16))
    normed_attn = lax.optimization_barrier(jnp.concatenate(normed_list, axis=0))
    projected = dot_nn(normed_attn, head_weight)
    projected_given = ring.swap(
        jnp.concatenate(
            [projected[:, 3 * head_size :], projected[:, head_size : 3 * head_size]], axis=1
        )
    )
    raw = (projected, projected_given)
    attn_a, attn_b, lse, *saved = attend(
        tables, raw, cosine, sine, query_row, key_row, half_rows, sorted_all, score_scale
    )
    gate_up_received = spread(after(gate_up_block, input_blocks[-2]))
    gate_up_partner = swap_rows(gate_up_received)
    down_received = spread(after(down_block, gate_up_received))
    down_partner = swap_rows(down_received)
    attn_a, attn_b = after((attn_a, attn_b), gate_up_received)
    attn_pair = jnp.concatenate([attn_a, ring.swap(attn_b)], axis=1)

    inputs32 = block_input[0].astype(f32)
    scale_attn = inv_root(inputs32)
    attn_terms = dot_nt(attn_pair, output_part).astype(bf16)
    attn_out, _ = ring.scatter_sum(
        lambda i: block_rows(attn_terms, i),
        {ring.reach - 1: down_received, ring.reach - 2: gate_up_partner},
    )
    attn_out, gate_up_partner, down_partner = lax.optimization_barrier(
        (attn_out, gate_up_partner, down_partner)
    )
    hidden_one = inputs32 + attn_out
    scale_mlp = inv_root(hidden_one)
    normed_mlp = (hidden_one * scale_mlp * mlp_gain).astype(bf16)
    gate_up_mine = to_columns(gate_up_received, gate_up_partner, fsdp_rank)
    gate_up = jnp.concatenate([gate_up_mine, ring.swap(gate_up_mine)], axis=1)
    down_mine = to_columns(down_received, down_partner, fsdp_rank)
    down_part = jnp.concatenate([down_mine, ring.swap(down_mine)], axis=1)

    normed_blocks = ring.gather(normed_mlp)
    normed_all = jnp.concatenate(normed_blocks, axis=0)
    cot_blocks = ring.gather(after(cotangent[0], normed_blocks[-2]))
    cot_all = jnp.concatenate(cot_blocks, axis=0)
    hidden_all = dot_nn(normed_all, gate_up)
    act_grad_all = dot_nn(cot_all, down_part)
    activated_list, back_list = [], []
    for member in range(2):
        gate_pre = hidden_all[:, 2 * member * hidden_slice : (2 * member + 1) * hidden_slice]
        up_pre = hidden_all[:, (2 * member + 1) * hidden_slice : (2 * member + 2) * hidden_slice]
        act_grad = act_grad_all[:, member * hidden_slice : (member + 1) * hidden_slice]
        sigma = jax.nn.sigmoid(gate_pre)
        activated_list.append((gate_pre * sigma * up_pre).astype(bf16))
        back_list.append(
            (act_grad * up_pre * sigma * (1.0 + gate_pre * (1.0 - sigma))).astype(bf16)
        )
        back_list.append((act_grad * gate_pre * sigma).astype(bf16))
    activated_all = jnp.concatenate(activated_list, axis=1)
    back_all = jnp.concatenate(back_list, axis=1)
    far = (2 * ring.reach - 3) * tokens
    far_terms = dot_nt(back_all[far:], gate_up).astype(bf16)
    near_terms = dot_nt(back_all[:far], gate_up).astype(bf16)
    near_blocks = far // tokens
    normed_mlp_grad, _ = ring.scatter_sum(
        lambda i: block_rows(near_terms, i) if i < near_blocks else block_rows(far_terms, i - near_blocks)
    )
    out_terms = dot_nt(activated_all, down_part).astype(bf16)
    mlp_out, _ = ring.scatter_sum(lambda i: block_rows(out_terms, i))
    block_out = (hidden_one + mlp_out).astype(bf16)
    grad32 = cotangent[0].astype(f32)
    hidden_grad = grad32 + norm_back(hidden_one, scale_mlp, mlp_gain, normed_mlp_grad)
    hidden_grad_bf = hidden_grad.astype(bf16)

    mlp_gain_part = (
        jnp.sum(near_terms.astype(f32) * normed_all[:far].astype(f32), axis=0)
        + jnp.sum(far_terms.astype(f32) * normed_all[far:].astype(f32), axis=0)
    ) / mlp_gain
    pair = 2 * hidden_slice
    add = lambda left, right: (left.astype(f32) + right.astype(f32)).astype(bf16)
    down_give = dot_tn(cot_all, activated_all[:, hidden_slice:]).astype(bf16)
    down_keep = dot_tn(cot_all, activated_all[:, :hidden_slice]).astype(bf16)
    gate_up_give = dot_tn(normed_all, back_all[:, pair:]).astype(bf16)
    gate_up_keep = dot_tn(normed_all, back_all[:, :pair]).astype(bf16)

    grad_blocks = ring.gather(hidden_grad_bf)
    grad_all = jnp.concatenate(grad_blocks, axis=0)
    attn_grad_pair = dot_nn(grad_all, output_part).astype(bf16)
    attn_grad = (attn_grad_pair[:, :head_size], ring.swap(attn_grad_pair[:, head_size:]))
    down_sent = to_rows(
        add(down_keep, ring.swap(down_give)), mlp_gain_part, fsdp_rank, ctx_size, (grad_blocks[1],)
    )
    gate_up_sent = to_rows(
        add(gate_up_keep, ring.swap(gate_up_give)), None, fsdp_rank, ctx_size, (grad_blocks[-1],)
    )
    attn_grad, down_sent, gate_up_sent = lax.optimization_barrier(
        (attn_grad, down_sent, gate_up_sent)
    )
    gate_up_rows = spread(gate_up_sent)
    down_rows, mlp_gain_sum = come_home(down_sent, weight_rows, model)
    first_a, first_b, query_gain_part, key_gain_part = attend_back(
        tables, raw, cosine, sine, query_row, key_row, saved, (attn_a, attn_b), attn_grad, lse,
        half_rows, sorted_all, score_scale,
    )
    given_grads = ring.swap(first_b)
    half_grads = jnp.concatenate(
        [
            first_a[:, :head_size],
            add(first_a[:, head_size:], given_grads[:, head_size:]),
            given_grads[:, :head_size],
        ],
        axis=1,
    )
    input_terms = dot_nt(half_grads, head_weight).astype(bf16)
    normed_attn_grad, marks = ring.scatter_sum(
        lambda i: block_rows(input_terms, i), {ring.reach - 2: gate_up_rows}
    )
    late_grads = after(half_grads, marks[ring.reach])
    input_grad = hidden_grad + norm_back(inputs32, scale_attn, attn_gain, normed_attn_grad)
    head_grad = dot_tn(normed_attn, late_grads).astype(bf16)
    output_grad = dot_tn(grad_all, attn_pair).astype(bf16)
    attn_gain_part = (
        jnp.sum(input_terms.astype(f32) * normed_attn.astype(f32), axis=0) / attn_gain
    )
    kv_keep, kv_give = key_first(column(head_grad, 1), column(head_grad, 2))
    attn_keep = jnp.concatenate([column(head_grad, 0), column(output_grad, 0), kv_keep], axis=1)
    attn_give = jnp.concatenate([column(head_grad, 3), column(output_grad, 1), kv_give], axis=1)
    attn_rows, attn_extra = come_home(
        to_rows(
            add(attn_keep, ring.swap(attn_give)),
            jnp.concatenate([attn_gain_part, query_gain_part[0], key_gain_part[0]]),
            fsdp_rank,
            ctx_size,
        ),
        weight_rows,
        model + 2 * head_size,
    )

    def home(index):
        part = attn_rows[:, :, index * head_size : (index + 1) * head_size].astype(f32)
        return jnp.sum(part.reshape(kv_heads, splits, 2, weight_rows, head_size), axis=1)

    key_value_rows = home(2)
    flat = lambda part: side_by_side(part.reshape(-1, weight_rows, head_size))

    gate_rows, up_rows = gate_up_rows[:, :, :hidden_slice], gate_up_rows[:, :, hidden_slice:]

    return (
        block_out[None],
        input_grad[None],
        flat(home(0)),
        flat(key_value_rows[:, 0]),
        flat(key_value_rows[:, 1]),
        flat(home(1)),
        side_by_side(gate_rows).astype(f32),
        side_by_side(up_rows).astype(f32),
        side_by_side(down_rows).astype(f32),
        attn_extra[:model],
        mlp_gain_sum,
        attn_extra[model : model + head_size],
        attn_extra[model + head_size :],
    )


def solution(mesh):
    in_specs = (
        P("fsdp", "ctx", None),
        P(("ctx", "fsdp"), None),
        P(("ctx", "fsdp"), None),
        P(("ctx", "fsdp"), None),
        P(("ctx", "fsdp"), None),
        P(("ctx", "fsdp"), None),
        P(("ctx", "fsdp"), None),
        P(("ctx", "fsdp"), None),
        P(),
        P(),
        P(),
        P(),
        P(),
        P("fsdp", "ctx", None),
    )
    out_specs = (
        P("fsdp", "ctx", None),
        P("fsdp", "ctx", None),
        P(("ctx", "fsdp"), None),
        P(("ctx", "fsdp"), None),
        P(("ctx", "fsdp"), None),
        P(("ctx", "fsdp"), None),
        P(("ctx", "fsdp"), None),
        P(("ctx", "fsdp"), None),
        P(("ctx", "fsdp"), None),
        P(),
        P(),
        P(),
        P(),
    )
    return jax.shard_map(shards, mesh=mesh, in_specs=in_specs, out_specs=out_specs, check_vma=False)
```

time: 812 us -> 644 us (0.79)
  waiting for transfers between devices: 431 us -> 289 us
  local copies, waits for them, and re-layouts: 87.6 us -> 46.4 us
  starting transfers between devices: 71.1 us -> 111 us
  matrix products: 92.7 us -> 67.9 us
  between operations: 25.1 us -> 2.39 us
  other arithmetic: 82.4 us -> 90.8 us
  Pallas kernels: 17.3 us -> 25.5 us
    all_to_all x6, waiting for transfers between devices: 125 us -> 0.02 us  [spread(): lax.all_to_all(rows_block, 'ctx', split_axis=0, concat_axis=0, tiled=False)]
    ppermute x20 -> x62, starting transfers between devices: 13 us -> 50.2 us  [the longest x28 35.6 us: home(): return lax.ppermute(field, 'ctx', self.home_pairs)]
    all_gather x4 -> x0, waiting for transfers between devices: 32.2 us -> none  [the longest x1 32.2 us: shards(): lax.all_gather(output_weight, ('ctx', 'fsdp'), axis=0, tiled=True)]
    unnamed x166 -> x144, local copies, waits for them, and re-layouts: 45.4 us -> 19.5 us
    concatenate x6 -> x5, local copies, waits for them, and re-layouts: 20.7 us -> 0.25 us  [the longest x2 0.12 us: shards(): normed_all = jnp.concatenate(normed_blocks, axis=0)]
    unnamed x20 -> x12, other arithmetic: 2.34 us -> 18.4 us
    dot_general x28 -> x5, matrix products: 36.1 us -> 21.4 us  [dot_nt(): lax.dot_general(left, right, (((1,), (1,)), ((), ())), preferred_element_...]
    ppermute x20 -> x18, starting transfers between devices: 15.9 us -> 28.6 us  [swap(): return lax.ppermute(field, 'ctx', self.swap_pairs)]
  transfers between devices with their start and end apart: 50 -> 86, of which waited for: 22 -> 49; matrix products, arithmetic and copies ran while one was open for 30% -> 25% of each run, Pallas kernels for 2% -> 1%
where the time goes in v2:
time: 644 us; the launch traced here: 633 us
  waiting for transfers between devices  289 us (45%)
  starting transfers between devices  111 us (17%)
  other arithmetic  90.8 us (14%)
  matrix products  67.9 us (11%)
  local copies, waits for them, and re-layouts  46.4 us (7%)
  Pallas kernels  25.5 us (4%)
    ppermute x28, waiting for transfers between devices, home(): return lax.ppermute(field, 'ctx', self.home_pairs)  131 us
    ppermute x28, waiting for transfers between devices, out(): return lax.ppermute(field, 'ctx', self.out_pairs)  111 us
    ppermute x6, waiting for transfers between devices, swap_rows(): return lax.ppermute(field, 'fsdp', [(0, 1), (1, 0)])  40.3 us
    ppermute x28, starting transfers between devices, home(): return lax.ppermute(field, 'ctx', self.home_pairs)  35.6 us
    all_to_all x6, starting transfers between devices, spread(): lax.all_to_all(rows_block, 'ctx', split_axis=0, concat_axis=0, tiled=False)  32 us
    ppermute x18, starting transfers between devices, swap(): return lax.ppermute(field, 'ctx', self.swap_pairs)  28.6 us
    dot_general x6, matrix products, dot_tn(): lax.dot_general(left, right, (((0,), (0,)), ((), ())), preferred_element_...  25.4 us
    dot_general x5, matrix products, dot_nt(): lax.dot_general(left, right, (((1,), (1,)), ((), ())), preferred_element_...  21.4 us
  transfers between devices with their start and end apart: 86, of which 49 were waited for; matrix products, arithmetic and copies ran while one was open for 25% of the time, Pallas kernels for 1%

profile of v2, /device:TPU:9, one launch (start us, length us, event | category | flops | bytes accessed | tf_op | source)
XLA Modules:
  0.0 633.0 jit_solution(7532474939144500760)
XLA Ops:
  8.4 5.0 all-to-all-start
  14.4 3.7 fusion.63
  30.2 8.5 %collective-permute-done.1 = bf16[128,2048]{1,0:T(8,128)(2,1)} collective-permute-done((bf16[128,2048]{1,0:T(8,128)(2,1)}, bf16[128,2048]{1,0:T(8,128)(2,1)}, u32[]{:S(2)}, u32[]{:S(2)}) %collective-permute-start.1) | collective-permute-done | bytes 524320 | tf_op jit(solution)/shard_map/ppermute | solution.py:366
  40.0 4.3 collective-permute-done.3
  50.9 4.6 collective-permute-done.4
  62.2 5.3 collective-permute-done.6
  69.1 5.7 all-to-all-start.1
  88.4 5.3 fusion.62.raw_a
  95.2 3.3 collective-permute-done.10.raw_b
  98.5 8.7 %attend.1 = (bf16[1024,128]{1,0:T(8,128)(2,1)S(1)}, bf16[1024,128]{1,0:T(8,128)(2,1)S(1)}, f32[1,2048]{1,0:T(1,128)S(1)}, bf16[2048,128]{1,0:T(8,128)(2,1)S(1)},...) custom-call(s32[32]{0:T(128)S(1)} %select_reduce_fusion.key_pos, s32[32]{0:T(128)S(1)} %iota.40.query_table.pos_table, ...), custom_call_target="tpu_custom_call" | custom-call | flops 2147483648 | bytes 7340032 | tf_op jit(solution)/shard_map/attend/pallas_call | solution.py:199
  114.1 5.8 all-to-all-start.2
  125.8 17.4 %collective-permute-done.12 = bf16[128,2048]{1,0:T(8,128)(2,1)S(1)} collective-permute-done((bf16[128,2048]{1,0:T(8,128)(2,1)S(1)}, bf16[128,2048]{1,0:T(8,128)(2,1)S(1)}, u32[]{:S(2)}, u32[]{:S(2)}) %collective-permute-start.12) | collective-permute-done | bytes 524320 | tf_op jit(solution)/shard_map/ppermute | solution.py:369
  146.8 9.0 %collective-permute-done.14 = bf16[16,64,768]{2,1,0:T(8,128)(2,1)} collective-permute-done((bf16[16,64,768]{2,1,0:T(8,128)(2,1)}, bf16[16,64,768]{2,1,0:T(8,128)(2,1)}, u32[]{:S(2)}, u32[]{:S(2)}) %collective-permute-start.14) | collective-permute-done | bytes 1572896 | tf_op jit(solution)/shard_map/ppermute | solution.py:420
  158.5 6.9 %collective-permute-done.15 = bf16[128,2048]{1,0:T(8,128)(2,1)S(1)} collective-permute-done((bf16[128,2048]{1,0:T(8,128)(2,1)S(1)}, bf16[128,2048]{1,0:T(8,128)(2,1)S(1)}, u32[]{:S(2)}, u32[]{:S(2)}) %collective-permute-start.15) | collective-permute-done | bytes 524320 | tf_op jit(solution)/shard_map/ppermute | solution.py:369
  168.2 7.1 %collective-permute-done.18 = bf16[128,2048]{1,0:T(8,128)(2,1)S(1)} collective-permute-done((bf16[128,2048]{1,0:T(8,128)(2,1)S(1)}, bf16[128,2048]{1,0:T(8,128)(2,1)S(1)}, u32[]{:S(2)}, u32[]{:S(2)}) %collective-permute-start.18) | collective-permute-done | bytes 524320 | tf_op jit(solution)/shard_map/ppermute | solution.py:369
  179.1 5.8 collective-permute-done.19
  184.9 3.8 collective-permute-start.20
  191.8 16.0 %collective-permute-done.21 = bf16[16,64,384]{2,1,0:T(8,128)(2,1)S(1)} collective-permute-done((bf16[16,64,384]{2,1,0:T(8,128)(2,1)S(1)}, bf16[16,64,384]{2,1,0:T(8,128)(2,1)S(1)}, u32[]{:S(2)}, u32[]{:S(2)}) %collective-permute-start.21) | collective-permute-done | bytes 786464 | tf_op jit(solution)/shard_map/ppermute | solution.py:420
  217.5 5.5 collective-permute-done.24
  228.8 5.5 collective-permute-done.26
  234.7 5.3 collective-permute-done.27
  240.0 5.5 collective-permute-done.28
  248.2 8.6 %collective-permute-done.40 = bf16[128,2048]{1,0:T(8,128)(2,1)S(1)} collective-permute-done((bf16[128,2048]{1,0:T(8,128)(2,1)S(1)}, bf16[128,2048]{1,0:T(8,128)(2,1)S(1)}, u32[]{:S(2)}, u32[]{:S(2)}) %collective-permute-start.40) | collective-permute-done | bytes 524320 | tf_op jit(solution)/shard_map/ppermute | solution.py:366
  257.0 5.4 collective-permute-done.42
  262.5 5.5 collective-permute-done.43
  268.1 9.6 %fusion.3 = f32[1024,1536]{1,0:T(8,128)S(1)} fusion(bf16[1024,2048]{1,0:T(8,128)(2,1)} %copy-done.48, bf16[2048,768]{1,0:T(8,128)(2,1)S(1)} %collective-permute-done.30, bf16[2048,768]{1,0:T(8,128)(2,1)S(1)} %bitcast.186), kind=kOutput, calls=%fused_computation.32 | convolution fusion | flops 6455033856 | bytes 16777216 | tf_op jit(solution)/shard_map/dot_general | solution.py:38
  280.8 5.4 collective-permute-done.46
  286.2 5.6 collective-permute-done.47
  291.9 4.8 fusion.1
  298.7 3.7 convolution_convert_fusion.8
  302.4 3.6 convolution_convert_fusion.7
  306.0 5.3 convolution_convert_fusion.2
  313.9 5.1 convolution_convert_fusion.4
  318.9 5.0 convolution_convert_fusion.3
  323.9 4.6 multiply_reduce_fusion.2
  340.4 6.1 convolution_convert_fusion.5
  346.5 8.3 %collective-permute-done.33 = bf16[128,2048]{1,0:T(8,128)(2,1)S(1)} collective-permute-done((bf16[128,2048]{1,0:T(8,128)(2,1)S(1)}, bf16[128,2048]{1,0:T(8,128)(2,1)S(1)}, u32[]{:S(2)}, u32[]{:S(2)}) %collective-permute-start.33) | collective-permute-done | bytes 524320 | tf_op jit(solution)/shard_map/ppermute | solution.py:369
  356.2 4.2 collective-permute-done.49
  362.9 3.2 collective-permute-done.34
  368.6 3.1 collective-permute-done.50
  388.8 10.9 %collective-permute-done.38 = bf16[128,2048]{1,0:T(8,128)(2,1)S(1)} collective-permute-done((bf16[128,2048]{1,0:T(8,128)(2,1)S(1)}, bf16[128,2048]{1,0:T(8,128)(2,1)S(1)}, u32[]{:S(2)}, u32[]{:S(2)}) %collective-permute-start.38) | collective-permute-done | bytes 524320 | tf_op jit(solution)/shard_map/ppermute | solution.py:369
  399.8 3.7 collective-permute-start.39
  405.4 3.7 collective-permute-start.55
  410.7 2.6 multiply_reduce_fusion.3
  419.4 4.3 collective-permute-done.56
  423.9 4.9 collective-permute-done.66
  429.5 5.5 collective-permute-done.59
  436.2 4.4 collective-permute-done.60
  440.8 5.5 collective-permute-done.61
  446.4 5.5 collective-permute-done.62
  451.9 5.6 collective-permute-done.63
  465.1 16.8 %attend_back.1 = (bf16[1024,384]{1,0:T(8,128)(2,1)}, bf16[1024,384]{1,0:T(8,128)(2,1)}, f32[1,128]{1,0:T(1,128)}, f32[1,128]{1,0:T(1,128)}) custom-call(s32[32]{0:T(128)} %copy-done.7, s32[32]{0:T(128)} %copy-done.8, s32[32]{0:T(128)} %copy-done.8, f32[1024,512]{1,0:T(8,128)} %copy-done.31, f32[1024,384]{1,0:T(8,128)} %copy-done.3, f32[2048,128]{1,0:T(8,128)} %copy-done, ...), custom_call_target="tpu_custom_call" | custom-call | flops 5368709120 | bytes 10485760 | tf_op jit(solution)/shard_map/attend_back/pallas_call | solution.py:314
  482.8 3.5 convolution_convert_fusion.10
  486.5 4.2 multiply_reduce_fusion
  495.9 5.6 all-to-all-start.3
  502.5 4.6 convolution_convert_fusion.6
  515.1 3.1 add_convert_fusion.1
  520.1 27.2 %collective-permute-done.71 = bf16[128,2048]{1,0:T(8,128)(2,1)} collective-permute-done((bf16[128,2048]{1,0:T(8,128)(2,1)}, bf16[128,2048]{1,0:T(8,128)(2,1)}, u32[]{:S(2)}, u32[]{:S(2)}) %collective-permute-start.71) | collective-permute-done | bytes 524320 | tf_op jit(solution)/shard_map/ppermute | solution.py:369
  553.6 5.1 all-to-all-start.5
  558.7 2.7 add_convert_fusion.5
  562.6 9.1 %collective-permute-done.79 = bf16[1040,384]{1,0:T(8,128)(2,1)} collective-permute-done((bf16[1040,384]{1,0:T(8,128)(2,1)}, bf16[1040,384]{1,0:T(8,128)(2,1)}, u32[]{:S(2)}, u32[]{:S(2)}) %collective-permute-start.79) | collective-permute-done | bytes 798752 | tf_op jit(solution)/shard_map/ppermute | solution.py:420
  573.2 13.0 %collective-permute-done.75 = bf16[128,2048]{1,0:T(8,128)(2,1)S(1)} collective-permute-done((bf16[128,2048]{1,0:T(8,128)(2,1)S(1)}, bf16[128,2048]{1,0:T(8,128)(2,1)S(1)}, u32[]{:S(2)}, u32[]{:S(2)}) %collective-permute-start.75) | collective-permute-done | bytes 524320 | tf_op jit(solution)/shard_map/ppermute | solution.py:369
  591.9 4.8 all-to-all-start.4
  606.8 17.5 %collective-permute-done.73 = bf16[128,2048]{1,0:T(8,128)(2,1)S(1)} collective-permute-done((bf16[128,2048]{1,0:T(8,128)(2,1)}, bf16[128,2048]{1,0:T(8,128)(2,1)S(1)}, u32[]{:S(2)}, u32[]{:S(2)}) %collective-permute-start.73) | collective-permute-done | bytes 524320 | tf_op jit(solution)/shard_map/ppermute | solution.py:369
  (421 shorter events, 211.6 us)
Async XLA Ops:
  0.6 24.8 %collective-permute-start = (bf16[128,2048]{1,0:T(8,128)(2,1)}, bf16[128,2048]{1,0:T(8,128)(2,1)}, u32[]{:S(2)}, u32[]{:S(2)}) collective-permute-start(bf16[128,2048]{1,0:T(8,128)(2,1)} %bitcast.174), channel_id=1, source_target_pairs={{0,8},{10,2},{8,16},{18,10},{16,24},{26,18},{24,28},{30,26},{28,20... | collective-permute-start | bytes 1572872 | tf_op jit(solution)/shard_map/ppermute | solution.py:366
  0.7 26.0 %collective-permute-start.2 = (bf16[128,2048]{1,0:T(8,128)(2,1)}, bf16[128,2048]{1,0:T(8,128)(2,1)}, u32[]{:S(2)}, u32[]{:S(2)}) collective-permute-start(bf16[128,2048]{1,0:T(8,128)(2,1)} %bitcast.175), channel_id=1, source_target_pairs={{0,2},{2,0},{4,6},{6,4},{8,10},{10,8},{12,14},{14,12},{16,18},{18,... | collective-permute-start | bytes 1572872 | tf_op jit(solution)/shard_map/ppermute | solution.py:363
  8.4 41.3 %all-to-all-start = ((bf16[16,64,384]{2,1,0:T(8,128)(2,1)}), bf16[16,64,384]{2,1,0:T(8,128)(2,1)S(1)}, u32[]{:S(2)}, u32[]{:S(2)}) async-start(bf16[16,64,384]{2,1,0:T(8,128)(2,1)} %pad_maximum_fusion.23), calls=%async_computation | async-start | bytes 1572864 | tf_op jit(solution)/shard_map/all_to_all | solution.py:416
  25.4 13.3 %collective-permute-start.1 = (bf16[128,2048]{1,0:T(8,128)(2,1)}, bf16[128,2048]{1,0:T(8,128)(2,1)}, u32[]{:S(2)}, u32[]{:S(2)}) collective-permute-start(bf16[128,2048]{1,0:T(8,128)(2,1)} %collective-permute-done), channel_id=1, source_target_pairs={{0,8},{10,2},{8,16},{18,10},{16,24},{26,18},{24,28},{30,26},{28,20... | collective-permute-start | bytes 1572872 | tf_op jit(solution)/shard_map/ppermute | solution.py:366
  26.8 17.5 %collective-permute-start.3 = (bf16[128,2048]{1,0:T(8,128)(2,1)}, bf16[128,2048]{1,0:T(8,128)(2,1)}, u32[]{:S(2)}, u32[]{:S(2)}) collective-permute-start(bf16[128,2048]{1,0:T(8,128)(2,1)} %collective-permute-done.2), channel_id=1, source_target_pairs={{0,8},{10,2},{8,16},{18,10},{16,24},{26,18},{24,28},{30,26},{28,20... | collective-permute-start | bytes 1572872 | tf_op jit(solution)/shard_map/ppermute | solution.py:366
  38.7 18.1 %collective-permute-start.5 = (bf16[128,2048]{1,0:T(8,128)(2,1)}, bf16[128,2048]{1,0:T(8,128)(2,1)}, u32[]{:S(2)}, u32[]{:S(2)}) collective-permute-start(bf16[128,2048]{1,0:T(8,128)(2,1)} %collective-permute-done.1), channel_id=1, source_target_pairs={{0,8},{10,2},{8,16},{18,10},{16,24},{26,18},{24,28},{30,26},{28,20... | collective-permute-start | bytes 1572872 | tf_op jit(solution)/shard_map/ppermute | solution.py:366
  44.3 11.2 %collective-permute-start.4 = (bf16[128,2048]{1,0:T(8,128)(2,1)}, bf16[128,2048]{1,0:T(8,128)(2,1)}, u32[]{:S(2)}, u32[]{:S(2)}) collective-permute-start(bf16[128,2048]{1,0:T(8,128)(2,1)} %collective-permute-done.3), channel_id=1, source_target_pairs={{0,8},{10,2},{8,16},{18,10},{16,24},{26,18},{24,28},{30,26},{28,20... | collective-permute-start | bytes 1572872 | tf_op jit(solution)/shard_map/ppermute | solution.py:366
  49.7 25.2 %collective-permute-start.8 = (bf16[16,64,384]{2,1,0:T(8,128)(2,1)S(1)}, bf16[16,64,384]{2,1,0:T(8,128)(2,1)}, u32[]{:S(2)}, u32[]{:S(2)}) collective-permute-start(bf16[16,64,384]{2,1,0:T(8,128)(2,1)S(1)} %all-to-all-done), channel_id=1, source_target_pairs={{0,1},{1,0},{2,3},{3,2},{4,5},{5,4},{6,7},{7,6},{8,9},{9,8},{10,11... | collective-permute-start | bytes 2359304 | tf_op jit(solution)/shard_map/ppermute | solution.py:420
  60.1 21.8 %collective-permute-start.7 = (bf16[128,2048]{1,0:T(8,128)(2,1)}, bf16[128,2048]{1,0:T(8,128)(2,1)}, u32[]{:S(2)}, u32[]{:S(2)}) collective-permute-start(bf16[128,2048]{1,0:T(8,128)(2,1)} %collective-permute-done.5), channel_id=1, source_target_pairs={{0,8},{10,2},{8,16},{18,10},{16,24},{26,18},{24,28},{30,26},{28,20... | collective-permute-start | bytes 1572872 | tf_op jit(solution)/shard_map/ppermute | solution.py:366
  69.1 42.3 %all-to-all-start.1 = ((bf16[16,64,768]{2,1,0:T(8,128)(2,1)}), bf16[16,64,768]{2,1,0:T(8,128)(2,1)}, u32[]{:S(2)}, u32[]{:S(2)}) async-start(bf16[16,64,768]{2,1,0:T(8,128)(2,1)} %copy.149), calls=%async_computation.1 | async-start | bytes 3145728 | tf_op jit(solution)/shard_map/all_to_all | solution.py:416
  114.1 29.1 %all-to-all-start.2 = ((bf16[16,64,384]{2,1,0:T(8,128)(2,1)}), bf16[16,64,384]{2,1,0:T(8,128)(2,1)S(1)}, u32[]{:S(2)}, u32[]{:S(2)}) async-start(bf16[16,64,384]{2,1,0:T(8,128)(2,1)} %copy.151), calls=%async_computation.2 | async-start | bytes 1572864 | tf_op jit(solution)/shard_map/all_to_all | solution.py:416
  119.9 35.9 %collective-permute-start.14 = (bf16[16,64,768]{2,1,0:T(8,128)(2,1)}, bf16[16,64,768]{2,1,0:T(8,128)(2,1)}, u32[]{:S(2)}, u32[]{:S(2)}) collective-permute-start(bf16[16,64,768]{2,1,0:T(8,128)(2,1)} %all-to-all-done.1), channel_id=1, source_target_pairs={{0,1},{1,0},{2,3},{3,2},{4,5},{5,4},{6,7},{7,6},{8,9},{9,8},{10,11... | collective-permute-start | bytes 4718600 | tf_op jit(solution)/shard_map/ppermute | solution.py:420
  124.6 18.6 %collective-permute-start.12 = (bf16[128,2048]{1,0:T(8,128)(2,1)S(1)}, bf16[128,2048]{1,0:T(8,128)(2,1)S(1)}, u32[]{:S(2)}, u32[]{:S(2)}) collective-permute-start(bf16[128,2048]{1,0:T(8,128)(2,1)S(1)} %get-tuple-element.110), channel_id=1, source_target_pairs={{8,0},{2,10},{16,8},{10,18},{24,16},{18,26},{28,24},{26,30},{20,28... | collective-permute-start | bytes 1572872 | tf_op jit(solution)/shard_map/ppermute | solution.py:369
  144.4 11.5 %collective-permute-start.13 = (bf16[128,2048]{1,0:T(8,128)(2,1)S(1)}, bf16[128,2048]{1,0:T(8,128)(2,1)S(1)}, u32[]{:S(2)}, u32[]{:S(2)}) collective-permute-start(bf16[128,2048]{1,0:T(8,128)(2,1)S(1)} %add_convert_fusion.24), channel_id=1, source_target_pairs={{8,0},{2,10},{16,8},{10,18},{24,16},{18,26},{28,24},{26,30},{20,28... | collective-permute-start | bytes 1572872 | tf_op jit(solution)/shard_map/ppermute | solution.py:369
  146.7 11.7 %collective-permute-start.17 = (bf16[128,2048]{1,0:T(8,128)(2,1)S(1)}, bf16[128,2048]{1,0:T(8,128)(2,1)S(1)}, u32[]{:S(2)}, u32[]{:S(2)}) collective-permute-start(bf16[128,2048]{1,0:T(8,128)(2,1)S(1)} %get-tuple-element.111), channel_id=1, source_target_pairs={{8,0},{2,10},{16,8},{10,18},{24,16},{18,26},{28,24},{26,30},{20,28... | collective-permute-start | bytes 1572872 | tf_op jit(solution)/shard_map/ppermute | solution.py:369
  177.8 12.8 %collective-permute-start.16 = (bf16[128,2048]{1,0:T(8,128)(2,1)S(1)}, bf16[128,2048]{1,0:T(8,128)(2,1)S(1)}, u32[]{:S(2)}, u32[]{:S(2)}) collective-permute-start(bf16[128,2048]{1,0:T(8,128)(2,1)S(1)} %get-tuple-element.108), channel_id=1, source_target_pairs={{8,0},{2,10},{16,8},{10,18},{24,16},{18,26},{28,24},{26,30},{20,28... | collective-permute-start | bytes 1572872 | tf_op jit(solution)/shard_map/ppermute | solution.py:369
  188.7 19.2 %collective-permute-start.21 = (bf16[16,64,384]{2,1,0:T(8,128)(2,1)S(1)}, bf16[16,64,384]{2,1,0:T(8,128)(2,1)S(1)}, u32[]{:S(2)}, u32[]{:S(2)}) collective-permute-start(bf16[16,64,384]{2,1,0:T(8,128)(2,1)S(1)} %all-to-all-done.2), channel_id=1, source_target_pairs={{0,1},{1,0},{2,3},{3,2},{4,5},{5,4},{6,7},{7,6},{8,9},{9,8},{10,11... | collective-permute-start | bytes 2359304 | tf_op jit(solution)/shard_map/ppermute | solution.py:420
  210.7 12.4 %collective-permute-start.24 = (bf16[128,2048]{1,0:T(8,128)(2,1)S(1)}, bf16[128,2048]{1,0:T(8,128)(2,1)S(1)}, u32[]{:S(2)}, u32[]{:S(2)}) collective-permute-start(bf16[128,2048]{1,0:T(8,128)(2,1)S(1)} %collective-permute-done.23), channel_id=1, source_target_pairs={{0,8},{10,2},{8,16},{18,10},{16,24},{26,18},{24,28},{30,26},{28,20... | collective-permute-start | bytes 1572872 | tf_op jit(solution)/shard_map/ppermute | solution.py:366
  213.1 55.0 %collective-permute-start.30 = (bf16[2048,768]{1,0:T(8,128)(2,1)S(1)}, bf16[2048,768]{1,0:T(8,128)(2,1)S(1)}, u32[]{:S(2)}, u32[]{:S(2)}) collective-permute-start(bf16[2048,768]{1,0:T(8,128)(2,1)S(1)} %bitcast.185), channel_id=1, source_target_pairs={{0,2},{2,0},{4,6},{6,4},{8,10},{10,8},{12,14},{14,12},{16,18},{18,... | collective-permute-start | bytes 9437192 | tf_op jit(solution)/shard_map/ppermute | solution.py:363
  217.5 11.2 %collective-permute-start.25 = (bf16[128,2048]{1,0:T(8,128)(2,1)S(1)}, bf16[128,2048]{1,0:T(8,128)(2,1)S(1)}, u32[]{:S(2)}, u32[]{:S(2)}) collective-permute-start(bf16[128,2048]{1,0:T(8,128)(2,1)S(1)} %collective-permute-done.22), channel_id=1, source_target_pairs={{0,8},{10,2},{8,16},{18,10},{16,24},{26,18},{24,28},{30,26},{28,20... | collective-permute-start | bytes 1572872 | tf_op jit(solution)/shard_map/ppermute | solution.py:366
  223.1 11.2 %collective-permute-start.26 = (bf16[128,2048]{1,0:T(8,128)(2,1)S(1)}, bf16[128,2048]{1,0:T(8,128)(2,1)S(1)}, u32[]{:S(2)}, u32[]{:S(2)}) collective-permute-start(bf16[128,2048]{1,0:T(8,128)(2,1)S(1)} %collective-permute-done.24), channel_id=1, source_target_pairs={{0,8},{10,2},{8,16},{18,10},{16,24},{26,18},{24,28},{30,26},{28,20... | collective-permute-start | bytes 1572872 | tf_op jit(solution)/shard_map/ppermute | solution.py:366
  223.7 68.1 %collective-permute-start.31 = (bf16[2048,384]{1,0:T(8,128)(2,1)S(1)}, bf16[2048,384]{1,0:T(8,128)(2,1)}, u32[]{:S(2)}, u32[]{:S(2)}) collective-permute-start(bf16[2048,384]{1,0:T(8,128)(2,1)S(1)} %bitcast.197), channel_id=1, source_target_pairs={{0,2},{2,0},{4,6},{6,4},{8,10},{10,8},{12,14},{14,12},{16,18},{18,... | collective-permute-start | bytes 4718600 | tf_op jit(solution)/shard_map/ppermute | solution.py:363
  228.7 11.2 %collective-permute-start.27 = (bf16[128,2048]{1,0:T(8,128)(2,1)S(1)}, bf16[128,2048]{1,0:T(8,128)(2,1)S(1)}, u32[]{:S(2)}, u32[]{:S(2)}) collective-permute-start(bf16[128,2048]{1,0:T(8,128)(2,1)S(1)} %collective-permute-done.25), channel_id=1, source_target_pairs={{0,8},{10,2},{8,16},{18,10},{16,24},{26,18},{24,28},{30,26},{28,20... | collective-permute-start | bytes 1572872 | tf_op jit(solution)/shard_map/ppermute | solution.py:366
  234.3 11.2 %collective-permute-start.28 = (bf16[128,2048]{1,0:T(8,128)(2,1)S(1)}, bf16[128,2048]{1,0:T(8,128)(2,1)S(1)}, u32[]{:S(2)}, u32[]{:S(2)}) collective-permute-start(bf16[128,2048]{1,0:T(8,128)(2,1)S(1)} %collective-permute-done.26), channel_id=1, source_target_pairs={{0,8},{10,2},{8,16},{18,10},{16,24},{26,18},{24,28},{30,26},{28,20... | collective-permute-start | bytes 1572872 | tf_op jit(solution)/shard_map/ppermute | solution.py:366
  239.9 17.0 %collective-permute-start.29 = (bf16[128,2048]{1,0:T(8,128)(2,1)S(1)}, bf16[128,2048]{1,0:T(8,128)(2,1)S(1)}, u32[]{:S(2)}, u32[]{:S(2)}) collective-permute-start(bf16[128,2048]{1,0:T(8,128)(2,1)S(1)} %collective-permute-done.27), channel_id=1, source_target_pairs={{0,8},{10,2},{8,16},{18,10},{16,24},{26,18},{24,28},{30,26},{28,20... | collective-permute-start | bytes 1572872 | tf_op jit(solution)/shard_map/ppermute | solution.py:366
  246.5 10.3 %collective-permute-start.40 = (bf16[128,2048]{1,0:T(8,128)(2,1)S(1)}, bf16[128,2048]{1,0:T(8,128)(2,1)S(1)}, u32[]{:S(2)}, u32[]{:S(2)}) collective-permute-start(bf16[128,2048]{1,0:T(8,128)(2,1)S(1)} %bitcast.195), channel_id=1, source_target_pairs={{0,8},{10,2},{8,16},{18,10},{16,24},{26,18},{24,28},{30,26},{28,20... | collective-permute-start | bytes 1572872 | tf_op jit(solution)/shard_map/ppermute | solution.py:366
  248.0 14.4 %collective-permute-start.42 = (bf16[128,2048]{1,0:T(8,128)(2,1)S(1)}, bf16[128,2048]{1,0:T(8,128)(2,1)S(1)}, u32[]{:S(2)}, u32[]{:S(2)}) collective-permute-start(bf16[128,2048]{1,0:T(8,128)(2,1)S(1)} %collective-permute-done.41), channel_id=1, source_target_pairs={{0,8},{10,2},{8,16},{18,10},{16,24},{26,18},{24,28},{30,26},{28,20... | collective-permute-start | bytes 1572872 | tf_op jit(solution)/shard_map/ppermute | solution.py:366
  256.8 11.2 %collective-permute-start.43 = (bf16[128,2048]{1,0:T(8,128)(2,1)S(1)}, bf16[128,2048]{1,0:T(8,128)(2,1)S(1)}, u32[]{:S(2)}, u32[]{:S(2)}) collective-permute-start(bf16[128,2048]{1,0:T(8,128)(2,1)S(1)} %collective-permute-done.40), channel_id=1, source_target_pairs={{0,8},{10,2},{8,16},{18,10},{16,24},{26,18},{24,28},{30,26},{28,20... | collective-permute-start | bytes 1572872 | tf_op jit(solution)/shard_map/ppermute | solution.py:366
  262.4 15.4 %collective-permute-start.44 = (bf16[128,2048]{1,0:T(8,128)(2,1)S(1)}, bf16[128,2048]{1,0:T(8,128)(2,1)S(1)}, u32[]{:S(2)}, u32[]{:S(2)}) collective-permute-start(bf16[128,2048]{1,0:T(8,128)(2,1)S(1)} %collective-permute-done.42), channel_id=1, source_target_pairs={{0,8},{10,2},{8,16},{18,10},{16,24},{26,18},{24,28},{30,26},{28,20... | collective-permute-start | bytes 1572872 | tf_op jit(solution)/shard_map/ppermute | solution.py:366
  268.0 11.3 %collective-permute-start.45 = (bf16[128,2048]{1,0:T(8,128)(2,1)S(1)}, bf16[128,2048]{1,0:T(8,128)(2,1)S(1)}, u32[]{:S(2)}, u32[]{:S(2)}) collective-permute-start(bf16[128,2048]{1,0:T(8,128)(2,1)S(1)} %collective-permute-done.43), channel_id=1, source_target_pairs={{0,8},{10,2},{8,16},{18,10},{16,24},{26,18},{24,28},{30,26},{28,20... | collective-permute-start | bytes 1572872 | tf_op jit(solution)/shard_map/ppermute | solution.py:366
  279.3 12.5 %collective-permute-start.47 = (bf16[128,2048]{1,0:T(8,128)(2,1)S(1)}, bf16[128,2048]{1,0:T(8,128)(2,1)S(1)}, u32[]{:S(2)}, u32[]{:S(2)}) collective-permute-start(bf16[128,2048]{1,0:T(8,128)(2,1)S(1)} %collective-permute-done.45), channel_id=1, source_target_pairs={{0,8},{10,2},{8,16},{18,10},{16,24},{26,18},{24,28},{30,26},{28,20... | collective-permute-start | bytes 1572872 | tf_op jit(solution)/shard_map/ppermute | solution.py:366
  312.2 23.6 %collective-permute-start.32 = (bf16[128,2048]{1,0:T(8,128)(2,1)S(1)}, bf16[128,2048]{1,0:T(8,128)(2,1)S(1)}, u32[]{:S(2)}, u32[]{:S(2)}) collective-permute-start(bf16[128,2048]{1,0:T(8,128)(2,1)S(1)} %get-tuple-element.106), channel_id=1, source_target_pairs={{8,0},{2,10},{16,8},{10,18},{24,16},{18,26},{28,24},{26,30},{20,28... | collective-permute-start | bytes 1572872 | tf_op jit(solution)/shard_map/ppermute | solution.py:369
  331.1 31.7 %collective-permute-start.36 = (bf16[128,2048]{1,0:T(8,128)(2,1)}, bf16[128,2048]{1,0:T(8,128)(2,1)S(1)}, u32[]{:S(2)}, u32[]{:S(2)}) collective-permute-start(bf16[128,2048]{1,0:T(8,128)(2,1)} %get-tuple-element.107), channel_id=1, source_target_pairs={{8,0},{2,10},{16,8},{10,18},{24,16},{18,26},{28,24},{26,30},{20,28... | collective-permute-start | bytes 1572872 | tf_op jit(solution)/shard_map/ppermute | solution.py:369
  332.4 36.2 %collective-permute-start.52 = (bf16[128,2048]{1,0:T(8,128)(2,1)S(1)}, bf16[128,2048]{1,0:T(8,128)(2,1)}, u32[]{:S(2)}, u32[]{:S(2)}) collective-permute-start(bf16[128,2048]{1,0:T(8,128)(2,1)S(1)} %get-tuple-element.127), channel_id=1, source_target_pairs={{8,0},{2,10},{16,8},{10,18},{24,16},{18,26},{28,24},{26,30},{20,28... | collective-permute-start | bytes 1572872 | tf_op jit(solution)/shard_map/ppermute | solution.py:369
  333.6 52.2 %collective-permute-start.65 = (bf16[2048,384]{1,0:T(8,128)(2,1)}, bf16[2048,384]{1,0:T(8,128)(2,1)}, u32[]{:S(2)}, u32[]{:S(2)}) collective-permute-start(bf16[2048,384]{1,0:T(8,128)(2,1)} %convolution_convert_fusion.7), channel_id=1, source_target_pairs={{0,2},{2,0},{4,6},{6,4},{8,10},{10,8},{12,14},{14,12},{16,18},{18,... | collective-permute-start | bytes 4718600 | tf_op jit(solution)/shard_map/ppermute | solution.py:363
  336.0 18.9 %collective-permute-start.33 = (bf16[128,2048]{1,0:T(8,128)(2,1)S(1)}, bf16[128,2048]{1,0:T(8,128)(2,1)S(1)}, u32[]{:S(2)}, u32[]{:S(2)}) collective-permute-start(bf16[128,2048]{1,0:T(8,128)(2,1)S(1)} %add_convert_fusion.19), channel_id=1, source_target_pairs={{8,0},{2,10},{16,8},{10,18},{24,16},{18,26},{28,24},{26,30},{20,28... | collective-permute-start | bytes 1572872 | tf_op jit(solution)/shard_map/ppermute | solution.py:369
  339.1 21.3 %collective-permute-start.49 = (bf16[128,2048]{1,0:T(8,128)(2,1)S(1)}, bf16[128,2048]{1,0:T(8,128)(2,1)S(1)}, u32[]{:S(2)}, u32[]{:S(2)}) collective-permute-start(bf16[128,2048]{1,0:T(8,128)(2,1)S(1)} %add_convert_fusion.13), channel_id=1, source_target_pairs={{8,0},{2,10},{16,8},{10,18},{24,16},{18,26},{28,24},{26,30},{20,28... | collective-permute-start | bytes 1572872 | tf_op jit(solution)/shard_map/ppermute | solution.py:369
  355.0 11.1 %collective-permute-start.34 = (bf16[128,2048]{1,0:T(8,128)(2,1)S(1)}, bf16[128,2048]{1,0:T(8,128)(2,1)S(1)}, u32[]{:S(2)}, u32[]{:S(2)}) collective-permute-start(bf16[128,2048]{1,0:T(8,128)(2,1)S(1)} %add_convert_fusion.18), channel_id=1, source_target_pairs={{8,0},{2,10},{16,8},{10,18},{24,16},{18,26},{28,24},{26,30},{20,28... | collective-permute-start | bytes 1572872 | tf_op jit(solution)/shard_map/ppermute | solution.py:369
  360.6 11.1 %collective-permute-start.50 = (bf16[128,2048]{1,0:T(8,128)(2,1)S(1)}, bf16[128,2048]{1,0:T(8,128)(2,1)S(1)}, u32[]{:S(2)}, u32[]{:S(2)}) collective-permute-start(bf16[128,2048]{1,0:T(8,128)(2,1)S(1)} %add_convert_fusion.12), channel_id=1, source_target_pairs={{8,0},{2,10},{16,8},{10,18},{24,16},{18,26},{28,24},{26,30},{20,28... | collective-permute-start | bytes 1572872 | tf_op jit(solution)/shard_map/ppermute | solution.py:369
  367.4 11.7 %collective-permute-start.37 = (bf16[128,2048]{1,0:T(8,128)(2,1)}, bf16[128,2048]{1,0:T(8,128)(2,1)S(1)}, u32[]{:S(2)}, u32[]{:S(2)}) collective-permute-start(bf16[128,2048]{1,0:T(8,128)(2,1)} %get-tuple-element.105), channel_id=1, source_target_pairs={{8,0},{2,10},{16,8},{10,18},{24,16},{18,26},{28,24},{26,30},{20,28... | collective-permute-start | bytes 1572872 | tf_op jit(solution)/shard_map/ppermute | solution.py:369
  375.3 40.2 %collective-permute-start.67 = (bf16[2048,768]{1,0:T(8,128)(2,1)}, bf16[2048,768]{1,0:T(8,128)(2,1)S(1)}, u32[]{:S(2)}, u32[]{:S(2)}) collective-permute-start(bf16[2048,768]{1,0:T(8,128)(2,1)} %convolution_convert_fusion.3), channel_id=1, source_target_pairs={{0,2},{2,0},{4,6},{6,4},{8,10},{10,8},{12,14},{14,12},{16,18},{18,... | collective-permute-start | bytes 9437192 | tf_op jit(solution)/shard_map/ppermute | solution.py:363
  377.7 31.6 %collective-permute-start.35 = (bf16[128,2048]{1,0:T(8,128)(2,1)}, bf16[128,2048]{1,0:T(8,128)(2,1)S(1)}, u32[]{:S(2)}, u32[]{:S(2)}) collective-permute-start(bf16[128,2048]{1,0:T(8,128)(2,1)} %get-tuple-element.104), channel_id=1, source_target_pairs={{8,0},{2,10},{16,8},{10,18},{24,16},{18,26},{28,24},{26,30},{20,28... | collective-permute-start | bytes 1572872 | tf_op jit(solution)/shard_map/ppermute | solution.py:369
  379.1 31.5 %collective-permute-start.51 = (bf16[128,2048]{1,0:T(8,128)(2,1)}, bf16[128,2048]{1,0:T(8,128)(2,1)S(1)}, u32[]{:S(2)}, u32[]{:S(2)}) collective-permute-start(bf16[128,2048]{1,0:T(8,128)(2,1)} %get-tuple-element.116), channel_id=1, source_target_pairs={{8,0},{2,10},{16,8},{10,18},{24,16},{18,26},{28,24},{26,30},{20,28... | collective-permute-start | bytes 1572872 | tf_op jit(solution)/shard_map/ppermute | solution.py:369
  382.9 16.9 %collective-permute-start.38 = (bf16[128,2048]{1,0:T(8,128)(2,1)S(1)}, bf16[128,2048]{1,0:T(8,128)(2,1)S(1)}, u32[]{:S(2)}, u32[]{:S(2)}) collective-permute-start(bf16[128,2048]{1,0:T(8,128)(2,1)S(1)} %add_convert_fusion.15), channel_id=1, source_target_pairs={{8,0},{2,10},{16,8},{10,18},{24,16},{18,26},{28,24},{26,30},{20,28... | collective-permute-start | bytes 1572872 | tf_op jit(solution)/shard_map/ppermute | solution.py:369
  385.8 19.6 %collective-permute-start.54 = (bf16[128,2048]{1,0:T(8,128)(2,1)S(1)}, bf16[128,2048]{1,0:T(8,128)(2,1)S(1)}, u32[]{:S(2)}, u32[]{:S(2)}) collective-permute-start(bf16[128,2048]{1,0:T(8,128)(2,1)S(1)} %add_convert_fusion.9), channel_id=1, source_target_pairs={{8,0},{2,10},{16,8},{10,18},{24,16},{18,26},{28,24},{26,30},{20,28... | collective-permute-start | bytes 1572872 | tf_op jit(solution)/shard_map/ppermute | solution.py:369
  399.8 10.9 %collective-permute-start.39 = (bf16[128,2048]{1,0:T(8,128)(2,1)S(1)}, bf16[128,2048]{1,0:T(8,128)(2,1)S(1)}, u32[]{:S(2)}, u32[]{:S(2)}) collective-permute-start(bf16[128,2048]{1,0:T(8,128)(2,1)S(1)} %collective-permute-done.38), channel_id=1, source_target_pairs={{0,2},{2,0},{4,6},{6,4},{8,10},{10,8},{12,14},{14,12},{16,18},{18,... | collective-permute-start | bytes 1572872 | tf_op jit(solution)/shard_map/ppermute | solution.py:363
  409.3 19.5 %collective-permute-start.66 = (bf16[1040,384]{1,0:T(8,128)(2,1)S(1)}, bf16[1040,384]{1,0:T(8,128)(2,1)S(1)}, u32[]{:S(2)}, u32[]{:S(2)}) collective-permute-start(bf16[1040,384]{1,0:T(8,128)(2,1)S(1)} %pad_maximum_fusion.21), channel_id=1, source_target_pairs={{0,1},{1,0},{2,3},{3,2},{4,5},{5,4},{6,7},{7,6},{8,9},{9,8},{10,11... | collective-permute-start | bytes 2396168 | tf_op jit(solution)/shard_map/ppermute | solution.py:420
  417.0 12.4 %collective-permute-start.58 = (bf16[128,2048]{1,0:T(8,128)(2,1)S(1)}, bf16[128,2048]{1,0:T(8,128)(2,1)S(1)}, u32[]{:S(2)}, u32[]{:S(2)}) collective-permute-start(bf16[128,2048]{1,0:T(8,128)(2,1)S(1)} %collective-permute-done.57), channel_id=1, source_target_pairs={{0,8},{10,2},{8,16},{18,10},{16,24},{26,18},{24,28},{30,26},{28,20... | collective-permute-start | bytes 1572872 | tf_op jit(solution)/shard_map/ppermute | solution.py:366
  418.1 44.4 %collective-permute-start.68 = (bf16[16,64,768]{2,1,0:T(8,128)(2,1)S(1)}, bf16[16,64,768]{2,1,0:T(8,128)(2,1)S(1)}, u32[]{:S(2)}, u32[]{:S(2)}) collective-permute-start(bf16[16,64,768]{2,1,0:T(8,128)(2,1)S(1)} %fusion.4), channel_id=1, source_target_pairs={{0,1},{1,0},{2,3},{3,2},{4,5},{5,4},{6,7},{7,6},{8,9},{9,8},{10,11... | collective-permute-start | bytes 4718600 | tf_op jit(solution)/shard_map/ppermute | solution.py:420
  423.8 11.2 %collective-permute-start.59 = (bf16[128,2048]{1,0:T(8,128)(2,1)S(1)}, bf16[128,2048]{1,0:T(8,128)(2,1)S(1)}, u32[]{:S(2)}, u32[]{:S(2)}) collective-permute-start(bf16[128,2048]{1,0:T(8,128)(2,1)S(1)} %collective-permute-done.56), channel_id=1, source_target_pairs={{0,8},{10,2},{8,16},{18,10},{16,24},{26,18},{24,28},{30,26},{28,20... | collective-permute-start | bytes 1572872 | tf_op jit(solution)/shard_map/ppermute | solution.py:366
  429.4 11.2 %collective-permute-start.60 = (bf16[128,2048]{1,0:T(8,128)(2,1)S(1)}, bf16[128,2048]{1,0:T(8,128)(2,1)S(1)}, u32[]{:S(2)}, u32[]{:S(2)}) collective-permute-start(bf16[128,2048]{1,0:T(8,128)(2,1)S(1)} %collective-permute-done.58), channel_id=1, source_target_pairs={{0,8},{10,2},{8,16},{18,10},{16,24},{26,18},{24,28},{30,26},{28,20... | collective-permute-start | bytes 1572872 | tf_op jit(solution)/shard_map/ppermute | solution.py:366
  435.0 11.2 %collective-permute-start.61 = (bf16[128,2048]{1,0:T(8,128)(2,1)S(1)}, bf16[128,2048]{1,0:T(8,128)(2,1)S(1)}, u32[]{:S(2)}, u32[]{:S(2)}) collective-permute-start(bf16[128,2048]{1,0:T(8,128)(2,1)S(1)} %collective-permute-done.59), channel_id=1, source_target_pairs={{0,8},{10,2},{8,16},{18,10},{16,24},{26,18},{24,28},{30,26},{28,20... | collective-permute-start | bytes 1572872 | tf_op jit(solution)/shard_map/ppermute | solution.py:366
  440.6 11.2 %collective-permute-start.62 = (bf16[128,2048]{1,0:T(8,128)(2,1)S(1)}, bf16[128,2048]{1,0:T(8,128)(2,1)S(1)}, u32[]{:S(2)}, u32[]{:S(2)}) collective-permute-start(bf16[128,2048]{1,0:T(8,128)(2,1)S(1)} %collective-permute-done.60), channel_id=1, source_target_pairs={{0,8},{10,2},{8,16},{18,10},{16,24},{26,18},{24,28},{30,26},{28,20... | collective-permute-start | bytes 1572872 | tf_op jit(solution)/shard_map/ppermute | solution.py:366
  446.2 11.2 %collective-permute-start.63 = (bf16[128,2048]{1,0:T(8,128)(2,1)S(1)}, bf16[128,2048]{1,0:T(8,128)(2,1)S(1)}, u32[]{:S(2)}, u32[]{:S(2)}) collective-permute-start(bf16[128,2048]{1,0:T(8,128)(2,1)S(1)} %collective-permute-done.61), channel_id=1, source_target_pairs={{0,8},{10,2},{8,16},{18,10},{16,24},{26,18},{24,28},{30,26},{28,20... | collective-permute-start | bytes 1572872 | tf_op jit(solution)/shard_map/ppermute | solution.py:366
  495.9 51.3 %all-to-all-start.3 = ((bf16[16,64,768]{2,1,0:T(8,128)(2,1)}), bf16[16,64,768]{2,1,0:T(8,128)(2,1)}, u32[]{:S(2)}, u32[]{:S(2)}) async-start(bf16[16,64,768]{2,1,0:T(8,128)(2,1)} %fusion), calls=%async_computation.3 | async-start | bytes 3145728 | tf_op jit(solution)/shard_map/all_to_all | solution.py:416
  510.5 48.2 %collective-permute-start.74 = (bf16[128,2048]{1,0:T(8,128)(2,1)}, bf16[128,2048]{1,0:T(8,128)(2,1)}, u32[]{:S(2)}, u32[]{:S(2)}) collective-permute-start(bf16[128,2048]{1,0:T(8,128)(2,1)} %get-tuple-element.103), channel_id=1, source_target_pairs={{8,0},{2,10},{16,8},{10,18},{24,16},{18,26},{28,24},{26,30},{20,28... | collective-permute-start | bytes 1572872 | tf_op jit(solution)/shard_map/ppermute | solution.py:369
  513.9 33.4 %collective-permute-start.71 = (bf16[128,2048]{1,0:T(8,128)(2,1)}, bf16[128,2048]{1,0:T(8,128)(2,1)}, u32[]{:S(2)}, u32[]{:S(2)}) collective-permute-start(bf16[128,2048]{1,0:T(8,128)(2,1)} %add_convert_fusion.7), channel_id=1, source_target_pairs={{8,0},{2,10},{16,8},{10,18},{24,16},{18,26},{28,24},{26,30},{20,28... | collective-permute-start | bytes 1572872 | tf_op jit(solution)/shard_map/ppermute | solution.py:369
  552.4 19.3 %collective-permute-start.79 = (bf16[1040,384]{1,0:T(8,128)(2,1)}, bf16[1040,384]{1,0:T(8,128)(2,1)}, u32[]{:S(2)}, u32[]{:S(2)}) collective-permute-start(bf16[1040,384]{1,0:T(8,128)(2,1)} %pad_maximum_fusion.22), channel_id=1, source_target_pairs={{0,1},{1,0},{2,3},{3,2},{4,5},{5,4},{6,7},{7,6},{8,9},{9,8},{10,11... | collective-permute-start | bytes 2396168 | tf_op jit(solution)/shard_map/ppermute | solution.py:420
  553.6 38.3 %all-to-all-start.5 = ((bf16[16,80,384]{2,1,0:T(8,128)(2,1)}), bf16[16,80,384]{2,1,0:T(8,128)(2,1)}, u32[]{:S(2)}, u32[]{:S(2)}) async-start(bf16[16,80,384]{2,1,0:T(8,128)(2,1)} %pad_maximum_fusion.19), calls=%async_computation.5 | async-start | bytes 1966080 | tf_op jit(solution)/shard_map/all_to_all | solution.py:416
  561.4 24.8 %collective-permute-start.75 = (bf16[128,2048]{1,0:T(8,128)(2,1)S(1)}, bf16[128,2048]{1,0:T(8,128)(2,1)S(1)}, u32[]{:S(2)}, u32[]{:S(2)}) collective-permute-start(bf16[128,2048]{1,0:T(8,128)(2,1)S(1)} %get-tuple-element.101), channel_id=1, source_target_pairs={{8,0},{2,10},{16,8},{10,18},{24,16},{18,26},{28,24},{26,30},{20,28... | collective-permute-start | bytes 1572872 | tf_op jit(solution)/shard_map/ppermute | solution.py:369
  588.2 11.3 %collective-permute-start.76 = (bf16[128,2048]{1,0:T(8,128)(2,1)}, bf16[128,2048]{1,0:T(8,128)(2,1)}, u32[]{:S(2)}, u32[]{:S(2)}) collective-permute-start(bf16[128,2048]{1,0:T(8,128)(2,1)} %add_convert_fusion.3), channel_id=1, source_target_pairs={{8,0},{2,10},{16,8},{10,18},{24,16},{18,26},{28,24},{26,30},{20,28... | collective-permute-start | bytes 1572872 | tf_op jit(solution)/shard_map/ppermute | solution.py:369
  591.9 36.4 %all-to-all-start.4 = ((bf16[16,80,384]{2,1,0:T(8,128)(2,1)}), bf16[16,80,384]{2,1,0:T(8,128)(2,1)S(1)}, u32[]{:S(2)}, u32[]{:S(2)}) async-start(bf16[16,80,384]{2,1,0:T(8,128)(2,1)} %pad_maximum_fusion.20), calls=%async_computation.4 | async-start | bytes 1966080 | tf_op jit(solution)/shard_map/all_to_all | solution.py:416
  598.3 26.0 %collective-permute-start.73 = (bf16[128,2048]{1,0:T(8,128)(2,1)}, bf16[128,2048]{1,0:T(8,128)(2,1)S(1)}, u32[]{:S(2)}, u32[]{:S(2)}) collective-permute-start(bf16[128,2048]{1,0:T(8,128)(2,1)} %get-tuple-element.100), channel_id=1, source_target_pairs={{8,0},{2,10},{16,8},{10,18},{24,16},{18,26},{28,24},{26,30},{20,28... | collective-permute-start | bytes 1572872 | tf_op jit(solution)/shard_map/ppermute | solution.py:369
  599.5 24.9 %collective-permute-start.77 = (bf16[128,2048]{1,0:T(8,128)(2,1)}, bf16[128,2048]{1,0:T(8,128)(2,1)S(1)}, u32[]{:S(2)}, u32[]{:S(2)}) collective-permute-start(bf16[128,2048]{1,0:T(8,128)(2,1)} %collective-permute-done.76), channel_id=1, source_target_pairs={{0,2},{2,0},{4,6},{6,4},{8,10},{10,8},{12,14},{14,12},{16,18},{18,... | collective-permute-start | bytes 1572872 | tf_op jit(solution)/shard_map/ppermute | solution.py:363
  (81 other events, 938.8 us)

commit v3 on v2

--- a/solution.py
+++ b/solution.py
@@ -6,6 +6,7 @@
 import numpy as np
 from jax import lax
 from jax.experimental import pallas as pl
+from jax.experimental.layout import Layout, with_layout_constraint
 from jax.experimental.pallas import tpu as pltpu
 from jax.sharding import PartitionSpec as P
 
@@ -187,7 +188,7 @@
 
 
 def whole_spec(shape):
-    return pl.BlockSpec(shape, lambda i, *_: (0, 0), pipeline_mode=pl.Buffered(1))
+    return pl.BlockSpec(memory_space=pltpu.VMEM)
 
 
 def attend(tables, raw, cosine, sine, query_gain, key_gain, rows, sorted_all, scale):
@@ -346,6 +347,39 @@
     )(*tables, *raw, cosine, sine, query_gain, key_gain, *saved, *out, *d_out, lse)
 
 
+def project_kernel(weight_ref, gain_ref, *refs):
+    count = len(refs) - 2
+    normed_ref, out_ref = refs[count:]
+    rows = refs[0].shape[0]
+    for index in range(count):
+        wide = refs[index][...].astype(f32)
+        normed = (wide * inv_root(wide) * gain_ref[...]).astype(bf16)
+        place = pl.ds(index * rows, rows)
+        normed_ref[place, :] = normed
+        out_ref[place, :] = dot_nn(normed, weight_ref[...])
+
+
+def project(blocks, gain, weight):
+    rows, width = blocks[0].shape
+    total, columns = rows * len(blocks), weight.shape[1]
+    return pl.pallas_call(
+        project_kernel,
+        out_shape=(
+            jax.ShapeDtypeStruct((total, width), bf16),
+            jax.ShapeDtypeStruct((total, columns), f32),
+        ),
+        grid=(1,),
+        in_specs=[whole_spec(weight.shape), whole_spec((1, width))]
+        + [whole_spec((rows, width))] * len(blocks),
+        out_specs=(whole_spec((total, width)), whole_spec((total, columns))),
+        compiler_params=pltpu.CompilerParams(vmem_limit_bytes=48 * 2**20),
+        cost_estimate=pl.CostEstimate(
+            flops=2 * total * width * columns, bytes_accessed=4 * total * width, transcendentals=total
+        ),
+        name="project",
+    )(weight, gain[None, :], *blocks)
+
+
 class Ring:
     def __init__(self, size):
         self.chips = size // 2
@@ -379,33 +413,50 @@
                 blocks.append(2 * near + 1 - core)
         return blocks
 
-    def gather(self, block):
-        first, second = block, self.swap(block)
+    def gather(self, block, hooks=None):
+        hooks = hooks or {}
+        streams = [block, self.swap(block)]
         blocks = [block]
-        for step in range(1, self.reach + 1):
-            first = self.out(first)
-            blocks.append(first)
-            if step < self.reach:
-                second = self.out(second)
-                blocks.append(second)
+        for hop in range(2 * self.reach - 1):
+            held = streams[hop % 2]
+            if hop >= 3:
+                held = after(held, blocks[hop - 2])
+            if hop in hooks:
+                held = after(held, hooks[hop](blocks))
+            streams[hop % 2] = self.out(held)
+            blocks.append(streams[hop % 2])
         return blocks
 
-    def scatter_sum(self, term, needs=None):
+    def scatter_hops(self, term, streams, hops, needs=None, first_twice=False):
         needs = needs or {}
-        first = self.home(term(2 * self.reach - 1))
-        second = None
-        marks = {self.reach: first}
-        for step in range(self.reach - 1, 0, -1):
-            if step in needs:
-                first = after(first, needs[step])
-            first = self.home((term(2 * step - 1).astype(f32) + first.astype(f32)).astype(bf16))
-            other = term(2 * step)
-            if second is not None:
-                other = (other.astype(f32) + second.astype(f32)).astype(bf16)
-            second = self.home(other)
-            marks[step] = first
-        total = first.astype(f32) + term(0).astype(f32) + self.swap(second).astype(f32)
-        return total, marks
+        order = list(range(2 * self.reach - 1, 0, -1))
+        if first_twice:
+            for place in range(1, len(order), 2):
+                order[place : place + 2] = reversed(order[place : place + 2])
+        streams, marks, total = list(streams), [], None
+        for hop in hops:
+            index = order[hop]
+            stream, held = 1 - index % 2, streams[1 - index % 2]
+            if held is None:
+                total = term(index)
+            else:
+                held = held if total is None else after(held, total)
+                total = (term(index).astype(f32) + held.astype(f32)).astype(bf16)
+            if hop in needs:
+                total = after(total, needs[hop](marks))
+            streams[stream] = self.home(total)
+            marks.append(streams[stream])
+        return streams, marks
+
+    def scatter_end(self, term, streams):
+        first, second = streams
+        return first.astype(f32) + term(0).astype(f32) + self.swap(second).astype(f32)
+
+    def scatter_sum(self, term, needs=None, first_twice=False):
+        streams, marks = self.scatter_hops(
+            term, [None, None], range(2 * self.reach - 1), needs, first_twice
+        )
+        return self.scatter_end(term, streams), marks
 
 
 def after(value, *events):
@@ -427,33 +478,35 @@
     return both.reshape(-1, received.shape[-1])
 
 
-def to_rows(grads, extra, fsdp_rank, ctx_size, events=()):
+def halves(grads, extra, fsdp_rank, ctx_size):
     width = grads.shape[1]
     split = grads.reshape(ctx_size, 2, -1, width)
-    rows = split.shape[2]
     keep = jnp.where(fsdp_rank == 0, split[:, 0], split[:, 1])
     give = jnp.where(fsdp_rank == 0, split[:, 1], split[:, 0])
     if extra is None:
-        given = after(swap_rows(give), *events)
-        return (keep.astype(f32) + given.astype(f32)).astype(bf16)
+        return keep, give, None
     count = extra.shape[0]
     lines = -(-count // width)
     lines = -(-lines // 16) * 16
     extra_block = jnp.pad(extra, (0, lines * width - count)).reshape(lines, width).astype(bf16)
-    given = swap_rows(jnp.concatenate([give.reshape(-1, width), extra_block], axis=0))
-    given = after(given, *events)
-    body = given[: ctx_size * rows].reshape(ctx_size, rows, width)
+    return keep, jnp.concatenate([give.reshape(-1, width), extra_block], axis=0), extra_block
+
+
+def join(keep, given, extra_block):
+    if extra_block is None:
+        return (keep.astype(f32) + given.astype(f32)).astype(bf16)
+    ctx_size, rows, width = keep.shape
+    body = given[: ctx_size * rows].reshape(keep.shape)
     total = (keep.astype(f32) + body.astype(f32)).astype(bf16)
     extras = (extra_block.astype(f32) + given[ctx_size * rows :].astype(f32)).astype(bf16)
     return jnp.concatenate(
-        [total, jnp.broadcast_to(extras[None], (ctx_size, lines, width))], axis=1
-    )
-
-
-def come_home(sent, rows, count):
-    received = spread(sent)
-    extra_sum = jnp.sum(received[:, rows:].astype(f32), axis=0).reshape(-1)[:count]
-    return received[:, :rows], extra_sum
+        [total, jnp.broadcast_to(extras[None], (ctx_size,) + extras.shape)], axis=1
+    )
+
+
+def apart(received, rows, width, count):
+    lines = received[:, rows:, :width].astype(f32)
+    return received[:, :rows], jnp.sum(lines, axis=0).reshape(-1)[:count]
 
 
 def side_by_side(pieces):
@@ -496,6 +549,12 @@
     sorted_all = splits == 1
     score_scale = 1.0 / math.sqrt(head_size)
     ring = Ring(ctx_size)
+    always = jnp.min(block_order) >= 0
+
+    def fenced(work, *values):
+        shapes = jax.eval_shape(work, *values)
+        blank = lambda *_: jax.tree.map(lambda leaf: jnp.zeros(leaf.shape, leaf.dtype), shapes)
+        return lax.cond(always, work, blank, *values)
 
     def block_rows(field, index):
         return field[index * tokens : (index + 1) * tokens]
@@ -530,6 +589,16 @@
     )
     output_part = jnp.concatenate([column(head_mine, 1), column(head_other, 1)], axis=1)
 
+    last_hop = 2 * ring.reach - 2
+    angles = {}
+
+    def make_angles(blocks):
+        angles["tables"] = rope_tables(
+            after(jnp.arange(length, dtype=jnp.int32), blocks[2]), head_size
+        )
+        return angles["tables"]
+
+    input_blocks = ring.gather(block_input[0], {last_hop - 1: make_angles})
     member_table = np.array(
         [ring.members(rank) + ring.members(rank ^ 1) for rank in range(ctx_size)], np.int32
     )
@@ -542,7 +611,7 @@
     local_pos = jnp.sum(
         jnp.where(local_slot[:, None] == slot_index[None, :], block_order[None, :], 0), axis=1
     )
-    cosine, sine = rope_tables(jnp.arange(length, dtype=jnp.int32), head_size)
+    cosine, sine = angles["tables"]
     if sorted_all:
         tables = (local_pos, slot_index, slot_index)
     else:
@@ -555,26 +624,14 @@
         tables = (local_pos, jnp.take(local_of_pos, own_pos), own_pos)
     query_row, key_row = query_gain[None, :], key_gain[None, :]
 
-    input_blocks = ring.gather(block_input[0])
-    input_blocks[3], tables, cosine, sine = lax.optimization_barrier(
-        (input_blocks[3], tables, cosine, sine)
-    )
     input_blocks[4] = after(input_blocks[4], head_received)
 
     def by_slice(weight):
         return jnp.transpose(weight.reshape(weight_rows, ctx_size, hidden_slice), (1, 0, 2))
 
-    gate_up_block = jnp.concatenate([by_slice(gate_weight), by_slice(up_weight)], axis=2)
-    down_block = by_slice(down_weight)
-    input_blocks[5], gate_up_block, down_block = lax.optimization_barrier(
-        (input_blocks[5], gate_up_block, down_block)
-    )
-    normed_list = []
-    for block in input_blocks:
-        wide = block.astype(f32)
-        normed_list.append((wide * inv_root(wide) * attn_gain).astype(bf16))
-    normed_attn = lax.optimization_barrier(jnp.concatenate(normed_list, axis=0))
-    projected = dot_nn(normed_attn, head_weight)
+    gate, up, down = after((gate_weight, up_weight, down_weight), input_blocks[3])
+    mlp_block = jnp.concatenate([by_slice(gate), by_slice(up), by_slice(down)], axis=2)
+    normed_attn, projected = project(input_blocks, attn_gain, head_weight)
     projected_given = ring.swap(
         jnp.concatenate(
             [projected[:, 3 * head_size :], projected[:, head_size : 3 * head_size]], axis=1
@@ -584,36 +641,40 @@
     attn_a, attn_b, lse, *saved = attend(
         tables, raw, cosine, sine, query_row, key_row, half_rows, sorted_all, score_scale
     )
-    gate_up_received = spread(after(gate_up_block, input_blocks[-2]))
-    gate_up_partner = swap_rows(gate_up_received)
-    down_received = spread(after(down_block, gate_up_received))
-    down_partner = swap_rows(down_received)
-    attn_a, attn_b = after((attn_a, attn_b), gate_up_received)
+    mlp_received = spread(after(mlp_block, input_blocks[-1], input_blocks[-2]))
+    mlp_received = after(mlp_received, attn_a)
+    mlp_partner = swap_rows(mlp_received)
     attn_pair = jnp.concatenate([attn_a, ring.swap(attn_b)], axis=1)
 
     inputs32 = block_input[0].astype(f32)
-    scale_attn = inv_root(inputs32)
     attn_terms = dot_nt(attn_pair, output_part).astype(bf16)
-    attn_out, _ = ring.scatter_sum(
-        lambda i: block_rows(attn_terms, i),
-        {ring.reach - 1: down_received, ring.reach - 2: gate_up_partner},
-    )
-    attn_out, gate_up_partner, down_partner = lax.optimization_barrier(
-        (attn_out, gate_up_partner, down_partner)
+    attn_out = fenced(
+        lambda terms: ring.scatter_sum(lambda i: block_rows(terms, i))[0], attn_terms
     )
     hidden_one = inputs32 + attn_out
     scale_mlp = inv_root(hidden_one)
     normed_mlp = (hidden_one * scale_mlp * mlp_gain).astype(bf16)
-    gate_up_mine = to_columns(gate_up_received, gate_up_partner, fsdp_rank)
-    gate_up = jnp.concatenate([gate_up_mine, ring.swap(gate_up_mine)], axis=1)
-    down_mine = to_columns(down_received, down_partner, fsdp_rank)
-    down_part = jnp.concatenate([down_mine, ring.swap(down_mine)], axis=1)
+    mlp_mine = to_columns(mlp_received, mlp_partner, fsdp_rank)
+    mlp_other = ring.swap(mlp_mine)
+    pair = 2 * hidden_slice
+    gate_up = jnp.concatenate([mlp_mine[:, :pair], mlp_other[:, :pair]], axis=1)
+    down_part = jnp.concatenate([mlp_mine[:, pair:], mlp_other[:, pair:]], axis=1)
 
     normed_blocks = ring.gather(normed_mlp)
     normed_all = jnp.concatenate(normed_blocks, axis=0)
-    cot_blocks = ring.gather(after(cotangent[0], normed_blocks[-2]))
+    gate_up, down_part = lax.optimization_barrier((gate_up, down_part))
+    middle = ring.reach * tokens
+    hidden_parts = [dot_nn(normed_all[:middle], gate_up), dot_nn(normed_all[middle:], gate_up)]
+    cot_blocks = ring.gather(
+        after(cotangent[0], normed_blocks[-2]),
+        {
+            last_hop - 4: lambda _: gate_up,
+            last_hop - 3: lambda _: hidden_parts[0],
+            last_hop - 1: lambda _: hidden_parts[1],
+        },
+    )
+    hidden_all = jnp.concatenate(hidden_parts, axis=0)
     cot_all = jnp.concatenate(cot_blocks, axis=0)
-    hidden_all = dot_nn(normed_all, gate_up)
     act_grad_all = dot_nn(cot_all, down_part)
     activated_list, back_list = [], []
     for member in range(2):
@@ -630,80 +691,160 @@
     back_all = jnp.concatenate(back_list, axis=1)
     far = (2 * ring.reach - 3) * tokens
     far_terms = dot_nt(back_all[far:], gate_up).astype(bf16)
-    near_terms = dot_nt(back_all[:far], gate_up).astype(bf16)
     near_blocks = far // tokens
-    normed_mlp_grad, _ = ring.scatter_sum(
-        lambda i: block_rows(near_terms, i) if i < near_blocks else block_rows(far_terms, i - near_blocks)
-    )
-    out_terms = dot_nt(activated_all, down_part).astype(bf16)
-    mlp_out, _ = ring.scatter_sum(lambda i: block_rows(out_terms, i))
-    block_out = (hidden_one + mlp_out).astype(bf16)
+    add = lambda left, right: (left.astype(f32) + right.astype(f32)).astype(bf16)
+
+    def feed_forward_grads(far_terms, back_all, activated_all, normed_all, cot_all, gate_up):
+        near_terms = dot_nt(back_all[:far], gate_up).astype(bf16)
+        ready = {}
+
+        def piece(left, right, mark):
+            grad = dot_tn(left, after(right, mark)).astype(bf16)
+            return with_layout_constraint(grad, Layout((0, 1)))
+
+        def down_away(marks):
+            ready["down_give"] = piece(cot_all, activated_all[:, hidden_slice:], marks[0])
+            return ready["down_give"]
+
+        def gate_up_away(marks):
+            ready["gate_up_give"] = piece(normed_all, back_all[:, pair:], marks[1])
+            return ready["gate_up_give"]
+
+        def down_here(marks):
+            ready["down"] = piece(cot_all, activated_all[:, :hidden_slice], marks[2])
+            return ready["down"]
+
+        def gate_up_here(marks):
+            ready["gate_up"] = piece(normed_all, back_all[:, :pair], marks[3])
+            return ready["gate_up"]
+
+        summed, marks = ring.scatter_sum(
+            lambda i: block_rows(near_terms, i)
+            if i < near_blocks
+            else block_rows(far_terms, i - near_blocks),
+            {2: down_away, 3: gate_up_away, 4: down_here, 5: gate_up_here},
+            first_twice=True,
+        )
+        ready["down"] = add(ready["down"], ring.swap(ready["down_give"]))
+        ready["gate_up"] = add(ready["gate_up"], ring.swap(ready["gate_up_give"]))
+        near_late, far_late = after((near_terms, far_terms), marks[4])
+        gain_part = jnp.sum(
+            near_late.astype(f32) * normed_all[:far].astype(f32), axis=0
+        ) + jnp.sum(far_late.astype(f32) * normed_all[far:].astype(f32), axis=0)
+        down_own, down_away, _ = halves(ready["down"], None, fsdp_rank, ctx_size)
+        gate_up_own, gate_up_away, _ = halves(ready["gate_up"], None, fsdp_rank, ctx_size)
+        return summed, gain_part / mlp_gain, down_own, down_away, gate_up_own, gate_up_away
+
+    normed_mlp_grad, mlp_gain_part, down_own, down_away, gate_up_own, gate_up_away = fenced(
+        feed_forward_grads, far_terms, back_all, activated_all, normed_all, cot_all, gate_up
+    )
     grad32 = cotangent[0].astype(f32)
     hidden_grad = grad32 + norm_back(hidden_one, scale_mlp, mlp_gain, normed_mlp_grad)
     hidden_grad_bf = hidden_grad.astype(bf16)
-
-    mlp_gain_part = (
-        jnp.sum(near_terms.astype(f32) * normed_all[:far].astype(f32), axis=0)
-        + jnp.sum(far_terms.astype(f32) * normed_all[far:].astype(f32), axis=0)
-    ) / mlp_gain
-    pair = 2 * hidden_slice
-    add = lambda left, right: (left.astype(f32) + right.astype(f32)).astype(bf16)
-    down_give = dot_tn(cot_all, activated_all[:, hidden_slice:]).astype(bf16)
-    down_keep = dot_tn(cot_all, activated_all[:, :hidden_slice]).astype(bf16)
-    gate_up_give = dot_tn(normed_all, back_all[:, pair:]).astype(bf16)
-    gate_up_keep = dot_tn(normed_all, back_all[:, :pair]).astype(bf16)
-
-    grad_blocks = ring.gather(hidden_grad_bf)
-    grad_all = jnp.concatenate(grad_blocks, axis=0)
+    down_other, gate_up_other = swap_rows(down_away), swap_rows(gate_up_away)
+
+    grad_all = fenced(lambda block: jnp.concatenate(ring.gather(block), axis=0), hidden_grad_bf)
     attn_grad_pair = dot_nn(grad_all, output_part).astype(bf16)
     attn_grad = (attn_grad_pair[:, :head_size], ring.swap(attn_grad_pair[:, head_size:]))
-    down_sent = to_rows(
-        add(down_keep, ring.swap(down_give)), mlp_gain_part, fsdp_rank, ctx_size, (grad_blocks[1],)
-    )
-    gate_up_sent = to_rows(
-        add(gate_up_keep, ring.swap(gate_up_give)), None, fsdp_rank, ctx_size, (grad_blocks[-1],)
-    )
-    attn_grad, down_sent, gate_up_sent = lax.optimization_barrier(
-        (attn_grad, down_sent, gate_up_sent)
-    )
-    gate_up_rows = spread(gate_up_sent)
-    down_rows, mlp_gain_sum = come_home(down_sent, weight_rows, model)
-    first_a, first_b, query_gain_part, key_gain_part = attend_back(
-        tables, raw, cosine, sine, query_row, key_row, saved, (attn_a, attn_b), attn_grad, lse,
-        half_rows, sorted_all, score_scale,
-    )
-    given_grads = ring.swap(first_b)
-    half_grads = jnp.concatenate(
-        [
-            first_a[:, :head_size],
-            add(first_a[:, head_size:], given_grads[:, head_size:]),
-            given_grads[:, :head_size],
-        ],
-        axis=1,
-    )
-    input_terms = dot_nt(half_grads, head_weight).astype(bf16)
-    normed_attn_grad, marks = ring.scatter_sum(
-        lambda i: block_rows(input_terms, i), {ring.reach - 2: gate_up_rows}
-    )
-    late_grads = after(half_grads, marks[ring.reach])
-    input_grad = hidden_grad + norm_back(inputs32, scale_attn, attn_gain, normed_attn_grad)
-    head_grad = dot_tn(normed_attn, late_grads).astype(bf16)
-    output_grad = dot_tn(grad_all, attn_pair).astype(bf16)
-    attn_gain_part = (
-        jnp.sum(input_terms.astype(f32) * normed_attn.astype(f32), axis=0) / attn_gain
-    )
-    kv_keep, kv_give = key_first(column(head_grad, 1), column(head_grad, 2))
-    attn_keep = jnp.concatenate([column(head_grad, 0), column(output_grad, 0), kv_keep], axis=1)
-    attn_give = jnp.concatenate([column(head_grad, 3), column(output_grad, 1), kv_give], axis=1)
-    attn_rows, attn_extra = come_home(
-        to_rows(
-            add(attn_keep, ring.swap(attn_give)),
-            jnp.concatenate([attn_gain_part, query_gain_part[0], key_gain_part[0]]),
-            fsdp_rank,
-            ctx_size,
-        ),
+    mlp_sent = jnp.concatenate(
+        [join(down_own, down_other, None), join(gate_up_own, gate_up_other, None)], axis=2
+    )
+    attn_grad, mlp_sent = lax.optimization_barrier((attn_grad, mlp_sent))
+
+    mlp_rows = spread(mlp_sent)
+
+    def attention_back(attn_grad, attn_a, attn_b, projected, given):
+        first_a, first_b, query_gain_part, key_gain_part = attend_back(
+            tables, (projected, given), cosine, sine, query_row, key_row, saved, (attn_a, attn_b),
+            attn_grad, lse, half_rows, sorted_all, score_scale,
+        )
+        given_grads = ring.swap(first_b)
+        half_grads = jnp.concatenate(
+            [
+                first_a[:, :head_size],
+                add(first_a[:, head_size:], given_grads[:, head_size:]),
+                given_grads[:, :head_size],
+            ],
+            axis=1,
+        )
+        input_terms = dot_nt(half_grads, head_weight).astype(bf16)
+        return half_grads, input_terms, query_gain_part[0], key_gain_part[0]
+
+    half_grads, input_terms, query_gain_part, key_gain_part = fenced(
+        attention_back, attn_grad, attn_a, attn_b, *raw
+    )
+
+    def attention_grads(input_terms, half_grads, grad_all, normed_attn, attn_pair):
+        ready = {}
+
+        def weight_grads(marks):
+            late_grads, late_attn = after((half_grads, attn_pair), marks[0])
+            head_grad = dot_tn(normed_attn, late_grads).astype(bf16)
+            output_grad = dot_tn(grad_all, late_attn).astype(bf16)
+            kv_keep, kv_give = key_first(column(head_grad, 1), column(head_grad, 2))
+            keep = jnp.concatenate([column(head_grad, 0), column(output_grad, 0), kv_keep], axis=1)
+            give = jnp.concatenate([column(head_grad, 3), column(output_grad, 1), kv_give], axis=1)
+            ready["gain"] = (
+                jnp.sum(after(input_terms, marks[1]).astype(f32) * normed_attn.astype(f32), axis=0)
+                / attn_gain
+            )
+            ready["grads"] = add(keep, ring.swap(give))
+            return ready["grads"], ready["gain"]
+
+        summed, _ = ring.scatter_sum(
+            lambda i: block_rows(input_terms, i), {last_hop: weight_grads}
+        )
+        return summed, ready["grads"], ready["gain"]
+
+    normed_attn_grad, attn_grads, attn_gain_part = fenced(
+        attention_grads, input_terms, half_grads, grad_all, normed_attn, attn_pair
+    )
+    gains = jnp.concatenate([attn_gain_part, query_gain_part, key_gain_part, mlp_gain_part])
+
+    def out_and_home(activated_all, down_part, attn_grads, gains, mlp_rows, summed_grad, hidden_grad, inputs32):
+        own, away, lines = halves(attn_grads, gains, fsdp_rank, ctx_size)
+        out_terms = dot_nt(activated_all, down_part).astype(bf16)
+        ready = {}
+
+        def other_rows(_):
+            ready["other"] = swap_rows(away)
+            return ready["other"]
+
+        def rows_home(_):
+            ready["rows"] = spread(join(own, ready["other"], lines))
+            return ready["rows"]
+
+        def unpack(marks):
+            rows = after(mlp_rows, marks[1])
+            ready["mlp"] = tuple(
+                side_by_side(rows[:, :, i * hidden_slice : (i + 1) * hidden_slice]).astype(f32)
+                for i in range(3)
+            )
+            return ready["mlp"]
+
+        def finish(marks):
+            ready["input"] = hidden_grad + norm_back(
+                inputs32, inv_root(inputs32), attn_gain, after(summed_grad, marks[0])
+            )
+            return ready["input"]
+
+        summed, _ = ring.scatter_sum(
+            lambda i: block_rows(out_terms, i),
+            {2: finish, last_hop - 2: other_rows, last_hop - 1: unpack, last_hop: rows_home},
+        )
+        return summed, ready["rows"], ready["input"], ready["mlp"]
+
+    attn_grads, mlp_rows = lax.optimization_barrier((attn_grads, mlp_rows))
+    mlp_out, attn_home, input_grad, mlp_grads = fenced(
+        out_and_home, activated_all, down_part, attn_grads, gains, mlp_rows, normed_attn_grad,
+        hidden_grad, inputs32,
+    )
+    block_out = (hidden_one + mlp_out).astype(bf16)
+    attn_rows, attn_extra = apart(
+        attn_home,
         weight_rows,
-        model + 2 * head_size,
+        3 * head_size,
+        2 * model + 2 * head_size,
     )
 
     def home(index):
@@ -713,7 +854,7 @@
     key_value_rows = home(2)
     flat = lambda part: side_by_side(part.reshape(-1, weight_rows, head_size))
 
-    gate_rows, up_rows = gate_up_rows[:, :, :hidden_slice], gate_up_rows[:, :, hidden_slice:]
+    down_rows, gate_rows, up_rows = mlp_grads
 
     return (
         block_out[None],
@@ -722,13 +863,13 @@
         flat(key_value_rows[:, 0]),
         flat(key_value_rows[:, 1]),
         flat(home(1)),
-        side_by_side(gate_rows).astype(f32),
-        side_by_side(up_rows).astype(f32),
-        side_by_side(down_rows).astype(f32),
+        gate_rows,
+        up_rows,
+        down_rows,
         attn_extra[:model],
-        mlp_gain_sum,
+        attn_extra[model + 2 * head_size :],
         attn_extra[model : model + head_size],
-        attn_extra[model + head_size :],
+        attn_extra[model + head_size : model + 2 * head_size],
     )
 
 

time: 644 us -> 632 us (0.981)
  starting transfers between devices: 111 us -> 87.5 us
  waiting for transfers between devices: 289 us -> 309 us
    ppermute x6 -> x5, waiting for transfers between devices: 40.3 us -> 7.76 us  [swap_rows(): return lax.ppermute(field, 'fsdp', [(0, 1), (1, 0)])]
    ppermute x28, waiting for transfers between devices: 111 us -> 137 us  [out(): return lax.ppermute(field, 'ctx', self.out_pairs)]
    all_to_all x6 -> x4, waiting for transfers between devices: 0.02 us -> 26.3 us  [spread(): lax.all_to_all(rows_block, 'ctx', split_axis=0, concat_axis=0, tiled=False)]
    unnamed x12 -> x2, other arithmetic: 18.4 us -> 1.4 us
    ppermute x18 -> x17, starting transfers between devices: 28.6 us -> 17.9 us  [swap(): return lax.ppermute(field, 'ctx', self.swap_pairs)]
    all_to_all x6 -> x4, starting transfers between devices: 32 us -> 21.4 us  [spread(): lax.all_to_all(rows_block, 'ctx', split_axis=0, concat_axis=0, tiled=False)]
    ppermute x28, waiting for transfers between devices: 131 us -> 121 us  [home(): return lax.ppermute(field, 'ctx', self.home_pairs)]
    ppermute x18 -> x17, waiting for transfers between devices: 6.57 us -> 16.5 us  [swap(): return lax.ppermute(field, 'ctx', self.swap_pairs)]
  transfers between devices with their start and end apart: 86 -> 82, of which waited for: 49 -> 57; matrix products, arithmetic and copies ran while one was open for 25% -> 22% of each run, Pallas kernels for 1% -> 5%
where the time goes in v3:
time: 632 us; the launch traced here: 623 us
  waiting for transfers between devices  309 us (49%)
  starting transfers between devices  87.5 us (14%)
  other arithmetic  86.3 us (14%)
  matrix products  62.8 us (10%)
  local copies, waits for them, and re-layouts  41.1 us (7%)
  Pallas kernels  31.8 us (5%)
    ppermute x28, waiting for transfers between devices, out(): return lax.ppermute(field, 'ctx', self.out_pairs)  137 us
    ppermute x28, waiting for transfers between devices, home(): return lax.ppermute(field, 'ctx', self.home_pairs)  121 us
    ppermute x28, starting transfers between devices, home(): return lax.ppermute(field, 'ctx', self.home_pairs)  39.5 us
    all_to_all x4, waiting for transfers between devices, spread(): lax.all_to_all(rows_block, 'ctx', split_axis=0, concat_axis=0, tiled=False)  26.3 us
    dot_general x6, matrix products, dot_tn(): lax.dot_general(left, right, (((0,), (0,)), ((), ())), preferred_element_...  23.3 us
    dot_general x5, matrix products, dot_nt(): lax.dot_general(left, right, (((1,), (1,)), ((), ())), preferred_element_...  23.3 us
    all_to_all x4, starting transfers between devices, spread(): lax.all_to_all(rows_block, 'ctx', split_axis=0, concat_axis=0, tiled=False)  21.4 us
    convert_element_type x20, other arithmetic, scatter_hops(): total = (term(index).astype(f32) + held.astype(f32)).astype(bf16)  19.2 us
  transfers between devices with their start and end apart: 82, of which 57 were waited for; matrix products, arithmetic and copies ran while one was open for 22% of the time, Pallas kernels for 5%

profile of v3, /device:TPU:9, one launch (start us, length us, event | category | flops | bytes accessed | tf_op | source)
XLA Modules:
  0.0 622.9 jit_solution(6795227925420086459)
XLA Ops:
  6.0 6.6 %all-to-all-start.1 = ((bf16[16,64,384]{2,1,0:T(8,128)(2,1)}), bf16[16,64,384]{2,1,0:T(8,128)(2,1)}, u32[]{:S(2)}, u32[]{:S(2)}) async-start(bf16[16,64,384]{2,1,0:T(8,128)(2,1)} %pad_maximum_fusion.18), calls=%async_computation.1 | async-start | bytes 1572864 | tf_op jit(solution)/shard_map/all_to_all | solution.py:467
  14.7 23.1 %collective-permute-done.47.refs_1_ = bf16[128,2048]{1,0:T(8,128)(2,1)S(1)} collective-permute-done((bf16[128,2048]{1,0:T(8,128)(2,1)S(1)}, bf16[128,2048]{1,0:T(8,128)(2,1)S(1)}, u32[]{:S(2)}, u32[]{:S(2)}) %collective-permute-start.47) | collective-permute-done | bytes 524320 | tf_op jit(solution)/shard_map/ppermute | solution.py:400
  37.8 5.6 collective-permute-done.49.refs_2_
  43.4 5.6 collective-permute-done.50.refs_3_
  50.4 3.7 fusion.29
  56.5 3.8 collective-permute-done.52.refs_5_
  60.3 7.2 %collective-permute-done.45 = bf16[16,64,384]{2,1,0:T(8,128)(2,1)S(1)} collective-permute-done((bf16[16,64,384]{2,1,0:T(8,128)(2,1)}, bf16[16,64,384]{2,1,0:T(8,128)(2,1)S(1)}, u32[]{:S(2)}, u32[]{:S(2)}) %collective-permute-start.45) | collective-permute-done | bytes 786464 | tf_op jit(solution)/shard_map/ppermute | solution.py:471
  75.2 4.5 all-to-all-start.2
  84.1 4.6 project.1
  93.7 11.0 %attend.1 = (bf16[1024,128]{1,0:T(8,128)(2,1)S(1)}, bf16[1024,128]{1,0:T(8,128)(2,1)S(1)}, f32[1,2048]{1,0:T(1,128)S(1)}, bf16[2048,128]{1,0:T(8,128)(2,1)}, bf1...) custom-call(s32[32]{0:T(128)S(1)} %select_reduce_fusion.key_pos, s32[32]{0:T(128)S(1)} %iota.30.query_table.pos_table, ...), custom_call_target="tpu_custom_call" | custom-call | flops 2147483648 | bytes 7340032 | tf_op jit(solution)/shard_map/attend/pallas_call | solution.py:200
  104.7 26.3 %all-to-all-done.2 = bf16[16,64,1152]{2,1,0:T(8,128)(2,1)} async-done(((bf16[16,64,1152]{2,1,0:T(8,128)(2,1)}), bf16[16,64,1152]{2,1,0:T(8,128)(2,1)}, u32[]{:S(2)}, u32[]{:S(2)}) %all-to-all-start.2) | async-done | bytes 2359328 | tf_op jit(solution)/shard_map/all_to_all | solution.py:467
  137.7 45.3 %conditional.6 = (f32[128,2048]{1,0:T(8,128)S(1)}) conditional(s32[]{:T(128)} %convert_element_type.468, () %tuple.125, bf16[1024,2048]{1,0:T(8,128)(2,1)} %convolution_convert_fusion.9), branch_computations={%region_3.4_spmd, %region_4.5_spmd} | conditional | flops 6553600 | bytes 46137700 | solution.py:557
  139.2 3.3 collective-permute-start.8
  142.6 6.1 collective-permute-done.8
  178.3 4.1 collective-permute-done.13
  188.9 7.7 %collective-permute-done.58 = bf16[128,2048]{1,0:T(8,128)(2,1)S(1)} collective-permute-done((bf16[128,2048]{1,0:T(8,128)(2,1)S(1)}, bf16[128,2048]{1,0:T(8,128)(2,1)S(1)}, u32[]{:S(2)}, u32[]{:S(2)}) %collective-permute-start.58) | collective-permute-done | bytes 524320 | tf_op jit(solution)/shard_map/ppermute | solution.py:397
  198.5 8.0 %collective-permute-done.59 = bf16[128,2048]{1,0:T(8,128)(2,1)S(1)} collective-permute-done((bf16[128,2048]{1,0:T(8,128)(2,1)S(1)}, bf16[128,2048]{1,0:T(8,128)(2,1)S(1)}, u32[]{:S(2)}, u32[]{:S(2)}) %collective-permute-start.59) | collective-permute-done | bytes 524320 | tf_op jit(solution)/shard_map/ppermute | solution.py:400
  206.5 5.6 collective-permute-done.60
  212.1 5.6 collective-permute-done.63
  217.9 5.5 collective-permute-done.64
  223.4 5.6 collective-permute-done.65
  234.6 5.6 collective-permute-done.67
  240.3 5.3 collective-permute-done.69
  249.0 3.4 pad_maximum_fusion.4
  252.4 5.9 fusion.8
  261.6 3.4 fusion.16
  267.7 5.0 collective-permute-done.72
  273.5 4.8 collective-permute-done.73
  278.4 5.6 collective-permute-done.74
  284.0 3.4 fusion.46
  293.5 65.1 %conditional.7 = (f32[128,2048]{1,0:T(8,128)S(1)}, bf16[2048]{0:T(1024)(128)(2,1)S(1)}, bf16[16,64,384]{2,1,0:T(8,128)(2,1)}, bf16[16,64,768]{2,1,0:T(8,128)(2,1...) conditional(s32[]{:T(128)} %convert_element_type.468, () %tuple.145, (bf16[1024,1536]{1,0:T(8,128)(2,1)S(1)}, ...), branch_computations={%region_6.7_spmd, %region_7.10_spmd} | conditional | flops 13724157952 | bytes 205173424 | solution.py:557
  296.5 5.6 convolution_convert_fusion.2
  307.6 4.7 fusion.2
  316.7 3.9 fusion
  327.7 3.6 collective-permute-done.18
  331.3 3.9 fusion.1
  340.6 10.3 %collective-permute-done.22 = bf16[128,2048]{1,0:T(8,128)(2,1)S(1)} collective-permute-done((bf16[128,2048]{1,0:T(8,128)(2,1)S(1)}, bf16[128,2048]{1,0:T(8,128)(2,1)S(1)}, u32[]{:S(2)}, u32[]{:S(2)}) %collective-permute-start.22) | collective-permute-done | bytes 524320 | tf_op jit(solution)/shard_map/cond/branch_1_fun/ppermute | solution.py:403
  363.2 43.8 %conditional.8 = (bf16[1024,2048]{1,0:T(8,128)(2,1)}) conditional(s32[]{:T(128)} %convert_element_type.468, () %tuple.144, bf16[128,2048]{1,0:T(8,128)(2,1)} %get-tuple-element.351), branch_computations={%region_11.12_spmd, %region_12.13_spmd} | conditional | bytes 25166152 | solution.py:557
  365.5 6.9 %collective-permute-done = bf16[128,2048]{1,0:T(8,128)(2,1)S(1)} collective-permute-done((bf16[128,2048]{1,0:T(8,128)(2,1)}, bf16[128,2048]{1,0:T(8,128)(2,1)S(1)}, u32[]{:S(2)}, u32[]{:S(2)}) %collective-permute-start) | collective-permute-done | bytes 524320 | tf_op jit(solution)/shard_map/cond/branch_1_fun/ppermute | solution.py:400
  372.4 5.6 collective-permute-done.2
  379.9 3.7 collective-permute-done.3
  385.3 3.9 collective-permute-done.4
  390.0 4.8 collective-permute-done.5
  396.5 3.9 collective-permute-done.6
  401.3 4.8 collective-permute-done.7
  406.9 3.4 convolution_convert_fusion.11
  419.0 4.5 all-to-all-start.3
  425.9 26.8 %conditional.9 = (bf16[1024,512]{1,0:T(8,128)(2,1)}, bf16[1024,2048]{1,0:T(8,128)(2,1)}, f32[128]{0:T(128)S(1)}, f32[128]{0:T(128)S(1)}) conditional(s32[]{:T(128)} %convert_element_type.468, () %tuple.143, (s32[32]{0:T(128)S(1)}, s32[32]{0:T(128)S(1)}, s32[32]{0:T(128)S(1)}, f32[1024,512]{1,0:T(8,128)}, f32[1024,384]{1,0:T(8,128)}, ...), branch_computations={%region_13.14_spmd, %region_14.15_spmd} | conditional | flops 7522484224 | bytes 34078820 | solution.py:557
  426.1 16.2 %attend_back.1 = (bf16[1024,384]{1,0:T(8,128)(2,1)}, bf16[1024,384]{1,0:T(8,128)(2,1)}, f32[1,128]{1,0:T(1,128)S(1)}, f32[1,128]{1,0:T(1,128)S(1)}) custom-call(s32[32]{0:T(128)S(1)} %get-tuple-element.131.key_pos, s32[32]{0:T(128)S(1)} %get-tuple-element.133.pos_table, s32[32]{0:T(128)S(1)} %get-tuple-element.133.pos_table, ...), custom_call_target="tpu_custom_call" | custom-call | flops 5368709120 | bytes 10485760 | tf_op jit(solution)/shard_map/cond/branch_1_fun/attend_back/pallas_call | solution.py:315
  447.1 5.6 convolution_convert_fusion.5
  452.7 75.3 %conditional.10 = (f32[128,2048]{1,0:T(8,128)S(1)}, bf16[2048,384]{0,1:T(8,128)(2,1)}, bf16[2048]{0:T(1024)(128)(2,1)S(1)}) conditional(s32[]{:T(128)} %convert_element_type.468, () %tuple.142, (bf16[1024,2048]{1,0:T(8,128)(2,1)}, bf16[1024,512]{1,0:T(8,128)(2,1)}, bf16[1024,256]{1,0:T(8,128)(2,1)S(1)}, bf16[1024,2048]{1,0:T(8,128)(2,1)}, ...), branch_computations={%region_15.16_spmd, %region_16.18_spmd} | conditional | flops 3250061312 | bytes 88109472 | solution.py:557
  457.2 23.4 %collective-permute-done.27 = bf16[128,2048]{1,0:T(8,128)(2,1)S(1)} collective-permute-done((bf16[128,2048]{1,0:T(8,128)(2,1)}, bf16[128,2048]{1,0:T(8,128)(2,1)S(1)}, u32[]{:S(2)}, u32[]{:S(2)}) %collective-permute-start.27) | collective-permute-done | bytes 524320 | tf_op jit(solution)/shard_map/cond/branch_1_fun/ppermute | solution.py:403
  489.6 4.9 fusion.5
  494.4 3.5 fusion.6
  502.6 3.9 multiply_reduce_fusion.2
  508.1 5.6 collective-permute-done.34
  519.3 7.2 %collective-permute-done.33 = bf16[128,2048]{1,0:T(8,128)(2,1)S(1)} collective-permute-done((bf16[128,2048]{1,0:T(8,128)(2,1)S(1)}, bf16[128,2048]{1,0:T(8,128)(2,1)S(1)}, u32[]{:S(2)}, u32[]{:S(2)}) %collective-permute-start.33) | collective-permute-done | bytes 524320 | tf_op jit(solution)/shard_map/cond/branch_1_fun/ppermute | solution.py:403
  528.0 85.6 %conditional.11 = (f32[128,2048]{1,0:T(8,128)}, bf16[16,80,384]{2,1,0:T(8,128)(2,1)}, f32[64,6144]{1,0:T(8,128)}, f32[64,6144]{1,0:T(8,128)}, f32[64,6144]{1,0:T(8,128)}, /*index=5*/f32[1,128,2048]{2,1,0:T(8,128)}) conditional(s32[]{:T(128)} %convert_element_type.468, () %tuple.133, (bf16[1024,768]{1,0:T(8,128)(2,1)}, ...), branch_computations={%region_18.19_spmd, %region_19.22_spmd} | conditional | flops 3239887360 | bytes 114878552 | solution.py:557
  528.1 6.2 convolution_convert_fusion.8
  540.1 4.0 collective-permute-done.36
  560.5 5.8 all-to-all-start
  571.5 22.4 %collective-permute-done.40 = bf16[128,2048]{1,0:T(8,128)(2,1)S(1)} collective-permute-done((bf16[128,2048]{1,0:T(8,128)(2,1)S(1)}, bf16[128,2048]{1,0:T(8,128)(2,1)S(1)}, u32[]{:S(2)}, u32[]{:S(2)}) %collective-permute-start.40) | collective-permute-done | bytes 524320 | tf_op jit(solution)/shard_map/cond/branch_1_fun/ppermute | solution.py:403
  593.9 5.6 collective-permute-done.43
  603.3 8.0 %collective-permute-done.42 = bf16[128,2048]{1,0:T(8,128)(2,1)S(1)} collective-permute-done((bf16[128,2048]{1,0:T(8,128)(2,1)S(1)}, bf16[128,2048]{1,0:T(8,128)(2,1)S(1)}, u32[]{:S(2)}, u32[]{:S(2)}) %collective-permute-start.42) | collective-permute-done | bytes 524320 | tf_op jit(solution)/shard_map/cond/branch_1_fun/ppermute | solution.py:403
  (411 shorter events, 227.0 us)
Async XLA Ops:
  6.0 43.0 %all-to-all-start.1 = ((bf16[16,64,384]{2,1,0:T(8,128)(2,1)}), bf16[16,64,384]{2,1,0:T(8,128)(2,1)}, u32[]{:S(2)}, u32[]{:S(2)}) async-start(bf16[16,64,384]{2,1,0:T(8,128)(2,1)} %pad_maximum_fusion.18), calls=%async_computation.1 | async-start | bytes 1572864 | tf_op jit(solution)/shard_map/all_to_all | solution.py:467
  13.0 24.8 %collective-permute-start.47 = (bf16[128,2048]{1,0:T(8,128)(2,1)S(1)}, bf16[128,2048]{1,0:T(8,128)(2,1)S(1)}, u32[]{:S(2)}, u32[]{:S(2)}) collective-permute-start(bf16[128,2048]{1,0:T(8,128)(2,1)S(1)} %bitcast.192), channel_id=1, source_target_pairs={{0,8},{10,2},{8,16},{18,10},{16,24},{26,18},{24,28},{30,26},{28,20... | collective-permute-start | bytes 1572872 | tf_op jit(solution)/shard_map/ppermute | solution.py:400
  14.6 28.8 %collective-permute-start.49 = (bf16[128,2048]{1,0:T(8,128)(2,1)S(1)}, bf16[128,2048]{1,0:T(8,128)(2,1)S(1)}, u32[]{:S(2)}, u32[]{:S(2)}) collective-permute-start(bf16[128,2048]{1,0:T(8,128)(2,1)S(1)} %collective-permute-done.48), channel_id=1, source_target_pairs={{0,8},{10,2},{8,16},{18,10},{16,24},{26,18},{24,28},{30,26},{28,20... | collective-permute-start | bytes 1572872 | tf_op jit(solution)/shard_map/ppermute | solution.py:400
  37.8 11.2 %collective-permute-start.50 = (bf16[128,2048]{1,0:T(8,128)(2,1)S(1)}, bf16[128,2048]{1,0:T(8,128)(2,1)S(1)}, u32[]{:S(2)}, u32[]{:S(2)}) collective-permute-start(bf16[128,2048]{1,0:T(8,128)(2,1)S(1)} %collective-permute-done.47.refs_1_), channel_id=1, source_target_pairs={{0,8},{10,2},{8,16},{18,10},{16,24},{26,18},{24,28},{30,26},{28,20... | collective-permute-start | bytes 1572872 | tf_op jit(solution)/shard_map/ppermute | solution.py:400
  43.4 13.0 %collective-permute-start.51 = (bf16[128,2048]{1,0:T(8,128)(2,1)S(1)}, bf16[128,2048]{1,0:T(8,128)(2,1)S(1)}, u32[]{:S(2)}, u32[]{:S(2)}) collective-permute-start(bf16[128,2048]{1,0:T(8,128)(2,1)S(1)} %collective-permute-done.49.refs_2_), channel_id=1, source_target_pairs={{0,8},{10,2},{8,16},{18,10},{16,24},{26,18},{24,28},{30,26},{28,20... | collective-permute-start | bytes 1572872 | tf_op jit(solution)/shard_map/ppermute | solution.py:400
  49.0 11.2 %collective-permute-start.52 = (bf16[128,2048]{1,0:T(8,128)(2,1)S(1)}, bf16[128,2048]{1,0:T(8,128)(2,1)S(1)}, u32[]{:S(2)}, u32[]{:S(2)}) collective-permute-start(bf16[128,2048]{1,0:T(8,128)(2,1)S(1)} %collective-permute-done.50.refs_3_), channel_id=1, source_target_pairs={{0,8},{10,2},{8,16},{18,10},{16,24},{26,18},{24,28},{30,26},{28,20... | collective-permute-start | bytes 1572872 | tf_op jit(solution)/shard_map/ppermute | solution.py:400
  49.1 18.4 %collective-permute-start.45 = (bf16[16,64,384]{2,1,0:T(8,128)(2,1)}, bf16[16,64,384]{2,1,0:T(8,128)(2,1)S(1)}, u32[]{:S(2)}, u32[]{:S(2)}) collective-permute-start(bf16[16,64,384]{2,1,0:T(8,128)(2,1)} %all-to-all-done.1), channel_id=1, source_target_pairs={{0,1},{1,0},{2,3},{3,2},{4,5},{5,4},{6,7},{7,6},{8,9},{9,8},{10,11... | collective-permute-start | bytes 2359304 | tf_op jit(solution)/shard_map/ppermute | solution.py:471
  56.5 17.2 %collective-permute-start.53 = (bf16[128,2048]{1,0:T(8,128)(2,1)S(1)}, bf16[128,2048]{1,0:T(8,128)(2,1)S(1)}, u32[]{:S(2)}, u32[]{:S(2)}) collective-permute-start(bf16[128,2048]{1,0:T(8,128)(2,1)S(1)} %collective-permute-done.51.refs_4_), channel_id=1, source_target_pairs={{0,8},{10,2},{8,16},{18,10},{16,24},{26,18},{24,28},{30,26},{28,20... | collective-permute-start | bytes 1572872 | tf_op jit(solution)/shard_map/ppermute | solution.py:400
  60.3 14.1 %collective-permute-start.54 = (bf16[128,2048]{1,0:T(8,128)(2,1)S(1)}, bf16[128,2048]{1,0:T(8,128)(2,1)S(1)}, u32[]{:S(2)}, u32[]{:S(2)}) collective-permute-start(bf16[128,2048]{1,0:T(8,128)(2,1)S(1)} %collective-permute-done.52.refs_5_), channel_id=1, source_target_pairs={{0,8},{10,2},{8,16},{18,10},{16,24},{26,18},{24,28},{30,26},{28,20... | collective-permute-start | bytes 1572872 | tf_op jit(solution)/shard_map/ppermute | solution.py:400
  70.1 9.7 %collective-permute-start.46 = (bf16[2048,384]{1,0:T(8,128)(2,1)}, bf16[2048,384]{1,0:T(8,128)(2,1)}, u32[]{:S(2)}, u32[]{:S(2)}) collective-permute-start(bf16[2048,384]{1,0:T(8,128)(2,1)} %bitcast.32), channel_id=1, source_target_pairs={{0,2},{2,0},{4,6},{6,4},{8,10},{10,8},{12,14},{14,12},{16,18},{18,... | collective-permute-start | bytes 4718600 | tf_op jit(solution)/shard_map/ppermute | solution.py:397
  75.2 55.7 %all-to-all-start.2 = ((bf16[16,64,1152]{2,1,0:T(8,128)(2,1)}), bf16[16,64,1152]{2,1,0:T(8,128)(2,1)}, u32[]{:S(2)}, u32[]{:S(2)}) async-start(bf16[16,64,1152]{2,1,0:T(8,128)(2,1)} %pad_maximum_fusion.8), calls=%async_computation.2 | async-start | bytes 4718592 | tf_op jit(solution)/shard_map/all_to_all | solution.py:467
  130.9 52.6 %collective-permute-start.61 = (bf16[16,64,1152]{2,1,0:T(8,128)(2,1)}, bf16[16,64,1152]{2,1,0:T(8,128)(2,1)}, u32[]{:S(2)}, u32[]{:S(2)}) collective-permute-start(bf16[16,64,1152]{2,1,0:T(8,128)(2,1)} %all-to-all-done.2), channel_id=1, source_target_pairs={{0,1},{1,0},{2,3},{3,2},{4,5},{5,4},{6,7},{7,6},{8,9},{9,8},{10,11... | collective-permute-start | bytes 7077896 | tf_op jit(solution)/shard_map/ppermute | solution.py:471
  139.2 9.5 %collective-permute-start.8 = (bf16[128,2048]{1,0:T(8,128)(2,1)S(1)}, bf16[128,2048]{1,0:T(8,128)(2,1)S(1)}, u32[]{:S(2)}, u32[]{:S(2)}) collective-permute-start(bf16[128,2048]{1,0:T(8,128)(2,1)S(1)} %get-tuple-element.357), channel_id=1, source_target_pairs={{8,0},{2,10},{16,8},{10,18},{24,16},{18,26},{28,24},{26,30},{20,28... | collective-permute-start | bytes 1572872 | tf_op jit(solution)/shard_map/cond/branch_1_fun/ppermute | solution.py:403
  142.5 11.7 %collective-permute-start.10 = (bf16[128,2048]{1,0:T(8,128)(2,1)S(1)}, bf16[128,2048]{1,0:T(8,128)(2,1)S(1)}, u32[]{:S(2)}, u32[]{:S(2)}) collective-permute-start(bf16[128,2048]{1,0:T(8,128)(2,1)S(1)} %get-tuple-element.358), channel_id=1, source_target_pairs={{8,0},{2,10},{16,8},{10,18},{24,16},{18,26},{28,24},{26,30},{20,28... | collective-permute-start | bytes 1572872 | tf_op jit(solution)/shard_map/cond/branch_1_fun/ppermute | solution.py:403
  149.8 10.1 %collective-permute-start.9 = (bf16[128,2048]{1,0:T(8,128)(2,1)S(1)}, bf16[128,2048]{1,0:T(8,128)(2,1)S(1)}, u32[]{:S(2)}, u32[]{:S(2)}) collective-permute-start(bf16[128,2048]{1,0:T(8,128)(2,1)S(1)} %add_convert_fusion.4), channel_id=1, source_target_pairs={{8,0},{2,10},{16,8},{10,18},{24,16},{18,26},{28,24},{26,30},{20,28... | collective-permute-start | bytes 1572872 | tf_op jit(solution)/shard_map/cond/branch_1_fun/ppermute | solution.py:403
  155.5 10.1 %collective-permute-start.12 = (bf16[128,2048]{1,0:T(8,128)(2,1)S(1)}, bf16[128,2048]{1,0:T(8,128)(2,1)S(1)}, u32[]{:S(2)}, u32[]{:S(2)}) collective-permute-start(bf16[128,2048]{1,0:T(8,128)(2,1)S(1)} %add_convert_fusion.3), channel_id=1, source_target_pairs={{8,0},{2,10},{16,8},{10,18},{24,16},{18,26},{28,24},{26,30},{20,28... | collective-permute-start | bytes 1572872 | tf_op jit(solution)/shard_map/cond/branch_1_fun/ppermute | solution.py:403
  160.0 11.1 %collective-permute-start.11 = (bf16[128,2048]{1,0:T(8,128)(2,1)S(1)}, bf16[128,2048]{1,0:T(8,128)(2,1)S(1)}, u32[]{:S(2)}, u32[]{:S(2)}) collective-permute-start(bf16[128,2048]{1,0:T(8,128)(2,1)S(1)} %add_convert_fusion.2), channel_id=1, source_target_pairs={{8,0},{2,10},{16,8},{10,18},{24,16},{18,26},{28,24},{26,30},{20,28... | collective-permute-start | bytes 1572872 | tf_op jit(solution)/shard_map/cond/branch_1_fun/ppermute | solution.py:403
  165.7 11.1 %collective-permute-start.14 = (bf16[128,2048]{1,0:T(8,128)(2,1)S(1)}, bf16[128,2048]{1,0:T(8,128)(2,1)S(1)}, u32[]{:S(2)}, u32[]{:S(2)}) collective-permute-start(bf16[128,2048]{1,0:T(8,128)(2,1)S(1)} %add_convert_fusion.1), channel_id=1, source_target_pairs={{8,0},{2,10},{16,8},{10,18},{24,16},{18,26},{28,24},{26,30},{20,28... | collective-permute-start | bytes 1572872 | tf_op jit(solution)/shard_map/cond/branch_1_fun/ppermute | solution.py:403
  171.3 11.1 %collective-permute-start.13 = (bf16[128,2048]{1,0:T(8,128)(2,1)S(1)}, bf16[128,2048]{1,0:T(8,128)(2,1)S(1)}, u32[]{:S(2)}, u32[]{:S(2)}) collective-permute-start(bf16[128,2048]{1,0:T(8,128)(2,1)S(1)} %add_convert_fusion), channel_id=1, source_target_pairs={{8,0},{2,10},{16,8},{10,18},{24,16},{18,26},{28,24},{26,30},{20,28... | collective-permute-start | bytes 1572872 | tf_op jit(solution)/shard_map/cond/branch_1_fun/ppermute | solution.py:403
  186.9 61.5 %collective-permute-start.62 = (bf16[2048,1152]{1,0:T(8,128)(2,1)S(1)}, bf16[2048,1152]{1,0:T(8,128)(2,1)S(1)}, u32[]{:S(2)}, u32[]{:S(2)}) collective-permute-start(bf16[2048,1152]{1,0:T(8,128)(2,1)S(1)} %bitcast.194), channel_id=1, source_target_pairs={{0,2},{2,0},{4,6},{6,4},{8,10},{10,8},{12,14},{14,12},{16,18},{18,... | collective-permute-start | bytes 14155784 | tf_op jit(solution)/shard_map/ppermute | solution.py:397
  188.8 9.7 %collective-permute-start.57 = (bf16[128,2048]{1,0:T(8,128)(2,1)S(1)}, bf16[128,2048]{1,0:T(8,128)(2,1)S(1)}, u32[]{:S(2)}, u32[]{:S(2)}) collective-permute-start(bf16[128,2048]{1,0:T(8,128)(2,1)S(1)} %get-tuple-element.354), channel_id=1, source_target_pairs={{0,8},{10,2},{8,16},{18,10},{16,24},{26,18},{24,28},{30,26},{28,20... | collective-permute-start | bytes 1572872 | tf_op jit(solution)/shard_map/ppermute | solution.py:400
  196.6 9.9 %collective-permute-start.59 = (bf16[128,2048]{1,0:T(8,128)(2,1)S(1)}, bf16[128,2048]{1,0:T(8,128)(2,1)S(1)}, u32[]{:S(2)}, u32[]{:S(2)}) collective-permute-start(bf16[128,2048]{1,0:T(8,128)(2,1)S(1)} %collective-permute-done.58), channel_id=1, source_target_pairs={{0,8},{10,2},{8,16},{18,10},{16,24},{26,18},{24,28},{30,26},{28,20... | collective-permute-start | bytes 1572872 | tf_op jit(solution)/shard_map/ppermute | solution.py:400
  198.5 13.6 %collective-permute-start.60 = (bf16[128,2048]{1,0:T(8,128)(2,1)S(1)}, bf16[128,2048]{1,0:T(8,128)(2,1)S(1)}, u32[]{:S(2)}, u32[]{:S(2)}) collective-permute-start(bf16[128,2048]{1,0:T(8,128)(2,1)S(1)} %collective-permute-done.57), channel_id=1, source_target_pairs={{0,8},{10,2},{8,16},{18,10},{16,24},{26,18},{24,28},{30,26},{28,20... | collective-permute-start | bytes 1572872 | tf_op jit(solution)/shard_map/ppermute | solution.py:400
  206.5 11.2 %collective-permute-start.63 = (bf16[128,2048]{1,0:T(8,128)(2,1)S(1)}, bf16[128,2048]{1,0:T(8,128)(2,1)S(1)}, u32[]{:S(2)}, u32[]{:S(2)}) collective-permute-start(bf16[128,2048]{1,0:T(8,128)(2,1)S(1)} %collective-permute-done.59), channel_id=1, source_target_pairs={{0,8},{10,2},{8,16},{18,10},{16,24},{26,18},{24,28},{30,26},{28,20... | collective-permute-start | bytes 1572872 | tf_op jit(solution)/shard_map/ppermute | solution.py:400
  212.1 11.2 %collective-permute-start.64 = (bf16[128,2048]{1,0:T(8,128)(2,1)S(1)}, bf16[128,2048]{1,0:T(8,128)(2,1)S(1)}, u32[]{:S(2)}, u32[]{:S(2)}) collective-permute-start(bf16[128,2048]{1,0:T(8,128)(2,1)S(1)} %collective-permute-done.60), channel_id=1, source_target_pairs={{0,8},{10,2},{8,16},{18,10},{16,24},{26,18},{24,28},{30,26},{28,20... | collective-permute-start | bytes 1572872 | tf_op jit(solution)/shard_map/ppermute | solution.py:400
  217.7 11.2 %collective-permute-start.65 = (bf16[128,2048]{1,0:T(8,128)(2,1)S(1)}, bf16[128,2048]{1,0:T(8,128)(2,1)S(1)}, u32[]{:S(2)}, u32[]{:S(2)}) collective-permute-start(bf16[128,2048]{1,0:T(8,128)(2,1)S(1)} %collective-permute-done.63), channel_id=1, source_target_pairs={{0,8},{10,2},{8,16},{18,10},{16,24},{26,18},{24,28},{30,26},{28,20... | collective-permute-start | bytes 1572872 | tf_op jit(solution)/shard_map/ppermute | solution.py:400
  223.4 11.2 %collective-permute-start.66 = (bf16[128,2048]{1,0:T(8,128)(2,1)S(1)}, bf16[128,2048]{1,0:T(8,128)(2,1)S(1)}, u32[]{:S(2)}, u32[]{:S(2)}) collective-permute-start(bf16[128,2048]{1,0:T(8,128)(2,1)S(1)} %collective-permute-done.64), channel_id=1, source_target_pairs={{0,8},{10,2},{8,16},{18,10},{16,24},{26,18},{24,28},{30,26},{28,20... | collective-permute-start | bytes 1572872 | tf_op jit(solution)/shard_map/ppermute | solution.py:400
  229.6 10.7 %collective-permute-start.67 = (bf16[128,2048]{1,0:T(8,128)(2,1)S(1)}, bf16[128,2048]{1,0:T(8,128)(2,1)S(1)}, u32[]{:S(2)}, u32[]{:S(2)}) collective-permute-start(bf16[128,2048]{1,0:T(8,128)(2,1)S(1)} %bitcast.206), channel_id=1, source_target_pairs={{0,8},{10,2},{8,16},{18,10},{16,24},{26,18},{24,28},{30,26},{28,20... | collective-permute-start | bytes 1572872 | tf_op jit(solution)/shard_map/ppermute | solution.py:400
  231.0 14.5 %collective-permute-start.69 = (bf16[128,2048]{1,0:T(8,128)(2,1)S(1)}, bf16[128,2048]{1,0:T(8,128)(2,1)S(1)}, u32[]{:S(2)}, u32[]{:S(2)}) collective-permute-start(bf16[128,2048]{1,0:T(8,128)(2,1)S(1)} %collective-permute-done.68), channel_id=1, source_target_pairs={{0,8},{10,2},{8,16},{18,10},{16,24},{26,18},{24,28},{30,26},{28,20... | collective-permute-start | bytes 1572872 | tf_op jit(solution)/shard_map/ppermute | solution.py:400
  252.4 8.9 %collective-permute-start.70 = (bf16[128,2048]{1,0:T(8,128)(2,1)}, bf16[128,2048]{1,0:T(8,128)(2,1)S(1)}, u32[]{:S(2)}, u32[]{:S(2)}) collective-permute-start(bf16[128,2048]{1,0:T(8,128)(2,1)} %copy-done.45), channel_id=1, source_target_pairs={{0,8},{10,2},{8,16},{18,10},{16,24},{26,18},{24,28},{30,26},{28,20... | collective-permute-start | bytes 1572872 | tf_op jit(solution)/shard_map/ppermute | solution.py:400
  258.4 8.7 %collective-permute-start.71 = (bf16[128,2048]{1,0:T(8,128)(2,1)S(1)}, bf16[128,2048]{1,0:T(8,128)(2,1)S(1)}, u32[]{:S(2)}, u32[]{:S(2)}) collective-permute-start(bf16[128,2048]{1,0:T(8,128)(2,1)S(1)} %copy-done.44), channel_id=1, source_target_pairs={{0,8},{10,2},{8,16},{18,10},{16,24},{26,18},{24,28},{30,26},{28,20... | collective-permute-start | bytes 1572872 | tf_op jit(solution)/shard_map/ppermute | solution.py:400
  261.3 11.4 %collective-permute-start.72 = (bf16[128,2048]{1,0:T(8,128)(2,1)S(1)}, bf16[128,2048]{1,0:T(8,128)(2,1)S(1)}, u32[]{:S(2)}, u32[]{:S(2)}) collective-permute-start(bf16[128,2048]{1,0:T(8,128)(2,1)S(1)} %collective-permute-done.70), channel_id=1, source_target_pairs={{0,8},{10,2},{8,16},{18,10},{16,24},{26,18},{24,28},{30,26},{28,20... | collective-permute-start | bytes 1572872 | tf_op jit(solution)/shard_map/ppermute | solution.py:400
  267.1 11.2 %collective-permute-start.73 = (bf16[128,2048]{1,0:T(8,128)(2,1)S(1)}, bf16[128,2048]{1,0:T(8,128)(2,1)S(1)}, u32[]{:S(2)}, u32[]{:S(2)}) collective-permute-start(bf16[128,2048]{1,0:T(8,128)(2,1)S(1)} %collective-permute-done.71), channel_id=1, source_target_pairs={{0,8},{10,2},{8,16},{18,10},{16,24},{26,18},{24,28},{30,26},{28,20... | collective-permute-start | bytes 1572872 | tf_op jit(solution)/shard_map/ppermute | solution.py:400
  272.7 11.2 %collective-permute-start.74 = (bf16[128,2048]{1,0:T(8,128)(2,1)S(1)}, bf16[128,2048]{1,0:T(8,128)(2,1)S(1)}, u32[]{:S(2)}, u32[]{:S(2)}) collective-permute-start(bf16[128,2048]{1,0:T(8,128)(2,1)S(1)} %collective-permute-done.72), channel_id=1, source_target_pairs={{0,8},{10,2},{8,16},{18,10},{16,24},{26,18},{24,28},{30,26},{28,20... | collective-permute-start | bytes 1572872 | tf_op jit(solution)/shard_map/ppermute | solution.py:400
  303.8 12.9 %collective-permute-start.17 = (bf16[128,2048]{1,0:T(8,128)(2,1)}, bf16[128,2048]{1,0:T(8,128)(2,1)}, u32[]{:S(2)}, u32[]{:S(2)}) collective-permute-start(bf16[128,2048]{1,0:T(8,128)(2,1)} %add_convert_fusion.11), channel_id=1, source_target_pairs={{8,0},{2,10},{16,8},{10,18},{24,16},{18,26},{28,24},{26,30},{20,28... | collective-permute-start | bytes 1572872 | tf_op jit(solution)/shard_map/cond/branch_1_fun/ppermute | solution.py:403
  312.4 40.3 %collective-permute-start.24 = (bf16[2048,384]{1,0:T(8,128)(2,1)S(1)}, bf16[2048,384]{1,0:T(8,128)(2,1)S(1)}, u32[]{:S(2)}, u32[]{:S(2)}) collective-permute-start(bf16[2048,384]{1,0:T(8,128)(2,1)S(1)} %fusion.2), channel_id=1, source_target_pairs={{0,2},{2,0},{4,6},{6,4},{8,10},{10,8},{12,14},{14,12},{16,18},{18,... | collective-permute-start | bytes 4718600 | tf_op jit(solution)/shard_map/cond/branch_1_fun/ppermute | solution.py:397
  320.7 34.2 %collective-permute-start.25 = (bf16[2048,768]{1,0:T(8,128)(2,1)S(1)}, bf16[2048,768]{1,0:T(8,128)(2,1)S(1)}, u32[]{:S(2)}, u32[]{:S(2)}) collective-permute-start(bf16[2048,768]{1,0:T(8,128)(2,1)S(1)} %fusion), channel_id=1, source_target_pairs={{0,2},{2,0},{4,6},{6,4},{8,10},{10,8},{12,14},{14,12},{16,18},{18,... | collective-permute-start | bytes 9437192 | tf_op jit(solution)/shard_map/cond/branch_1_fun/ppermute | solution.py:397
  325.9 11.1 %collective-permute-start.21 = (bf16[128,2048]{1,0:T(8,128)(2,1)S(1)}, bf16[128,2048]{1,0:T(8,128)(2,1)S(1)}, u32[]{:S(2)}, u32[]{:S(2)}) collective-permute-start(bf16[128,2048]{1,0:T(8,128)(2,1)S(1)} %add_convert_fusion.9), channel_id=1, source_target_pairs={{8,0},{2,10},{16,8},{10,18},{24,16},{18,26},{28,24},{26,30},{20,28... | collective-permute-start | bytes 1572872 | tf_op jit(solution)/shard_map/cond/branch_1_fun/ppermute | solution.py:403
  337.0 17.7 %collective-permute-start.20 = (bf16[128,2048]{1,0:T(8,128)(2,1)S(1)}, bf16[128,2048]{1,0:T(8,128)(2,1)S(1)}, u32[]{:S(2)}, u32[]{:S(2)}) collective-permute-start(bf16[128,2048]{1,0:T(8,128)(2,1)S(1)} %add_convert_fusion.8), channel_id=1, source_target_pairs={{8,0},{2,10},{16,8},{10,18},{24,16},{18,26},{28,24},{26,30},{20,28... | collective-permute-start | bytes 1572872 | tf_op jit(solution)/shard_map/cond/branch_1_fun/ppermute | solution.py:403
  337.1 13.8 %collective-permute-start.22 = (bf16[128,2048]{1,0:T(8,128)(2,1)S(1)}, bf16[128,2048]{1,0:T(8,128)(2,1)S(1)}, u32[]{:S(2)}, u32[]{:S(2)}) collective-permute-start(bf16[128,2048]{1,0:T(8,128)(2,1)S(1)} %add_convert_fusion.7), channel_id=1, source_target_pairs={{8,0},{2,10},{16,8},{10,18},{24,16},{18,26},{28,24},{26,30},{20,28... | collective-permute-start | bytes 1572872 | tf_op jit(solution)/shard_map/cond/branch_1_fun/ppermute | solution.py:403
  358.7 53.3 %collective-permute-start.76 = (bf16[16,64,384]{2,1,0:T(8,128)(2,1)}, bf16[16,64,384]{2,1,0:T(8,128)(2,1)}, u32[]{:S(2)}, u32[]{:S(2)}) collective-permute-start(bf16[16,64,384]{2,1,0:T(8,128)(2,1)} %get-tuple-element.295), channel_id=1, source_target_pairs={{0,1},{1,0},{2,3},{3,2},{4,5},{5,4},{6,7},{7,6},{8,9},{9,8},{10,11... | collective-permute-start | bytes 2359304 | tf_op jit(solution)/shard_map/ppermute | solution.py:471
  360.0 53.8 %collective-permute-start.77 = (bf16[16,64,768]{2,1,0:T(8,128)(2,1)}, bf16[16,64,768]{2,1,0:T(8,128)(2,1)}, u32[]{:S(2)}, u32[]{:S(2)}) collective-permute-start(bf16[16,64,768]{2,1,0:T(8,128)(2,1)} %get-tuple-element.297), channel_id=1, source_target_pairs={{0,1},{1,0},{2,3},{3,2},{4,5},{5,4},{6,7},{7,6},{8,9},{9,8},{10,11... | collective-permute-start | bytes 4718600 | tf_op jit(solution)/shard_map/ppermute | solution.py:471
  363.7 8.6 %collective-permute-start = (bf16[128,2048]{1,0:T(8,128)(2,1)}, bf16[128,2048]{1,0:T(8,128)(2,1)S(1)}, u32[]{:S(2)}, u32[]{:S(2)}) collective-permute-start(bf16[128,2048]{1,0:T(8,128)(2,1)} %param.5), channel_id=1, source_target_pairs={{0,8},{10,2},{8,16},{18,10},{16,24},{26,18},{24,28},{30,26},{28,20... | collective-permute-start | bytes 1572872 | tf_op jit(solution)/shard_map/cond/branch_1_fun/ppermute | solution.py:400
  365.5 12.5 %collective-permute-start.2 = (bf16[128,2048]{1,0:T(8,128)(2,1)S(1)}, bf16[128,2048]{1,0:T(8,128)(2,1)S(1)}, u32[]{:S(2)}, u32[]{:S(2)}) collective-permute-start(bf16[128,2048]{1,0:T(8,128)(2,1)S(1)} %collective-permute-done.1), channel_id=1, source_target_pairs={{0,8},{10,2},{8,16},{18,10},{16,24},{26,18},{24,28},{30,26},{28,20... | collective-permute-start | bytes 1572872 | tf_op jit(solution)/shard_map/cond/branch_1_fun/ppermute | solution.py:400
  372.4 11.2 %collective-permute-start.3 = (bf16[128,2048]{1,0:T(8,128)(2,1)S(1)}, bf16[128,2048]{1,0:T(8,128)(2,1)S(1)}, u32[]{:S(2)}, u32[]{:S(2)}) collective-permute-start(bf16[128,2048]{1,0:T(8,128)(2,1)S(1)} %collective-permute-done), channel_id=1, source_target_pairs={{0,8},{10,2},{8,16},{18,10},{16,24},{26,18},{24,28},{30,26},{28,20... | collective-permute-start | bytes 1572872 | tf_op jit(solution)/shard_map/cond/branch_1_fun/ppermute | solution.py:400
  378.0 11.2 %collective-permute-start.4 = (bf16[128,2048]{1,0:T(8,128)(2,1)S(1)}, bf16[128,2048]{1,0:T(8,128)(2,1)S(1)}, u32[]{:S(2)}, u32[]{:S(2)}) collective-permute-start(bf16[128,2048]{1,0:T(8,128)(2,1)S(1)} %collective-permute-done.2), channel_id=1, source_target_pairs={{0,8},{10,2},{8,16},{18,10},{16,24},{26,18},{24,28},{30,26},{28,20... | collective-permute-start | bytes 1572872 | tf_op jit(solution)/shard_map/cond/branch_1_fun/ppermute | solution.py:400
  383.6 11.2 %collective-permute-start.5 = (bf16[128,2048]{1,0:T(8,128)(2,1)S(1)}, bf16[128,2048]{1,0:T(8,128)(2,1)S(1)}, u32[]{:S(2)}, u32[]{:S(2)}) collective-permute-start(bf16[128,2048]{1,0:T(8,128)(2,1)S(1)} %collective-permute-done.3), channel_id=1, source_target_pairs={{0,8},{10,2},{8,16},{18,10},{16,24},{26,18},{24,28},{30,26},{28,20... | collective-permute-start | bytes 1572872 | tf_op jit(solution)/shard_map/cond/branch_1_fun/ppermute | solution.py:400
  389.2 11.2 %collective-permute-start.6 = (bf16[128,2048]{1,0:T(8,128)(2,1)S(1)}, bf16[128,2048]{1,0:T(8,128)(2,1)S(1)}, u32[]{:S(2)}, u32[]{:S(2)}) collective-permute-start(bf16[128,2048]{1,0:T(8,128)(2,1)S(1)} %collective-permute-done.4), channel_id=1, source_target_pairs={{0,8},{10,2},{8,16},{18,10},{16,24},{26,18},{24,28},{30,26},{28,20... | collective-permute-start | bytes 1572872 | tf_op jit(solution)/shard_map/cond/branch_1_fun/ppermute | solution.py:400
  394.8 11.2 %collective-permute-start.7 = (bf16[128,2048]{1,0:T(8,128)(2,1)S(1)}, bf16[128,2048]{1,0:T(8,128)(2,1)S(1)}, u32[]{:S(2)}, u32[]{:S(2)}) collective-permute-start(bf16[128,2048]{1,0:T(8,128)(2,1)S(1)} %collective-permute-done.5), channel_id=1, source_target_pairs={{0,8},{10,2},{8,16},{18,10},{16,24},{26,18},{24,28},{30,26},{28,20... | collective-permute-start | bytes 1572872 | tf_op jit(solution)/shard_map/cond/branch_1_fun/ppermute | solution.py:400
  419.0 109.1 %all-to-all-start.3 = ((bf16[16,64,1152]{2,1,0:T(8,128)(2,1)}), bf16[16,64,1152]{2,1,0:T(8,128)(2,1)}, u32[]{:S(2)}, u32[]{:S(2)}) async-start(bf16[16,64,1152]{2,1,0:T(8,128)(2,1)} %pad_maximum_fusion.9), calls=%async_computation.3 | async-start | bytes 4718592 | tf_op jit(solution)/shard_map/all_to_all | solution.py:467
  454.9 25.7 %collective-permute-start.27 = (bf16[128,2048]{1,0:T(8,128)(2,1)}, bf16[128,2048]{1,0:T(8,128)(2,1)S(1)}, u32[]{:S(2)}, u32[]{:S(2)}) collective-permute-start(bf16[128,2048]{1,0:T(8,128)(2,1)} %get-tuple-element.367), channel_id=1, source_target_pairs={{8,0},{2,10},{16,8},{10,18},{24,16},{18,26},{28,24},{26,30},{20,28... | collective-permute-start | bytes 1572872 | tf_op jit(solution)/shard_map/cond/branch_1_fun/ppermute | solution.py:403
  456.0 30.2 %collective-permute-start.29 = (bf16[128,2048]{1,0:T(8,128)(2,1)}, bf16[128,2048]{1,0:T(8,128)(2,1)S(1)}, u32[]{:S(2)}, u32[]{:S(2)}) collective-permute-start(bf16[128,2048]{1,0:T(8,128)(2,1)} %get-tuple-element.368), channel_id=1, source_target_pairs={{8,0},{2,10},{16,8},{10,18},{24,16},{18,26},{28,24},{26,30},{20,28... | collective-permute-start | bytes 1572872 | tf_op jit(solution)/shard_map/cond/branch_1_fun/ppermute | solution.py:403
  481.8 16.6 %collective-permute-start.28 = (bf16[128,2048]{1,0:T(8,128)(2,1)S(1)}, bf16[128,2048]{1,0:T(8,128)(2,1)S(1)}, u32[]{:S(2)}, u32[]{:S(2)}) collective-permute-start(bf16[128,2048]{1,0:T(8,128)(2,1)S(1)} %add_convert_fusion.18), channel_id=1, source_target_pairs={{8,0},{2,10},{16,8},{10,18},{24,16},{18,26},{28,24},{26,30},{20,28... | collective-permute-start | bytes 1572872 | tf_op jit(solution)/shard_map/cond/branch_1_fun/ppermute | solution.py:403
  487.4 14.0 %collective-permute-start.31 = (bf16[128,2048]{1,0:T(8,128)(2,1)S(1)}, bf16[128,2048]{1,0:T(8,128)(2,1)S(1)}, u32[]{:S(2)}, u32[]{:S(2)}) collective-permute-start(bf16[128,2048]{1,0:T(8,128)(2,1)S(1)} %add_convert_fusion.17), channel_id=1, source_target_pairs={{8,0},{2,10},{16,8},{10,18},{24,16},{18,26},{28,24},{26,30},{20,28... | collective-permute-start | bytes 1572872 | tf_op jit(solution)/shard_map/cond/branch_1_fun/ppermute | solution.py:403
  498.3 18.1 %collective-permute-start.32 = (bf16[2048,384]{0,1:T(8,128)(2,1)S(1)}, bf16[2048,384]{0,1:T(8,128)(2,1)S(1)}, u32[]{:S(2)}, u32[]{:S(2)}) collective-permute-start(bf16[2048,384]{0,1:T(8,128)(2,1)S(1)} %pad_maximum_fusion.1), channel_id=1, source_target_pairs={{0,2},{2,0},{4,6},{6,4},{8,10},{10,8},{12,14},{14,12},{16,18},{18,... | collective-permute-start | bytes 4718600 | tf_op jit(solution)/shard_map/cond/branch_1_fun/ppermute | solution.py:397
  502.6 11.2 %collective-permute-start.34 = (bf16[128,2048]{1,0:T(8,128)(2,1)S(1)}, bf16[128,2048]{1,0:T(8,128)(2,1)S(1)}, u32[]{:S(2)}, u32[]{:S(2)}) collective-permute-start(bf16[128,2048]{1,0:T(8,128)(2,1)S(1)} %add_convert_fusion.15), channel_id=1, source_target_pairs={{8,0},{2,10},{16,8},{10,18},{24,16},{18,26},{28,24},{26,30},{20,28... | collective-permute-start | bytes 1572872 | tf_op jit(solution)/shard_map/cond/branch_1_fun/ppermute | solution.py:403
  535.4 8.6 %collective-permute-start.36 = (bf16[128,2048]{1,0:T(8,128)(2,1)}, bf16[128,2048]{1,0:T(8,128)(2,1)}, u32[]{:S(2)}, u32[]{:S(2)}) collective-permute-start(bf16[128,2048]{1,0:T(8,128)(2,1)} %get-tuple-element.377), channel_id=1, source_target_pairs={{8,0},{2,10},{16,8},{10,18},{24,16},{18,26},{28,24},{26,30},{20,28... | collective-permute-start | bytes 1572872 | tf_op jit(solution)/shard_map/cond/branch_1_fun/ppermute | solution.py:403
  536.5 13.2 %collective-permute-start.38 = (bf16[128,2048]{1,0:T(8,128)(2,1)}, bf16[128,2048]{1,0:T(8,128)(2,1)}, u32[]{:S(2)}, u32[]{:S(2)}) collective-permute-start(bf16[128,2048]{1,0:T(8,128)(2,1)} %get-tuple-element.378), channel_id=1, source_target_pairs={{8,0},{2,10},{16,8},{10,18},{24,16},{18,26},{28,24},{26,30},{20,28... | collective-permute-start | bytes 1572872 | tf_op jit(solution)/shard_map/cond/branch_1_fun/ppermute | solution.py:403
  538.8 20.1 %collective-permute-start.39 = (bf16[1040,384]{1,0:T(8,128)(2,1)S(1)}, bf16[1040,384]{1,0:T(8,128)(2,1)S(1)}, u32[]{:S(2)}, u32[]{:S(2)}) collective-permute-start(bf16[1040,384]{1,0:T(8,128)(2,1)S(1)} %pad_maximum_fusion.3), channel_id=1, source_target_pairs={{0,1},{1,0},{2,3},{3,2},{4,5},{5,4},{6,7},{7,6},{8,9},{9,8},{10,11... | collective-permute-start | bytes 2396168 | tf_op jit(solution)/shard_map/cond/branch_1_fun/ppermute | solution.py:471
  547.8 18.6 %collective-permute-start.37 = (bf16[128,2048]{1,0:T(8,128)(2,1)}, bf16[128,2048]{1,0:T(8,128)(2,1)}, u32[]{:S(2)}, u32[]{:S(2)}) collective-permute-start(bf16[128,2048]{1,0:T(8,128)(2,1)} %add_convert_fusion.23), channel_id=1, source_target_pairs={{8,0},{2,10},{16,8},{10,18},{24,16},{18,26},{28,24},{26,30},{20,28... | collective-permute-start | bytes 1572872 | tf_op jit(solution)/shard_map/cond/branch_1_fun/ppermute | solution.py:403
  551.8 17.1 %collective-permute-start.41 = (bf16[128,2048]{1,0:T(8,128)(2,1)}, bf16[128,2048]{1,0:T(8,128)(2,1)}, u32[]{:S(2)}, u32[]{:S(2)}) collective-permute-start(bf16[128,2048]{1,0:T(8,128)(2,1)} %add_convert_fusion.22), channel_id=1, source_target_pairs={{8,0},{2,10},{16,8},{10,18},{24,16},{18,26},{28,24},{26,30},{20,28... | collective-permute-start | bytes 1572872 | tf_op jit(solution)/shard_map/cond/branch_1_fun/ppermute | solution.py:403
  560.5 42.4 %all-to-all-start = ((bf16[16,80,384]{2,1,0:T(8,128)(2,1)}), bf16[16,80,384]{2,1,0:T(8,128)(2,1)}, u32[]{:S(2)}, u32[]{:S(2)}) async-start(bf16[16,80,384]{2,1,0:T(8,128)(2,1)} %pad_maximum_fusion.2), calls=%async_computation | async-start | bytes 1966080 | tf_op jit(solution)/shard_map/cond/branch_1_fun/all_to_all | solution.py:467
  567.7 26.2 %collective-permute-start.40 = (bf16[128,2048]{1,0:T(8,128)(2,1)S(1)}, bf16[128,2048]{1,0:T(8,128)(2,1)S(1)}, u32[]{:S(2)}, u32[]{:S(2)}) collective-permute-start(bf16[128,2048]{1,0:T(8,128)(2,1)S(1)} %add_convert_fusion.21), channel_id=1, source_target_pairs={{8,0},{2,10},{16,8},{10,18},{24,16},{18,26},{28,24},{26,30},{20,28... | collective-permute-start | bytes 1572872 | tf_op jit(solution)/shard_map/cond/branch_1_fun/ppermute | solution.py:403
  570.3 29.2 %collective-permute-start.43 = (bf16[128,2048]{1,0:T(8,128)(2,1)S(1)}, bf16[128,2048]{1,0:T(8,128)(2,1)S(1)}, u32[]{:S(2)}, u32[]{:S(2)}) collective-permute-start(bf16[128,2048]{1,0:T(8,128)(2,1)S(1)} %add_convert_fusion.20), channel_id=1, source_target_pairs={{8,0},{2,10},{16,8},{10,18},{24,16},{18,26},{28,24},{26,30},{20,28... | collective-permute-start | bytes 1572872 | tf_op jit(solution)/shard_map/cond/branch_1_fun/ppermute | solution.py:403
  (83 other events, 824.9 us)

commit v4 on v3

--- a/solution.py
+++ b/solution.py
@@ -219,7 +219,7 @@
                 pltpu.VMEM((queries, head), bf16),
             ],
         ),
-        compiler_params=pltpu.CompilerParams(vmem_limit_bytes=48 * 2**20),
+        compiler_params=pltpu.CompilerParams(vmem_limit_bytes=(12 << 20) + 5120 * keys),
         cost_estimate=pl.CostEstimate(
             flops=4 * queries * keys * head, bytes_accessed=28 * keys * head, transcendentals=queries * keys
         ),
@@ -339,7 +339,9 @@
                 pltpu.VMEM((keys, head), f32),
             ],
         ),
-        compiler_params=pltpu.CompilerParams(vmem_limit_bytes=60 * 2**20),
+        compiler_params=pltpu.CompilerParams(
+            vmem_limit_bytes=min(60 << 20, (16 << 20) + 7168 * keys)
+        ),
         cost_estimate=pl.CostEstimate(
             flops=10 * queries * keys * head, bytes_accessed=40 * keys * head, transcendentals=queries * keys
         ),
@@ -372,7 +374,9 @@
         in_specs=[whole_spec(weight.shape), whole_spec((1, width))]
         + [whole_spec((rows, width))] * len(blocks),
         out_specs=(whole_spec((total, width)), whole_spec((total, columns))),
-        compiler_params=pltpu.CompilerParams(vmem_limit_bytes=48 * 2**20),
+        compiler_params=pltpu.CompilerParams(
+            vmem_limit_bytes=(12 << 20) + 12 * total * width
+        ),
         cost_estimate=pl.CostEstimate(
             flops=2 * total * width * columns, bytes_accessed=4 * total * width, transcendentals=total
         ),
@@ -741,9 +745,21 @@
     grad32 = cotangent[0].astype(f32)
     hidden_grad = grad32 + norm_back(hidden_one, scale_mlp, mlp_gain, normed_mlp_grad)
     hidden_grad_bf = hidden_grad.astype(bf16)
+    down_own, gate_up_own = lax.optimization_barrier((down_own, gate_up_own))
     down_other, gate_up_other = swap_rows(down_away), swap_rows(gate_up_away)
 
-    grad_all = fenced(lambda block: jnp.concatenate(ring.gather(block), axis=0), hidden_grad_bf)
+
+    def gather_grads(block, activated_all, down_part):
+        ready = {}
+
+        def output_terms(blocks):
+            ready["out"] = dot_nt(after(activated_all, blocks[2]), down_part).astype(bf16)
+            return ready["out"]
+
+        blocks = ring.gather(block, {last_hop - 1: output_terms})
+        return jnp.concatenate(blocks, axis=0), ready["out"]
+
+    grad_all, out_terms = fenced(gather_grads, hidden_grad_bf, activated_all, down_part)
     attn_grad_pair = dot_nn(grad_all, output_part).astype(bf16)
     attn_grad = (attn_grad_pair[:, :head_size], ring.swap(attn_grad_pair[:, head_size:]))
     mlp_sent = jnp.concatenate(
@@ -801,9 +817,8 @@
     )
     gains = jnp.concatenate([attn_gain_part, query_gain_part, key_gain_part, mlp_gain_part])
 
-    def out_and_home(activated_all, down_part, attn_grads, gains, mlp_rows, summed_grad, hidden_grad, inputs32):
+    def out_and_home(out_terms, attn_grads, gains, mlp_rows, summed_grad, hidden_grad, inputs32):
         own, away, lines = halves(attn_grads, gains, fsdp_rank, ctx_size)
-        out_terms = dot_nt(activated_all, down_part).astype(bf16)
         ready = {}
 
         def other_rows(_):
@@ -811,11 +826,12 @@
             return ready["other"]
 
         def rows_home(_):
-            ready["rows"] = spread(join(own, ready["other"], lines))
-            return ready["rows"]
+            sent = join(own, ready["other"], lines)
+            ready["rows"] = spread(sent)
+            return sent
 
         def unpack(marks):
-            rows = after(mlp_rows, marks[1])
+            rows = after(mlp_rows, marks[4])
             ready["mlp"] = tuple(
                 side_by_side(rows[:, :, i * hidden_slice : (i + 1) * hidden_slice]).astype(f32)
                 for i in range(3)
@@ -824,19 +840,21 @@
 
         def finish(marks):
             ready["input"] = hidden_grad + norm_back(
-                inputs32, inv_root(inputs32), attn_gain, after(summed_grad, marks[0])
+                inputs32, inv_root(inputs32), attn_gain, after(summed_grad, marks[3])
             )
             return ready["input"]
 
-        summed, _ = ring.scatter_sum(
+        summed, marks = ring.scatter_sum(
             lambda i: block_rows(out_terms, i),
-            {2: finish, last_hop - 2: other_rows, last_hop - 1: unpack, last_hop: rows_home},
-        )
+            {4: other_rows, 5: rows_home},
+        )
+        finish(marks)
+        unpack(marks)
         return summed, ready["rows"], ready["input"], ready["mlp"]
 
     attn_grads, mlp_rows = lax.optimization_barrier((attn_grads, mlp_rows))
     mlp_out, attn_home, input_grad, mlp_grads = fenced(
-        out_and_home, activated_all, down_part, attn_grads, gains, mlp_rows, normed_attn_grad,
+        out_and_home, out_terms, attn_grads, gains, mlp_rows, normed_attn_grad,
         hidden_grad, inputs32,
     )
     block_out = (hidden_one + mlp_out).astype(bf16)

time: 632 us -> 625 us (0.989)
  local copies, waits for them, and re-layouts: 41.1 us -> 56 us
  other arithmetic: 86.3 us -> 76.4 us
    unnamed x116 -> x122, local copies, waits for them, and re-layouts: 11.1 us -> 21.2 us
    ppermute x28, waiting for transfers between devices: 137 us -> 129 us  [out(): return lax.ppermute(field, 'ctx', self.out_pairs)]
  transfers between devices with their start and end apart: 82 -> 82, of which waited for: 57 -> 53; matrix products, arithmetic and copies ran while one was open for 22% -> 22% of each run, Pallas kernels for 5% -> 5%
where the time goes in v4:
time: 625 us; the launch traced here: 618 us
  waiting for transfers between devices  304 us (49%)
  starting transfers between devices  86.6 us (14%)
  other arithmetic  76.4 us (12%)
  matrix products  61.3 us (10%)
  local copies, waits for them, and re-layouts  56 us (9%)
  Pallas kernels  30.2 us (5%)
    ppermute x28, waiting for transfers between devices, out(): return lax.ppermute(field, 'ctx', self.out_pairs)  129 us
    ppermute x28, waiting for transfers between devices, home(): return lax.ppermute(field, 'ctx', self.home_pairs)  123 us
    ppermute x28, starting transfers between devices, home(): return lax.ppermute(field, 'ctx', self.home_pairs)  40.5 us
    all_to_all x4, waiting for transfers between devices, spread(): lax.all_to_all(rows_block, 'ctx', split_axis=0, concat_axis=0, tiled=False)  26.6 us
    dot_general x6, matrix products, dot_tn(): lax.dot_general(left, right, (((0,), (0,)), ((), ())), preferred_element_...  25.5 us
    all_to_all x4, starting transfers between devices, spread(): lax.all_to_all(rows_block, 'ctx', split_axis=0, concat_axis=0, tiled=False)  22.9 us
    unnamed x122, local copies, waits for them, and re-layouts  21.2 us
    dot_general x5, matrix products, dot_nt(): lax.dot_general(left, right, (((1,), (1,)), ((), ())), preferred_element_...  18.8 us
  transfers between devices with their start and end apart: 82, of which 53 were waited for; matrix products, arithmetic and copies ran while one was open for 22% of the time, Pallas kernels for 5%

profile of v4, /device:TPU:9, one launch (start us, length us, event | category | flops | bytes accessed | tf_op | source)
XLA Modules:
  0.0 618.3 jit_solution(15682928243239555375)
XLA Ops:
  6.0 6.6 %all-to-all-start.1 = ((bf16[16,64,384]{2,1,0:T(8,128)(2,1)}), bf16[16,64,384]{2,1,0:T(8,128)(2,1)}, u32[]{:S(2)}, u32[]{:S(2)}) async-start(bf16[16,64,384]{2,1,0:T(8,128)(2,1)} %pad_maximum_fusion.18), calls=%async_computation.1 | async-start | bytes 1572864 | tf_op jit(solution)/shard_map/all_to_all | solution.py:471
  14.7 23.1 %collective-permute-done.47.refs_1_ = bf16[128,2048]{1,0:T(8,128)(2,1)S(1)} collective-permute-done((bf16[128,2048]{1,0:T(8,128)(2,1)S(1)}, bf16[128,2048]{1,0:T(8,128)(2,1)S(1)}, u32[]{:S(2)}, u32[]{:S(2)}) %collective-permute-start.47) | collective-permute-done | bytes 524320 | tf_op jit(solution)/shard_map/ppermute | solution.py:404
  37.8 5.6 collective-permute-done.49.refs_2_
  43.4 5.6 collective-permute-done.50.refs_3_
  50.4 3.7 fusion.29
  56.6 3.7 collective-permute-done.52.refs_5_
  60.3 7.1 %collective-permute-done.45 = bf16[16,64,384]{2,1,0:T(8,128)(2,1)S(1)} collective-permute-done((bf16[16,64,384]{2,1,0:T(8,128)(2,1)}, bf16[16,64,384]{2,1,0:T(8,128)(2,1)S(1)}, u32[]{:S(2)}, u32[]{:S(2)}) %collective-permute-start.45) | collective-permute-done | bytes 786464 | tf_op jit(solution)/shard_map/ppermute | solution.py:475
  75.2 4.6 all-to-all-start.2
  84.2 4.6 project.1
  93.8 10.6 %attend.1 = (bf16[1024,128]{1,0:T(8,128)(2,1)S(1)}, bf16[1024,128]{1,0:T(8,128)(2,1)S(1)}, f32[1,2048]{1,0:T(1,128)S(1)}, bf16[2048,128]{1,0:T(8,128)(2,1)}, bf1...) custom-call(s32[32]{0:T(128)S(1)} %select_reduce_fusion.key_pos, s32[32]{0:T(128)S(1)} %iota.30.query_table.pos_table, ...), custom_call_target="tpu_custom_call" | custom-call | flops 2147483648 | bytes 7340032 | tf_op jit(solution)/shard_map/attend/pallas_call | solution.py:200
  104.4 26.6 %all-to-all-done.2 = bf16[16,64,1152]{2,1,0:T(8,128)(2,1)} async-done(((bf16[16,64,1152]{2,1,0:T(8,128)(2,1)}), bf16[16,64,1152]{2,1,0:T(8,128)(2,1)}, u32[]{:S(2)}, u32[]{:S(2)}) %all-to-all-start.2) | async-done | bytes 2359328 | tf_op jit(solution)/shard_map/all_to_all | solution.py:471
  134.5 3.3 convolution_convert_fusion.9
  137.8 49.5 %conditional.6 = (f32[128,2048]{1,0:T(8,128)S(1)}) conditional(s32[]{:T(128)} %convert_element_type.453, () %tuple.124, bf16[1024,2048]{1,0:T(8,128)(2,1)} %convolution_convert_fusion.9), branch_computations={%region_3.4_spmd, %region_4.5_spmd} | conditional | flops 6553600 | bytes 46137700 | solution.py:561
  139.3 3.4 collective-permute-start
  142.7 6.1 collective-permute-done
  171.4 5.5 collective-permute-done.6
  180.1 6.6 %collective-permute-done.5 = bf16[128,2048]{1,0:T(8,128)(2,1)S(1)} collective-permute-done((bf16[128,2048]{1,0:T(8,128)(2,1)S(1)}, bf16[128,2048]{1,0:T(8,128)(2,1)S(1)}, u32[]{:S(2)}, u32[]{:S(2)}) %collective-permute-start.5) | collective-permute-done | bytes 524320 | tf_op jit(solution)/shard_map/cond/branch_1_fun/ppermute | solution.py:407
  192.1 7.7 %collective-permute-done.57 = bf16[128,2048]{1,0:T(8,128)(2,1)S(1)} collective-permute-done((bf16[128,2048]{1,0:T(8,128)(2,1)S(1)}, bf16[128,2048]{1,0:T(8,128)(2,1)S(1)}, u32[]{:S(2)}, u32[]{:S(2)}) %collective-permute-start.57) | collective-permute-done | bytes 524320 | tf_op jit(solution)/shard_map/ppermute | solution.py:401
  200.7 7.7 %collective-permute-done.58 = bf16[128,2048]{1,0:T(8,128)(2,1)S(1)} collective-permute-done((bf16[128,2048]{1,0:T(8,128)(2,1)S(1)}, bf16[128,2048]{1,0:T(8,128)(2,1)S(1)}, u32[]{:S(2)}, u32[]{:S(2)}) %collective-permute-start.58) | collective-permute-done | bytes 524320 | tf_op jit(solution)/shard_map/ppermute | solution.py:404
  208.4 5.6 collective-permute-done.61
  214.0 5.6 collective-permute-done.60
  219.8 5.5 collective-permute-done.71
  225.3 5.6 collective-permute-done.62
  236.6 5.6 collective-permute-done.63
  243.0 4.7 collective-permute-done.65
  252.2 3.1 pad_maximum_fusion.4
  257.2 3.6 copy-done.13
  260.8 3.4 fusion.8
  265.5 3.4 fusion.16
  273.5 4.8 collective-permute-done.70
  280.1 3.7 collective-permute-done.73
  284.7 4.7 collective-permute-done.74
  290.3 5.2 fusion.46
  300.3 60.9 %conditional.7 = (f32[128,2048]{1,0:T(8,128)S(1)}, bf16[2048]{0:T(1024)(128)(2,1)S(1)}, bf16[16,64,384]{2,1,0:T(8,128)(2,1)}, bf16[16,64,384]{2,1,0:T(8,128)(2,1...) conditional(s32[]{:T(128)} %convert_element_type.453, () %tuple.134, ...), branch_computations={%region_6.7_spmd, %region_7.10_spmd} | conditional | flops 13722978304 | bytes 186036880 | solution.py:561
  302.8 5.6 convolution_convert_fusion.2
  313.9 4.7 fusion.2
  321.7 3.9 fusion
  329.9 4.7 fusion.3
  336.3 3.9 fusion.1
  345.5 8.8 %collective-permute-done.23 = bf16[128,2048]{1,0:T(8,128)(2,1)S(1)} collective-permute-done((bf16[128,2048]{1,0:T(8,128)(2,1)S(1)}, bf16[128,2048]{1,0:T(8,128)(2,1)S(1)}, u32[]{:S(2)}, u32[]{:S(2)}) %collective-permute-start.23) | collective-permute-done | bytes 524320 | tf_op jit(solution)/shard_map/cond/branch_1_fun/ppermute | solution.py:407
  366.0 44.1 %conditional.8 = (bf16[1024,2048]{1,0:T(8,128)(2,1)}, bf16[1024,2048]{1,0:T(8,128)(2,1)S(1)}) conditional(s32[]{:T(128)} %convert_element_type.453, () %tuple.133, (bf16[128,2048]{1,0:T(8,128)(2,1)S(1)}, bf16[1024,768]{1,0:T(8,128)(2,1)S(1)}, bf16[2048,768]{1,0:T(8,128)(2,1)S(1)}) %tuple.222), branch_computations={%region_11.12_spmd, %region_12.13_spmd} | conditional | flops 3223322624 | bytes 34079056 | solution.py:561
  368.8 6.7 %collective-permute-done.27 = bf16[128,2048]{1,0:T(8,128)(2,1)S(1)} collective-permute-done((bf16[128,2048]{1,0:T(8,128)(2,1)S(1)}, bf16[128,2048]{1,0:T(8,128)(2,1)S(1)}, u32[]{:S(2)}, u32[]{:S(2)}) %collective-permute-start.27) | collective-permute-done | bytes 524320 | tf_op jit(solution)/shard_map/cond/branch_1_fun/ppermute | solution.py:404
  377.4 3.8 collective-permute-done.29
  381.3 5.5 collective-permute-done.30
  386.9 3.7 convolution_convert_fusion.5
  393.4 4.6 collective-permute-done.32
  399.9 3.8 collective-permute-done.33
  404.4 4.8 collective-permute-done.34
  410.1 4.9 convolution_convert_fusion.11
  422.8 4.9 all-to-all-start.3
  428.8 22.4 %conditional.9 = (bf16[1024,512]{1,0:T(8,128)(2,1)}, bf16[1024,2048]{1,0:T(8,128)(2,1)S(1)}, f32[128]{0:T(128)S(1)}, f32[128]{0:T(128)S(1)}) conditional(s32[]{:T(128)} %convert_element_type.453, () %tuple.154, (s32[32]{0:T(128)S(1)}, s32[32]{0:T(128)S(1)}, s32[32]{0:T(128)S(1)}, f32[1024,512]{1,0:T(8,128)}, f32[1024,384]{1,0:T(8,128)}, ...), branch_computations={%region_13.14_spmd, %region_14.15_spmd} | conditional | flops 7522484224 | bytes 34078820 | solution.py:561
  429.0 15.0 %attend_back.1 = (bf16[1024,384]{1,0:T(8,128)(2,1)S(1)}, bf16[1024,384]{1,0:T(8,128)(2,1)S(1)}, f32[1,128]{1,0:T(1,128)S(1)}, f32[1,128]{1,0:T(1,128)S(1)}) custom-call(s32[32]{0:T(128)S(1)} %get-tuple-element.134.key_pos, s32[32]{0:T(128)S(1)} %get-tuple-element.136.pos_table, s32[32]{0:T(128)S(1)} %get-tuple-element.136.pos_table, ...), custom_call_target="tpu_custom_call" | custom-call | flops 5368709120 | bytes 10485760 | tf_op jit(solution)/shard_map/cond/branch_1_fun/attend_back/pallas_call | solution.py:315
  447.5 3.6 convolution_convert_fusion.6
  451.2 78.9 %conditional.10 = (f32[128,2048]{1,0:T(8,128)S(1)}, bf16[2048,384]{0,1:T(8,128)(2,1)}, bf16[2048]{0:T(1024)(128)(2,1)S(1)}) conditional(s32[]{:T(128)} %convert_element_type.453, () %tuple.153, (bf16[1024,2048]{1,0:T(8,128)(2,1)S(1)}, bf16[1024,512]{1,0:T(8,128)(2,1)}, bf16[1024,256]{1,0:T(8,128)(2,1)S(1)}, bf16[1024,2048]{1,0:T(8,128)(2,1)}, ...), branch_computations={%region_15.16_spmd, %region_16.18_spmd} | conditional | flops 3250061312 | bytes 121663968 | solution.py:561
  456.6 28.3 %collective-permute-done.36 = bf16[128,2048]{1,0:T(8,128)(2,1)S(1)} collective-permute-done((bf16[128,2048]{1,0:T(8,128)(2,1)}, bf16[128,2048]{1,0:T(8,128)(2,1)S(1)}, u32[]{:S(2)}, u32[]{:S(2)}) %collective-permute-start.36) | collective-permute-done | bytes 524320 | tf_op jit(solution)/shard_map/cond/branch_1_fun/ppermute | solution.py:407
  493.8 4.9 fusion.5
  498.7 3.5 fusion.6
  507.7 5.2 collective-permute-done.39
  512.9 5.6 collective-permute-done.43
  523.0 6.6 %collective-permute-done.42 = bf16[128,2048]{1,0:T(8,128)(2,1)S(1)} collective-permute-done((bf16[128,2048]{1,0:T(8,128)(2,1)S(1)}, bf16[128,2048]{1,0:T(8,128)(2,1)S(1)}, u32[]{:S(2)}, u32[]{:S(2)}) %collective-permute-start.42) | collective-permute-done | bytes 524320 | tf_op jit(solution)/shard_map/cond/branch_1_fun/ppermute | solution.py:407
  530.1 78.9 %conditional.11 = (f32[128,2048]{1,0:T(8,128)}, bf16[16,80,384]{2,1,0:T(8,128)(2,1)}, f32[64,6144]{1,0:T(8,128)}, f32[64,6144]{1,0:T(8,128)}, f32[64,6144]{1,0:T(8,128)}, /*index=5*/f32[1,128,2048]{2,1,0:T(8,128)}) conditional(s32[]{:T(128)} %convert_element_type.453, () %tuple.132, (bf16[1024,2048]{1,0:T(8,128)(2,1)}, s32[]{:T(128)}, ...), branch_computations={%region_18.19_spmd, %region_19.22_spmd} | conditional | flops 16564609 | bytes 89188408 | solution.py:561
  537.0 10.1 %collective-permute-done.8 = bf16[128,2048]{1,0:T(8,128)(2,1)} collective-permute-done((bf16[128,2048]{1,0:T(8,128)(2,1)}, bf16[128,2048]{1,0:T(8,128)(2,1)}, u32[]{:S(2)}, u32[]{:S(2)}) %collective-permute-start.8) | collective-permute-done | bytes 524320 | tf_op jit(solution)/shard_map/cond/branch_1_fun/ppermute | solution.py:407
  557.2 6.9 %all-to-all-start = ((bf16[16,80,384]{2,1,0:T(8,128)(2,1)}), bf16[16,80,384]{2,1,0:T(8,128)(2,1)}, u32[]{:S(2)}, u32[]{:S(2)}) async-start(bf16[16,80,384]{2,1,0:T(8,128)(2,1)} %pad_maximum_fusion.2), calls=%async_computation | async-start | bytes 1966080 | tf_op jit(solution)/shard_map/cond/branch_1_fun/all_to_all | solution.py:471
  569.7 21.9 %collective-permute-done.12 = bf16[128,2048]{1,0:T(8,128)(2,1)S(1)} collective-permute-done((bf16[128,2048]{1,0:T(8,128)(2,1)S(1)}, bf16[128,2048]{1,0:T(8,128)(2,1)S(1)}, u32[]{:S(2)}, u32[]{:S(2)}) %collective-permute-start.12) | collective-permute-done | bytes 524320 | tf_op jit(solution)/shard_map/cond/branch_1_fun/ppermute | solution.py:407
  (419 shorter events, 221.8 us)
Async XLA Ops:
  6.0 43.0 %all-to-all-start.1 = ((bf16[16,64,384]{2,1,0:T(8,128)(2,1)}), bf16[16,64,384]{2,1,0:T(8,128)(2,1)}, u32[]{:S(2)}, u32[]{:S(2)}) async-start(bf16[16,64,384]{2,1,0:T(8,128)(2,1)} %pad_maximum_fusion.18), calls=%async_computation.1 | async-start | bytes 1572864 | tf_op jit(solution)/shard_map/all_to_all | solution.py:471
  13.0 24.8 %collective-permute-start.47 = (bf16[128,2048]{1,0:T(8,128)(2,1)S(1)}, bf16[128,2048]{1,0:T(8,128)(2,1)S(1)}, u32[]{:S(2)}, u32[]{:S(2)}) collective-permute-start(bf16[128,2048]{1,0:T(8,128)(2,1)S(1)} %bitcast.191), channel_id=1, source_target_pairs={{0,8},{10,2},{8,16},{18,10},{16,24},{26,18},{24,28},{30,26},{28,20... | collective-permute-start | bytes 1572872 | tf_op jit(solution)/shard_map/ppermute | solution.py:404
  14.6 28.8 %collective-permute-start.49 = (bf16[128,2048]{1,0:T(8,128)(2,1)S(1)}, bf16[128,2048]{1,0:T(8,128)(2,1)S(1)}, u32[]{:S(2)}, u32[]{:S(2)}) collective-permute-start(bf16[128,2048]{1,0:T(8,128)(2,1)S(1)} %collective-permute-done.48), channel_id=1, source_target_pairs={{0,8},{10,2},{8,16},{18,10},{16,24},{26,18},{24,28},{30,26},{28,20... | collective-permute-start | bytes 1572872 | tf_op jit(solution)/shard_map/ppermute | solution.py:404
  37.8 11.2 %collective-permute-start.50 = (bf16[128,2048]{1,0:T(8,128)(2,1)S(1)}, bf16[128,2048]{1,0:T(8,128)(2,1)S(1)}, u32[]{:S(2)}, u32[]{:S(2)}) collective-permute-start(bf16[128,2048]{1,0:T(8,128)(2,1)S(1)} %collective-permute-done.47.refs_1_), channel_id=1, source_target_pairs={{0,8},{10,2},{8,16},{18,10},{16,24},{26,18},{24,28},{30,26},{28,20... | collective-permute-start | bytes 1572872 | tf_op jit(solution)/shard_map/ppermute | solution.py:404
  43.4 13.1 %collective-permute-start.51 = (bf16[128,2048]{1,0:T(8,128)(2,1)S(1)}, bf16[128,2048]{1,0:T(8,128)(2,1)S(1)}, u32[]{:S(2)}, u32[]{:S(2)}) collective-permute-start(bf16[128,2048]{1,0:T(8,128)(2,1)S(1)} %collective-permute-done.49.refs_2_), channel_id=1, source_target_pairs={{0,8},{10,2},{8,16},{18,10},{16,24},{26,18},{24,28},{30,26},{28,20... | collective-permute-start | bytes 1572872 | tf_op jit(solution)/shard_map/ppermute | solution.py:404
  49.0 11.2 %collective-permute-start.52 = (bf16[128,2048]{1,0:T(8,128)(2,1)S(1)}, bf16[128,2048]{1,0:T(8,128)(2,1)S(1)}, u32[]{:S(2)}, u32[]{:S(2)}) collective-permute-start(bf16[128,2048]{1,0:T(8,128)(2,1)S(1)} %collective-permute-done.50.refs_3_), channel_id=1, source_target_pairs={{0,8},{10,2},{8,16},{18,10},{16,24},{26,18},{24,28},{30,26},{28,20... | collective-permute-start | bytes 1572872 | tf_op jit(solution)/shard_map/ppermute | solution.py:404
  49.1 18.3 %collective-permute-start.45 = (bf16[16,64,384]{2,1,0:T(8,128)(2,1)}, bf16[16,64,384]{2,1,0:T(8,128)(2,1)S(1)}, u32[]{:S(2)}, u32[]{:S(2)}) collective-permute-start(bf16[16,64,384]{2,1,0:T(8,128)(2,1)} %all-to-all-done.1), channel_id=1, source_target_pairs={{0,1},{1,0},{2,3},{3,2},{4,5},{5,4},{6,7},{7,6},{8,9},{9,8},{10,11... | collective-permute-start | bytes 2359304 | tf_op jit(solution)/shard_map/ppermute | solution.py:475
  56.5 17.1 %collective-permute-start.53 = (bf16[128,2048]{1,0:T(8,128)(2,1)S(1)}, bf16[128,2048]{1,0:T(8,128)(2,1)S(1)}, u32[]{:S(2)}, u32[]{:S(2)}) collective-permute-start(bf16[128,2048]{1,0:T(8,128)(2,1)S(1)} %collective-permute-done.51.refs_4_), channel_id=1, source_target_pairs={{0,8},{10,2},{8,16},{18,10},{16,24},{26,18},{24,28},{30,26},{28,20... | collective-permute-start | bytes 1572872 | tf_op jit(solution)/shard_map/ppermute | solution.py:404
  60.3 14.2 %collective-permute-start.54 = (bf16[128,2048]{1,0:T(8,128)(2,1)S(1)}, bf16[128,2048]{1,0:T(8,128)(2,1)S(1)}, u32[]{:S(2)}, u32[]{:S(2)}) collective-permute-start(bf16[128,2048]{1,0:T(8,128)(2,1)S(1)} %collective-permute-done.52.refs_5_), channel_id=1, source_target_pairs={{0,8},{10,2},{8,16},{18,10},{16,24},{26,18},{24,28},{30,26},{28,20... | collective-permute-start | bytes 1572872 | tf_op jit(solution)/shard_map/ppermute | solution.py:404
  70.0 9.8 %collective-permute-start.46 = (bf16[2048,384]{1,0:T(8,128)(2,1)}, bf16[2048,384]{1,0:T(8,128)(2,1)}, u32[]{:S(2)}, u32[]{:S(2)}) collective-permute-start(bf16[2048,384]{1,0:T(8,128)(2,1)} %bitcast.32), channel_id=1, source_target_pairs={{0,2},{2,0},{4,6},{6,4},{8,10},{10,8},{12,14},{14,12},{16,18},{18,... | collective-permute-start | bytes 4718600 | tf_op jit(solution)/shard_map/ppermute | solution.py:401
  75.2 55.8 %all-to-all-start.2 = ((bf16[16,64,1152]{2,1,0:T(8,128)(2,1)}), bf16[16,64,1152]{2,1,0:T(8,128)(2,1)}, u32[]{:S(2)}, u32[]{:S(2)}) async-start(bf16[16,64,1152]{2,1,0:T(8,128)(2,1)} %pad_maximum_fusion.8), calls=%async_computation.2 | async-start | bytes 4718592 | tf_op jit(solution)/shard_map/all_to_all | solution.py:471
  131.0 56.2 %collective-permute-start.66 = (bf16[16,64,1152]{2,1,0:T(8,128)(2,1)}, bf16[16,64,1152]{2,1,0:T(8,128)(2,1)}, u32[]{:S(2)}, u32[]{:S(2)}) collective-permute-start(bf16[16,64,1152]{2,1,0:T(8,128)(2,1)} %all-to-all-done.2), channel_id=1, source_target_pairs={{0,1},{1,0},{2,3},{3,2},{4,5},{5,4},{6,7},{7,6},{8,9},{9,8},{10,11... | collective-permute-start | bytes 7077896 | tf_op jit(solution)/shard_map/ppermute | solution.py:475
  139.3 9.5 %collective-permute-start = (bf16[128,2048]{1,0:T(8,128)(2,1)S(1)}, bf16[128,2048]{1,0:T(8,128)(2,1)S(1)}, u32[]{:S(2)}, u32[]{:S(2)}) collective-permute-start(bf16[128,2048]{1,0:T(8,128)(2,1)S(1)} %get-tuple-element.362), channel_id=1, source_target_pairs={{8,0},{2,10},{16,8},{10,18},{24,16},{18,26},{28,24},{26,30},{20,28... | collective-permute-start | bytes 1572872 | tf_op jit(solution)/shard_map/cond/branch_1_fun/ppermute | solution.py:407
  142.6 11.7 %collective-permute-start.2 = (bf16[128,2048]{1,0:T(8,128)(2,1)S(1)}, bf16[128,2048]{1,0:T(8,128)(2,1)S(1)}, u32[]{:S(2)}, u32[]{:S(2)}) collective-permute-start(bf16[128,2048]{1,0:T(8,128)(2,1)S(1)} %get-tuple-element.363), channel_id=1, source_target_pairs={{8,0},{2,10},{16,8},{10,18},{24,16},{18,26},{28,24},{26,30},{20,28... | collective-permute-start | bytes 1572872 | tf_op jit(solution)/shard_map/cond/branch_1_fun/ppermute | solution.py:407
  149.9 10.1 %collective-permute-start.1 = (bf16[128,2048]{1,0:T(8,128)(2,1)S(1)}, bf16[128,2048]{1,0:T(8,128)(2,1)S(1)}, u32[]{:S(2)}, u32[]{:S(2)}) collective-permute-start(bf16[128,2048]{1,0:T(8,128)(2,1)S(1)} %add_convert_fusion.4), channel_id=1, source_target_pairs={{8,0},{2,10},{16,8},{10,18},{24,16},{18,26},{28,24},{26,30},{20,28... | collective-permute-start | bytes 1572872 | tf_op jit(solution)/shard_map/cond/branch_1_fun/ppermute | solution.py:407
  155.6 10.1 %collective-permute-start.4 = (bf16[128,2048]{1,0:T(8,128)(2,1)S(1)}, bf16[128,2048]{1,0:T(8,128)(2,1)S(1)}, u32[]{:S(2)}, u32[]{:S(2)}) collective-permute-start(bf16[128,2048]{1,0:T(8,128)(2,1)S(1)} %add_convert_fusion.3), channel_id=1, source_target_pairs={{8,0},{2,10},{16,8},{10,18},{24,16},{18,26},{28,24},{26,30},{20,28... | collective-permute-start | bytes 1572872 | tf_op jit(solution)/shard_map/cond/branch_1_fun/ppermute | solution.py:407
  160.1 11.1 %collective-permute-start.3 = (bf16[128,2048]{1,0:T(8,128)(2,1)S(1)}, bf16[128,2048]{1,0:T(8,128)(2,1)S(1)}, u32[]{:S(2)}, u32[]{:S(2)}) collective-permute-start(bf16[128,2048]{1,0:T(8,128)(2,1)S(1)} %add_convert_fusion.2), channel_id=1, source_target_pairs={{8,0},{2,10},{16,8},{10,18},{24,16},{18,26},{28,24},{26,30},{20,28... | collective-permute-start | bytes 1572872 | tf_op jit(solution)/shard_map/cond/branch_1_fun/ppermute | solution.py:407
  165.7 11.1 %collective-permute-start.6 = (bf16[128,2048]{1,0:T(8,128)(2,1)S(1)}, bf16[128,2048]{1,0:T(8,128)(2,1)S(1)}, u32[]{:S(2)}, u32[]{:S(2)}) collective-permute-start(bf16[128,2048]{1,0:T(8,128)(2,1)S(1)} %add_convert_fusion.1), channel_id=1, source_target_pairs={{8,0},{2,10},{16,8},{10,18},{24,16},{18,26},{28,24},{26,30},{20,28... | collective-permute-start | bytes 1572872 | tf_op jit(solution)/shard_map/cond/branch_1_fun/ppermute | solution.py:407
  190.6 59.2 %collective-permute-start.67 = (bf16[2048,1152]{1,0:T(8,128)(2,1)S(1)}, bf16[2048,1152]{1,0:T(8,128)(2,1)S(1)}, u32[]{:S(2)}, u32[]{:S(2)}) collective-permute-start(bf16[2048,1152]{1,0:T(8,128)(2,1)S(1)} %bitcast.193), channel_id=1, source_target_pairs={{0,2},{2,0},{4,6},{6,4},{8,10},{10,8},{12,14},{14,12},{16,18},{18,... | collective-permute-start | bytes 14155784 | tf_op jit(solution)/shard_map/ppermute | solution.py:401
  192.1 8.7 %collective-permute-start.59 = (bf16[128,2048]{1,0:T(8,128)(2,1)S(1)}, bf16[128,2048]{1,0:T(8,128)(2,1)S(1)}, u32[]{:S(2)}, u32[]{:S(2)}) collective-permute-start(bf16[128,2048]{1,0:T(8,128)(2,1)S(1)} %get-tuple-element.359), channel_id=1, source_target_pairs={{0,8},{10,2},{8,16},{18,10},{16,24},{26,18},{24,28},{30,26},{28,20... | collective-permute-start | bytes 1572872 | tf_op jit(solution)/shard_map/ppermute | solution.py:404
  199.8 8.6 %collective-permute-start.58 = (bf16[128,2048]{1,0:T(8,128)(2,1)S(1)}, bf16[128,2048]{1,0:T(8,128)(2,1)S(1)}, u32[]{:S(2)}, u32[]{:S(2)}) collective-permute-start(bf16[128,2048]{1,0:T(8,128)(2,1)S(1)} %collective-permute-done.57), channel_id=1, source_target_pairs={{0,8},{10,2},{8,16},{18,10},{16,24},{26,18},{24,28},{30,26},{28,20... | collective-permute-start | bytes 1572872 | tf_op jit(solution)/shard_map/ppermute | solution.py:404
  200.7 13.3 %collective-permute-start.61 = (bf16[128,2048]{1,0:T(8,128)(2,1)S(1)}, bf16[128,2048]{1,0:T(8,128)(2,1)S(1)}, u32[]{:S(2)}, u32[]{:S(2)}) collective-permute-start(bf16[128,2048]{1,0:T(8,128)(2,1)S(1)} %collective-permute-done.59), channel_id=1, source_target_pairs={{0,8},{10,2},{8,16},{18,10},{16,24},{26,18},{24,28},{30,26},{28,20... | collective-permute-start | bytes 1572872 | tf_op jit(solution)/shard_map/ppermute | solution.py:404
  208.4 11.2 %collective-permute-start.60 = (bf16[128,2048]{1,0:T(8,128)(2,1)S(1)}, bf16[128,2048]{1,0:T(8,128)(2,1)S(1)}, u32[]{:S(2)}, u32[]{:S(2)}) collective-permute-start(bf16[128,2048]{1,0:T(8,128)(2,1)S(1)} %collective-permute-done.58), channel_id=1, source_target_pairs={{0,8},{10,2},{8,16},{18,10},{16,24},{26,18},{24,28},{30,26},{28,20... | collective-permute-start | bytes 1572872 | tf_op jit(solution)/shard_map/ppermute | solution.py:404
  214.0 11.2 %collective-permute-start.71 = (bf16[128,2048]{1,0:T(8,128)(2,1)S(1)}, bf16[128,2048]{1,0:T(8,128)(2,1)S(1)}, u32[]{:S(2)}, u32[]{:S(2)}) collective-permute-start(bf16[128,2048]{1,0:T(8,128)(2,1)S(1)} %collective-permute-done.61), channel_id=1, source_target_pairs={{0,8},{10,2},{8,16},{18,10},{16,24},{26,18},{24,28},{30,26},{28,20... | collective-permute-start | bytes 1572872 | tf_op jit(solution)/shard_map/ppermute | solution.py:404
  219.6 11.2 %collective-permute-start.62 = (bf16[128,2048]{1,0:T(8,128)(2,1)S(1)}, bf16[128,2048]{1,0:T(8,128)(2,1)S(1)}, u32[]{:S(2)}, u32[]{:S(2)}) collective-permute-start(bf16[128,2048]{1,0:T(8,128)(2,1)S(1)} %collective-permute-done.60), channel_id=1, source_target_pairs={{0,8},{10,2},{8,16},{18,10},{16,24},{26,18},{24,28},{30,26},{28,20... | collective-permute-start | bytes 1572872 | tf_op jit(solution)/shard_map/ppermute | solution.py:404
  225.3 11.2 %collective-permute-start.72 = (bf16[128,2048]{1,0:T(8,128)(2,1)S(1)}, bf16[128,2048]{1,0:T(8,128)(2,1)S(1)}, u32[]{:S(2)}, u32[]{:S(2)}) collective-permute-start(bf16[128,2048]{1,0:T(8,128)(2,1)S(1)} %collective-permute-done.71), channel_id=1, source_target_pairs={{0,8},{10,2},{8,16},{18,10},{16,24},{26,18},{24,28},{30,26},{28,20... | collective-permute-start | bytes 1572872 | tf_op jit(solution)/shard_map/ppermute | solution.py:404
  231.9 10.2 %collective-permute-start.63 = (bf16[128,2048]{1,0:T(8,128)(2,1)S(1)}, bf16[128,2048]{1,0:T(8,128)(2,1)S(1)}, u32[]{:S(2)}, u32[]{:S(2)}) collective-permute-start(bf16[128,2048]{1,0:T(8,128)(2,1)S(1)} %bitcast.205), channel_id=1, source_target_pairs={{0,8},{10,2},{8,16},{18,10},{16,24},{26,18},{24,28},{30,26},{28,20... | collective-permute-start | bytes 1572872 | tf_op jit(solution)/shard_map/ppermute | solution.py:404
  233.4 14.4 %collective-permute-start.65 = (bf16[128,2048]{1,0:T(8,128)(2,1)S(1)}, bf16[128,2048]{1,0:T(8,128)(2,1)S(1)}, u32[]{:S(2)}, u32[]{:S(2)}) collective-permute-start(bf16[128,2048]{1,0:T(8,128)(2,1)S(1)} %collective-permute-done.64), channel_id=1, source_target_pairs={{0,8},{10,2},{8,16},{18,10},{16,24},{26,18},{24,28},{30,26},{28,20... | collective-permute-start | bytes 1572872 | tf_op jit(solution)/shard_map/ppermute | solution.py:404
  257.1 8.4 %collective-permute-start.68 = (bf16[128,2048]{1,0:T(8,128)(2,1)S(1)}, bf16[128,2048]{1,0:T(8,128)(2,1)S(1)}, u32[]{:S(2)}, u32[]{:S(2)}) collective-permute-start(bf16[128,2048]{1,0:T(8,128)(2,1)S(1)} %copy-done.53), channel_id=1, source_target_pairs={{0,8},{10,2},{8,16},{18,10},{16,24},{26,18},{24,28},{30,26},{28,20... | collective-permute-start | bytes 1572872 | tf_op jit(solution)/shard_map/ppermute | solution.py:404
  265.5 12.8 %collective-permute-start.70 = (bf16[128,2048]{1,0:T(8,128)(2,1)S(1)}, bf16[128,2048]{1,0:T(8,128)(2,1)S(1)}, u32[]{:S(2)}, u32[]{:S(2)}) collective-permute-start(bf16[128,2048]{1,0:T(8,128)(2,1)S(1)} %collective-permute-done.68), channel_id=1, source_target_pairs={{0,8},{10,2},{8,16},{18,10},{16,24},{26,18},{24,28},{30,26},{28,20... | collective-permute-start | bytes 1572872 | tf_op jit(solution)/shard_map/ppermute | solution.py:404
  272.6 11.2 %collective-permute-start.73 = (bf16[128,2048]{1,0:T(8,128)(2,1)S(1)}, bf16[128,2048]{1,0:T(8,128)(2,1)S(1)}, u32[]{:S(2)}, u32[]{:S(2)}) collective-permute-start(bf16[128,2048]{1,0:T(8,128)(2,1)S(1)} %collective-permute-done.69), channel_id=1, source_target_pairs={{0,8},{10,2},{8,16},{18,10},{16,24},{26,18},{24,28},{30,26},{28,20... | collective-permute-start | bytes 1572872 | tf_op jit(solution)/shard_map/ppermute | solution.py:404
  278.2 11.2 %collective-permute-start.74 = (bf16[128,2048]{1,0:T(8,128)(2,1)S(1)}, bf16[128,2048]{1,0:T(8,128)(2,1)S(1)}, u32[]{:S(2)}, u32[]{:S(2)}) collective-permute-start(bf16[128,2048]{1,0:T(8,128)(2,1)S(1)} %collective-permute-done.70), channel_id=1, source_target_pairs={{0,8},{10,2},{8,16},{18,10},{16,24},{26,18},{24,28},{30,26},{28,20... | collective-permute-start | bytes 1572872 | tf_op jit(solution)/shard_map/ppermute | solution.py:404
  310.6 11.1 %collective-permute-start.18 = (bf16[128,2048]{1,0:T(8,128)(2,1)}, bf16[128,2048]{1,0:T(8,128)(2,1)}, u32[]{:S(2)}, u32[]{:S(2)}) collective-permute-start(bf16[128,2048]{1,0:T(8,128)(2,1)} %add_convert_fusion.11), channel_id=1, source_target_pairs={{8,0},{2,10},{16,8},{10,18},{24,16},{18,26},{28,24},{26,30},{20,28... | collective-permute-start | bytes 1572872 | tf_op jit(solution)/shard_map/cond/branch_1_fun/ppermute | solution.py:407
  318.7 37.4 %collective-permute-start.25 = (bf16[2048,384]{1,0:T(8,128)(2,1)S(1)}, bf16[2048,384]{1,0:T(8,128)(2,1)S(1)}, u32[]{:S(2)}, u32[]{:S(2)}) collective-permute-start(bf16[2048,384]{1,0:T(8,128)(2,1)S(1)} %fusion.2), channel_id=1, source_target_pairs={{0,2},{2,0},{4,6},{6,4},{8,10},{10,8},{12,14},{14,12},{16,18},{18,... | collective-permute-start | bytes 4718600 | tf_op jit(solution)/shard_map/cond/branch_1_fun/ppermute | solution.py:401
  319.9 9.8 %collective-permute-start.20 = (bf16[128,2048]{1,0:T(8,128)(2,1)S(1)}, bf16[128,2048]{1,0:T(8,128)(2,1)S(1)}, u32[]{:S(2)}, u32[]{:S(2)}) collective-permute-start(bf16[128,2048]{1,0:T(8,128)(2,1)S(1)} %copy-done.56), channel_id=1, source_target_pairs={{8,0},{2,10},{16,8},{10,18},{24,16},{18,26},{28,24},{26,30},{20,28... | collective-permute-start | bytes 1572872 | tf_op jit(solution)/shard_map/cond/branch_1_fun/ppermute | solution.py:407
  325.6 32.4 %collective-permute-start.26 = (bf16[2048,768]{1,0:T(8,128)(2,1)S(1)}, bf16[2048,768]{1,0:T(8,128)(2,1)S(1)}, u32[]{:S(2)}, u32[]{:S(2)}) collective-permute-start(bf16[2048,768]{1,0:T(8,128)(2,1)S(1)} %fusion), channel_id=1, source_target_pairs={{0,2},{2,0},{4,6},{6,4},{8,10},{10,8},{12,14},{14,12},{16,18},{18,... | collective-permute-start | bytes 9437192 | tf_op jit(solution)/shard_map/cond/branch_1_fun/ppermute | solution.py:401
  340.4 17.4 %collective-permute-start.21 = (bf16[128,2048]{1,0:T(8,128)(2,1)S(1)}, bf16[128,2048]{1,0:T(8,128)(2,1)S(1)}, u32[]{:S(2)}, u32[]{:S(2)}) collective-permute-start(bf16[128,2048]{1,0:T(8,128)(2,1)S(1)} %add_convert_fusion.8), channel_id=1, source_target_pairs={{8,0},{2,10},{16,8},{10,18},{24,16},{18,26},{28,24},{26,30},{20,28... | collective-permute-start | bytes 1572872 | tf_op jit(solution)/shard_map/cond/branch_1_fun/ppermute | solution.py:407
  343.0 11.4 %collective-permute-start.23 = (bf16[128,2048]{1,0:T(8,128)(2,1)S(1)}, bf16[128,2048]{1,0:T(8,128)(2,1)S(1)}, u32[]{:S(2)}, u32[]{:S(2)}) collective-permute-start(bf16[128,2048]{1,0:T(8,128)(2,1)S(1)} %add_convert_fusion.7), channel_id=1, source_target_pairs={{8,0},{2,10},{16,8},{10,18},{24,16},{18,26},{28,24},{26,30},{20,28... | collective-permute-start | bytes 1572872 | tf_op jit(solution)/shard_map/cond/branch_1_fun/ppermute | solution.py:407
  361.6 56.4 %collective-permute-start.77 = (bf16[16,64,768]{2,1,0:T(8,128)(2,1)}, bf16[16,64,768]{2,1,0:T(8,128)(2,1)}, u32[]{:S(2)}, u32[]{:S(2)}) collective-permute-start(bf16[16,64,768]{2,1,0:T(8,128)(2,1)} %get-tuple-element.305), channel_id=1, source_target_pairs={{0,1},{1,0},{2,3},{3,2},{4,5},{5,4},{6,7},{7,6},{8,9},{9,8},{10,11... | collective-permute-start | bytes 4718600 | tf_op jit(solution)/shard_map/ppermute | solution.py:475
  361.8 54.5 %collective-permute-start.76 = (bf16[16,64,384]{2,1,0:T(8,128)(2,1)}, bf16[16,64,384]{2,1,0:T(8,128)(2,1)}, u32[]{:S(2)}, u32[]{:S(2)}) collective-permute-start(bf16[16,64,384]{2,1,0:T(8,128)(2,1)} %get-tuple-element.303), channel_id=1, source_target_pairs={{0,1},{1,0},{2,3},{3,2},{4,5},{5,4},{6,7},{7,6},{8,9},{9,8},{10,11... | collective-permute-start | bytes 2359304 | tf_op jit(solution)/shard_map/ppermute | solution.py:475
  366.8 8.7 %collective-permute-start.27 = (bf16[128,2048]{1,0:T(8,128)(2,1)S(1)}, bf16[128,2048]{1,0:T(8,128)(2,1)S(1)}, u32[]{:S(2)}, u32[]{:S(2)}) collective-permute-start(bf16[128,2048]{1,0:T(8,128)(2,1)S(1)} %get-tuple-element.125), channel_id=1, source_target_pairs={{0,8},{10,2},{8,16},{18,10},{16,24},{26,18},{24,28},{30,26},{28,20... | collective-permute-start | bytes 1572872 | tf_op jit(solution)/shard_map/cond/branch_1_fun/ppermute | solution.py:404
  368.4 12.8 %collective-permute-start.29 = (bf16[128,2048]{1,0:T(8,128)(2,1)S(1)}, bf16[128,2048]{1,0:T(8,128)(2,1)S(1)}, u32[]{:S(2)}, u32[]{:S(2)}) collective-permute-start(bf16[128,2048]{1,0:T(8,128)(2,1)S(1)} %collective-permute-done.28), channel_id=1, source_target_pairs={{0,8},{10,2},{8,16},{18,10},{16,24},{26,18},{24,28},{30,26},{28,20... | collective-permute-start | bytes 1572872 | tf_op jit(solution)/shard_map/cond/branch_1_fun/ppermute | solution.py:404
  375.5 11.2 %collective-permute-start.30 = (bf16[128,2048]{1,0:T(8,128)(2,1)S(1)}, bf16[128,2048]{1,0:T(8,128)(2,1)S(1)}, u32[]{:S(2)}, u32[]{:S(2)}) collective-permute-start(bf16[128,2048]{1,0:T(8,128)(2,1)S(1)} %collective-permute-done.27), channel_id=1, source_target_pairs={{0,8},{10,2},{8,16},{18,10},{16,24},{26,18},{24,28},{30,26},{28,20... | collective-permute-start | bytes 1572872 | tf_op jit(solution)/shard_map/cond/branch_1_fun/ppermute | solution.py:404
  381.2 11.2 %collective-permute-start.31 = (bf16[128,2048]{1,0:T(8,128)(2,1)S(1)}, bf16[128,2048]{1,0:T(8,128)(2,1)S(1)}, u32[]{:S(2)}, u32[]{:S(2)}) collective-permute-start(bf16[128,2048]{1,0:T(8,128)(2,1)S(1)} %collective-permute-done.29), channel_id=1, source_target_pairs={{0,8},{10,2},{8,16},{18,10},{16,24},{26,18},{24,28},{30,26},{28,20... | collective-permute-start | bytes 1572872 | tf_op jit(solution)/shard_map/cond/branch_1_fun/ppermute | solution.py:404
  386.8 11.2 %collective-permute-start.32 = (bf16[128,2048]{1,0:T(8,128)(2,1)S(1)}, bf16[128,2048]{1,0:T(8,128)(2,1)S(1)}, u32[]{:S(2)}, u32[]{:S(2)}) collective-permute-start(bf16[128,2048]{1,0:T(8,128)(2,1)S(1)} %collective-permute-done.30), channel_id=1, source_target_pairs={{0,8},{10,2},{8,16},{18,10},{16,24},{26,18},{24,28},{30,26},{28,20... | collective-permute-start | bytes 1572872 | tf_op jit(solution)/shard_map/cond/branch_1_fun/ppermute | solution.py:404
  392.4 11.2 %collective-permute-start.33 = (bf16[128,2048]{1,0:T(8,128)(2,1)S(1)}, bf16[128,2048]{1,0:T(8,128)(2,1)S(1)}, u32[]{:S(2)}, u32[]{:S(2)}) collective-permute-start(bf16[128,2048]{1,0:T(8,128)(2,1)S(1)} %collective-permute-done.31), channel_id=1, source_target_pairs={{0,8},{10,2},{8,16},{18,10},{16,24},{26,18},{24,28},{30,26},{28,20... | collective-permute-start | bytes 1572872 | tf_op jit(solution)/shard_map/cond/branch_1_fun/ppermute | solution.py:404
  398.0 11.2 %collective-permute-start.34 = (bf16[128,2048]{1,0:T(8,128)(2,1)S(1)}, bf16[128,2048]{1,0:T(8,128)(2,1)S(1)}, u32[]{:S(2)}, u32[]{:S(2)}) collective-permute-start(bf16[128,2048]{1,0:T(8,128)(2,1)S(1)} %collective-permute-done.32), channel_id=1, source_target_pairs={{0,8},{10,2},{8,16},{18,10},{16,24},{26,18},{24,28},{30,26},{28,20... | collective-permute-start | bytes 1572872 | tf_op jit(solution)/shard_map/cond/branch_1_fun/ppermute | solution.py:404
  422.8 107.3 %all-to-all-start.3 = ((bf16[16,64,1152]{2,1,0:T(8,128)(2,1)}), bf16[16,64,1152]{2,1,0:T(8,128)(2,1)}, u32[]{:S(2)}, u32[]{:S(2)}) async-start(bf16[16,64,1152]{2,1,0:T(8,128)(2,1)} %pad_maximum_fusion.9), calls=%async_computation.3 | async-start | bytes 4718592 | tf_op jit(solution)/shard_map/all_to_all | solution.py:471
  454.3 30.6 %collective-permute-start.36 = (bf16[128,2048]{1,0:T(8,128)(2,1)}, bf16[128,2048]{1,0:T(8,128)(2,1)S(1)}, u32[]{:S(2)}, u32[]{:S(2)}) collective-permute-start(bf16[128,2048]{1,0:T(8,128)(2,1)} %get-tuple-element.372), channel_id=1, source_target_pairs={{8,0},{2,10},{16,8},{10,18},{24,16},{18,26},{28,24},{26,30},{20,28... | collective-permute-start | bytes 1572872 | tf_op jit(solution)/shard_map/cond/branch_1_fun/ppermute | solution.py:407
  455.6 34.9 %collective-permute-start.38 = (bf16[128,2048]{1,0:T(8,128)(2,1)}, bf16[128,2048]{1,0:T(8,128)(2,1)S(1)}, u32[]{:S(2)}, u32[]{:S(2)}) collective-permute-start(bf16[128,2048]{1,0:T(8,128)(2,1)} %get-tuple-element.373), channel_id=1, source_target_pairs={{8,0},{2,10},{16,8},{10,18},{24,16},{18,26},{28,24},{26,30},{20,28... | collective-permute-start | bytes 1572872 | tf_op jit(solution)/shard_map/cond/branch_1_fun/ppermute | solution.py:407
  486.1 16.6 %collective-permute-start.37 = (bf16[128,2048]{1,0:T(8,128)(2,1)S(1)}, bf16[128,2048]{1,0:T(8,128)(2,1)S(1)}, u32[]{:S(2)}, u32[]{:S(2)}) collective-permute-start(bf16[128,2048]{1,0:T(8,128)(2,1)S(1)} %add_convert_fusion.18), channel_id=1, source_target_pairs={{8,0},{2,10},{16,8},{10,18},{24,16},{18,26},{28,24},{26,30},{20,28... | collective-permute-start | bytes 1572872 | tf_op jit(solution)/shard_map/cond/branch_1_fun/ppermute | solution.py:407
  491.7 12.9 %collective-permute-start.40 = (bf16[128,2048]{1,0:T(8,128)(2,1)S(1)}, bf16[128,2048]{1,0:T(8,128)(2,1)S(1)}, u32[]{:S(2)}, u32[]{:S(2)}) collective-permute-start(bf16[128,2048]{1,0:T(8,128)(2,1)S(1)} %add_convert_fusion.17), channel_id=1, source_target_pairs={{8,0},{2,10},{16,8},{10,18},{24,16},{18,26},{28,24},{26,30},{20,28... | collective-permute-start | bytes 1572872 | tf_op jit(solution)/shard_map/cond/branch_1_fun/ppermute | solution.py:407
  502.6 16.9 %collective-permute-start.41 = (bf16[2048,384]{0,1:T(8,128)(2,1)S(1)}, bf16[2048,384]{0,1:T(8,128)(2,1)S(1)}, u32[]{:S(2)}, u32[]{:S(2)}) collective-permute-start(bf16[2048,384]{0,1:T(8,128)(2,1)S(1)} %pad_maximum_fusion.1), channel_id=1, source_target_pairs={{0,2},{2,0},{4,6},{6,4},{8,10},{10,8},{12,14},{14,12},{16,18},{18,... | collective-permute-start | bytes 4718600 | tf_op jit(solution)/shard_map/cond/branch_1_fun/ppermute | solution.py:401
  504.8 13.8 %collective-permute-start.43 = (bf16[128,2048]{1,0:T(8,128)(2,1)S(1)}, bf16[128,2048]{1,0:T(8,128)(2,1)S(1)}, u32[]{:S(2)}, u32[]{:S(2)}) collective-permute-start(bf16[128,2048]{1,0:T(8,128)(2,1)S(1)} %add_convert_fusion.15), channel_id=1, source_target_pairs={{8,0},{2,10},{16,8},{10,18},{24,16},{18,26},{28,24},{26,30},{20,28... | collective-permute-start | bytes 1572872 | tf_op jit(solution)/shard_map/cond/branch_1_fun/ppermute | solution.py:407
  532.8 18.1 %collective-permute-start.10 = (bf16[128,2048]{1,0:T(8,128)(2,1)}, bf16[128,2048]{1,0:T(8,128)(2,1)}, u32[]{:S(2)}, u32[]{:S(2)}) collective-permute-start(bf16[128,2048]{1,0:T(8,128)(2,1)} %get-tuple-element.383), channel_id=1, source_target_pairs={{8,0},{2,10},{16,8},{10,18},{24,16},{18,26},{28,24},{26,30},{20,28... | collective-permute-start | bytes 1572872 | tf_op jit(solution)/shard_map/cond/branch_1_fun/ppermute | solution.py:407
  534.5 12.5 %collective-permute-start.8 = (bf16[128,2048]{1,0:T(8,128)(2,1)}, bf16[128,2048]{1,0:T(8,128)(2,1)}, u32[]{:S(2)}, u32[]{:S(2)}) collective-permute-start(bf16[128,2048]{1,0:T(8,128)(2,1)} %get-tuple-element.382), channel_id=1, source_target_pairs={{8,0},{2,10},{16,8},{10,18},{24,16},{18,26},{28,24},{26,30},{20,28... | collective-permute-start | bytes 1572872 | tf_op jit(solution)/shard_map/cond/branch_1_fun/ppermute | solution.py:407
  536.7 18.8 %collective-permute-start.11 = (bf16[1040,384]{1,0:T(8,128)(2,1)S(1)}, bf16[1040,384]{1,0:T(8,128)(2,1)S(1)}, u32[]{:S(2)}, u32[]{:S(2)}) collective-permute-start(bf16[1040,384]{1,0:T(8,128)(2,1)S(1)} %pad_maximum_fusion.3), channel_id=1, source_target_pairs={{0,1},{1,0},{2,3},{3,2},{4,5},{5,4},{6,7},{7,6},{8,9},{9,8},{10,11... | collective-permute-start | bytes 2396168 | tf_op jit(solution)/shard_map/cond/branch_1_fun/ppermute | solution.py:475
  549.2 14.9 %collective-permute-start.9 = (bf16[128,2048]{1,0:T(8,128)(2,1)}, bf16[128,2048]{1,0:T(8,128)(2,1)}, u32[]{:S(2)}, u32[]{:S(2)}) collective-permute-start(bf16[128,2048]{1,0:T(8,128)(2,1)} %add_convert_fusion.23), channel_id=1, source_target_pairs={{8,0},{2,10},{16,8},{10,18},{24,16},{18,26},{28,24},{26,30},{20,28... | collective-permute-start | bytes 1572872 | tf_op jit(solution)/shard_map/cond/branch_1_fun/ppermute | solution.py:407
  553.0 13.8 %collective-permute-start.13 = (bf16[128,2048]{1,0:T(8,128)(2,1)}, bf16[128,2048]{1,0:T(8,128)(2,1)}, u32[]{:S(2)}, u32[]{:S(2)}) collective-permute-start(bf16[128,2048]{1,0:T(8,128)(2,1)} %add_convert_fusion.22), channel_id=1, source_target_pairs={{8,0},{2,10},{16,8},{10,18},{24,16},{18,26},{28,24},{26,30},{20,28... | collective-permute-start | bytes 1572872 | tf_op jit(solution)/shard_map/cond/branch_1_fun/ppermute | solution.py:407
  557.2 51.9 %all-to-all-start = ((bf16[16,80,384]{2,1,0:T(8,128)(2,1)}), bf16[16,80,384]{2,1,0:T(8,128)(2,1)}, u32[]{:S(2)}, u32[]{:S(2)}) async-start(bf16[16,80,384]{2,1,0:T(8,128)(2,1)} %pad_maximum_fusion.2), calls=%async_computation | async-start | bytes 1966080 | tf_op jit(solution)/shard_map/cond/branch_1_fun/all_to_all | solution.py:471
  565.5 26.0 %collective-permute-start.12 = (bf16[128,2048]{1,0:T(8,128)(2,1)S(1)}, bf16[128,2048]{1,0:T(8,128)(2,1)S(1)}, u32[]{:S(2)}, u32[]{:S(2)}) collective-permute-start(bf16[128,2048]{1,0:T(8,128)(2,1)S(1)} %add_convert_fusion.21), channel_id=1, source_target_pairs={{8,0},{2,10},{16,8},{10,18},{24,16},{18,26},{28,24},{26,30},{20,28... | collective-permute-start | bytes 1572872 | tf_op jit(solution)/shard_map/cond/branch_1_fun/ppermute | solution.py:407
  568.1 29.0 %collective-permute-start.15 = (bf16[128,2048]{1,0:T(8,128)(2,1)S(1)}, bf16[128,2048]{1,0:T(8,128)(2,1)S(1)}, u32[]{:S(2)}, u32[]{:S(2)}) collective-permute-start(bf16[128,2048]{1,0:T(8,128)(2,1)S(1)} %add_convert_fusion.20), channel_id=1, source_target_pairs={{8,0},{2,10},{16,8},{10,18},{24,16},{18,26},{28,24},{26,30},{20,28... | collective-permute-start | bytes 1572872 | tf_op jit(solution)/shard_map/cond/branch_1_fun/ppermute | solution.py:407
  592.7 14.1 %collective-permute-start.14 = (bf16[128,2048]{1,0:T(8,128)(2,1)S(1)}, bf16[128,2048]{1,0:T(8,128)(2,1)S(1)}, u32[]{:S(2)}, u32[]{:S(2)}) collective-permute-start(bf16[128,2048]{1,0:T(8,128)(2,1)S(1)} %add_convert_fusion.19), channel_id=1, source_target_pairs={{8,0},{2,10},{16,8},{10,18},{24,16},{18,26},{28,24},{26,30},{20,28... | collective-permute-start | bytes 1572872 | tf_op jit(solution)/shard_map/cond/branch_1_fun/ppermute | solution.py:407
  597.2 9.6 %collective-permute-start.16 = (bf16[128,2048]{1,0:T(8,128)(2,1)S(1)}, bf16[128,2048]{1,0:T(8,128)(2,1)S(1)}, u32[]{:S(2)}, u32[]{:S(2)}) collective-permute-start(bf16[128,2048]{1,0:T(8,128)(2,1)S(1)} %collective-permute-done.15), channel_id=1, source_target_pairs={{0,2},{2,0},{4,6},{6,4},{8,10},{10,8},{12,14},{14,12},{16,18},{18,... | collective-permute-start | bytes 1572872 | tf_op jit(solution)/shard_map/cond/branch_1_fun/ppermute | solution.py:401
  (87 other events, 847.6 us)

commit v5 on v4

--- a/solution.py
+++ b/solution.py
@@ -577,7 +577,7 @@
     head_block = jnp.concatenate(
         [by_head(query_weight), by_head(output_weight), by_head(key_value)], axis=2
     )
-    head_received = spread(head_block)
+    head_received = spread(after(head_block, ring.swap(block_input[0])))
     head_mine = to_columns(head_received, swap_rows(head_received), fsdp_rank)
     head_other = ring.swap(head_mine)
 

time: 625 us -> 623 us (level)
    unnamed x122 -> x128, local copies, waits for them, and re-layouts: 21.2 us -> 17.2 us
  transfers between devices with their start and end apart: 82 -> 82, of which waited for: 53 -> 51; matrix products, arithmetic and copies ran while one was open for 22% -> 22% of each run, Pallas kernels for 5% -> 5%
where the time goes in v5:
time: 623 us; the launch traced here: 616 us
  waiting for transfers between devices  308 us (49%)
  starting transfers between devices  88.1 us (14%)
  other arithmetic  76.4 us (12%)
  matrix products  57.3 us (9%)
  local copies, waits for them, and re-layouts  51.3 us (8%)
  Pallas kernels  30.2 us (5%)
    ppermute x28, waiting for transfers between devices, out(): return lax.ppermute(field, 'ctx', self.out_pairs)  133 us
    ppermute x28, waiting for transfers between devices, home(): return lax.ppermute(field, 'ctx', self.home_pairs)  125 us
    ppermute x28, starting transfers between devices, home(): return lax.ppermute(field, 'ctx', self.home_pairs)  41.3 us
    all_to_all x4, waiting for transfers between devices, spread(): lax.all_to_all(rows_block, 'ctx', split_axis=0, concat_axis=0, tiled=False)  26.6 us
    dot_general x6, matrix products, dot_tn(): lax.dot_general(left, right, (((0,), (0,)), ((), ())), preferred_element_...  23.3 us
    all_to_all x4, starting transfers between devices, spread(): lax.all_to_all(rows_block, 'ctx', split_axis=0, concat_axis=0, tiled=False)  22.4 us
    dot_general x5, matrix products, dot_nt(): lax.dot_general(left, right, (((1,), (1,)), ((), ())), preferred_element_...  18.8 us
    unnamed x128, local copies, waits for them, and re-layouts  17.2 us
  transfers between devices with their start and end apart: 82, of which 51 were waited for; matrix products, arithmetic and copies ran while one was open for 22% of the time, Pallas kernels for 5%

profile of v5, /device:TPU:9, one launch (start us, length us, event | category | flops | bytes accessed | tf_op | source)
XLA Modules:
  0.0 616.0 jit_solution(11361723828071927267)
XLA Ops:
  6.8 6.0 all-to-all-start.1
  14.3 23.7 %collective-permute-done.48.refs_1_ = bf16[128,2048]{1,0:T(8,128)(2,1)S(1)} collective-permute-done((bf16[128,2048]{1,0:T(8,128)(2,1)S(1)}, bf16[128,2048]{1,0:T(8,128)(2,1)S(1)}, u32[]{:S(2)}, u32[]{:S(2)}) %collective-permute-start.48) | collective-permute-done | bytes 524320 | tf_op jit(solution)/shard_map/ppermute | solution.py:404
  38.0 5.6 collective-permute-done.49.refs_2_
  43.6 5.6 collective-permute-done.50.refs_3_
  50.6 3.7 fusion.29
  56.7 3.7 collective-permute-done.52.refs_5_
  60.5 7.1 %collective-permute-done.46 = bf16[16,64,384]{2,1,0:T(8,128)(2,1)S(1)} collective-permute-done((bf16[16,64,384]{2,1,0:T(8,128)(2,1)}, bf16[16,64,384]{2,1,0:T(8,128)(2,1)S(1)}, u32[]{:S(2)}, u32[]{:S(2)}) %collective-permute-start.46) | collective-permute-done | bytes 786464 | tf_op jit(solution)/shard_map/ppermute | solution.py:475
  75.4 4.6 all-to-all-start.2
  84.5 4.6 project.1
  94.0 10.6 %attend.1 = (bf16[1024,128]{1,0:T(8,128)(2,1)S(1)}, bf16[1024,128]{1,0:T(8,128)(2,1)S(1)}, f32[1,2048]{1,0:T(1,128)S(1)}, bf16[2048,128]{1,0:T(8,128)(2,1)}, bf1...) custom-call(s32[32]{0:T(128)S(1)} %select_reduce_fusion.key_pos, s32[32]{0:T(128)S(1)} %iota.30.query_table.pos_table, ...), custom_call_target="tpu_custom_call" | custom-call | flops 2147483648 | bytes 7340032 | tf_op jit(solution)/shard_map/attend/pallas_call | solution.py:200
  104.7 26.6 %all-to-all-done.2 = bf16[16,64,1152]{2,1,0:T(8,128)(2,1)} async-done(((bf16[16,64,1152]{2,1,0:T(8,128)(2,1)}), bf16[16,64,1152]{2,1,0:T(8,128)(2,1)}, u32[]{:S(2)}, u32[]{:S(2)}) %all-to-all-start.2) | async-done | bytes 2359328 | tf_op jit(solution)/shard_map/all_to_all | solution.py:471
  134.7 3.3 convolution_convert_fusion.9
  138.0 49.5 %conditional.6 = (f32[128,2048]{1,0:T(8,128)S(1)}) conditional(s32[]{:T(128)} %convert_element_type.453, () %tuple.125, bf16[1024,2048]{1,0:T(8,128)(2,1)} %convolution_convert_fusion.9), branch_computations={%region_3.4_spmd, %region_4.5_spmd} | conditional | flops 6553600 | bytes 46137700 | solution.py:561
  139.5 3.3 collective-permute-start
  142.9 6.1 collective-permute-done
  171.6 5.5 collective-permute-done.6
  180.3 6.6 %collective-permute-done.5 = bf16[128,2048]{1,0:T(8,128)(2,1)S(1)} collective-permute-done((bf16[128,2048]{1,0:T(8,128)(2,1)S(1)}, bf16[128,2048]{1,0:T(8,128)(2,1)S(1)}, u32[]{:S(2)}, u32[]{:S(2)}) %collective-permute-start.5) | collective-permute-done | bytes 524320 | tf_op jit(solution)/shard_map/cond/branch_1_fun/ppermute | solution.py:407
  192.3 7.7 %collective-permute-done.57 = bf16[128,2048]{1,0:T(8,128)(2,1)S(1)} collective-permute-done((bf16[128,2048]{1,0:T(8,128)(2,1)S(1)}, bf16[128,2048]{1,0:T(8,128)(2,1)S(1)}, u32[]{:S(2)}, u32[]{:S(2)}) %collective-permute-start.57) | collective-permute-done | bytes 524320 | tf_op jit(solution)/shard_map/ppermute | solution.py:401
  200.9 7.7 %collective-permute-done.58 = bf16[128,2048]{1,0:T(8,128)(2,1)S(1)} collective-permute-done((bf16[128,2048]{1,0:T(8,128)(2,1)S(1)}, bf16[128,2048]{1,0:T(8,128)(2,1)S(1)}, u32[]{:S(2)}, u32[]{:S(2)}) %collective-permute-start.58) | collective-permute-done | bytes 524320 | tf_op jit(solution)/shard_map/ppermute | solution.py:404
  208.6 5.6 collective-permute-done.61
  214.2 5.6 collective-permute-done.60
  220.0 5.5 collective-permute-done.71
  225.5 5.6 collective-permute-done.62
  236.7 5.6 collective-permute-done.63
  243.3 4.6 collective-permute-done.65
  252.5 3.1 pad_maximum_fusion.4
  257.5 3.6 copy-done.13
  261.1 3.4 fusion.8
  265.8 3.4 fusion.16
  272.9 5.6 collective-permute-done.70
  278.8 5.4 collective-permute-done.73
  284.2 5.6 collective-permute-done.74
  289.8 3.4 fusion.46
  298.0 60.9 %conditional.7 = (f32[128,2048]{1,0:T(8,128)S(1)}, bf16[2048]{0:T(1024)(128)(2,1)S(1)}, bf16[16,64,384]{2,1,0:T(8,128)(2,1)}, bf16[16,64,384]{2,1,0:T(8,128)(2,1...) conditional(s32[]{:T(128)} %convert_element_type.453, () %tuple.136, ...), branch_computations={%region_6.7_spmd, %region_7.10_spmd} | conditional | flops 13722978304 | bytes 202814128 | solution.py:561
  300.5 5.6 convolution_convert_fusion.2
  311.6 4.7 fusion.2
  319.4 3.9 fusion
  330.3 3.6 collective-permute-done.19
  334.0 3.9 fusion.1
  343.2 8.8 %collective-permute-done.23 = bf16[128,2048]{1,0:T(8,128)(2,1)S(1)} collective-permute-done((bf16[128,2048]{1,0:T(8,128)(2,1)S(1)}, bf16[128,2048]{1,0:T(8,128)(2,1)S(1)}, u32[]{:S(2)}, u32[]{:S(2)}) %collective-permute-start.23) | collective-permute-done | bytes 524320 | tf_op jit(solution)/shard_map/cond/branch_1_fun/ppermute | solution.py:407
  363.7 44.1 %conditional.8 = (bf16[1024,2048]{1,0:T(8,128)(2,1)}, bf16[1024,2048]{1,0:T(8,128)(2,1)S(1)}) conditional(s32[]{:T(128)} %convert_element_type.453, () %tuple.135, (bf16[128,2048]{1,0:T(8,128)(2,1)S(1)}, bf16[1024,768]{1,0:T(8,128)(2,1)S(1)}, bf16[2048,768]{1,0:T(8,128)(2,1)S(1)}) %tuple.224), branch_computations={%region_11.12_spmd, %region_12.13_spmd} | conditional | flops 3223322624 | bytes 34079056 | solution.py:561
  366.5 6.7 %collective-permute-done.27 = bf16[128,2048]{1,0:T(8,128)(2,1)S(1)} collective-permute-done((bf16[128,2048]{1,0:T(8,128)(2,1)S(1)}, bf16[128,2048]{1,0:T(8,128)(2,1)S(1)}, u32[]{:S(2)}, u32[]{:S(2)}) %collective-permute-start.27) | collective-permute-done | bytes 524320 | tf_op jit(solution)/shard_map/cond/branch_1_fun/ppermute | solution.py:404
  375.0 3.8 collective-permute-done.29
  379.0 5.5 collective-permute-done.30
  384.6 3.7 convolution_convert_fusion.5
  391.1 4.6 collective-permute-done.32
  397.6 3.7 collective-permute-done.33
  402.1 4.8 collective-permute-done.34
  407.8 4.9 convolution_convert_fusion.11
  420.4 4.9 all-to-all-start.3
  426.5 22.4 %conditional.9 = (bf16[1024,512]{1,0:T(8,128)(2,1)}, bf16[1024,2048]{1,0:T(8,128)(2,1)S(1)}, f32[128]{0:T(128)S(1)}, f32[128]{0:T(128)S(1)}) conditional(s32[]{:T(128)} %convert_element_type.453, () %tuple.156, (s32[32]{0:T(128)S(1)}, s32[32]{0:T(128)S(1)}, s32[32]{0:T(128)S(1)}, f32[1024,512]{1,0:T(8,128)}, f32[1024,384]{1,0:T(8,128)}, ...), branch_computations={%region_13.14_spmd, %region_14.15_spmd} | conditional | flops 7522484224 | bytes 34078820 | solution.py:561
  426.7 15.0 %attend_back.1 = (bf16[1024,384]{1,0:T(8,128)(2,1)S(1)}, bf16[1024,384]{1,0:T(8,128)(2,1)S(1)}, f32[1,128]{1,0:T(1,128)S(1)}, f32[1,128]{1,0:T(1,128)S(1)}) custom-call(s32[32]{0:T(128)S(1)} %get-tuple-element.134.key_pos, s32[32]{0:T(128)S(1)} %get-tuple-element.136.pos_table, s32[32]{0:T(128)S(1)} %get-tuple-element.136.pos_table, ...), custom_call_target="tpu_custom_call" | custom-call | flops 5368709120 | bytes 10485760 | tf_op jit(solution)/shard_map/cond/branch_1_fun/attend_back/pallas_call | solution.py:315
  445.2 3.6 convolution_convert_fusion.6
  448.9 78.9 %conditional.10 = (f32[128,2048]{1,0:T(8,128)S(1)}, bf16[2048,384]{0,1:T(8,128)(2,1)}, bf16[2048]{0:T(1024)(128)(2,1)S(1)}) conditional(s32[]{:T(128)} %convert_element_type.453, () %tuple.155, (bf16[1024,2048]{1,0:T(8,128)(2,1)S(1)}, bf16[1024,512]{1,0:T(8,128)(2,1)}, bf16[1024,256]{1,0:T(8,128)(2,1)S(1)}, bf16[1024,2048]{1,0:T(8,128)(2,1)}, ...), branch_computations={%region_15.16_spmd, %region_16.18_spmd} | conditional | flops 3250061312 | bytes 121663968 | solution.py:561
  454.3 28.3 %collective-permute-done.36 = bf16[128,2048]{1,0:T(8,128)(2,1)S(1)} collective-permute-done((bf16[128,2048]{1,0:T(8,128)(2,1)}, bf16[128,2048]{1,0:T(8,128)(2,1)S(1)}, u32[]{:S(2)}, u32[]{:S(2)}) %collective-permute-start.36) | collective-permute-done | bytes 524320 | tf_op jit(solution)/shard_map/cond/branch_1_fun/ppermute | solution.py:407
  491.5 4.9 fusion.5
  496.4 3.5 fusion.6
  505.4 5.2 collective-permute-done.39
  510.6 5.6 collective-permute-done.43
  520.7 6.6 %collective-permute-done.42 = bf16[128,2048]{1,0:T(8,128)(2,1)S(1)} collective-permute-done((bf16[128,2048]{1,0:T(8,128)(2,1)S(1)}, bf16[128,2048]{1,0:T(8,128)(2,1)S(1)}, u32[]{:S(2)}, u32[]{:S(2)}) %collective-permute-start.42) | collective-permute-done | bytes 524320 | tf_op jit(solution)/shard_map/cond/branch_1_fun/ppermute | solution.py:407
  527.8 78.9 %conditional.11 = (f32[128,2048]{1,0:T(8,128)}, bf16[16,80,384]{2,1,0:T(8,128)(2,1)}, f32[64,6144]{1,0:T(8,128)}, f32[64,6144]{1,0:T(8,128)}, f32[64,6144]{1,0:T(8,128)}, /*index=5*/f32[1,128,2048]{2,1,0:T(8,128)}) conditional(s32[]{:T(128)} %convert_element_type.453, () %tuple.134, (bf16[1024,2048]{1,0:T(8,128)(2,1)}, s32[]{:T(128)}, ...), branch_computations={%region_18.19_spmd, %region_19.22_spmd} | conditional | flops 16564609 | bytes 89188408 | solution.py:561
  534.7 10.1 %collective-permute-done.8 = bf16[128,2048]{1,0:T(8,128)(2,1)} collective-permute-done((bf16[128,2048]{1,0:T(8,128)(2,1)}, bf16[128,2048]{1,0:T(8,128)(2,1)}, u32[]{:S(2)}, u32[]{:S(2)}) %collective-permute-start.8) | collective-permute-done | bytes 524320 | tf_op jit(solution)/shard_map/cond/branch_1_fun/ppermute | solution.py:407
  554.8 6.9 %all-to-all-start = ((bf16[16,80,384]{2,1,0:T(8,128)(2,1)}), bf16[16,80,384]{2,1,0:T(8,128)(2,1)}, u32[]{:S(2)}, u32[]{:S(2)}) async-start(bf16[16,80,384]{2,1,0:T(8,128)(2,1)} %pad_maximum_fusion.2), calls=%async_computation | async-start | bytes 1966080 | tf_op jit(solution)/shard_map/cond/branch_1_fun/all_to_all | solution.py:471
  567.4 21.9 %collective-permute-done.12 = bf16[128,2048]{1,0:T(8,128)(2,1)S(1)} collective-permute-done((bf16[128,2048]{1,0:T(8,128)(2,1)S(1)}, bf16[128,2048]{1,0:T(8,128)(2,1)S(1)}, u32[]{:S(2)}, u32[]{:S(2)}) %collective-permute-start.12) | collective-permute-done | bytes 524320 | tf_op jit(solution)/shard_map/cond/branch_1_fun/ppermute | solution.py:407
  (427 shorter events, 219.0 us)
Async XLA Ops:
  6.8 42.5 %all-to-all-start.1 = ((bf16[16,64,384]{2,1,0:T(8,128)(2,1)}), bf16[16,64,384]{2,1,0:T(8,128)(2,1)}, u32[]{:S(2)}, u32[]{:S(2)}) async-start(bf16[16,64,384]{2,1,0:T(8,128)(2,1)} %pad_maximum_fusion.18), calls=%async_computation.1 | async-start | bytes 1572864 | tf_op jit(solution)/shard_map/all_to_all | solution.py:471
  12.8 25.2 %collective-permute-start.48 = (bf16[128,2048]{1,0:T(8,128)(2,1)S(1)}, bf16[128,2048]{1,0:T(8,128)(2,1)S(1)}, u32[]{:S(2)}, u32[]{:S(2)}) collective-permute-start(bf16[128,2048]{1,0:T(8,128)(2,1)S(1)} %bitcast.191), channel_id=1, source_target_pairs={{0,8},{10,2},{8,16},{18,10},{16,24},{26,18},{24,28},{30,26},{28,20... | collective-permute-start | bytes 1572872 | tf_op jit(solution)/shard_map/ppermute | solution.py:404
  12.9 30.7 %collective-permute-start.49 = (bf16[128,2048]{1,0:T(8,128)(2,1)S(1)}, bf16[128,2048]{1,0:T(8,128)(2,1)S(1)}, u32[]{:S(2)}, u32[]{:S(2)}) collective-permute-start(bf16[128,2048]{1,0:T(8,128)(2,1)S(1)} %collective-permute-done.45), channel_id=1, source_target_pairs={{0,8},{10,2},{8,16},{18,10},{16,24},{26,18},{24,28},{30,26},{28,20... | collective-permute-start | bytes 1572872 | tf_op jit(solution)/shard_map/ppermute | solution.py:404
  38.0 11.2 %collective-permute-start.50 = (bf16[128,2048]{1,0:T(8,128)(2,1)S(1)}, bf16[128,2048]{1,0:T(8,128)(2,1)S(1)}, u32[]{:S(2)}, u32[]{:S(2)}) collective-permute-start(bf16[128,2048]{1,0:T(8,128)(2,1)S(1)} %collective-permute-done.48.refs_1_), channel_id=1, source_target_pairs={{0,8},{10,2},{8,16},{18,10},{16,24},{26,18},{24,28},{30,26},{28,20... | collective-permute-start | bytes 1572872 | tf_op jit(solution)/shard_map/ppermute | solution.py:404
  43.6 13.0 %collective-permute-start.51 = (bf16[128,2048]{1,0:T(8,128)(2,1)S(1)}, bf16[128,2048]{1,0:T(8,128)(2,1)S(1)}, u32[]{:S(2)}, u32[]{:S(2)}) collective-permute-start(bf16[128,2048]{1,0:T(8,128)(2,1)S(1)} %collective-permute-done.49.refs_2_), channel_id=1, source_target_pairs={{0,8},{10,2},{8,16},{18,10},{16,24},{26,18},{24,28},{30,26},{28,20... | collective-permute-start | bytes 1572872 | tf_op jit(solution)/shard_map/ppermute | solution.py:404
  49.2 11.2 %collective-permute-start.52 = (bf16[128,2048]{1,0:T(8,128)(2,1)S(1)}, bf16[128,2048]{1,0:T(8,128)(2,1)S(1)}, u32[]{:S(2)}, u32[]{:S(2)}) collective-permute-start(bf16[128,2048]{1,0:T(8,128)(2,1)S(1)} %collective-permute-done.50.refs_3_), channel_id=1, source_target_pairs={{0,8},{10,2},{8,16},{18,10},{16,24},{26,18},{24,28},{30,26},{28,20... | collective-permute-start | bytes 1572872 | tf_op jit(solution)/shard_map/ppermute | solution.py:404
  49.3 18.3 %collective-permute-start.46 = (bf16[16,64,384]{2,1,0:T(8,128)(2,1)}, bf16[16,64,384]{2,1,0:T(8,128)(2,1)S(1)}, u32[]{:S(2)}, u32[]{:S(2)}) collective-permute-start(bf16[16,64,384]{2,1,0:T(8,128)(2,1)} %all-to-all-done.1), channel_id=1, source_target_pairs={{0,1},{1,0},{2,3},{3,2},{4,5},{5,4},{6,7},{7,6},{8,9},{9,8},{10,11... | collective-permute-start | bytes 2359304 | tf_op jit(solution)/shard_map/ppermute | solution.py:475
  56.7 17.2 %collective-permute-start.53 = (bf16[128,2048]{1,0:T(8,128)(2,1)S(1)}, bf16[128,2048]{1,0:T(8,128)(2,1)S(1)}, u32[]{:S(2)}, u32[]{:S(2)}) collective-permute-start(bf16[128,2048]{1,0:T(8,128)(2,1)S(1)} %collective-permute-done.51.refs_4_), channel_id=1, source_target_pairs={{0,8},{10,2},{8,16},{18,10},{16,24},{26,18},{24,28},{30,26},{28,20... | collective-permute-start | bytes 1572872 | tf_op jit(solution)/shard_map/ppermute | solution.py:404
  60.5 14.2 %collective-permute-start.54 = (bf16[128,2048]{1,0:T(8,128)(2,1)S(1)}, bf16[128,2048]{1,0:T(8,128)(2,1)S(1)}, u32[]{:S(2)}, u32[]{:S(2)}) collective-permute-start(bf16[128,2048]{1,0:T(8,128)(2,1)S(1)} %collective-permute-done.52.refs_5_), channel_id=1, source_target_pairs={{0,8},{10,2},{8,16},{18,10},{16,24},{26,18},{24,28},{30,26},{28,20... | collective-permute-start | bytes 1572872 | tf_op jit(solution)/shard_map/ppermute | solution.py:404
  70.2 9.9 %collective-permute-start.47 = (bf16[2048,384]{1,0:T(8,128)(2,1)}, bf16[2048,384]{1,0:T(8,128)(2,1)}, u32[]{:S(2)}, u32[]{:S(2)}) collective-permute-start(bf16[2048,384]{1,0:T(8,128)(2,1)} %bitcast.32), channel_id=1, source_target_pairs={{0,2},{2,0},{4,6},{6,4},{8,10},{10,8},{12,14},{14,12},{16,18},{18,... | collective-permute-start | bytes 4718600 | tf_op jit(solution)/shard_map/ppermute | solution.py:401
  75.4 55.8 %all-to-all-start.2 = ((bf16[16,64,1152]{2,1,0:T(8,128)(2,1)}), bf16[16,64,1152]{2,1,0:T(8,128)(2,1)}, u32[]{:S(2)}, u32[]{:S(2)}) async-start(bf16[16,64,1152]{2,1,0:T(8,128)(2,1)} %pad_maximum_fusion.8), calls=%async_computation.2 | async-start | bytes 4718592 | tf_op jit(solution)/shard_map/all_to_all | solution.py:471
  131.2 56.2 %collective-permute-start.66 = (bf16[16,64,1152]{2,1,0:T(8,128)(2,1)}, bf16[16,64,1152]{2,1,0:T(8,128)(2,1)}, u32[]{:S(2)}, u32[]{:S(2)}) collective-permute-start(bf16[16,64,1152]{2,1,0:T(8,128)(2,1)} %all-to-all-done.2), channel_id=1, source_target_pairs={{0,1},{1,0},{2,3},{3,2},{4,5},{5,4},{6,7},{7,6},{8,9},{9,8},{10,11... | collective-permute-start | bytes 7077896 | tf_op jit(solution)/shard_map/ppermute | solution.py:475
  139.5 9.5 %collective-permute-start = (bf16[128,2048]{1,0:T(8,128)(2,1)S(1)}, bf16[128,2048]{1,0:T(8,128)(2,1)S(1)}, u32[]{:S(2)}, u32[]{:S(2)}) collective-permute-start(bf16[128,2048]{1,0:T(8,128)(2,1)S(1)} %get-tuple-element.364), channel_id=1, source_target_pairs={{8,0},{2,10},{16,8},{10,18},{24,16},{18,26},{28,24},{26,30},{20,28... | collective-permute-start | bytes 1572872 | tf_op jit(solution)/shard_map/cond/branch_1_fun/ppermute | solution.py:407
  142.8 11.7 %collective-permute-start.2 = (bf16[128,2048]{1,0:T(8,128)(2,1)S(1)}, bf16[128,2048]{1,0:T(8,128)(2,1)S(1)}, u32[]{:S(2)}, u32[]{:S(2)}) collective-permute-start(bf16[128,2048]{1,0:T(8,128)(2,1)S(1)} %get-tuple-element.365), channel_id=1, source_target_pairs={{8,0},{2,10},{16,8},{10,18},{24,16},{18,26},{28,24},{26,30},{20,28... | collective-permute-start | bytes 1572872 | tf_op jit(solution)/shard_map/cond/branch_1_fun/ppermute | solution.py:407
  150.1 10.1 %collective-permute-start.1 = (bf16[128,2048]{1,0:T(8,128)(2,1)S(1)}, bf16[128,2048]{1,0:T(8,128)(2,1)S(1)}, u32[]{:S(2)}, u32[]{:S(2)}) collective-permute-start(bf16[128,2048]{1,0:T(8,128)(2,1)S(1)} %add_convert_fusion.4), channel_id=1, source_target_pairs={{8,0},{2,10},{16,8},{10,18},{24,16},{18,26},{28,24},{26,30},{20,28... | collective-permute-start | bytes 1572872 | tf_op jit(solution)/shard_map/cond/branch_1_fun/ppermute | solution.py:407
  155.7 10.1 %collective-permute-start.4 = (bf16[128,2048]{1,0:T(8,128)(2,1)S(1)}, bf16[128,2048]{1,0:T(8,128)(2,1)S(1)}, u32[]{:S(2)}, u32[]{:S(2)}) collective-permute-start(bf16[128,2048]{1,0:T(8,128)(2,1)S(1)} %add_convert_fusion.3), channel_id=1, source_target_pairs={{8,0},{2,10},{16,8},{10,18},{24,16},{18,26},{28,24},{26,30},{20,28... | collective-permute-start | bytes 1572872 | tf_op jit(solution)/shard_map/cond/branch_1_fun/ppermute | solution.py:407
  160.3 11.1 %collective-permute-start.3 = (bf16[128,2048]{1,0:T(8,128)(2,1)S(1)}, bf16[128,2048]{1,0:T(8,128)(2,1)S(1)}, u32[]{:S(2)}, u32[]{:S(2)}) collective-permute-start(bf16[128,2048]{1,0:T(8,128)(2,1)S(1)} %add_convert_fusion.2), channel_id=1, source_target_pairs={{8,0},{2,10},{16,8},{10,18},{24,16},{18,26},{28,24},{26,30},{20,28... | collective-permute-start | bytes 1572872 | tf_op jit(solution)/shard_map/cond/branch_1_fun/ppermute | solution.py:407
  165.9 11.1 %collective-permute-start.6 = (bf16[128,2048]{1,0:T(8,128)(2,1)S(1)}, bf16[128,2048]{1,0:T(8,128)(2,1)S(1)}, u32[]{:S(2)}, u32[]{:S(2)}) collective-permute-start(bf16[128,2048]{1,0:T(8,128)(2,1)S(1)} %add_convert_fusion.1), channel_id=1, source_target_pairs={{8,0},{2,10},{16,8},{10,18},{24,16},{18,26},{28,24},{26,30},{20,28... | collective-permute-start | bytes 1572872 | tf_op jit(solution)/shard_map/cond/branch_1_fun/ppermute | solution.py:407
  190.8 57.2 %collective-permute-start.67 = (bf16[2048,1152]{1,0:T(8,128)(2,1)S(1)}, bf16[2048,1152]{1,0:T(8,128)(2,1)S(1)}, u32[]{:S(2)}, u32[]{:S(2)}) collective-permute-start(bf16[2048,1152]{1,0:T(8,128)(2,1)S(1)} %bitcast.193), channel_id=1, source_target_pairs={{0,2},{2,0},{4,6},{6,4},{8,10},{10,8},{12,14},{14,12},{16,18},{18,... | collective-permute-start | bytes 14155784 | tf_op jit(solution)/shard_map/ppermute | solution.py:401
  192.3 8.7 %collective-permute-start.59 = (bf16[128,2048]{1,0:T(8,128)(2,1)S(1)}, bf16[128,2048]{1,0:T(8,128)(2,1)S(1)}, u32[]{:S(2)}, u32[]{:S(2)}) collective-permute-start(bf16[128,2048]{1,0:T(8,128)(2,1)S(1)} %get-tuple-element.361), channel_id=1, source_target_pairs={{0,8},{10,2},{8,16},{18,10},{16,24},{26,18},{24,28},{30,26},{28,20... | collective-permute-start | bytes 1572872 | tf_op jit(solution)/shard_map/ppermute | solution.py:404
  200.0 8.6 %collective-permute-start.58 = (bf16[128,2048]{1,0:T(8,128)(2,1)S(1)}, bf16[128,2048]{1,0:T(8,128)(2,1)S(1)}, u32[]{:S(2)}, u32[]{:S(2)}) collective-permute-start(bf16[128,2048]{1,0:T(8,128)(2,1)S(1)} %collective-permute-done.57), channel_id=1, source_target_pairs={{0,8},{10,2},{8,16},{18,10},{16,24},{26,18},{24,28},{30,26},{28,20... | collective-permute-start | bytes 1572872 | tf_op jit(solution)/shard_map/ppermute | solution.py:404
  200.9 13.3 %collective-permute-start.61 = (bf16[128,2048]{1,0:T(8,128)(2,1)S(1)}, bf16[128,2048]{1,0:T(8,128)(2,1)S(1)}, u32[]{:S(2)}, u32[]{:S(2)}) collective-permute-start(bf16[128,2048]{1,0:T(8,128)(2,1)S(1)} %collective-permute-done.59), channel_id=1, source_target_pairs={{0,8},{10,2},{8,16},{18,10},{16,24},{26,18},{24,28},{30,26},{28,20... | collective-permute-start | bytes 1572872 | tf_op jit(solution)/shard_map/ppermute | solution.py:404
  208.6 11.2 %collective-permute-start.60 = (bf16[128,2048]{1,0:T(8,128)(2,1)S(1)}, bf16[128,2048]{1,0:T(8,128)(2,1)S(1)}, u32[]{:S(2)}, u32[]{:S(2)}) collective-permute-start(bf16[128,2048]{1,0:T(8,128)(2,1)S(1)} %collective-permute-done.58), channel_id=1, source_target_pairs={{0,8},{10,2},{8,16},{18,10},{16,24},{26,18},{24,28},{30,26},{28,20... | collective-permute-start | bytes 1572872 | tf_op jit(solution)/shard_map/ppermute | solution.py:404
  214.2 11.2 %collective-permute-start.71 = (bf16[128,2048]{1,0:T(8,128)(2,1)S(1)}, bf16[128,2048]{1,0:T(8,128)(2,1)S(1)}, u32[]{:S(2)}, u32[]{:S(2)}) collective-permute-start(bf16[128,2048]{1,0:T(8,128)(2,1)S(1)} %collective-permute-done.61), channel_id=1, source_target_pairs={{0,8},{10,2},{8,16},{18,10},{16,24},{26,18},{24,28},{30,26},{28,20... | collective-permute-start | bytes 1572872 | tf_op jit(solution)/shard_map/ppermute | solution.py:404
  219.8 11.2 %collective-permute-start.62 = (bf16[128,2048]{1,0:T(8,128)(2,1)S(1)}, bf16[128,2048]{1,0:T(8,128)(2,1)S(1)}, u32[]{:S(2)}, u32[]{:S(2)}) collective-permute-start(bf16[128,2048]{1,0:T(8,128)(2,1)S(1)} %collective-permute-done.60), channel_id=1, source_target_pairs={{0,8},{10,2},{8,16},{18,10},{16,24},{26,18},{24,28},{30,26},{28,20... | collective-permute-start | bytes 1572872 | tf_op jit(solution)/shard_map/ppermute | solution.py:404
  225.5 11.2 %collective-permute-start.72 = (bf16[128,2048]{1,0:T(8,128)(2,1)S(1)}, bf16[128,2048]{1,0:T(8,128)(2,1)S(1)}, u32[]{:S(2)}, u32[]{:S(2)}) collective-permute-start(bf16[128,2048]{1,0:T(8,128)(2,1)S(1)} %collective-permute-done.71), channel_id=1, source_target_pairs={{0,8},{10,2},{8,16},{18,10},{16,24},{26,18},{24,28},{30,26},{28,20... | collective-permute-start | bytes 1572872 | tf_op jit(solution)/shard_map/ppermute | solution.py:404
  232.1 10.2 %collective-permute-start.63 = (bf16[128,2048]{1,0:T(8,128)(2,1)S(1)}, bf16[128,2048]{1,0:T(8,128)(2,1)S(1)}, u32[]{:S(2)}, u32[]{:S(2)}) collective-permute-start(bf16[128,2048]{1,0:T(8,128)(2,1)S(1)} %bitcast.205), channel_id=1, source_target_pairs={{0,8},{10,2},{8,16},{18,10},{16,24},{26,18},{24,28},{30,26},{28,20... | collective-permute-start | bytes 1572872 | tf_op jit(solution)/shard_map/ppermute | solution.py:404
  233.6 14.4 %collective-permute-start.65 = (bf16[128,2048]{1,0:T(8,128)(2,1)S(1)}, bf16[128,2048]{1,0:T(8,128)(2,1)S(1)}, u32[]{:S(2)}, u32[]{:S(2)}) collective-permute-start(bf16[128,2048]{1,0:T(8,128)(2,1)S(1)} %collective-permute-done.64), channel_id=1, source_target_pairs={{0,8},{10,2},{8,16},{18,10},{16,24},{26,18},{24,28},{30,26},{28,20... | collective-permute-start | bytes 1572872 | tf_op jit(solution)/shard_map/ppermute | solution.py:404
  265.7 12.8 %collective-permute-start.70 = (bf16[128,2048]{1,0:T(8,128)(2,1)S(1)}, bf16[128,2048]{1,0:T(8,128)(2,1)S(1)}, u32[]{:S(2)}, u32[]{:S(2)}) collective-permute-start(bf16[128,2048]{1,0:T(8,128)(2,1)S(1)} %collective-permute-done.68), channel_id=1, source_target_pairs={{0,8},{10,2},{8,16},{18,10},{16,24},{26,18},{24,28},{30,26},{28,20... | collective-permute-start | bytes 1572872 | tf_op jit(solution)/shard_map/ppermute | solution.py:404
  272.9 11.2 %collective-permute-start.73 = (bf16[128,2048]{1,0:T(8,128)(2,1)S(1)}, bf16[128,2048]{1,0:T(8,128)(2,1)S(1)}, u32[]{:S(2)}, u32[]{:S(2)}) collective-permute-start(bf16[128,2048]{1,0:T(8,128)(2,1)S(1)} %collective-permute-done.69), channel_id=1, source_target_pairs={{0,8},{10,2},{8,16},{18,10},{16,24},{26,18},{24,28},{30,26},{28,20... | collective-permute-start | bytes 1572872 | tf_op jit(solution)/shard_map/ppermute | solution.py:404
  278.5 11.2 %collective-permute-start.74 = (bf16[128,2048]{1,0:T(8,128)(2,1)S(1)}, bf16[128,2048]{1,0:T(8,128)(2,1)S(1)}, u32[]{:S(2)}, u32[]{:S(2)}) collective-permute-start(bf16[128,2048]{1,0:T(8,128)(2,1)S(1)} %collective-permute-done.70), channel_id=1, source_target_pairs={{0,8},{10,2},{8,16},{18,10},{16,24},{26,18},{24,28},{30,26},{28,20... | collective-permute-start | bytes 1572872 | tf_op jit(solution)/shard_map/ppermute | solution.py:404
  308.3 11.1 %collective-permute-start.18 = (bf16[128,2048]{1,0:T(8,128)(2,1)}, bf16[128,2048]{1,0:T(8,128)(2,1)}, u32[]{:S(2)}, u32[]{:S(2)}) collective-permute-start(bf16[128,2048]{1,0:T(8,128)(2,1)} %add_convert_fusion.11), channel_id=1, source_target_pairs={{8,0},{2,10},{16,8},{10,18},{24,16},{18,26},{28,24},{26,30},{20,28... | collective-permute-start | bytes 1572872 | tf_op jit(solution)/shard_map/cond/branch_1_fun/ppermute | solution.py:407
  316.3 37.4 %collective-permute-start.25 = (bf16[2048,384]{1,0:T(8,128)(2,1)S(1)}, bf16[2048,384]{1,0:T(8,128)(2,1)S(1)}, u32[]{:S(2)}, u32[]{:S(2)}) collective-permute-start(bf16[2048,384]{1,0:T(8,128)(2,1)S(1)} %fusion.2), channel_id=1, source_target_pairs={{0,2},{2,0},{4,6},{6,4},{8,10},{10,8},{12,14},{14,12},{16,18},{18,... | collective-permute-start | bytes 4718600 | tf_op jit(solution)/shard_map/cond/branch_1_fun/ppermute | solution.py:401
  317.6 9.8 %collective-permute-start.20 = (bf16[128,2048]{1,0:T(8,128)(2,1)S(1)}, bf16[128,2048]{1,0:T(8,128)(2,1)S(1)}, u32[]{:S(2)}, u32[]{:S(2)}) collective-permute-start(bf16[128,2048]{1,0:T(8,128)(2,1)S(1)} %copy-done.56), channel_id=1, source_target_pairs={{8,0},{2,10},{16,8},{10,18},{24,16},{18,26},{28,24},{26,30},{20,28... | collective-permute-start | bytes 1572872 | tf_op jit(solution)/shard_map/cond/branch_1_fun/ppermute | solution.py:407
  323.3 32.4 %collective-permute-start.26 = (bf16[2048,768]{1,0:T(8,128)(2,1)S(1)}, bf16[2048,768]{1,0:T(8,128)(2,1)S(1)}, u32[]{:S(2)}, u32[]{:S(2)}) collective-permute-start(bf16[2048,768]{1,0:T(8,128)(2,1)S(1)} %fusion), channel_id=1, source_target_pairs={{0,2},{2,0},{4,6},{6,4},{8,10},{10,8},{12,14},{14,12},{16,18},{18,... | collective-permute-start | bytes 9437192 | tf_op jit(solution)/shard_map/cond/branch_1_fun/ppermute | solution.py:401
  330.0 9.8 %collective-permute-start.22 = (bf16[128,2048]{1,0:T(8,128)(2,1)S(1)}, bf16[128,2048]{1,0:T(8,128)(2,1)S(1)}, u32[]{:S(2)}, u32[]{:S(2)}) collective-permute-start(bf16[128,2048]{1,0:T(8,128)(2,1)S(1)} %add_convert_fusion.9), channel_id=1, source_target_pairs={{8,0},{2,10},{16,8},{10,18},{24,16},{18,26},{28,24},{26,30},{20,28... | collective-permute-start | bytes 1572872 | tf_op jit(solution)/shard_map/cond/branch_1_fun/ppermute | solution.py:407
  338.0 17.4 %collective-permute-start.21 = (bf16[128,2048]{1,0:T(8,128)(2,1)S(1)}, bf16[128,2048]{1,0:T(8,128)(2,1)S(1)}, u32[]{:S(2)}, u32[]{:S(2)}) collective-permute-start(bf16[128,2048]{1,0:T(8,128)(2,1)S(1)} %add_convert_fusion.8), channel_id=1, source_target_pairs={{8,0},{2,10},{16,8},{10,18},{24,16},{18,26},{28,24},{26,30},{20,28... | collective-permute-start | bytes 1572872 | tf_op jit(solution)/shard_map/cond/branch_1_fun/ppermute | solution.py:407
  340.0 12.1 %collective-permute-start.23 = (bf16[128,2048]{1,0:T(8,128)(2,1)S(1)}, bf16[128,2048]{1,0:T(8,128)(2,1)S(1)}, u32[]{:S(2)}, u32[]{:S(2)}) collective-permute-start(bf16[128,2048]{1,0:T(8,128)(2,1)S(1)} %add_convert_fusion.7), channel_id=1, source_target_pairs={{8,0},{2,10},{16,8},{10,18},{24,16},{18,26},{28,24},{26,30},{20,28... | collective-permute-start | bytes 1572872 | tf_op jit(solution)/shard_map/cond/branch_1_fun/ppermute | solution.py:407
  359.2 56.4 %collective-permute-start.77 = (bf16[16,64,768]{2,1,0:T(8,128)(2,1)}, bf16[16,64,768]{2,1,0:T(8,128)(2,1)}, u32[]{:S(2)}, u32[]{:S(2)}) collective-permute-start(bf16[16,64,768]{2,1,0:T(8,128)(2,1)} %get-tuple-element.307), channel_id=1, source_target_pairs={{0,1},{1,0},{2,3},{3,2},{4,5},{5,4},{6,7},{7,6},{8,9},{9,8},{10,11... | collective-permute-start | bytes 4718600 | tf_op jit(solution)/shard_map/ppermute | solution.py:475
  359.5 54.5 %collective-permute-start.76 = (bf16[16,64,384]{2,1,0:T(8,128)(2,1)}, bf16[16,64,384]{2,1,0:T(8,128)(2,1)}, u32[]{:S(2)}, u32[]{:S(2)}) collective-permute-start(bf16[16,64,384]{2,1,0:T(8,128)(2,1)} %get-tuple-element.305), channel_id=1, source_target_pairs={{0,1},{1,0},{2,3},{3,2},{4,5},{5,4},{6,7},{7,6},{8,9},{9,8},{10,11... | collective-permute-start | bytes 2359304 | tf_op jit(solution)/shard_map/ppermute | solution.py:475
  364.5 8.7 %collective-permute-start.27 = (bf16[128,2048]{1,0:T(8,128)(2,1)S(1)}, bf16[128,2048]{1,0:T(8,128)(2,1)S(1)}, u32[]{:S(2)}, u32[]{:S(2)}) collective-permute-start(bf16[128,2048]{1,0:T(8,128)(2,1)S(1)} %get-tuple-element.125), channel_id=1, source_target_pairs={{0,8},{10,2},{8,16},{18,10},{16,24},{26,18},{24,28},{30,26},{28,20... | collective-permute-start | bytes 1572872 | tf_op jit(solution)/shard_map/cond/branch_1_fun/ppermute | solution.py:404
  366.1 12.8 %collective-permute-start.29 = (bf16[128,2048]{1,0:T(8,128)(2,1)S(1)}, bf16[128,2048]{1,0:T(8,128)(2,1)S(1)}, u32[]{:S(2)}, u32[]{:S(2)}) collective-permute-start(bf16[128,2048]{1,0:T(8,128)(2,1)S(1)} %collective-permute-done.28), channel_id=1, source_target_pairs={{0,8},{10,2},{8,16},{18,10},{16,24},{26,18},{24,28},{30,26},{28,20... | collective-permute-start | bytes 1572872 | tf_op jit(solution)/shard_map/cond/branch_1_fun/ppermute | solution.py:404
  373.2 11.2 %collective-permute-start.30 = (bf16[128,2048]{1,0:T(8,128)(2,1)S(1)}, bf16[128,2048]{1,0:T(8,128)(2,1)S(1)}, u32[]{:S(2)}, u32[]{:S(2)}) collective-permute-start(bf16[128,2048]{1,0:T(8,128)(2,1)S(1)} %collective-permute-done.27), channel_id=1, source_target_pairs={{0,8},{10,2},{8,16},{18,10},{16,24},{26,18},{24,28},{30,26},{28,20... | collective-permute-start | bytes 1572872 | tf_op jit(solution)/shard_map/cond/branch_1_fun/ppermute | solution.py:404
  378.8 11.2 %collective-permute-start.31 = (bf16[128,2048]{1,0:T(8,128)(2,1)S(1)}, bf16[128,2048]{1,0:T(8,128)(2,1)S(1)}, u32[]{:S(2)}, u32[]{:S(2)}) collective-permute-start(bf16[128,2048]{1,0:T(8,128)(2,1)S(1)} %collective-permute-done.29), channel_id=1, source_target_pairs={{0,8},{10,2},{8,16},{18,10},{16,24},{26,18},{24,28},{30,26},{28,20... | collective-permute-start | bytes 1572872 | tf_op jit(solution)/shard_map/cond/branch_1_fun/ppermute | solution.py:404
  384.5 11.2 %collective-permute-start.32 = (bf16[128,2048]{1,0:T(8,128)(2,1)S(1)}, bf16[128,2048]{1,0:T(8,128)(2,1)S(1)}, u32[]{:S(2)}, u32[]{:S(2)}) collective-permute-start(bf16[128,2048]{1,0:T(8,128)(2,1)S(1)} %collective-permute-done.30), channel_id=1, source_target_pairs={{0,8},{10,2},{8,16},{18,10},{16,24},{26,18},{24,28},{30,26},{28,20... | collective-permute-start | bytes 1572872 | tf_op jit(solution)/shard_map/cond/branch_1_fun/ppermute | solution.py:404
  390.1 11.2 %collective-permute-start.33 = (bf16[128,2048]{1,0:T(8,128)(2,1)S(1)}, bf16[128,2048]{1,0:T(8,128)(2,1)S(1)}, u32[]{:S(2)}, u32[]{:S(2)}) collective-permute-start(bf16[128,2048]{1,0:T(8,128)(2,1)S(1)} %collective-permute-done.31), channel_id=1, source_target_pairs={{0,8},{10,2},{8,16},{18,10},{16,24},{26,18},{24,28},{30,26},{28,20... | collective-permute-start | bytes 1572872 | tf_op jit(solution)/shard_map/cond/branch_1_fun/ppermute | solution.py:404
  395.7 11.2 %collective-permute-start.34 = (bf16[128,2048]{1,0:T(8,128)(2,1)S(1)}, bf16[128,2048]{1,0:T(8,128)(2,1)S(1)}, u32[]{:S(2)}, u32[]{:S(2)}) collective-permute-start(bf16[128,2048]{1,0:T(8,128)(2,1)S(1)} %collective-permute-done.32), channel_id=1, source_target_pairs={{0,8},{10,2},{8,16},{18,10},{16,24},{26,18},{24,28},{30,26},{28,20... | collective-permute-start | bytes 1572872 | tf_op jit(solution)/shard_map/cond/branch_1_fun/ppermute | solution.py:404
  420.4 107.3 %all-to-all-start.3 = ((bf16[16,64,1152]{2,1,0:T(8,128)(2,1)}), bf16[16,64,1152]{2,1,0:T(8,128)(2,1)}, u32[]{:S(2)}, u32[]{:S(2)}) async-start(bf16[16,64,1152]{2,1,0:T(8,128)(2,1)} %pad_maximum_fusion.9), calls=%async_computation.3 | async-start | bytes 4718592 | tf_op jit(solution)/shard_map/all_to_all | solution.py:471
  451.9 30.7 %collective-permute-start.36 = (bf16[128,2048]{1,0:T(8,128)(2,1)}, bf16[128,2048]{1,0:T(8,128)(2,1)S(1)}, u32[]{:S(2)}, u32[]{:S(2)}) collective-permute-start(bf16[128,2048]{1,0:T(8,128)(2,1)} %get-tuple-element.374), channel_id=1, source_target_pairs={{8,0},{2,10},{16,8},{10,18},{24,16},{18,26},{28,24},{26,30},{20,28... | collective-permute-start | bytes 1572872 | tf_op jit(solution)/shard_map/cond/branch_1_fun/ppermute | solution.py:407
  453.3 34.9 %collective-permute-start.38 = (bf16[128,2048]{1,0:T(8,128)(2,1)}, bf16[128,2048]{1,0:T(8,128)(2,1)S(1)}, u32[]{:S(2)}, u32[]{:S(2)}) collective-permute-start(bf16[128,2048]{1,0:T(8,128)(2,1)} %get-tuple-element.375), channel_id=1, source_target_pairs={{8,0},{2,10},{16,8},{10,18},{24,16},{18,26},{28,24},{26,30},{20,28... | collective-permute-start | bytes 1572872 | tf_op jit(solution)/shard_map/cond/branch_1_fun/ppermute | solution.py:407
  483.8 16.6 %collective-permute-start.37 = (bf16[128,2048]{1,0:T(8,128)(2,1)S(1)}, bf16[128,2048]{1,0:T(8,128)(2,1)S(1)}, u32[]{:S(2)}, u32[]{:S(2)}) collective-permute-start(bf16[128,2048]{1,0:T(8,128)(2,1)S(1)} %add_convert_fusion.18), channel_id=1, source_target_pairs={{8,0},{2,10},{16,8},{10,18},{24,16},{18,26},{28,24},{26,30},{20,28... | collective-permute-start | bytes 1572872 | tf_op jit(solution)/shard_map/cond/branch_1_fun/ppermute | solution.py:407
  489.4 12.9 %collective-permute-start.40 = (bf16[128,2048]{1,0:T(8,128)(2,1)S(1)}, bf16[128,2048]{1,0:T(8,128)(2,1)S(1)}, u32[]{:S(2)}, u32[]{:S(2)}) collective-permute-start(bf16[128,2048]{1,0:T(8,128)(2,1)S(1)} %add_convert_fusion.17), channel_id=1, source_target_pairs={{8,0},{2,10},{16,8},{10,18},{24,16},{18,26},{28,24},{26,30},{20,28... | collective-permute-start | bytes 1572872 | tf_op jit(solution)/shard_map/cond/branch_1_fun/ppermute | solution.py:407
  500.3 16.9 %collective-permute-start.41 = (bf16[2048,384]{0,1:T(8,128)(2,1)S(1)}, bf16[2048,384]{0,1:T(8,128)(2,1)S(1)}, u32[]{:S(2)}, u32[]{:S(2)}) collective-permute-start(bf16[2048,384]{0,1:T(8,128)(2,1)S(1)} %pad_maximum_fusion.1), channel_id=1, source_target_pairs={{0,2},{2,0},{4,6},{6,4},{8,10},{10,8},{12,14},{14,12},{16,18},{18,... | collective-permute-start | bytes 4718600 | tf_op jit(solution)/shard_map/cond/branch_1_fun/ppermute | solution.py:401
  502.4 13.8 %collective-permute-start.43 = (bf16[128,2048]{1,0:T(8,128)(2,1)S(1)}, bf16[128,2048]{1,0:T(8,128)(2,1)S(1)}, u32[]{:S(2)}, u32[]{:S(2)}) collective-permute-start(bf16[128,2048]{1,0:T(8,128)(2,1)S(1)} %add_convert_fusion.15), channel_id=1, source_target_pairs={{8,0},{2,10},{16,8},{10,18},{24,16},{18,26},{28,24},{26,30},{20,28... | collective-permute-start | bytes 1572872 | tf_op jit(solution)/shard_map/cond/branch_1_fun/ppermute | solution.py:407
  530.5 18.1 %collective-permute-start.10 = (bf16[128,2048]{1,0:T(8,128)(2,1)}, bf16[128,2048]{1,0:T(8,128)(2,1)}, u32[]{:S(2)}, u32[]{:S(2)}) collective-permute-start(bf16[128,2048]{1,0:T(8,128)(2,1)} %get-tuple-element.385), channel_id=1, source_target_pairs={{8,0},{2,10},{16,8},{10,18},{24,16},{18,26},{28,24},{26,30},{20,28... | collective-permute-start | bytes 1572872 | tf_op jit(solution)/shard_map/cond/branch_1_fun/ppermute | solution.py:407
  532.2 12.5 %collective-permute-start.8 = (bf16[128,2048]{1,0:T(8,128)(2,1)}, bf16[128,2048]{1,0:T(8,128)(2,1)}, u32[]{:S(2)}, u32[]{:S(2)}) collective-permute-start(bf16[128,2048]{1,0:T(8,128)(2,1)} %get-tuple-element.384), channel_id=1, source_target_pairs={{8,0},{2,10},{16,8},{10,18},{24,16},{18,26},{28,24},{26,30},{20,28... | collective-permute-start | bytes 1572872 | tf_op jit(solution)/shard_map/cond/branch_1_fun/ppermute | solution.py:407
  534.4 18.8 %collective-permute-start.11 = (bf16[1040,384]{1,0:T(8,128)(2,1)S(1)}, bf16[1040,384]{1,0:T(8,128)(2,1)S(1)}, u32[]{:S(2)}, u32[]{:S(2)}) collective-permute-start(bf16[1040,384]{1,0:T(8,128)(2,1)S(1)} %pad_maximum_fusion.3), channel_id=1, source_target_pairs={{0,1},{1,0},{2,3},{3,2},{4,5},{5,4},{6,7},{7,6},{8,9},{9,8},{10,11... | collective-permute-start | bytes 2396168 | tf_op jit(solution)/shard_map/cond/branch_1_fun/ppermute | solution.py:475
  546.9 14.9 %collective-permute-start.9 = (bf16[128,2048]{1,0:T(8,128)(2,1)}, bf16[128,2048]{1,0:T(8,128)(2,1)}, u32[]{:S(2)}, u32[]{:S(2)}) collective-permute-start(bf16[128,2048]{1,0:T(8,128)(2,1)} %add_convert_fusion.23), channel_id=1, source_target_pairs={{8,0},{2,10},{16,8},{10,18},{24,16},{18,26},{28,24},{26,30},{20,28... | collective-permute-start | bytes 1572872 | tf_op jit(solution)/shard_map/cond/branch_1_fun/ppermute | solution.py:407
  550.7 13.8 %collective-permute-start.13 = (bf16[128,2048]{1,0:T(8,128)(2,1)}, bf16[128,2048]{1,0:T(8,128)(2,1)}, u32[]{:S(2)}, u32[]{:S(2)}) collective-permute-start(bf16[128,2048]{1,0:T(8,128)(2,1)} %add_convert_fusion.22), channel_id=1, source_target_pairs={{8,0},{2,10},{16,8},{10,18},{24,16},{18,26},{28,24},{26,30},{20,28... | collective-permute-start | bytes 1572872 | tf_op jit(solution)/shard_map/cond/branch_1_fun/ppermute | solution.py:407
  554.8 51.9 %all-to-all-start = ((bf16[16,80,384]{2,1,0:T(8,128)(2,1)}), bf16[16,80,384]{2,1,0:T(8,128)(2,1)}, u32[]{:S(2)}, u32[]{:S(2)}) async-start(bf16[16,80,384]{2,1,0:T(8,128)(2,1)} %pad_maximum_fusion.2), calls=%async_computation | async-start | bytes 1966080 | tf_op jit(solution)/shard_map/cond/branch_1_fun/all_to_all | solution.py:471
  563.2 26.0 %collective-permute-start.12 = (bf16[128,2048]{1,0:T(8,128)(2,1)S(1)}, bf16[128,2048]{1,0:T(8,128)(2,1)S(1)}, u32[]{:S(2)}, u32[]{:S(2)}) collective-permute-start(bf16[128,2048]{1,0:T(8,128)(2,1)S(1)} %add_convert_fusion.21), channel_id=1, source_target_pairs={{8,0},{2,10},{16,8},{10,18},{24,16},{18,26},{28,24},{26,30},{20,28... | collective-permute-start | bytes 1572872 | tf_op jit(solution)/shard_map/cond/branch_1_fun/ppermute | solution.py:407
  565.8 29.0 %collective-permute-start.15 = (bf16[128,2048]{1,0:T(8,128)(2,1)S(1)}, bf16[128,2048]{1,0:T(8,128)(2,1)S(1)}, u32[]{:S(2)}, u32[]{:S(2)}) collective-permute-start(bf16[128,2048]{1,0:T(8,128)(2,1)S(1)} %add_convert_fusion.20), channel_id=1, source_target_pairs={{8,0},{2,10},{16,8},{10,18},{24,16},{18,26},{28,24},{26,30},{20,28... | collective-permute-start | bytes 1572872 | tf_op jit(solution)/shard_map/cond/branch_1_fun/ppermute | solution.py:407
  590.4 14.1 %collective-permute-start.14 = (bf16[128,2048]{1,0:T(8,128)(2,1)S(1)}, bf16[128,2048]{1,0:T(8,128)(2,1)S(1)}, u32[]{:S(2)}, u32[]{:S(2)}) collective-permute-start(bf16[128,2048]{1,0:T(8,128)(2,1)S(1)} %add_convert_fusion.19), channel_id=1, source_target_pairs={{8,0},{2,10},{16,8},{10,18},{24,16},{18,26},{28,24},{26,30},{20,28... | collective-permute-start | bytes 1572872 | tf_op jit(solution)/shard_map/cond/branch_1_fun/ppermute | solution.py:407
  594.9 9.6 %collective-permute-start.16 = (bf16[128,2048]{1,0:T(8,128)(2,1)S(1)}, bf16[128,2048]{1,0:T(8,128)(2,1)S(1)}, u32[]{:S(2)}, u32[]{:S(2)}) collective-permute-start(bf16[128,2048]{1,0:T(8,128)(2,1)S(1)} %collective-permute-done.15), channel_id=1, source_target_pairs={{0,2},{2,0},{4,6},{6,4},{8,10},{10,8},{12,14},{14,12},{16,18},{18,... | collective-permute-start | bytes 1572872 | tf_op jit(solution)/shard_map/cond/branch_1_fun/ppermute | solution.py:401
  (91 other events, 850.5 us)

commit v6 on v5

--- a/solution.py
+++ b/solution.py
@@ -790,7 +790,7 @@
         attention_back, attn_grad, attn_a, attn_b, *raw
     )
 
-    def attention_grads(input_terms, half_grads, grad_all, normed_attn, attn_pair):
+    def attention_grads(input_terms, half_grads, grad_all, normed_attn, attn_pair, other_gains):
         ready = {}
 
         def weight_grads(marks):
@@ -804,21 +804,26 @@
                 jnp.sum(after(input_terms, marks[1]).astype(f32) * normed_attn.astype(f32), axis=0)
                 / attn_gain
             )
-            ready["grads"] = add(keep, ring.swap(give))
-            return ready["grads"], ready["gain"]
+            ready["parts"] = halves(
+                add(keep, ring.swap(give)),
+                jnp.concatenate([ready["gain"], other_gains]),
+                fsdp_rank,
+                ctx_size,
+            )
+            return ready["gain"]
 
         summed, _ = ring.scatter_sum(
             lambda i: block_rows(input_terms, i), {last_hop: weight_grads}
         )
-        return summed, ready["grads"], ready["gain"]
-
-    normed_attn_grad, attn_grads, attn_gain_part = fenced(
-        attention_grads, input_terms, half_grads, grad_all, normed_attn, attn_pair
-    )
-    gains = jnp.concatenate([attn_gain_part, query_gain_part, key_gain_part, mlp_gain_part])
-
-    def out_and_home(out_terms, attn_grads, gains, mlp_rows, summed_grad, hidden_grad, inputs32):
-        own, away, lines = halves(attn_grads, gains, fsdp_rank, ctx_size)
+        return summed, ready["parts"]
+
+    normed_attn_grad, attn_parts = fenced(
+        attention_grads, input_terms, half_grads, grad_all, normed_attn, attn_pair,
+        jnp.concatenate([query_gain_part, key_gain_part, mlp_gain_part]),
+    )
+
+    def out_and_home(out_terms, attn_parts, mlp_rows, summed_grad, hidden_grad, inputs32):
+        own, away, lines = attn_parts
         ready = {}
 
         def other_rows(_):
@@ -852,9 +857,9 @@
         unpack(marks)
         return summed, ready["rows"], ready["input"], ready["mlp"]
 
-    attn_grads, mlp_rows = lax.optimization_barrier((attn_grads, mlp_rows))
+    attn_parts, mlp_rows = lax.optimization_barrier((attn_parts, mlp_rows))
     mlp_out, attn_home, input_grad, mlp_grads = fenced(
-        out_and_home, out_terms, attn_grads, gains, mlp_rows, normed_attn_grad,
+        out_and_home, out_terms, attn_parts, mlp_rows, normed_attn_grad,
         hidden_grad, inputs32,
     )
     block_out = (hidden_one + mlp_out).astype(bf16)

time: 623 us -> 627 us (level)
  other arithmetic: 76.4 us -> 91 us
  waiting for transfers between devices: 308 us -> 298 us
    ppermute x28, waiting for transfers between devices: 125 us -> 113 us  [home(): return lax.ppermute(field, 'ctx', self.home_pairs)]
    unnamed x128 -> x126, local copies, waits for them, and re-layouts: 17.2 us -> 17.2 us
  transfers between devices with their start and end apart: 82 -> 82, of which waited for: 51 -> 51; matrix products, arithmetic and copies ran while one was open for 22% -> 24% of each run, Pallas kernels for 5% -> 5%
where the time goes in v6:
time: 627 us; the launch traced here: 620 us
  waiting for transfers between devices  298 us (48%)
  other arithmetic  91 us (15%)
  starting transfers between devices  89.6 us (14%)
  matrix products  57.5 us (9%)
  local copies, waits for them, and re-layouts  49.2 us (8%)
  Pallas kernels  30.3 us (5%)
    ppermute x28, waiting for transfers between devices, out(): return lax.ppermute(field, 'ctx', self.out_pairs)  133 us
    ppermute x28, waiting for transfers between devices, home(): return lax.ppermute(field, 'ctx', self.home_pairs)  113 us
    ppermute x28, starting transfers between devices, home(): return lax.ppermute(field, 'ctx', self.home_pairs)  43.3 us
    all_to_all x4, waiting for transfers between devices, spread(): lax.all_to_all(rows_block, 'ctx', split_axis=0, concat_axis=0, tiled=False)  26.6 us
    dot_general x6, matrix products, dot_tn(): lax.dot_general(left, right, (((0,), (0,)), ((), ())), preferred_element_...  23.5 us
    all_to_all x4, starting transfers between devices, spread(): lax.all_to_all(rows_block, 'ctx', split_axis=0, concat_axis=0, tiled=False)  21.5 us
    convert_element_type x20, other arithmetic, scatter_hops(): total = (term(index).astype(f32) + held.astype(f32)).astype(bf16)  19.5 us
    dot_general x5, matrix products, dot_nt(): lax.dot_general(left, right, (((1,), (1,)), ((), ())), preferred_element_...  18.8 us
  transfers between devices with their start and end apart: 82, of which 51 were waited for; matrix products, arithmetic and copies ran while one was open for 24% of the time, Pallas kernels for 5%

profile of v6, /device:TPU:9, one launch (start us, length us, event | category | flops | bytes accessed | tf_op | source)
XLA Modules:
  0.0 620.1 jit_solution(13450976193495790674)
XLA Ops:
  6.8 6.0 all-to-all-start.1
  14.3 23.7 %collective-permute-done.48.refs_1_ = bf16[128,2048]{1,0:T(8,128)(2,1)S(1)} collective-permute-done((bf16[128,2048]{1,0:T(8,128)(2,1)S(1)}, bf16[128,2048]{1,0:T(8,128)(2,1)S(1)}, u32[]{:S(2)}, u32[]{:S(2)}) %collective-permute-start.48) | collective-permute-done | bytes 524320 | tf_op jit(solution)/shard_map/ppermute | solution.py:404
  38.0 5.6 collective-permute-done.49.refs_2_
  43.6 5.6 collective-permute-done.50.refs_3_
  50.6 3.7 fusion.36
  56.8 3.7 collective-permute-done.52.refs_5_
  60.5 7.1 %collective-permute-done.46 = bf16[16,64,384]{2,1,0:T(8,128)(2,1)S(1)} collective-permute-done((bf16[16,64,384]{2,1,0:T(8,128)(2,1)}, bf16[16,64,384]{2,1,0:T(8,128)(2,1)S(1)}, u32[]{:S(2)}, u32[]{:S(2)}) %collective-permute-start.46) | collective-permute-done | bytes 786464 | tf_op jit(solution)/shard_map/ppermute | solution.py:475
  75.4 4.6 all-to-all-start.2
  84.4 4.6 project.1
  94.0 10.6 %attend.1 = (bf16[1024,128]{1,0:T(8,128)(2,1)S(1)}, bf16[1024,128]{1,0:T(8,128)(2,1)S(1)}, f32[1,2048]{1,0:T(1,128)S(1)}, bf16[2048,128]{1,0:T(8,128)(2,1)}, bf1...) custom-call(s32[32]{0:T(128)S(1)} %select_reduce_fusion.key_pos, s32[32]{0:T(128)S(1)} %iota.30.query_table.pos_table, ...), custom_call_target="tpu_custom_call" | custom-call | flops 2147483648 | bytes 7340032 | tf_op jit(solution)/shard_map/attend/pallas_call | solution.py:200
  104.7 26.6 %all-to-all-done.2 = bf16[16,64,1152]{2,1,0:T(8,128)(2,1)} async-done(((bf16[16,64,1152]{2,1,0:T(8,128)(2,1)}), bf16[16,64,1152]{2,1,0:T(8,128)(2,1)}, u32[]{:S(2)}, u32[]{:S(2)}) %all-to-all-start.2) | async-done | bytes 2359328 | tf_op jit(solution)/shard_map/all_to_all | solution.py:471
  134.7 3.3 convolution_convert_fusion.9
  138.0 49.5 %conditional.6 = (f32[128,2048]{1,0:T(8,128)S(1)}) conditional(s32[]{:T(128)} %convert_element_type.450, () %tuple.125, bf16[1024,2048]{1,0:T(8,128)(2,1)} %convolution_convert_fusion.9), branch_computations={%region_3.4_spmd, %region_4.5_spmd} | conditional | flops 6553600 | bytes 46137700 | solution.py:561
  139.5 3.4 collective-permute-start
  142.9 6.1 collective-permute-done
  171.6 5.5 collective-permute-done.6
  180.3 6.6 %collective-permute-done.5 = bf16[128,2048]{1,0:T(8,128)(2,1)S(1)} collective-permute-done((bf16[128,2048]{1,0:T(8,128)(2,1)S(1)}, bf16[128,2048]{1,0:T(8,128)(2,1)S(1)}, u32[]{:S(2)}, u32[]{:S(2)}) %collective-permute-start.5) | collective-permute-done | bytes 524320 | tf_op jit(solution)/shard_map/cond/branch_1_fun/ppermute | solution.py:407
  192.3 7.7 %collective-permute-done.57 = bf16[128,2048]{1,0:T(8,128)(2,1)S(1)} collective-permute-done((bf16[128,2048]{1,0:T(8,128)(2,1)S(1)}, bf16[128,2048]{1,0:T(8,128)(2,1)S(1)}, u32[]{:S(2)}, u32[]{:S(2)}) %collective-permute-start.57) | collective-permute-done | bytes 524320 | tf_op jit(solution)/shard_map/ppermute | solution.py:401
  200.9 7.7 %collective-permute-done.58 = bf16[128,2048]{1,0:T(8,128)(2,1)S(1)} collective-permute-done((bf16[128,2048]{1,0:T(8,128)(2,1)S(1)}, bf16[128,2048]{1,0:T(8,128)(2,1)S(1)}, u32[]{:S(2)}, u32[]{:S(2)}) %collective-permute-start.58) | collective-permute-done | bytes 524320 | tf_op jit(solution)/shard_map/ppermute | solution.py:404
  208.6 5.6 collective-permute-done.61
  214.2 5.6 collective-permute-done.60
  220.0 5.5 collective-permute-done.71
  225.5 5.6 collective-permute-done.62
  236.8 5.6 collective-permute-done.63
  243.3 4.6 collective-permute-done.65
  252.5 3.1 pad_maximum_fusion.4
  257.4 3.6 copy-done.10
  261.0 3.4 fusion.15
  265.7 3.4 fusion.23
  272.9 5.6 collective-permute-done.70
  278.7 5.4 collective-permute-done.73
  284.1 5.6 collective-permute-done.74
  289.8 3.4 fusion.53
  297.9 60.9 %conditional.7 = (f32[128,2048]{1,0:T(8,128)S(1)}, bf16[2048]{0:T(1024)(128)(2,1)S(1)}, bf16[16,64,384]{2,1,0:T(8,128)(2,1)}, bf16[16,64,384]{2,1,0:T(8,128)(2,1...) conditional(s32[]{:T(128)} %convert_element_type.450, () %tuple.136, ...), branch_computations={%region_6.7_spmd, %region_7.10_spmd} | conditional | flops 13722978304 | bytes 202814128 | solution.py:561
  300.4 5.6 convolution_convert_fusion.2
  311.6 4.7 fusion.2
  319.3 3.9 fusion
  330.3 3.6 collective-permute-done.19
  334.0 3.9 fusion.1
  343.2 8.8 %collective-permute-done.23 = bf16[128,2048]{1,0:T(8,128)(2,1)S(1)} collective-permute-done((bf16[128,2048]{1,0:T(8,128)(2,1)S(1)}, bf16[128,2048]{1,0:T(8,128)(2,1)S(1)}, u32[]{:S(2)}, u32[]{:S(2)}) %collective-permute-start.23) | collective-permute-done | bytes 524320 | tf_op jit(solution)/shard_map/cond/branch_1_fun/ppermute | solution.py:407
  363.6 44.1 %conditional.8 = (bf16[1024,2048]{1,0:T(8,128)(2,1)}, bf16[1024,2048]{1,0:T(8,128)(2,1)S(1)}) conditional(s32[]{:T(128)} %convert_element_type.450, () %tuple.135, (bf16[128,2048]{1,0:T(8,128)(2,1)S(1)}, bf16[1024,768]{1,0:T(8,128)(2,1)S(1)}, bf16[2048,768]{1,0:T(8,128)(2,1)S(1)}) %tuple.223), branch_computations={%region_11.12_spmd, %region_12.13_spmd} | conditional | flops 3223322624 | bytes 34079056 | solution.py:561
  366.4 6.7 %collective-permute-done.27 = bf16[128,2048]{1,0:T(8,128)(2,1)S(1)} collective-permute-done((bf16[128,2048]{1,0:T(8,128)(2,1)S(1)}, bf16[128,2048]{1,0:T(8,128)(2,1)S(1)}, u32[]{:S(2)}, u32[]{:S(2)}) %collective-permute-start.27) | collective-permute-done | bytes 524320 | tf_op jit(solution)/shard_map/cond/branch_1_fun/ppermute | solution.py:404
  375.0 3.8 collective-permute-done.29
  378.9 5.5 collective-permute-done.30
  384.5 3.7 convolution_convert_fusion.5
  391.0 4.6 collective-permute-done.32
  397.4 3.8 collective-permute-done.33
  402.1 4.8 collective-permute-done.34
  407.7 4.9 convolution_convert_fusion.11
  419.7 4.9 all-to-all-start.3
  424.7 22.5 %conditional.9 = (bf16[1024,512]{1,0:T(8,128)(2,1)}, bf16[1024,2048]{1,0:T(8,128)(2,1)S(1)}, f32[128]{0:T(128)S(1)}, f32[128]{0:T(128)S(1)}) conditional(s32[]{:T(128)} %convert_element_type.450, () %tuple.156, (s32[32]{0:T(128)S(1)}, s32[32]{0:T(128)S(1)}, s32[32]{0:T(128)S(1)}, f32[1024,512]{1,0:T(8,128)}, f32[1024,384]{1,0:T(8,128)}, ...), branch_computations={%region_13.14_spmd, %region_14.15_spmd} | conditional | flops 7522484224 | bytes 34078820 | solution.py:561
  424.9 15.1 %attend_back.1 = (bf16[1024,384]{1,0:T(8,128)(2,1)S(1)}, bf16[1024,384]{1,0:T(8,128)(2,1)S(1)}, f32[1,128]{1,0:T(1,128)S(1)}, f32[1,128]{1,0:T(1,128)S(1)}) custom-call(s32[32]{0:T(128)S(1)} %get-tuple-element.142.key_pos, s32[32]{0:T(128)S(1)} %get-tuple-element.144.pos_table, s32[32]{0:T(128)S(1)} %get-tuple-element.144.pos_table, ...), custom_call_target="tpu_custom_call" | custom-call | flops 5368709120 | bytes 10485760 | tf_op jit(solution)/shard_map/cond/branch_1_fun/attend_back/pallas_call | solution.py:315
  443.6 3.6 convolution_convert_fusion.6
  447.3 86.7 %conditional.10 = (f32[128,2048]{1,0:T(8,128)}, bf16[16,64,384]{2,1,0:T(8,128)(2,1)S(1)}, bf16[1040,384]{1,0:T(8,128)(2,1)}, bf16[16,384]{1,0:T(8,128)(2,1)}) conditional(s32[]{:T(128)} %convert_element_type.450, () %tuple.155, (bf16[1024,2048]{1,0:T(8,128)(2,1)S(1)}, bf16[1024,2048]{1,0:T(8,128)(2,1)}, f32[2048]{0:T(1024)S(1)}, s32[]{:T(128)}, ...), branch_computations={%region_15.16_spmd, %region_16.18_spmd} | conditional | flops 3252525056 | bytes 131697160 | solution.py:561
  452.8 29.1 %collective-permute-done.36 = bf16[128,2048]{1,0:T(8,128)(2,1)} collective-permute-done((bf16[128,2048]{1,0:T(8,128)(2,1)}, bf16[128,2048]{1,0:T(8,128)(2,1)}, u32[]{:S(2)}, u32[]{:S(2)}) %collective-permute-start.36) | collective-permute-done | bytes 524320 | tf_op jit(solution)/shard_map/cond/branch_1_fun/ppermute | solution.py:407
  490.8 4.9 fusion.5
  495.8 3.6 fusion.6
  509.5 5.4 collective-permute-done.39
  521.8 3.5 add_convert_fusion.13
  533.9 76.9 %conditional.11 = (f32[128,2048]{1,0:T(8,128)}, bf16[16,80,384]{2,1,0:T(8,128)(2,1)}, f32[64,6144]{1,0:T(8,128)}, f32[64,6144]{1,0:T(8,128)}, f32[64,6144]{1,0:T(8,128)}, /*index=5*/f32[1,128,2048]{2,1,0:T(8,128)}) conditional(s32[]{:T(128)} %convert_element_type.450, () %tuple.134, (bf16[1024,2048]{1,0:T(8,128)(2,1)}, ...), branch_computations={%region_18.19_spmd, %region_19.22_spmd} | conditional | flops 14180736 | bytes 68670928 | solution.py:561
  536.8 6.8 %collective-permute-done.8 = bf16[128,2048]{1,0:T(8,128)(2,1)S(1)} collective-permute-done((bf16[128,2048]{1,0:T(8,128)(2,1)S(1)}, bf16[128,2048]{1,0:T(8,128)(2,1)S(1)}, u32[]{:S(2)}, u32[]{:S(2)}) %collective-permute-start.8) | collective-permute-done | bytes 524320 | tf_op jit(solution)/shard_map/cond/branch_1_fun/ppermute | solution.py:407
  552.5 4.0 collective-permute-done.11
  558.7 6.0 all-to-all-start
  571.5 20.7 %collective-permute-done.12 = bf16[128,2048]{1,0:T(8,128)(2,1)S(1)} collective-permute-done((bf16[128,2048]{1,0:T(8,128)(2,1)S(1)}, bf16[128,2048]{1,0:T(8,128)(2,1)S(1)}, u32[]{:S(2)}, u32[]{:S(2)}) %collective-permute-start.12) | collective-permute-done | bytes 524320 | tf_op jit(solution)/shard_map/cond/branch_1_fun/ppermute | solution.py:407
  (422 shorter events, 231.9 us)
Async XLA Ops:
  6.8 42.5 %all-to-all-start.1 = ((bf16[16,64,384]{2,1,0:T(8,128)(2,1)}), bf16[16,64,384]{2,1,0:T(8,128)(2,1)}, u32[]{:S(2)}, u32[]{:S(2)}) async-start(bf16[16,64,384]{2,1,0:T(8,128)(2,1)} %pad_maximum_fusion.18), calls=%async_computation.1 | async-start | bytes 1572864 | tf_op jit(solution)/shard_map/all_to_all | solution.py:471
  12.8 25.2 %collective-permute-start.48 = (bf16[128,2048]{1,0:T(8,128)(2,1)S(1)}, bf16[128,2048]{1,0:T(8,128)(2,1)S(1)}, u32[]{:S(2)}, u32[]{:S(2)}) collective-permute-start(bf16[128,2048]{1,0:T(8,128)(2,1)S(1)} %bitcast.190), channel_id=1, source_target_pairs={{0,8},{10,2},{8,16},{18,10},{16,24},{26,18},{24,28},{30,26},{28,20... | collective-permute-start | bytes 1572872 | tf_op jit(solution)/shard_map/ppermute | solution.py:404
  12.9 30.7 %collective-permute-start.49 = (bf16[128,2048]{1,0:T(8,128)(2,1)S(1)}, bf16[128,2048]{1,0:T(8,128)(2,1)S(1)}, u32[]{:S(2)}, u32[]{:S(2)}) collective-permute-start(bf16[128,2048]{1,0:T(8,128)(2,1)S(1)} %collective-permute-done.45), channel_id=1, source_target_pairs={{0,8},{10,2},{8,16},{18,10},{16,24},{26,18},{24,28},{30,26},{28,20... | collective-permute-start | bytes 1572872 | tf_op jit(solution)/shard_map/ppermute | solution.py:404
  38.0 11.2 %collective-permute-start.50 = (bf16[128,2048]{1,0:T(8,128)(2,1)S(1)}, bf16[128,2048]{1,0:T(8,128)(2,1)S(1)}, u32[]{:S(2)}, u32[]{:S(2)}) collective-permute-start(bf16[128,2048]{1,0:T(8,128)(2,1)S(1)} %collective-permute-done.48.refs_1_), channel_id=1, source_target_pairs={{0,8},{10,2},{8,16},{18,10},{16,24},{26,18},{24,28},{30,26},{28,20... | collective-permute-start | bytes 1572872 | tf_op jit(solution)/shard_map/ppermute | solution.py:404
  43.6 13.1 %collective-permute-start.51 = (bf16[128,2048]{1,0:T(8,128)(2,1)S(1)}, bf16[128,2048]{1,0:T(8,128)(2,1)S(1)}, u32[]{:S(2)}, u32[]{:S(2)}) collective-permute-start(bf16[128,2048]{1,0:T(8,128)(2,1)S(1)} %collective-permute-done.49.refs_2_), channel_id=1, source_target_pairs={{0,8},{10,2},{8,16},{18,10},{16,24},{26,18},{24,28},{30,26},{28,20... | collective-permute-start | bytes 1572872 | tf_op jit(solution)/shard_map/ppermute | solution.py:404
  49.2 11.2 %collective-permute-start.52 = (bf16[128,2048]{1,0:T(8,128)(2,1)S(1)}, bf16[128,2048]{1,0:T(8,128)(2,1)S(1)}, u32[]{:S(2)}, u32[]{:S(2)}) collective-permute-start(bf16[128,2048]{1,0:T(8,128)(2,1)S(1)} %collective-permute-done.50.refs_3_), channel_id=1, source_target_pairs={{0,8},{10,2},{8,16},{18,10},{16,24},{26,18},{24,28},{30,26},{28,20... | collective-permute-start | bytes 1572872 | tf_op jit(solution)/shard_map/ppermute | solution.py:404
  49.3 18.3 %collective-permute-start.46 = (bf16[16,64,384]{2,1,0:T(8,128)(2,1)}, bf16[16,64,384]{2,1,0:T(8,128)(2,1)S(1)}, u32[]{:S(2)}, u32[]{:S(2)}) collective-permute-start(bf16[16,64,384]{2,1,0:T(8,128)(2,1)} %all-to-all-done.1), channel_id=1, source_target_pairs={{0,1},{1,0},{2,3},{3,2},{4,5},{5,4},{6,7},{7,6},{8,9},{9,8},{10,11... | collective-permute-start | bytes 2359304 | tf_op jit(solution)/shard_map/ppermute | solution.py:475
  56.7 17.2 %collective-permute-start.53 = (bf16[128,2048]{1,0:T(8,128)(2,1)S(1)}, bf16[128,2048]{1,0:T(8,128)(2,1)S(1)}, u32[]{:S(2)}, u32[]{:S(2)}) collective-permute-start(bf16[128,2048]{1,0:T(8,128)(2,1)S(1)} %collective-permute-done.51.refs_4_), channel_id=1, source_target_pairs={{0,8},{10,2},{8,16},{18,10},{16,24},{26,18},{24,28},{30,26},{28,20... | collective-permute-start | bytes 1572872 | tf_op jit(solution)/shard_map/ppermute | solution.py:404
  60.5 14.2 %collective-permute-start.54 = (bf16[128,2048]{1,0:T(8,128)(2,1)S(1)}, bf16[128,2048]{1,0:T(8,128)(2,1)S(1)}, u32[]{:S(2)}, u32[]{:S(2)}) collective-permute-start(bf16[128,2048]{1,0:T(8,128)(2,1)S(1)} %collective-permute-done.52.refs_5_), channel_id=1, source_target_pairs={{0,8},{10,2},{8,16},{18,10},{16,24},{26,18},{24,28},{30,26},{28,20... | collective-permute-start | bytes 1572872 | tf_op jit(solution)/shard_map/ppermute | solution.py:404
  70.2 9.9 %collective-permute-start.47 = (bf16[2048,384]{1,0:T(8,128)(2,1)}, bf16[2048,384]{1,0:T(8,128)(2,1)}, u32[]{:S(2)}, u32[]{:S(2)}) collective-permute-start(bf16[2048,384]{1,0:T(8,128)(2,1)} %bitcast.32), channel_id=1, source_target_pairs={{0,2},{2,0},{4,6},{6,4},{8,10},{10,8},{12,14},{14,12},{16,18},{18,... | collective-permute-start | bytes 4718600 | tf_op jit(solution)/shard_map/ppermute | solution.py:401
  75.4 55.8 %all-to-all-start.2 = ((bf16[16,64,1152]{2,1,0:T(8,128)(2,1)}), bf16[16,64,1152]{2,1,0:T(8,128)(2,1)}, u32[]{:S(2)}, u32[]{:S(2)}) async-start(bf16[16,64,1152]{2,1,0:T(8,128)(2,1)} %pad_maximum_fusion.8), calls=%async_computation.2 | async-start | bytes 4718592 | tf_op jit(solution)/shard_map/all_to_all | solution.py:471
  131.3 56.2 %collective-permute-start.66 = (bf16[16,64,1152]{2,1,0:T(8,128)(2,1)}, bf16[16,64,1152]{2,1,0:T(8,128)(2,1)}, u32[]{:S(2)}, u32[]{:S(2)}) collective-permute-start(bf16[16,64,1152]{2,1,0:T(8,128)(2,1)} %all-to-all-done.2), channel_id=1, source_target_pairs={{0,1},{1,0},{2,3},{3,2},{4,5},{5,4},{6,7},{7,6},{8,9},{9,8},{10,11... | collective-permute-start | bytes 7077896 | tf_op jit(solution)/shard_map/ppermute | solution.py:475
  139.5 9.5 %collective-permute-start = (bf16[128,2048]{1,0:T(8,128)(2,1)S(1)}, bf16[128,2048]{1,0:T(8,128)(2,1)S(1)}, u32[]{:S(2)}, u32[]{:S(2)}) collective-permute-start(bf16[128,2048]{1,0:T(8,128)(2,1)S(1)} %get-tuple-element.364), channel_id=1, source_target_pairs={{8,0},{2,10},{16,8},{10,18},{24,16},{18,26},{28,24},{26,30},{20,28... | collective-permute-start | bytes 1572872 | tf_op jit(solution)/shard_map/cond/branch_1_fun/ppermute | solution.py:407
  142.8 11.7 %collective-permute-start.2 = (bf16[128,2048]{1,0:T(8,128)(2,1)S(1)}, bf16[128,2048]{1,0:T(8,128)(2,1)S(1)}, u32[]{:S(2)}, u32[]{:S(2)}) collective-permute-start(bf16[128,2048]{1,0:T(8,128)(2,1)S(1)} %get-tuple-element.365), channel_id=1, source_target_pairs={{8,0},{2,10},{16,8},{10,18},{24,16},{18,26},{28,24},{26,30},{20,28... | collective-permute-start | bytes 1572872 | tf_op jit(solution)/shard_map/cond/branch_1_fun/ppermute | solution.py:407
  150.1 10.1 %collective-permute-start.1 = (bf16[128,2048]{1,0:T(8,128)(2,1)S(1)}, bf16[128,2048]{1,0:T(8,128)(2,1)S(1)}, u32[]{:S(2)}, u32[]{:S(2)}) collective-permute-start(bf16[128,2048]{1,0:T(8,128)(2,1)S(1)} %add_convert_fusion.4), channel_id=1, source_target_pairs={{8,0},{2,10},{16,8},{10,18},{24,16},{18,26},{28,24},{26,30},{20,28... | collective-permute-start | bytes 1572872 | tf_op jit(solution)/shard_map/cond/branch_1_fun/ppermute | solution.py:407
  155.8 10.1 %collective-permute-start.4 = (bf16[128,2048]{1,0:T(8,128)(2,1)S(1)}, bf16[128,2048]{1,0:T(8,128)(2,1)S(1)}, u32[]{:S(2)}, u32[]{:S(2)}) collective-permute-start(bf16[128,2048]{1,0:T(8,128)(2,1)S(1)} %add_convert_fusion.3), channel_id=1, source_target_pairs={{8,0},{2,10},{16,8},{10,18},{24,16},{18,26},{28,24},{26,30},{20,28... | collective-permute-start | bytes 1572872 | tf_op jit(solution)/shard_map/cond/branch_1_fun/ppermute | solution.py:407
  160.3 11.1 %collective-permute-start.3 = (bf16[128,2048]{1,0:T(8,128)(2,1)S(1)}, bf16[128,2048]{1,0:T(8,128)(2,1)S(1)}, u32[]{:S(2)}, u32[]{:S(2)}) collective-permute-start(bf16[128,2048]{1,0:T(8,128)(2,1)S(1)} %add_convert_fusion.2), channel_id=1, source_target_pairs={{8,0},{2,10},{16,8},{10,18},{24,16},{18,26},{28,24},{26,30},{20,28... | collective-permute-start | bytes 1572872 | tf_op jit(solution)/shard_map/cond/branch_1_fun/ppermute | solution.py:407
  165.9 11.1 %collective-permute-start.6 = (bf16[128,2048]{1,0:T(8,128)(2,1)S(1)}, bf16[128,2048]{1,0:T(8,128)(2,1)S(1)}, u32[]{:S(2)}, u32[]{:S(2)}) collective-permute-start(bf16[128,2048]{1,0:T(8,128)(2,1)S(1)} %add_convert_fusion.1), channel_id=1, source_target_pairs={{8,0},{2,10},{16,8},{10,18},{24,16},{18,26},{28,24},{26,30},{20,28... | collective-permute-start | bytes 1572872 | tf_op jit(solution)/shard_map/cond/branch_1_fun/ppermute | solution.py:407
  190.8 57.2 %collective-permute-start.67 = (bf16[2048,1152]{1,0:T(8,128)(2,1)S(1)}, bf16[2048,1152]{1,0:T(8,128)(2,1)S(1)}, u32[]{:S(2)}, u32[]{:S(2)}) collective-permute-start(bf16[2048,1152]{1,0:T(8,128)(2,1)S(1)} %bitcast.192), channel_id=1, source_target_pairs={{0,2},{2,0},{4,6},{6,4},{8,10},{10,8},{12,14},{14,12},{16,18},{18,... | collective-permute-start | bytes 14155784 | tf_op jit(solution)/shard_map/ppermute | solution.py:401
  192.3 8.7 %collective-permute-start.59 = (bf16[128,2048]{1,0:T(8,128)(2,1)S(1)}, bf16[128,2048]{1,0:T(8,128)(2,1)S(1)}, u32[]{:S(2)}, u32[]{:S(2)}) collective-permute-start(bf16[128,2048]{1,0:T(8,128)(2,1)S(1)} %get-tuple-element.361), channel_id=1, source_target_pairs={{0,8},{10,2},{8,16},{18,10},{16,24},{26,18},{24,28},{30,26},{28,20... | collective-permute-start | bytes 1572872 | tf_op jit(solution)/shard_map/ppermute | solution.py:404
  200.9 13.3 %collective-permute-start.61 = (bf16[128,2048]{1,0:T(8,128)(2,1)S(1)}, bf16[128,2048]{1,0:T(8,128)(2,1)S(1)}, u32[]{:S(2)}, u32[]{:S(2)}) collective-permute-start(bf16[128,2048]{1,0:T(8,128)(2,1)S(1)} %collective-permute-done.59), channel_id=1, source_target_pairs={{0,8},{10,2},{8,16},{18,10},{16,24},{26,18},{24,28},{30,26},{28,20... | collective-permute-start | bytes 1572872 | tf_op jit(solution)/shard_map/ppermute | solution.py:404
  208.6 11.2 %collective-permute-start.60 = (bf16[128,2048]{1,0:T(8,128)(2,1)S(1)}, bf16[128,2048]{1,0:T(8,128)(2,1)S(1)}, u32[]{:S(2)}, u32[]{:S(2)}) collective-permute-start(bf16[128,2048]{1,0:T(8,128)(2,1)S(1)} %collective-permute-done.58), channel_id=1, source_target_pairs={{0,8},{10,2},{8,16},{18,10},{16,24},{26,18},{24,28},{30,26},{28,20... | collective-permute-start | bytes 1572872 | tf_op jit(solution)/shard_map/ppermute | solution.py:404
  214.2 11.2 %collective-permute-start.71 = (bf16[128,2048]{1,0:T(8,128)(2,1)S(1)}, bf16[128,2048]{1,0:T(8,128)(2,1)S(1)}, u32[]{:S(2)}, u32[]{:S(2)}) collective-permute-start(bf16[128,2048]{1,0:T(8,128)(2,1)S(1)} %collective-permute-done.61), channel_id=1, source_target_pairs={{0,8},{10,2},{8,16},{18,10},{16,24},{26,18},{24,28},{30,26},{28,20... | collective-permute-start | bytes 1572872 | tf_op jit(solution)/shard_map/ppermute | solution.py:404
  219.8 11.2 %collective-permute-start.62 = (bf16[128,2048]{1,0:T(8,128)(2,1)S(1)}, bf16[128,2048]{1,0:T(8,128)(2,1)S(1)}, u32[]{:S(2)}, u32[]{:S(2)}) collective-permute-start(bf16[128,2048]{1,0:T(8,128)(2,1)S(1)} %collective-permute-done.60), channel_id=1, source_target_pairs={{0,8},{10,2},{8,16},{18,10},{16,24},{26,18},{24,28},{30,26},{28,20... | collective-permute-start | bytes 1572872 | tf_op jit(solution)/shard_map/ppermute | solution.py:404
  225.5 11.2 %collective-permute-start.72 = (bf16[128,2048]{1,0:T(8,128)(2,1)S(1)}, bf16[128,2048]{1,0:T(8,128)(2,1)S(1)}, u32[]{:S(2)}, u32[]{:S(2)}) collective-permute-start(bf16[128,2048]{1,0:T(8,128)(2,1)S(1)} %collective-permute-done.71), channel_id=1, source_target_pairs={{0,8},{10,2},{8,16},{18,10},{16,24},{26,18},{24,28},{30,26},{28,20... | collective-permute-start | bytes 1572872 | tf_op jit(solution)/shard_map/ppermute | solution.py:404
  232.1 10.2 %collective-permute-start.63 = (bf16[128,2048]{1,0:T(8,128)(2,1)S(1)}, bf16[128,2048]{1,0:T(8,128)(2,1)S(1)}, u32[]{:S(2)}, u32[]{:S(2)}) collective-permute-start(bf16[128,2048]{1,0:T(8,128)(2,1)S(1)} %bitcast.203), channel_id=1, source_target_pairs={{0,8},{10,2},{8,16},{18,10},{16,24},{26,18},{24,28},{30,26},{28,20... | collective-permute-start | bytes 1572872 | tf_op jit(solution)/shard_map/ppermute | solution.py:404
  233.6 14.4 %collective-permute-start.65 = (bf16[128,2048]{1,0:T(8,128)(2,1)S(1)}, bf16[128,2048]{1,0:T(8,128)(2,1)S(1)}, u32[]{:S(2)}, u32[]{:S(2)}) collective-permute-start(bf16[128,2048]{1,0:T(8,128)(2,1)S(1)} %collective-permute-done.64), channel_id=1, source_target_pairs={{0,8},{10,2},{8,16},{18,10},{16,24},{26,18},{24,28},{30,26},{28,20... | collective-permute-start | bytes 1572872 | tf_op jit(solution)/shard_map/ppermute | solution.py:404
  265.7 12.8 %collective-permute-start.70 = (bf16[128,2048]{1,0:T(8,128)(2,1)S(1)}, bf16[128,2048]{1,0:T(8,128)(2,1)S(1)}, u32[]{:S(2)}, u32[]{:S(2)}) collective-permute-start(bf16[128,2048]{1,0:T(8,128)(2,1)S(1)} %collective-permute-done.68), channel_id=1, source_target_pairs={{0,8},{10,2},{8,16},{18,10},{16,24},{26,18},{24,28},{30,26},{28,20... | collective-permute-start | bytes 1572872 | tf_op jit(solution)/shard_map/ppermute | solution.py:404
  272.9 11.2 %collective-permute-start.73 = (bf16[128,2048]{1,0:T(8,128)(2,1)S(1)}, bf16[128,2048]{1,0:T(8,128)(2,1)S(1)}, u32[]{:S(2)}, u32[]{:S(2)}) collective-permute-start(bf16[128,2048]{1,0:T(8,128)(2,1)S(1)} %collective-permute-done.69), channel_id=1, source_target_pairs={{0,8},{10,2},{8,16},{18,10},{16,24},{26,18},{24,28},{30,26},{28,20... | collective-permute-start | bytes 1572872 | tf_op jit(solution)/shard_map/ppermute | solution.py:404
  278.5 11.2 %collective-permute-start.74 = (bf16[128,2048]{1,0:T(8,128)(2,1)S(1)}, bf16[128,2048]{1,0:T(8,128)(2,1)S(1)}, u32[]{:S(2)}, u32[]{:S(2)}) collective-permute-start(bf16[128,2048]{1,0:T(8,128)(2,1)S(1)} %collective-permute-done.70), channel_id=1, source_target_pairs={{0,8},{10,2},{8,16},{18,10},{16,24},{26,18},{24,28},{30,26},{28,20... | collective-permute-start | bytes 1572872 | tf_op jit(solution)/shard_map/ppermute | solution.py:404
  308.2 11.1 %collective-permute-start.18 = (bf16[128,2048]{1,0:T(8,128)(2,1)}, bf16[128,2048]{1,0:T(8,128)(2,1)}, u32[]{:S(2)}, u32[]{:S(2)}) collective-permute-start(bf16[128,2048]{1,0:T(8,128)(2,1)} %add_convert_fusion.11), channel_id=1, source_target_pairs={{8,0},{2,10},{16,8},{10,18},{24,16},{18,26},{28,24},{26,30},{20,28... | collective-permute-start | bytes 1572872 | tf_op jit(solution)/shard_map/cond/branch_1_fun/ppermute | solution.py:407
  316.3 37.4 %collective-permute-start.25 = (bf16[2048,384]{1,0:T(8,128)(2,1)S(1)}, bf16[2048,384]{1,0:T(8,128)(2,1)S(1)}, u32[]{:S(2)}, u32[]{:S(2)}) collective-permute-start(bf16[2048,384]{1,0:T(8,128)(2,1)S(1)} %fusion.2), channel_id=1, source_target_pairs={{0,2},{2,0},{4,6},{6,4},{8,10},{10,8},{12,14},{14,12},{16,18},{18,... | collective-permute-start | bytes 4718600 | tf_op jit(solution)/shard_map/cond/branch_1_fun/ppermute | solution.py:401
  317.6 9.8 %collective-permute-start.20 = (bf16[128,2048]{1,0:T(8,128)(2,1)S(1)}, bf16[128,2048]{1,0:T(8,128)(2,1)S(1)}, u32[]{:S(2)}, u32[]{:S(2)}) collective-permute-start(bf16[128,2048]{1,0:T(8,128)(2,1)S(1)} %copy-done.52), channel_id=1, source_target_pairs={{8,0},{2,10},{16,8},{10,18},{24,16},{18,26},{28,24},{26,30},{20,28... | collective-permute-start | bytes 1572872 | tf_op jit(solution)/shard_map/cond/branch_1_fun/ppermute | solution.py:407
  323.3 32.4 %collective-permute-start.26 = (bf16[2048,768]{1,0:T(8,128)(2,1)S(1)}, bf16[2048,768]{1,0:T(8,128)(2,1)S(1)}, u32[]{:S(2)}, u32[]{:S(2)}) collective-permute-start(bf16[2048,768]{1,0:T(8,128)(2,1)S(1)} %fusion), channel_id=1, source_target_pairs={{0,2},{2,0},{4,6},{6,4},{8,10},{10,8},{12,14},{14,12},{16,18},{18,... | collective-permute-start | bytes 9437192 | tf_op jit(solution)/shard_map/cond/branch_1_fun/ppermute | solution.py:401
  330.0 9.8 %collective-permute-start.22 = (bf16[128,2048]{1,0:T(8,128)(2,1)S(1)}, bf16[128,2048]{1,0:T(8,128)(2,1)S(1)}, u32[]{:S(2)}, u32[]{:S(2)}) collective-permute-start(bf16[128,2048]{1,0:T(8,128)(2,1)S(1)} %add_convert_fusion.9), channel_id=1, source_target_pairs={{8,0},{2,10},{16,8},{10,18},{24,16},{18,26},{28,24},{26,30},{20,28... | collective-permute-start | bytes 1572872 | tf_op jit(solution)/shard_map/cond/branch_1_fun/ppermute | solution.py:407
  338.0 17.4 %collective-permute-start.21 = (bf16[128,2048]{1,0:T(8,128)(2,1)S(1)}, bf16[128,2048]{1,0:T(8,128)(2,1)S(1)}, u32[]{:S(2)}, u32[]{:S(2)}) collective-permute-start(bf16[128,2048]{1,0:T(8,128)(2,1)S(1)} %add_convert_fusion.8), channel_id=1, source_target_pairs={{8,0},{2,10},{16,8},{10,18},{24,16},{18,26},{28,24},{26,30},{20,28... | collective-permute-start | bytes 1572872 | tf_op jit(solution)/shard_map/cond/branch_1_fun/ppermute | solution.py:407
  339.9 12.1 %collective-permute-start.23 = (bf16[128,2048]{1,0:T(8,128)(2,1)S(1)}, bf16[128,2048]{1,0:T(8,128)(2,1)S(1)}, u32[]{:S(2)}, u32[]{:S(2)}) collective-permute-start(bf16[128,2048]{1,0:T(8,128)(2,1)S(1)} %add_convert_fusion.7), channel_id=1, source_target_pairs={{8,0},{2,10},{16,8},{10,18},{24,16},{18,26},{28,24},{26,30},{20,28... | collective-permute-start | bytes 1572872 | tf_op jit(solution)/shard_map/cond/branch_1_fun/ppermute | solution.py:407
  359.2 55.7 %collective-permute-start.77 = (bf16[16,64,768]{2,1,0:T(8,128)(2,1)}, bf16[16,64,768]{2,1,0:T(8,128)(2,1)}, u32[]{:S(2)}, u32[]{:S(2)}) collective-permute-start(bf16[16,64,768]{2,1,0:T(8,128)(2,1)} %get-tuple-element.322), channel_id=1, source_target_pairs={{0,1},{1,0},{2,3},{3,2},{4,5},{5,4},{6,7},{7,6},{8,9},{9,8},{10,11... | collective-permute-start | bytes 4718600 | tf_op jit(solution)/shard_map/ppermute | solution.py:475
  359.5 53.8 %collective-permute-start.76 = (bf16[16,64,384]{2,1,0:T(8,128)(2,1)}, bf16[16,64,384]{2,1,0:T(8,128)(2,1)}, u32[]{:S(2)}, u32[]{:S(2)}) collective-permute-start(bf16[16,64,384]{2,1,0:T(8,128)(2,1)} %get-tuple-element.320), channel_id=1, source_target_pairs={{0,1},{1,0},{2,3},{3,2},{4,5},{5,4},{6,7},{7,6},{8,9},{9,8},{10,11... | collective-permute-start | bytes 2359304 | tf_op jit(solution)/shard_map/ppermute | solution.py:475
  364.4 8.7 %collective-permute-start.27 = (bf16[128,2048]{1,0:T(8,128)(2,1)S(1)}, bf16[128,2048]{1,0:T(8,128)(2,1)S(1)}, u32[]{:S(2)}, u32[]{:S(2)}) collective-permute-start(bf16[128,2048]{1,0:T(8,128)(2,1)S(1)} %get-tuple-element.133), channel_id=1, source_target_pairs={{0,8},{10,2},{8,16},{18,10},{16,24},{26,18},{24,28},{30,26},{28,20... | collective-permute-start | bytes 1572872 | tf_op jit(solution)/shard_map/cond/branch_1_fun/ppermute | solution.py:404
  366.0 12.8 %collective-permute-start.29 = (bf16[128,2048]{1,0:T(8,128)(2,1)S(1)}, bf16[128,2048]{1,0:T(8,128)(2,1)S(1)}, u32[]{:S(2)}, u32[]{:S(2)}) collective-permute-start(bf16[128,2048]{1,0:T(8,128)(2,1)S(1)} %collective-permute-done.28), channel_id=1, source_target_pairs={{0,8},{10,2},{8,16},{18,10},{16,24},{26,18},{24,28},{30,26},{28,20... | collective-permute-start | bytes 1572872 | tf_op jit(solution)/shard_map/cond/branch_1_fun/ppermute | solution.py:404
  373.1 11.2 %collective-permute-start.30 = (bf16[128,2048]{1,0:T(8,128)(2,1)S(1)}, bf16[128,2048]{1,0:T(8,128)(2,1)S(1)}, u32[]{:S(2)}, u32[]{:S(2)}) collective-permute-start(bf16[128,2048]{1,0:T(8,128)(2,1)S(1)} %collective-permute-done.27), channel_id=1, source_target_pairs={{0,8},{10,2},{8,16},{18,10},{16,24},{26,18},{24,28},{30,26},{28,20... | collective-permute-start | bytes 1572872 | tf_op jit(solution)/shard_map/cond/branch_1_fun/ppermute | solution.py:404
  378.8 11.2 %collective-permute-start.31 = (bf16[128,2048]{1,0:T(8,128)(2,1)S(1)}, bf16[128,2048]{1,0:T(8,128)(2,1)S(1)}, u32[]{:S(2)}, u32[]{:S(2)}) collective-permute-start(bf16[128,2048]{1,0:T(8,128)(2,1)S(1)} %collective-permute-done.29), channel_id=1, source_target_pairs={{0,8},{10,2},{8,16},{18,10},{16,24},{26,18},{24,28},{30,26},{28,20... | collective-permute-start | bytes 1572872 | tf_op jit(solution)/shard_map/cond/branch_1_fun/ppermute | solution.py:404
  384.4 11.2 %collective-permute-start.32 = (bf16[128,2048]{1,0:T(8,128)(2,1)S(1)}, bf16[128,2048]{1,0:T(8,128)(2,1)S(1)}, u32[]{:S(2)}, u32[]{:S(2)}) collective-permute-start(bf16[128,2048]{1,0:T(8,128)(2,1)S(1)} %collective-permute-done.30), channel_id=1, source_target_pairs={{0,8},{10,2},{8,16},{18,10},{16,24},{26,18},{24,28},{30,26},{28,20... | collective-permute-start | bytes 1572872 | tf_op jit(solution)/shard_map/cond/branch_1_fun/ppermute | solution.py:404
  390.0 11.2 %collective-permute-start.33 = (bf16[128,2048]{1,0:T(8,128)(2,1)S(1)}, bf16[128,2048]{1,0:T(8,128)(2,1)S(1)}, u32[]{:S(2)}, u32[]{:S(2)}) collective-permute-start(bf16[128,2048]{1,0:T(8,128)(2,1)S(1)} %collective-permute-done.31), channel_id=1, source_target_pairs={{0,8},{10,2},{8,16},{18,10},{16,24},{26,18},{24,28},{30,26},{28,20... | collective-permute-start | bytes 1572872 | tf_op jit(solution)/shard_map/cond/branch_1_fun/ppermute | solution.py:404
  395.6 11.2 %collective-permute-start.34 = (bf16[128,2048]{1,0:T(8,128)(2,1)S(1)}, bf16[128,2048]{1,0:T(8,128)(2,1)S(1)}, u32[]{:S(2)}, u32[]{:S(2)}) collective-permute-start(bf16[128,2048]{1,0:T(8,128)(2,1)S(1)} %collective-permute-done.32), channel_id=1, source_target_pairs={{0,8},{10,2},{8,16},{18,10},{16,24},{26,18},{24,28},{30,26},{28,20... | collective-permute-start | bytes 1572872 | tf_op jit(solution)/shard_map/cond/branch_1_fun/ppermute | solution.py:404
  419.7 114.2 %all-to-all-start.3 = ((bf16[16,64,1152]{2,1,0:T(8,128)(2,1)}), bf16[16,64,1152]{2,1,0:T(8,128)(2,1)}, u32[]{:S(2)}, u32[]{:S(2)}) async-start(bf16[16,64,1152]{2,1,0:T(8,128)(2,1)} %pad_maximum_fusion.9), calls=%async_computation.3 | async-start | bytes 4718592 | tf_op jit(solution)/shard_map/all_to_all | solution.py:471
  450.4 31.4 %collective-permute-start.36 = (bf16[128,2048]{1,0:T(8,128)(2,1)}, bf16[128,2048]{1,0:T(8,128)(2,1)}, u32[]{:S(2)}, u32[]{:S(2)}) collective-permute-start(bf16[128,2048]{1,0:T(8,128)(2,1)} %get-tuple-element.374), channel_id=1, source_target_pairs={{8,0},{2,10},{16,8},{10,18},{24,16},{18,26},{28,24},{26,30},{20,28... | collective-permute-start | bytes 1572872 | tf_op jit(solution)/shard_map/cond/branch_1_fun/ppermute | solution.py:407
  451.8 35.7 %collective-permute-start.38 = (bf16[128,2048]{1,0:T(8,128)(2,1)}, bf16[128,2048]{1,0:T(8,128)(2,1)S(1)}, u32[]{:S(2)}, u32[]{:S(2)}) collective-permute-start(bf16[128,2048]{1,0:T(8,128)(2,1)} %get-tuple-element.375), channel_id=1, source_target_pairs={{8,0},{2,10},{16,8},{10,18},{24,16},{18,26},{28,24},{26,30},{20,28... | collective-permute-start | bytes 1572872 | tf_op jit(solution)/shard_map/cond/branch_1_fun/ppermute | solution.py:407
  483.2 22.0 %collective-permute-start.37 = (bf16[128,2048]{1,0:T(8,128)(2,1)S(1)}, bf16[128,2048]{1,0:T(8,128)(2,1)S(1)}, u32[]{:S(2)}, u32[]{:S(2)}) collective-permute-start(bf16[128,2048]{1,0:T(8,128)(2,1)S(1)} %add_convert_fusion.18), channel_id=1, source_target_pairs={{8,0},{2,10},{16,8},{10,18},{24,16},{18,26},{28,24},{26,30},{20,28... | collective-permute-start | bytes 1572872 | tf_op jit(solution)/shard_map/cond/branch_1_fun/ppermute | solution.py:407
  488.7 19.2 %collective-permute-start.40 = (bf16[128,2048]{1,0:T(8,128)(2,1)S(1)}, bf16[128,2048]{1,0:T(8,128)(2,1)S(1)}, u32[]{:S(2)}, u32[]{:S(2)}) collective-permute-start(bf16[128,2048]{1,0:T(8,128)(2,1)S(1)} %add_convert_fusion.17), channel_id=1, source_target_pairs={{8,0},{2,10},{16,8},{10,18},{24,16},{18,26},{28,24},{26,30},{20,28... | collective-permute-start | bytes 1572872 | tf_op jit(solution)/shard_map/cond/branch_1_fun/ppermute | solution.py:407
  505.2 16.6 %collective-permute-start.44 = (bf16[2048,384]{0,1:T(8,128)(2,1)}, bf16[2048,384]{0,1:T(8,128)(2,1)}, u32[]{:S(2)}, u32[]{:S(2)}) collective-permute-start(bf16[2048,384]{0,1:T(8,128)(2,1)} %pad_maximum_fusion.1), channel_id=1, source_target_pairs={{0,2},{2,0},{4,6},{6,4},{8,10},{10,8},{12,14},{14,12},{16,18},{18,... | collective-permute-start | bytes 4718600 | tf_op jit(solution)/shard_map/cond/branch_1_fun/ppermute | solution.py:401
  508.8 11.6 %collective-permute-start.42 = (bf16[128,2048]{1,0:T(8,128)(2,1)}, bf16[128,2048]{1,0:T(8,128)(2,1)}, u32[]{:S(2)}, u32[]{:S(2)}) collective-permute-start(bf16[128,2048]{1,0:T(8,128)(2,1)} %add_convert_fusion.15), channel_id=1, source_target_pairs={{8,0},{2,10},{16,8},{10,18},{24,16},{18,26},{28,24},{26,30},{20,28... | collective-permute-start | bytes 1572872 | tf_op jit(solution)/shard_map/cond/branch_1_fun/ppermute | solution.py:407
  516.9 14.2 %collective-permute-start.41 = (bf16[128,2048]{1,0:T(8,128)(2,1)}, bf16[128,2048]{1,0:T(8,128)(2,1)}, u32[]{:S(2)}, u32[]{:S(2)}) collective-permute-start(bf16[128,2048]{1,0:T(8,128)(2,1)} %add_convert_fusion.14), channel_id=1, source_target_pairs={{8,0},{2,10},{16,8},{10,18},{24,16},{18,26},{28,24},{26,30},{20,28... | collective-permute-start | bytes 1572872 | tf_op jit(solution)/shard_map/cond/branch_1_fun/ppermute | solution.py:407
  520.4 10.7 %collective-permute-start.43 = (bf16[128,2048]{1,0:T(8,128)(2,1)}, bf16[128,2048]{1,0:T(8,128)(2,1)}, u32[]{:S(2)}, u32[]{:S(2)}) collective-permute-start(bf16[128,2048]{1,0:T(8,128)(2,1)} %collective-permute-done.42), channel_id=1, source_target_pairs={{0,2},{2,0},{4,6},{6,4},{8,10},{10,8},{12,14},{14,12},{16,18},{18,... | collective-permute-start | bytes 1572872 | tf_op jit(solution)/shard_map/cond/branch_1_fun/ppermute | solution.py:401
  536.6 12.7 %collective-permute-start.10 = (bf16[128,2048]{1,0:T(8,128)(2,1)S(1)}, bf16[128,2048]{1,0:T(8,128)(2,1)S(1)}, u32[]{:S(2)}, u32[]{:S(2)}) collective-permute-start(bf16[128,2048]{1,0:T(8,128)(2,1)S(1)} %get-tuple-element.387), channel_id=1, source_target_pairs={{8,0},{2,10},{16,8},{10,18},{24,16},{18,26},{28,24},{26,30},{20,28... | collective-permute-start | bytes 1572872 | tf_op jit(solution)/shard_map/cond/branch_1_fun/ppermute | solution.py:407
  536.6 19.9 %collective-permute-start.11 = (bf16[1040,384]{1,0:T(8,128)(2,1)}, bf16[1040,384]{1,0:T(8,128)(2,1)S(1)}, u32[]{:S(2)}, u32[]{:S(2)}) collective-permute-start(bf16[1040,384]{1,0:T(8,128)(2,1)} %get-tuple-element.188), channel_id=1, source_target_pairs={{0,1},{1,0},{2,3},{3,2},{4,5},{5,4},{6,7},{7,6},{8,9},{9,8},{10,11... | collective-permute-start | bytes 2396168 | tf_op jit(solution)/shard_map/cond/branch_1_fun/ppermute | solution.py:475
  545.6 19.1 %collective-permute-start.9 = (bf16[128,2048]{1,0:T(8,128)(2,1)}, bf16[128,2048]{1,0:T(8,128)(2,1)}, u32[]{:S(2)}, u32[]{:S(2)}) collective-permute-start(bf16[128,2048]{1,0:T(8,128)(2,1)} %add_convert_fusion.23), channel_id=1, source_target_pairs={{8,0},{2,10},{16,8},{10,18},{24,16},{18,26},{28,24},{26,30},{20,28... | collective-permute-start | bytes 1572872 | tf_op jit(solution)/shard_map/cond/branch_1_fun/ppermute | solution.py:407
  551.2 16.2 %collective-permute-start.13 = (bf16[128,2048]{1,0:T(8,128)(2,1)}, bf16[128,2048]{1,0:T(8,128)(2,1)}, u32[]{:S(2)}, u32[]{:S(2)}) collective-permute-start(bf16[128,2048]{1,0:T(8,128)(2,1)} %add_convert_fusion.22), channel_id=1, source_target_pairs={{8,0},{2,10},{16,8},{10,18},{24,16},{18,26},{28,24},{26,30},{20,28... | collective-permute-start | bytes 1572872 | tf_op jit(solution)/shard_map/cond/branch_1_fun/ppermute | solution.py:407
  558.7 52.2 %all-to-all-start = ((bf16[16,80,384]{2,1,0:T(8,128)(2,1)}), bf16[16,80,384]{2,1,0:T(8,128)(2,1)}, u32[]{:S(2)}, u32[]{:S(2)}) async-start(bf16[16,80,384]{2,1,0:T(8,128)(2,1)} %pad_maximum_fusion.3), calls=%async_computation | async-start | bytes 1966080 | tf_op jit(solution)/shard_map/cond/branch_1_fun/all_to_all | solution.py:471
  566.1 26.1 %collective-permute-start.12 = (bf16[128,2048]{1,0:T(8,128)(2,1)S(1)}, bf16[128,2048]{1,0:T(8,128)(2,1)S(1)}, u32[]{:S(2)}, u32[]{:S(2)}) collective-permute-start(bf16[128,2048]{1,0:T(8,128)(2,1)S(1)} %add_convert_fusion.21), channel_id=1, source_target_pairs={{8,0},{2,10},{16,8},{10,18},{24,16},{18,26},{28,24},{26,30},{20,28... | collective-permute-start | bytes 1572872 | tf_op jit(solution)/shard_map/cond/branch_1_fun/ppermute | solution.py:407
  568.7 29.1 %collective-permute-start.15 = (bf16[128,2048]{1,0:T(8,128)(2,1)S(1)}, bf16[128,2048]{1,0:T(8,128)(2,1)S(1)}, u32[]{:S(2)}, u32[]{:S(2)}) collective-permute-start(bf16[128,2048]{1,0:T(8,128)(2,1)S(1)} %add_convert_fusion.20), channel_id=1, source_target_pairs={{8,0},{2,10},{16,8},{10,18},{24,16},{18,26},{28,24},{26,30},{20,28... | collective-permute-start | bytes 1572872 | tf_op jit(solution)/shard_map/cond/branch_1_fun/ppermute | solution.py:407
  593.4 15.3 %collective-permute-start.14 = (bf16[128,2048]{1,0:T(8,128)(2,1)S(1)}, bf16[128,2048]{1,0:T(8,128)(2,1)S(1)}, u32[]{:S(2)}, u32[]{:S(2)}) collective-permute-start(bf16[128,2048]{1,0:T(8,128)(2,1)S(1)} %add_convert_fusion.19), channel_id=1, source_target_pairs={{8,0},{2,10},{16,8},{10,18},{24,16},{18,26},{28,24},{26,30},{20,28... | collective-permute-start | bytes 1572872 | tf_op jit(solution)/shard_map/cond/branch_1_fun/ppermute | solution.py:407
  597.8 10.8 %collective-permute-start.16 = (bf16[128,2048]{1,0:T(8,128)(2,1)S(1)}, bf16[128,2048]{1,0:T(8,128)(2,1)S(1)}, u32[]{:S(2)}, u32[]{:S(2)}) collective-permute-start(bf16[128,2048]{1,0:T(8,128)(2,1)S(1)} %collective-permute-done.15), channel_id=1, source_target_pairs={{0,2},{2,0},{4,6},{6,4},{8,10},{10,8},{12,14},{14,12},{16,18},{18,... | collective-permute-start | bytes 1572872 | tf_op jit(solution)/shard_map/cond/branch_1_fun/ppermute | solution.py:401
  (88 other events, 813.6 us)
